TPU v7x, 32 devices: a whole 2x2x4 slice. The times are simulated.
32 devices in a mesh: segment: 2 (over x), slab: 16 (over z, y, core).
Axes of the slice: x: 2, y: 2, z: 4, core: 2. Of those that a mesh axis runs over, the one named last changes fastest.
Arguments:
- activations: bfloat16 [2, 2, 64, 8, 8, 128], P('segment', None, 'slab'), may hold values from -6 to 6
- weights: bfloat16 [2, 3456, 128], P('segment'), may hold values from -0.109375 to 0.109375
- out_grad: bfloat16 [2, 64, 8, 8, 128], P(None, 'slab'), may hold values from -6 to 6
Outputs:
- update: float32 [2, 3456, 128], P('segment')
- input_grads: bfloat16 [2, 2, 64, 8, 8, 128], P('segment', None, 'slab')
All inputs are finite; a program needn't handle non-finite values.
Results may differ from a plain program's by a relative error of at most 0.017.
Values may be sent and summed in bfloat16 or wider, within the bound.
No kernel may reach another device: no remote copies, remote signals or barrier semaphores. Data moves between devices by JAX's collectives and lax.ppermute only.
A program may use at most 64 MiB of HBM per device.

v0:
```python
import math

import jax
import jax.numpy as jnp
from jax import lax
from jax.sharding import PartitionSpec as P


def padded(cells, sides, width):
    for axis, dim in sides:
        count = lax.axis_size(axis)
        ends = count - 1
        head = lax.slice_in_dim(cells, 0, width, axis=dim)
        tail = lax.slice_in_dim(cells, cells.shape[dim] - width, cells.shape[dim], axis=dim)
        cells = jnp.concatenate(
            [
                lax.ppermute(tail, axis, [(i, (i + 1) % count) for i in range(ends)]),
                cells,
                lax.ppermute(head, axis, [((i + 1) % count, i) for i in range(ends)]),
            ],
            axis=dim,
        )
    return cells


def from_behind(block, axis, distance):
    devices = range(lax.axis_size(axis))
    route = [(i - distance, i) for i in devices if i - distance in devices]
    return lax.ppermute(block, axis, route)


def patches_of(rimmed):
    depth_count = rimmed.shape[0] - 2
    width_count = rimmed.shape[1]
    height = rimmed.shape[2]
    padded_all = jnp.pad(rimmed, ((0, 0), (1, 1), (1, 1), (0, 0)))
    pieces = []
    for offset in range(27):
        depth_off = offset // 9
        width_off = offset // 3 % 3
        height_off = offset % 3
        pieces.append(
            padded_all[
                depth_off : depth_off + depth_count,
                width_off : width_off + width_count,
                height_off : height_off + height,
            ]
        )
    joined = jnp.concatenate(pieces, axis=-1)
    return joined.reshape(depth_count * width_count * height, joined.shape[-1])


def shards(activations, weights, out_grad):
    stored_inputs = activations[0]
    weight = weights[0]
    channels = weight.shape[1]
    micro_count, depth_count, width_count, height = stored_inputs.shape[:4]
    cell_count = depth_count * width_count * height
    segments = lax.axis_size("segment")
    sindex = lax.axis_index("segment")
    flipped = (
        weight.reshape(27, channels, channels)[::-1]
        .transpose(0, 2, 1)
        .reshape(27 * channels, channels)
    )

    def advance(counter, state_tuple):
        incoming, partial_value, gradients = state_tuple
        micro_index = counter - (segments - 1 - sindex)
        active = (micro_index >= 0) & (micro_index < micro_count)
        chosen = jnp.clip(micro_index, 0, micro_count - 1)
        one_input = lax.dynamic_index_in_dim(stored_inputs, chosen, 0, False)
        rimmed_one = padded(one_input, (("slab", 0),), 1)
        patches = patches_of(rimmed_one)
        preact = jnp.dot(patches, weight, preferred_element_type=jnp.float32)
        from_loss = lax.dynamic_index_in_dim(out_grad, chosen, 0, False)
        upstream = (
            jnp.where(sindex == segments - 1, from_loss, incoming)
            .astype(jnp.float32)
            .reshape(cell_count, channels)
        )
        sigval = jax.nn.sigmoid(preact)
        deltas = jnp.where(active, upstream * sigval * (1.0 + preact * (1.0 - sigval)), 0.0).astype(
            jnp.bfloat16
        )
        partial_value = partial_value + lax.dot_general(
            patches, deltas, (((0,), (0,)), ((), ())), preferred_element_type=jnp.float32
        )
        delta_rim = padded(
            deltas.reshape(depth_count, width_count, height, channels), (("slab", 0),), 1
        )
        backward = jnp.dot(patches_of(delta_rim), flipped, preferred_element_type=jnp.float32)
        result = (
            (upstream + backward)
            .astype(jnp.bfloat16)
            .reshape(depth_count, width_count, height, channels)
        )
        current = lax.dynamic_index_in_dim(gradients, chosen, 0, False)
        gradients = lax.dynamic_update_index_in_dim(
            gradients, jnp.where(active, result, current), chosen, 0
        )
        incoming = from_behind(result, "segment", -1)
        return (incoming, partial_value, gradients)

    start_state = (
        jnp.zeros((depth_count, width_count, height, channels), jnp.bfloat16),
        jnp.zeros((27 * channels, channels), jnp.float32),
        jnp.zeros(stored_inputs.shape, jnp.bfloat16),
    )
    final_state = lax.fori_loop(0, segments + micro_count - 1, advance, start_state)
    partial_value = final_state[1]
    gradients = final_state[2]
    bound_value = math.sqrt(27.0 * channels * channels * segments)
    summed = lax.psum(partial_value, "slab")
    squares = lax.psum(jnp.sum(summed * summed), "segment")
    factor = jnp.minimum(1.0, bound_value / (jnp.sqrt(squares) + 1e-06))
    update = summed * factor
    return (update[None], gradients[None])


def solution(mesh):
    return jax.shard_map(
        shards,
        mesh=mesh,
        in_specs=(
            P("segment", None, "slab", None, None, None),
            P("segment", None, None),
            P(None, "slab", None, None, None),
        ),
        out_specs=(P("segment", None, None), P("segment", None, "slab", None, None, None)),
        check_vma=False,
    )
```

profile of v0, /device:TPU:0, one launch (start us, length us, event | category | flops | bytes accessed | tf_op | source)
XLA Modules:
  0.0 205.5 jit_solution(9570711436723103198)
XLA Ops:
  7.2 2.3 %copy.5 = bf16[27,128,128]{1,2,0:T(8,128)(2,1)} copy(bf16[27,128,128]{2,1,0:T(8,128)(2,1)} %bitcast.282) | data formatting | bytes 1769472 | tf_op jit(solution)/shard_map/reshape;squeeze | solution.py:62
  9.5 1.2 rev.3
  10.8 71.9 %while.20 = (s32[]{:T(128)}, bf16[4,8,8,128]{3,2,1,0:T(8,128)(2,1)S(1)}, f32[3456,128]{1,0:T(8,128)S(1)}, bf16[2,4,8,8,128]{4,3,2,1,0:T(8,128)(2,1)S(1)}, pred[]...) while((s32[]{:T(128)}, ...), condition=%wide.region_1.2_spmd.clone, body=%wide.region_0.1_spmd.clone.sunk | while | flops 684656640 | bytes 30519764 | solution.py:110
  10.9 1.3 collective-permute-start
  12.2 3.0 %collective-permute-start.1 = (bf16[1,8,8,128]{3,2,1,0:T(8,128)(2,1)S(1)}, bf16[1,8,8,128]{3,2,1,0:T(8,128)(2,1)S(1)}, u32[]{:S(2)}, u32[]{:S(2)}) collective-permute-start(bf16[1,8,8,128]{3,2,1,0:T(8,128)(2,1)S(1)} %get-tuple-element.463), channel_id=1, source_target_pairs={{0,1},{1,2},{2,3},{3,4},{4,5},{5,6},{6,7},{7,8},{8,9},{9,10},{10,1... | collective-permute-start | bytes 49160 | tf_op jit(solution)/shard_map/while/body/eval_jaxpr/ppermute | solution.py:17
  15.3 0.7 collective-permute-done.1
  16.2 0.2 fusion.56
  17.1 0.5 copy-done.4
  17.6 0.7 fusion.57
  18.3 1.3 collective-permute-start.2
  19.6 5.1 %collective-permute-start.3 = (bf16[1,8,8,128]{3,2,1,0:T(8,128)(2,1)S(1)}, bf16[1,8,8,128]{3,2,1,0:T(8,128)(2,1)S(1)}, u32[]{:S(2)}, u32[]{:S(2)}) collective-permute-start(bf16[1,8,8,128]{3,2,1,0:T(8,128)(2,1)S(1)} %get-tuple-element.492), channel_id=1, source_target_pairs={{0,1},{1,2},{2,3},{3,4},{4,5},{5,6},{6,7},{7,8},{8,9},{9,10},{10,1... | collective-permute-start | bytes 49160 | tf_op jit(solution)/shard_map/while/body/eval_jaxpr/ppermute | solution.py:17
  24.8 1.2 convolution_add_fusion.3
  26.1 0.2 fusion.59
  26.7 0.1 fusion.60
  27.1 0.6 fusion.61
  27.7 1.3 collective-permute-start.4
  29.1 4.8 %collective-permute-done.4 = bf16[4,8,8,128]{3,2,1,0:T(8,128)(2,1)S(1)} collective-permute-done((bf16[4,8,8,128]{3,2,1,0:T(8,128)(2,1)S(1)}, bf16[4,8,8,128]{3,2,1,0:T(8,128)(2,1)S(1)}, u32[]{:S(2)}, u32[]{:S(2)}) %collective-permute-start.4) | collective-permute-done | bytes 65568 | tf_op jit(solution)/shard_map/while/body/eval_jaxpr/ppermute | solution.py:29
  33.9 1.3 collective-permute-start
  35.2 3.7 %collective-permute-start.1 = (bf16[1,8,8,128]{3,2,1,0:T(8,128)(2,1)S(1)}, bf16[1,8,8,128]{3,2,1,0:T(8,128)(2,1)S(1)}, u32[]{:S(2)}, u32[]{:S(2)}) collective-permute-start(bf16[1,8,8,128]{3,2,1,0:T(8,128)(2,1)S(1)} %get-tuple-element.463), channel_id=1, source_target_pairs={{0,1},{1,2},{2,3},{3,4},{4,5},{5,6},{6,7},{7,8},{8,9},{9,10},{10,1... | collective-permute-start | bytes 49160 | tf_op jit(solution)/shard_map/while/body/eval_jaxpr/ppermute | solution.py:17
  39.0 0.7 collective-permute-done.1
  39.9 0.2 fusion.56
  40.8 0.5 copy-done.4
  41.3 0.7 fusion.57
  42.0 1.3 collective-permute-start.2
  43.3 6.1 %collective-permute-start.3 = (bf16[1,8,8,128]{3,2,1,0:T(8,128)(2,1)S(1)}, bf16[1,8,8,128]{3,2,1,0:T(8,128)(2,1)S(1)}, u32[]{:S(2)}, u32[]{:S(2)}) collective-permute-start(bf16[1,8,8,128]{3,2,1,0:T(8,128)(2,1)S(1)} %get-tuple-element.492), channel_id=1, source_target_pairs={{0,1},{1,2},{2,3},{3,4},{4,5},{5,6},{6,7},{7,8},{8,9},{9,10},{10,1... | collective-permute-start | bytes 49160 | tf_op jit(solution)/shard_map/while/body/eval_jaxpr/ppermute | solution.py:17
  49.4 1.2 convolution_add_fusion.3
  50.7 0.2 fusion.59
  51.7 0.6 fusion.61
  52.3 1.3 collective-permute-start.4
  53.7 4.8 %collective-permute-done.4 = bf16[4,8,8,128]{3,2,1,0:T(8,128)(2,1)S(1)} collective-permute-done((bf16[4,8,8,128]{3,2,1,0:T(8,128)(2,1)S(1)}, bf16[4,8,8,128]{3,2,1,0:T(8,128)(2,1)S(1)}, u32[]{:S(2)}, u32[]{:S(2)}) %collective-permute-start.4) | collective-permute-done | bytes 65568 | tf_op jit(solution)/shard_map/while/body/eval_jaxpr/ppermute | solution.py:29
  58.5 1.3 collective-permute-start
  59.8 3.7 %collective-permute-start.1 = (bf16[1,8,8,128]{3,2,1,0:T(8,128)(2,1)S(1)}, bf16[1,8,8,128]{3,2,1,0:T(8,128)(2,1)S(1)}, u32[]{:S(2)}, u32[]{:S(2)}) collective-permute-start(bf16[1,8,8,128]{3,2,1,0:T(8,128)(2,1)S(1)} %get-tuple-element.463), channel_id=1, source_target_pairs={{0,1},{1,2},{2,3},{3,4},{4,5},{5,6},{6,7},{7,8},{8,9},{9,10},{10,1... | collective-permute-start | bytes 49160 | tf_op jit(solution)/shard_map/while/body/eval_jaxpr/ppermute | solution.py:17
  63.6 0.7 collective-permute-done.1
  64.5 0.2 fusion.56
  65.4 0.5 copy-done.4
  65.9 0.7 fusion.57
  66.6 1.3 collective-permute-start.2
  67.9 5.7 %collective-permute-start.3 = (bf16[1,8,8,128]{3,2,1,0:T(8,128)(2,1)S(1)}, bf16[1,8,8,128]{3,2,1,0:T(8,128)(2,1)S(1)}, u32[]{:S(2)}, u32[]{:S(2)}) collective-permute-start(bf16[1,8,8,128]{3,2,1,0:T(8,128)(2,1)S(1)} %get-tuple-element.492), channel_id=1, source_target_pairs={{0,1},{1,2},{2,3},{3,4},{4,5},{5,6},{6,7},{7,8},{8,9},{9,10},{10,1... | collective-permute-start | bytes 49160 | tf_op jit(solution)/shard_map/while/body/eval_jaxpr/ppermute | solution.py:17
  73.6 1.2 convolution_add_fusion.3
  74.9 0.2 fusion.59
  75.9 0.6 fusion.61
  76.5 1.3 collective-permute-start.4
  77.9 4.8 %collective-permute-done.4 = bf16[4,8,8,128]{3,2,1,0:T(8,128)(2,1)S(1)} collective-permute-done((bf16[4,8,8,128]{3,2,1,0:T(8,128)(2,1)S(1)}, bf16[4,8,8,128]{3,2,1,0:T(8,128)(2,1)S(1)}, u32[]{:S(2)}, u32[]{:S(2)}) %collective-permute-start.4) | collective-permute-done | bytes 65568 | tf_op jit(solution)/shard_map/while/body/eval_jaxpr/ppermute | solution.py:29
  82.7 1.2 copy-done
  83.9 104.4 %all-reduce.4.cloned.1.call-done = f32[3456,128]{1,0:T(8,128)} async-done(((f32[3456,128]{1,0:T(8,128)}), f32[3456,128]{1,0:T(8,128)}) %all-reduce.4.cloned.1.call-update) | async-done | bytes 1769488 | tf_op jit(solution)/shard_map/psum | solution.py:114
  188.3 2.7 %multiply_reduce_fusion = f32[]{:T(128)} fusion(f32[3456,128]{1,0:T(8,128)} %all-reduce.4.cloned.1.call-done), kind=kLoop, calls=%fused_computation.95 | loop fusion | flops 884735 | bytes 1769476 | tf_op jit(solution)/shard_map/reduce_sum | solution.py:115
  191.0 5.6 %psum.15 = f32[]{:T(128)} all-reduce(f32[]{:T(128)} %multiply_reduce_fusion), channel_id=1, replica_groups=mesh['segment'=2,'slab'=16] {'segment'}, use_global_device_ids=true, to_apply=%region_4.5 | all-reduce | flops 1 | bytes 8 | tf_op jit(solution)/shard_map/psum | solution.py:115
  197.3 1.3 multiply_bitcast_fusion
  (223 shorter events, 4.6 us)
Async XLA Ops:
  7.2 181.2 %all-reduce.4.cloned.1.call-start = ((), (), s32[]{:S(2)}) async-start(), calls=%async_computation | async-start | bytes 3538944 | tf_op jit(solution)/shard_map/psum | solution.py:114
  7.2 3.6 %copy-start.2 = (bf16[1,2,4,8,8,128]{5,4,3,2,1,0:T(8,128)(2,1)S(1)}, bf16[1,2,4,8,8,128]{5,4,3,2,1,0:T(8,128)(2,1)}, u32[]{:S(2)}) copy-start(bf16[1,2,4,8,8,128]{5,4,3,2,1,0:T(8,128)(2,1)} %param.5) | copy-start | bytes 393220
  7.2 3.6 %copy-start.5 = (bf16[2,4,8,8,128]{4,3,2,1,0:T(8,128)(2,1)S(1)}, bf16[2,4,8,8,128]{4,3,2,1,0:T(8,128)(2,1)}, u32[]{:S(2)}) copy-start(bf16[2,4,8,8,128]{4,3,2,1,0:T(8,128)(2,1)} %param.7) | copy-start | bytes 393220
  10.9 4.4 %collective-permute-start = (bf16[1,8,8,128]{3,2,1,0:T(8,128)(2,1)S(1)}, bf16[1,8,8,128]{3,2,1,0:T(8,128)(2,1)S(1)}, u32[]{:S(2)}, u32[]{:S(2)}) collective-permute-start(bf16[1,8,8,128]{3,2,1,0:T(8,128)(2,1)S(1)} %get-tuple-element.462), channel_id=1, source_target_pairs={{1,0},{2,1},{3,2},{4,3},{5,4},{6,5},{7,6},{8,7},{9,8},{10,9},{11,1... | collective-permute-start | bytes 49160 | tf_op jit(solution)/shard_map/while/body/eval_jaxpr/ppermute | solution.py:19
  12.2 3.9 %collective-permute-start.1 = (bf16[1,8,8,128]{3,2,1,0:T(8,128)(2,1)S(1)}, bf16[1,8,8,128]{3,2,1,0:T(8,128)(2,1)S(1)}, u32[]{:S(2)}, u32[]{:S(2)}) collective-permute-start(bf16[1,8,8,128]{3,2,1,0:T(8,128)(2,1)S(1)} %get-tuple-element.463), channel_id=1, source_target_pairs={{0,1},{1,2},{2,3},{3,4},{4,5},{5,6},{6,7},{7,8},{8,9},{9,10},{10,1... | collective-permute-start | bytes 49160 | tf_op jit(solution)/shard_map/while/body/eval_jaxpr/ppermute | solution.py:17
  16.4 1.2 copy-start.4
  18.3 7.6 %collective-permute-start.2 = (bf16[1,8,8,128]{3,2,1,0:T(8,128)(2,1)S(1)}, bf16[1,8,8,128]{3,2,1,0:T(8,128)(2,1)S(1)}, u32[]{:S(2)}, u32[]{:S(2)}) collective-permute-start(bf16[1,8,8,128]{3,2,1,0:T(8,128)(2,1)S(1)} %get-tuple-element.491), channel_id=1, source_target_pairs={{1,0},{2,1},{3,2},{4,3},{5,4},{6,5},{7,6},{8,7},{9,8},{10,9},{11,1... | collective-permute-start | bytes 49160 | tf_op jit(solution)/shard_map/while/body/eval_jaxpr/ppermute | solution.py:19
  19.6 6.3 %collective-permute-start.3 = (bf16[1,8,8,128]{3,2,1,0:T(8,128)(2,1)S(1)}, bf16[1,8,8,128]{3,2,1,0:T(8,128)(2,1)S(1)}, u32[]{:S(2)}, u32[]{:S(2)}) collective-permute-start(bf16[1,8,8,128]{3,2,1,0:T(8,128)(2,1)S(1)} %get-tuple-element.492), channel_id=1, source_target_pairs={{0,1},{1,2},{2,3},{3,4},{4,5},{5,6},{6,7},{7,8},{8,9},{9,10},{10,1... | collective-permute-start | bytes 49160 | tf_op jit(solution)/shard_map/while/body/eval_jaxpr/ppermute | solution.py:17
  27.7 6.2 %collective-permute-start.4 = (bf16[4,8,8,128]{3,2,1,0:T(8,128)(2,1)S(1)}, bf16[4,8,8,128]{3,2,1,0:T(8,128)(2,1)S(1)}, u32[]{:S(2)}, u32[]{:S(2)}) collective-permute-start(bf16[4,8,8,128]{3,2,1,0:T(8,128)(2,1)S(1)} %bitcast.225), channel_id=1, source_target_pairs={{16,0},{17,1},{18,2},{19,3},{20,4},{21,5},{22,6},{23,7},{24,8},{25... | collective-permute-start | bytes 196616 | tf_op jit(solution)/shard_map/while/body/eval_jaxpr/ppermute | solution.py:29
  33.9 5.1 %collective-permute-start = (bf16[1,8,8,128]{3,2,1,0:T(8,128)(2,1)S(1)}, bf16[1,8,8,128]{3,2,1,0:T(8,128)(2,1)S(1)}, u32[]{:S(2)}, u32[]{:S(2)}) collective-permute-start(bf16[1,8,8,128]{3,2,1,0:T(8,128)(2,1)S(1)} %get-tuple-element.462), channel_id=1, source_target_pairs={{1,0},{2,1},{3,2},{4,3},{5,4},{6,5},{7,6},{8,7},{9,8},{10,9},{11,1... | collective-permute-start | bytes 49160 | tf_op jit(solution)/shard_map/while/body/eval_jaxpr/ppermute | solution.py:19
  35.2 4.5 %collective-permute-start.1 = (bf16[1,8,8,128]{3,2,1,0:T(8,128)(2,1)S(1)}, bf16[1,8,8,128]{3,2,1,0:T(8,128)(2,1)S(1)}, u32[]{:S(2)}, u32[]{:S(2)}) collective-permute-start(bf16[1,8,8,128]{3,2,1,0:T(8,128)(2,1)S(1)} %get-tuple-element.463), channel_id=1, source_target_pairs={{0,1},{1,2},{2,3},{3,4},{4,5},{5,6},{6,7},{7,8},{8,9},{9,10},{10,1... | collective-permute-start | bytes 49160 | tf_op jit(solution)/shard_map/while/body/eval_jaxpr/ppermute | solution.py:17
  40.1 1.2 copy-start.4
  42.0 8.6 %collective-permute-start.2 = (bf16[1,8,8,128]{3,2,1,0:T(8,128)(2,1)S(1)}, bf16[1,8,8,128]{3,2,1,0:T(8,128)(2,1)S(1)}, u32[]{:S(2)}, u32[]{:S(2)}) collective-permute-start(bf16[1,8,8,128]{3,2,1,0:T(8,128)(2,1)S(1)} %get-tuple-element.491), channel_id=1, source_target_pairs={{1,0},{2,1},{3,2},{4,3},{5,4},{6,5},{7,6},{8,7},{9,8},{10,9},{11,1... | collective-permute-start | bytes 49160 | tf_op jit(solution)/shard_map/while/body/eval_jaxpr/ppermute | solution.py:19
  43.3 7.3 %collective-permute-start.3 = (bf16[1,8,8,128]{3,2,1,0:T(8,128)(2,1)S(1)}, bf16[1,8,8,128]{3,2,1,0:T(8,128)(2,1)S(1)}, u32[]{:S(2)}, u32[]{:S(2)}) collective-permute-start(bf16[1,8,8,128]{3,2,1,0:T(8,128)(2,1)S(1)} %get-tuple-element.492), channel_id=1, source_target_pairs={{0,1},{1,2},{2,3},{3,4},{4,5},{5,6},{6,7},{7,8},{8,9},{9,10},{10,1... | collective-permute-start | bytes 49160 | tf_op jit(solution)/shard_map/while/body/eval_jaxpr/ppermute | solution.py:17
  52.3 6.2 %collective-permute-start.4 = (bf16[4,8,8,128]{3,2,1,0:T(8,128)(2,1)S(1)}, bf16[4,8,8,128]{3,2,1,0:T(8,128)(2,1)S(1)}, u32[]{:S(2)}, u32[]{:S(2)}) collective-permute-start(bf16[4,8,8,128]{3,2,1,0:T(8,128)(2,1)S(1)} %bitcast.225), channel_id=1, source_target_pairs={{16,0},{17,1},{18,2},{19,3},{20,4},{21,5},{22,6},{23,7},{24,8},{25... | collective-permute-start | bytes 196616 | tf_op jit(solution)/shard_map/while/body/eval_jaxpr/ppermute | solution.py:29
  58.5 5.1 %collective-permute-start = (bf16[1,8,8,128]{3,2,1,0:T(8,128)(2,1)S(1)}, bf16[1,8,8,128]{3,2,1,0:T(8,128)(2,1)S(1)}, u32[]{:S(2)}, u32[]{:S(2)}) collective-permute-start(bf16[1,8,8,128]{3,2,1,0:T(8,128)(2,1)S(1)} %get-tuple-element.462), channel_id=1, source_target_pairs={{1,0},{2,1},{3,2},{4,3},{5,4},{6,5},{7,6},{8,7},{9,8},{10,9},{11,1... | collective-permute-start | bytes 49160 | tf_op jit(solution)/shard_map/while/body/eval_jaxpr/ppermute | solution.py:19
  59.8 4.5 %collective-permute-start.1 = (bf16[1,8,8,128]{3,2,1,0:T(8,128)(2,1)S(1)}, bf16[1,8,8,128]{3,2,1,0:T(8,128)(2,1)S(1)}, u32[]{:S(2)}, u32[]{:S(2)}) collective-permute-start(bf16[1,8,8,128]{3,2,1,0:T(8,128)(2,1)S(1)} %get-tuple-element.463), channel_id=1, source_target_pairs={{0,1},{1,2},{2,3},{3,4},{4,5},{5,6},{6,7},{7,8},{8,9},{9,10},{10,1... | collective-permute-start | bytes 49160 | tf_op jit(solution)/shard_map/while/body/eval_jaxpr/ppermute | solution.py:17
  64.7 1.2 copy-start.4
  66.6 8.1 %collective-permute-start.2 = (bf16[1,8,8,128]{3,2,1,0:T(8,128)(2,1)S(1)}, bf16[1,8,8,128]{3,2,1,0:T(8,128)(2,1)S(1)}, u32[]{:S(2)}, u32[]{:S(2)}) collective-permute-start(bf16[1,8,8,128]{3,2,1,0:T(8,128)(2,1)S(1)} %get-tuple-element.491), channel_id=1, source_target_pairs={{1,0},{2,1},{3,2},{4,3},{5,4},{6,5},{7,6},{8,7},{9,8},{10,9},{11,1... | collective-permute-start | bytes 49160 | tf_op jit(solution)/shard_map/while/body/eval_jaxpr/ppermute | solution.py:19
  67.9 6.9 %collective-permute-start.3 = (bf16[1,8,8,128]{3,2,1,0:T(8,128)(2,1)S(1)}, bf16[1,8,8,128]{3,2,1,0:T(8,128)(2,1)S(1)}, u32[]{:S(2)}, u32[]{:S(2)}) collective-permute-start(bf16[1,8,8,128]{3,2,1,0:T(8,128)(2,1)S(1)} %get-tuple-element.492), channel_id=1, source_target_pairs={{0,1},{1,2},{2,3},{3,4},{4,5},{5,6},{6,7},{7,8},{8,9},{9,10},{10,1... | collective-permute-start | bytes 49160 | tf_op jit(solution)/shard_map/while/body/eval_jaxpr/ppermute | solution.py:17
  76.5 6.2 %collective-permute-start.4 = (bf16[4,8,8,128]{3,2,1,0:T(8,128)(2,1)S(1)}, bf16[4,8,8,128]{3,2,1,0:T(8,128)(2,1)S(1)}, u32[]{:S(2)}, u32[]{:S(2)}) collective-permute-start(bf16[4,8,8,128]{3,2,1,0:T(8,128)(2,1)S(1)} %bitcast.225), channel_id=1, source_target_pairs={{16,0},{17,1},{18,2},{19,3},{20,4},{21,5},{22,6},{23,7},{24,8},{25... | collective-permute-start | bytes 196616 | tf_op jit(solution)/shard_map/while/body/eval_jaxpr/ppermute | solution.py:29
  82.7 1.2 copy-start
  82.7 108.3 %copy-start.3 = (bf16[2,4,8,8,128]{4,3,2,1,0:T(8,128)(2,1)}, bf16[2,4,8,8,128]{4,3,2,1,0:T(8,128)(2,1)S(1)}, u32[]{:S(2)}) copy-start(bf16[2,4,8,8,128]{4,3,2,1,0:T(8,128)(2,1)S(1)} %get-tuple-element.231) | copy-start | bytes 393220
  188.3 9.0 %copy-start.1 = (f32[3456,128]{1,0:T(8,128)S(1)}, f32[3456,128]{1,0:T(8,128)}, u32[]{:S(2)}) copy-start(f32[3456,128]{1,0:T(8,128)} %all-reduce.4.cloned.1.call-done) | copy-start | bytes 5308420
Sparse Core Ops, SparseCore 0:
  84.0 104.2 all-reduce.3
where the time goes:
time: 206 us; the launch traced here: 205 us
  waiting for transfers between devices  121 us (59%)
  starting transfers between devices  38.9 us (19%)
  between operations  14.8 us (7%)
  local copies, waits for them, and re-layouts  11 us (5%)
  matrix products  7.38 us (4%)
  blocking collectives  5.55 us (3%)
  other arithmetic  5.06 us (2%)
    psum x1, waiting for transfers between devices, shards(): summed = lax.psum(partial_value, 'slab')  104 us
    ppermute x6, starting transfers between devices, padded(): lax.ppermute(tail, axis, [(i, (i + 1) % count) for i in range(ends)])  27.3 us
    ppermute x3, waiting for transfers between devices, from_behind(): return lax.ppermute(block, axis, route)  14.5 us
    ppermute x6, starting transfers between devices, padded(): lax.ppermute(head, axis, [((i + 1) % count, i) for i in range(ends)])  7.73 us
    psum x1, blocking collectives, shards(): squares = lax.psum(jnp.sum(summed * summed), 'segment')  5.55 us
    while x159, local copies, waits for them, and re-layouts  4.43 us
  transfers between devices with their start and end apart: 16, of which 7 were waited for; matrix products, arithmetic and copies ran while one was open for 2% of the time, Pallas kernels for 0%

commit v1 on v0

v1 whole, which is shorter than its diff:
```python
import math

import jax
import jax.numpy as jnp
from jax import lax
from jax.sharding import PartitionSpec as P

BF16 = jnp.bfloat16
F32 = jnp.float32


def pair_routes(count):
    near = [(i, i ^ 1) for i in range(count)]
    far = [(i, ((i + 1) ^ 1) - 1) for i in range(1, count - 1)]
    return near, far


def rims(low_planes, high_planes):
    near, far = pair_routes(lax.axis_size("slab"))
    even = lax.axis_index("slab") % 2 == 0
    got_near = lax.ppermute(jnp.where(even, high_planes, low_planes), "slab", near)
    got_far = lax.ppermute(jnp.where(even, low_planes, high_planes), "slab", far)
    return jnp.where(even, got_far, got_near), jnp.where(even, got_near, got_far)


def patches_of(rimmed, order):
    micro, depth, width, height, channels = rimmed.shape
    depth -= 2
    padded = jnp.pad(rimmed, ((0, 0), (0, 0), (1, 1), (1, 1), (0, 0)))
    pieces = []
    for offset in order:
        dz, dx, dy = offset // 9, offset // 3 % 3, offset % 3
        pieces.append(padded[:, dz : dz + depth, dx : dx + width, dy : dy + height])
    joined = jnp.concatenate(pieces, axis=-1)
    return joined.reshape(micro * depth * width * height, 27 * channels)


FORWARD = tuple(range(27))
BACKWARD = tuple(reversed(range(27)))


def exchange(value, bit):
    count = lax.axis_size("slab")
    return lax.ppermute(value, "slab", [(i, i ^ bit) for i in range(count)])


def shards(activations, weights, out_grad):
    acts = activations[0]
    weight = weights[0]
    channels = weight.shape[1]
    micro, depth, width, height = acts.shape[:4]
    cells = micro * depth * width * height
    segments = lax.axis_size("segment")
    count = lax.axis_size("slab")
    sindex = lax.axis_index("segment")
    index = lax.axis_index("slab")
    last = sindex == segments - 1

    low = jnp.concatenate([acts[:, :2], out_grad[:, :1]], axis=1)
    high = jnp.concatenate([acts[:, -2:], out_grad[:, -1:]], axis=1)
    below, above = rims(low, high)
    wide = jnp.concatenate([below[:, :2], acts, above[:, :2]], axis=1)
    wide_up = jnp.concatenate([below[:, 2:], out_grad, above[:, 2:]], axis=1)

    patches = patches_of(wide, FORWARD)
    preact = jnp.dot(patches, weight, preferred_element_type=F32)
    sig = jax.nn.sigmoid(preact)
    slope = (sig * (1.0 + preact * (1.0 - sig))).reshape(micro, depth + 2, width, height, channels)
    inner_patches = patches.reshape(micro, depth + 2, width * height, 27 * channels)[:, 1:-1]
    inner_patches = inner_patches.reshape(cells, 27 * channels)
    inner_slope = slope[:, 1:-1]

    kernel = weight.reshape(27, channels, channels)

    def conv_back(delta_rim):
        moved = patches_of(delta_rim, BACKWARD).reshape(cells, 27, channels)
        out = lax.dot_general(
            moved, kernel, (((1, 2), (0, 2)), ((), ())), preferred_element_type=F32
        )
        return out.reshape(micro, depth, width, height, channels)

    back = [(i, (i - 1) % segments) for i in range(segments)]
    delta_rim = (wide_up.astype(F32) * slope).astype(BF16)
    result = (out_grad.astype(F32) + conv_back(delta_rim)).astype(BF16)
    upstream = out_grad
    deltas = delta_rim[:, 1:-1]
    for step in range(1, segments):
        incoming = lax.ppermute(result, "segment", back)
        upstream = jnp.where(last, out_grad, incoming)
        deltas = (upstream.astype(F32) * inner_slope).astype(BF16)
        if step < segments - 1:
            below, above = rims(deltas[:, :1], deltas[:, -1:])
            around = jnp.concatenate([below, deltas, above], axis=1)
            result = (upstream.astype(F32) + conv_back(around)).astype(BF16)

    partial = lax.dot_general(
        inner_patches,
        deltas.reshape(cells, channels),
        (((0,), (0,)), ((), ())),
        preferred_element_type=F32,
    )
    below, above = rims(deltas[:, :1], deltas[:, -1:])
    around = jnp.concatenate([below, deltas, above], axis=1)
    gradients = (upstream.astype(F32) + conv_back(around)).astype(BF16)

    bits = []
    while 1 << len(bits) < count:
        bits.append(1 << len(bits))
    for bit in bits:
        half = partial.shape[0] // 2
        mine = jnp.where(index & bit, half, 0)
        keep = lax.dynamic_slice_in_dim(partial, mine, half, 0)
        send = lax.dynamic_slice_in_dim(partial, half - mine, half, 0).astype(BF16)
        partial = keep + exchange(send, bit).astype(F32)

    squares = jnp.broadcast_to(jnp.sum(partial * partial), (8, 128))
    total = squares
    turn = squares
    for _ in range(segments - 1):
        turn = lax.ppermute(turn, "segment", back)
        total = total + turn
    for bit in reversed(bits):
        total = total + exchange(total, bit)
    bound = math.sqrt(27.0 * channels * channels * segments)
    factor = jnp.minimum(1.0, bound / (jnp.sqrt(total[0, 0]) + 1e-06))

    gathered = partial.astype(BF16)
    for bit in reversed(bits):
        got = exchange(gathered, bit)
        odd = (index & bit) != 0
        gathered = jnp.concatenate(
            [jnp.where(odd, got, gathered), jnp.where(odd, gathered, got)], axis=0
        )
    update = gathered.astype(F32) * factor
    return (update[None], gradients[None])


def solution(mesh):
    return jax.shard_map(
        shards,
        mesh=mesh,
        in_specs=(
            P("segment", None, "slab", None, None, None),
            P("segment", None, None),
            P(None, "slab", None, None, None),
        ),
        out_specs=(P("segment", None, None), P("segment", None, "slab", None, None, None)),
        check_vma=False,
    )
```

time: 206 us -> 74 us (0.36)
  waiting for transfers between devices: 121 us -> 18.9 us
  between operations: 14.8 us -> 2.16 us
  starting transfers between devices: 38.9 us -> 31.2 us
  blocking collectives: 5.55 us -> 0 us
    psum x1 -> x0, waiting for transfers between devices: 104 us -> none  [shards(): summed = lax.psum(partial_value, 'slab')]
    ppermute x15 -> x18, starting transfers between devices: 38.9 us -> 31.2 us  [the longest x12 17.6 us: exchange(): return lax.ppermute(value, 'slab', [(i, i ^ bit) for i in range(count)])]
    psum x1 -> x0, blocking collectives: 5.55 us -> none  [shards(): squares = lax.psum(jnp.sum(summed * summed), 'segment')]
    while x159 -> x0, local copies, waits for them, and re-layouts: 4.43 us -> none
    unnamed x10 -> x82, local copies, waits for them, and re-layouts: 1.22 us -> 5.12 us
    slice x18 -> x8, local copies, waits for them, and re-layouts: 1.61 us -> 4.56 us  [the longest x1 2.24 us: shards(): patches.reshape(micro, depth + 2, width * height, 27 * channels)[:, 1:-1]]
    another operation x1 -> x0, local copies, waits for them, and re-layouts: 2.26 us -> none  [shards(): weight.reshape(27, channels, channels)[::-1].transpose(0, 2, 1)]
    ppermute x15 -> x18, waiting for transfers between devices: 16.7 us -> 18.9 us  [the longest x12 15.6 us: exchange(): return lax.ppermute(value, 'slab', [(i, i ^ bit) for i in range(count)])]
  transfers between devices with their start and end apart: 16 -> 18, of which waited for: 7 -> 10; matrix products, arithmetic and copies ran while one was open for 2% -> 12% of each run, Pallas kernels for 0% -> 0%
where the time goes in v1:
time: 74 us; the launch traced here: 73.7 us
  starting transfers between devices  31.2 us (42%)
  waiting for transfers between devices  18.9 us (26%)
  local copies, waits for them, and re-layouts  10.6 us (14%)
  matrix products  5.54 us (7%)
  other arithmetic  5.29 us (7%)
  between operations  2.16 us (3%)
    ppermute x12, starting transfers between devices, exchange(): return lax.ppermute(value, 'slab', [(i, i ^ bit) for i in range(count)])  17.6 us
    ppermute x12, waiting for transfers between devices, exchange(): return lax.ppermute(value, 'slab', [(i, i ^ bit) for i in range(count)])  15.6 us
    ppermute x2, starting transfers between devices, rims(): lax.ppermute(jnp.where(even, high_planes, low_planes), 'slab', near)  8.9 us
    unnamed x82, local copies, waits for them, and re-layouts  5.12 us
    dot_general x2, matrix products, conv_back(): lax.dot_general(moved, kernel, (((1, 2), (0, 2)), ((), ())), preferred_el...  2.84 us
    ppermute x1, waiting for transfers between devices, shards(): incoming = lax.ppermute(result, 'segment', back)  2.32 us
    slice x1, local copies, waits for them, and re-layouts, shards(): patches.reshape(micro, depth + 2, width * height, 27 * channels)[:, 1:-1]  2.24 us
    slice x2, local copies, waits for them, and re-layouts, shards(): low = jnp.concatenate([acts[:, :2], out_grad[:, :1]], axis=1)  1.78 us
  transfers between devices with their start and end apart: 18, of which 10 were waited for; matrix products, arithmetic and copies ran while one was open for 12% of the time, Pallas kernels for 0%

profile of v1, /device:TPU:0, one launch (start us, length us, event | category | flops | bytes accessed | tf_op | source)
XLA Modules:
  0.0 73.7 jit_solution(17272938256994897233)
XLA Ops:
  0.7 0.9 %fusion.62 = (bf16[2,1,8,8,128]{4,3,2,1,0:T(8,128)(2,1)S(1)}, bf16[2,1,8,8,128]{4,3,2,1,0:T(8,128)(2,1)S(1)}) fusion(bf16[2,4,8,8,128]{4,3,2,1,0:T(8,128)(2,1)} %param.5), kind=kLoop, calls=%fused_computation.196 | loop fusion | bytes 131072 | tf_op jit(solution)/shard_map/slice | solution.py:59
  1.6 0.9 %fusion.61 = (bf16[2,2,8,8,128]{4,3,2,1,0:T(8,128)(2,1)S(1)}, bf16[2,2,8,8,128]{4,3,2,1,0:T(8,128)(2,1)S(1)}) fusion(bf16[2,4,8,8,128]{4,3,2,1,0:T(8,128)(2,1)} %bitcast.70), kind=kLoop, calls=%fused_computation.195 | loop fusion | bytes 262144 | tf_op jit(solution)/shard_map/slice | solution.py:59
  2.5 0.7 collective-permute-start
  3.2 4.4 %collective-permute-start.1 = (bf16[2,3,8,8,128]{4,3,2,1,0:T(8,128)(2,1)S(1)}, bf16[2,3,8,8,128]{4,3,2,1,0:T(8,128)(2,1)S(1)}, u32[]{:S(2)}, u32[]{:S(2)}) collective-permute-start(bf16[2,3,8,8,128]{4,3,2,1,0:T(8,128)(2,1)S(1)} %get-tuple-element.13), channel_id=1, source_target_pairs={{0,1},{1,0},{2,3},{3,2},{4,5},{5,4},{6,7},{7,6},{8,9},{9,8},{10,11... | collective-permute-start | bytes 294920 | tf_op jit(solution)/shard_map/ppermute | solution.py:21
  7.5 0.9 %collective-permute-done.1 = bf16[2,3,8,8,128]{4,3,2,1,0:T(8,128)(2,1)S(1)} collective-permute-done((bf16[2,3,8,8,128]{4,3,2,1,0:T(8,128)(2,1)S(1)}, bf16[2,3,8,8,128]{4,3,2,1,0:T(8,128)(2,1)S(1)}, u32[]{:S(2)}, u32[]{:S(2)}) %collective-permute-start.1) | collective-permute-done | bytes 98336 | tf_op jit(solution)/shard_map/ppermute | solution.py:21
  8.6 0.9 %pad_maximum_fusion.1 = bf16[2,8,8,8,128]{4,3,2,1,0:T(8,128)(2,1)S(1)} fusion(bf16[2,2,8,8,128]{4,3,2,1,0:T(8,128)(2,1)S(1)} %slice.383, bf16[2,4,8,8,128]{4,3,2,1,0:T(8,128)(2,1)} %bitcast.71, bf16[2,2,8,8,128]{4,3,2,1,0:T(8,128)(2,1)S(1)} %slice.382), kind=kLoop, calls=%fused_computation.85 | loop fusion | flops 262144 | bytes 524288 | tf_op jit(solution)/shard_map/concatenate | solution.py:62
  9.7 0.1 fusion.39
  10.4 0.1 fusion.47
  10.6 0.1 fusion.48
  11.1 0.1 fusion.55
  11.6 1.6 %add_multiply_fusion = f32[768,128]{1,0:T(8,128)S(1)} fusion(bf16[768,3456]{1,0:T(8,128)(2,1)S(1)} %bitcast.68, bf16[1,3456,128]{2,1,0:T(8,128)(2,1)S(1)} %copy-done), kind=kOutput, calls=%fused_computation.82 | convolution fusion | flops 680165376 | bytes 6586368 | tf_op jit(solution)/shard_map/dot_general | solution.py:66
  13.2 0.7 %copy-done.2 = bf16[2,6,8,8,3456]{4,3,2,1,0:T(8,128)(2,1)} copy-done((bf16[2,6,8,8,3456]{4,3,2,1,0:T(8,128)(2,1)}, bf16[2,6,8,8,3456]{4,3,2,1,0:T(8,128)(2,1)S(1)}, u32[]{:S(2)}) %copy-start.2) | copy-done | bytes 5308440
  15.5 1.1 %fusion.16 = bf16[2,4,8,8,128]{4,3,2,1,0:T(8,128)(2,1)S(1)} fusion(bf16[27,128,128,1,1,1]{2,1,0,5,4,3:T(8,128)(2,1)S(1)} %bitcast.64, bf16[2,4,8,8,3456]{4,3,2,1,0:T(8,128)(2,1)S(1)} %constant_dynamic-update-slice_fusion, bf16[2,4,8,8,128]{4,3,2,1,0:T(8,128)(2,1)S(1)} %copy-done.1), kind=kOutput, calls=%fused_computation.61 | convolution fusion | flops 453181440 | bytes 4685824 | tf_op jit(solution)/shard_map/dot_general | solution.py:77
  16.5 1.6 %collective-permute-start.2 = (bf16[2,4,8,8,128]{4,3,2,1,0:T(8,128)(2,1)S(1)}, bf16[2,4,8,8,128]{4,3,2,1,0:T(8,128)(2,1)S(1)}, u32[]{:S(2)}, u32[]{:S(2)}) collective-permute-start(bf16[2,4,8,8,128]{4,3,2,1,0:T(8,128)(2,1)S(1)} %fusion.16), channel_id=1, source_target_pairs={{0,16},{16,0},{1,17},{17,1},{2,18},{18,2},{3,19},{19,3},{4,20},{20... | collective-permute-start | bytes 393224 | tf_op jit(solution)/shard_map/ppermute | solution.py:88
  18.1 2.2 %slice.385 = bf16[2,4,64,3456]{3,2,1,0:T(8,128)(2,1)S(1)} slice(bf16[2,6,64,3456]{3,2,1,0:T(8,128)(2,1)} %bitcast.69), slice={[0:2], [1:5], [0:64], [0:3456]} | slice | bytes 7077888 | tf_op jit(solution)/shard_map/slice | solution.py:69
  20.3 2.3 %collective-permute-done.2 = bf16[2,4,8,8,128]{4,3,2,1,0:T(8,128)(2,1)S(1)} collective-permute-done((bf16[2,4,8,8,128]{4,3,2,1,0:T(8,128)(2,1)S(1)}, bf16[2,4,8,8,128]{4,3,2,1,0:T(8,128)(2,1)S(1)}, u32[]{:S(2)}, u32[]{:S(2)}) %collective-permute-start.2) | collective-permute-done | bytes 131104 | tf_op jit(solution)/shard_map/ppermute | solution.py:88
  22.7 0.8 %collective-permute-start.16 = (bf16[2,1,8,8,128]{4,3,2,1,0:T(8,128)(2,1)S(1)}, bf16[2,1,8,8,128]{4,3,2,1,0:T(8,128)(2,1)S(1)}, u32[]{:S(2)}, u32[]{:S(2)}) collective-permute-start(bf16[2,1,8,8,128]{4,3,2,1,0:T(8,128)(2,1)S(1)} %get-tuple-element.14), channel_id=1, source_target_pairs={{1,2},{2,1},{3,4},{4,3},{5,6},{6,5},{7,8},{8,7},{9,10},{10,9},{11,... | collective-permute-start | bytes 98312 | tf_op jit(solution)/shard_map/ppermute | solution.py:22
  23.6 4.5 %collective-permute-start.17 = (bf16[2,1,8,8,128]{4,3,2,1,0:T(8,128)(2,1)S(1)}, bf16[2,1,8,8,128]{4,3,2,1,0:T(8,128)(2,1)S(1)}, u32[]{:S(2)}, u32[]{:S(2)}) collective-permute-start(bf16[2,1,8,8,128]{4,3,2,1,0:T(8,128)(2,1)S(1)} %get-tuple-element.15), channel_id=1, source_target_pairs={{0,1},{1,0},{2,3},{3,2},{4,5},{5,4},{6,7},{7,6},{8,9},{9,8},{10,11... | collective-permute-start | bytes 98312 | tf_op jit(solution)/shard_map/ppermute | solution.py:21
  28.1 1.1 %fusion.63 = f32[3456,128]{1,0:T(8,128)S(1)} fusion(bf16[512,3456]{1,0:T(8,128)(2,1)S(1)} %bitcast.66, bf16[512,128]{1,0:T(8,128)(2,1)S(1)} %bitcast.67), kind=kOutput, calls=%fused_computation.197 | convolution fusion | flops 452984832 | bytes 5439488 | tf_op jit(solution)/shard_map/dot_general | solution.py:96
  29.4 0.2 select_maximum_fusion
  30.9 0.3 collective-permute-done.3
  31.3 1.8 %collective-permute-start.4 = (bf16[864,128]{1,0:T(8,128)(2,1)S(1)}, bf16[864,128]{1,0:T(8,128)(2,1)S(1)}, u32[]{:S(2)}, u32[]{:S(2)}) collective-permute-start(bf16[864,128]{1,0:T(8,128)(2,1)S(1)} %dynamic-slice_convert_fusion.1), channel_id=1, source_target_pairs={{0,2},{1,3},{2,0},{3,1},{4,6},{5,7},{6,4},{7,5},{8,10},{9,11},{10,... | collective-permute-start | bytes 663560 | tf_op jit(solution)/shard_map/ppermute | solution.py:44
  33.1 5.8 %collective-permute-done.4 = bf16[864,128]{1,0:T(8,128)(2,1)S(1)} collective-permute-done((bf16[864,128]{1,0:T(8,128)(2,1)S(1)}, bf16[864,128]{1,0:T(8,128)(2,1)S(1)}, u32[]{:S(2)}, u32[]{:S(2)}) %collective-permute-start.4) | collective-permute-done | bytes 221216 | tf_op jit(solution)/shard_map/ppermute | solution.py:44
  39.0 1.6 %collective-permute-start.5 = (bf16[432,128]{1,0:T(8,128)(2,1)S(1)}, bf16[432,128]{1,0:T(8,128)(2,1)S(1)}, u32[]{:S(2)}, u32[]{:S(2)}) collective-permute-start(bf16[432,128]{1,0:T(8,128)(2,1)S(1)} %dynamic-slice_convert_fusion.2), channel_id=1, source_target_pairs={{0,4},{1,5},{2,6},{3,7},{4,0},{5,1},{6,2},{7,3},{8,12},{9,13},{10,... | collective-permute-start | bytes 331784 | tf_op jit(solution)/shard_map/ppermute | solution.py:44
  40.7 3.1 %collective-permute-done.5 = bf16[432,128]{1,0:T(8,128)(2,1)S(1)} collective-permute-done((bf16[432,128]{1,0:T(8,128)(2,1)S(1)}, bf16[432,128]{1,0:T(8,128)(2,1)S(1)}, u32[]{:S(2)}, u32[]{:S(2)}) %collective-permute-start.5) | collective-permute-done | bytes 110624 | tf_op jit(solution)/shard_map/ppermute | solution.py:44
  43.8 2.7 %collective-permute-start.6 = (bf16[216,128]{1,0:T(8,128)(2,1)S(1)}, bf16[216,128]{1,0:T(8,128)(2,1)S(1)}, u32[]{:S(2)}, u32[]{:S(2)}) collective-permute-start(bf16[216,128]{1,0:T(8,128)(2,1)S(1)} %dynamic-slice_convert_fusion.3), channel_id=1, source_target_pairs={{0,8},{1,9},{2,10},{3,11},{4,12},{5,13},{6,14},{7,15},{8,0},{9,1},... | collective-permute-start | bytes 165896 | tf_op jit(solution)/shard_map/ppermute | solution.py:44
  46.6 2.4 %collective-permute-done.6 = bf16[216,128]{1,0:T(8,128)(2,1)S(1)} collective-permute-done((bf16[216,128]{1,0:T(8,128)(2,1)S(1)}, bf16[216,128]{1,0:T(8,128)(2,1)S(1)}, u32[]{:S(2)}, u32[]{:S(2)}) %collective-permute-start.6) | collective-permute-done | bytes 55328 | tf_op jit(solution)/shard_map/ppermute | solution.py:44
  49.0 0.6 multiply_reduce_fusion
  49.6 0.6 broadcast_in_dim.7
  50.3 1.6 %collective-permute-start.11 = (f32[8,128]{1,0:T(8,128)S(1)}, f32[8,128]{1,0:T(8,128)S(1)}, u32[]{:S(2)}, u32[]{:S(2)}) collective-permute-start(f32[8,128]{1,0:T(8,128)S(1)} %broadcast_in_dim.7), channel_id=1, source_target_pairs={{0,16},{16,0},{1,17},{17,1},{2,18},{18,2},{3,19},{19,3},{4,20},{20... | collective-permute-start | bytes 12296 | tf_op jit(solution)/shard_map/ppermute | solution.py:120
  51.9 2.7 %collective-permute-start.7 = (bf16[216,128]{1,0:T(8,128)(2,1)S(1)}, bf16[216,128]{1,0:T(8,128)(2,1)S(1)}, u32[]{:S(2)}, u32[]{:S(2)}) collective-permute-start(bf16[216,128]{1,0:T(8,128)(2,1)S(1)} %get-tuple-element.7), channel_id=1, source_target_pairs={{0,8},{1,9},{2,10},{3,11},{4,12},{5,13},{6,14},{7,15},{8,0},{9,1},... | collective-permute-start | bytes 165896 | tf_op jit(solution)/shard_map/ppermute | solution.py:44
  54.6 0.6 broadcast_add_fusion
  55.3 2.0 %collective-permute-start.12 = (f32[8,128]{1,0:T(8,128)S(1)}, f32[8,128]{1,0:T(8,128)S(1)}, u32[]{:S(2)}, u32[]{:S(2)}) collective-permute-start(f32[8,128]{1,0:T(8,128)S(1)} %broadcast_add_fusion), channel_id=1, source_target_pairs={{0,8},{1,9},{2,10},{3,11},{4,12},{5,13},{6,14},{7,15},{8,0},{9,1},... | collective-permute-start | bytes 12296 | tf_op jit(solution)/shard_map/ppermute | solution.py:44
  57.4 1.7 %collective-permute-start.8 = (bf16[432,128]{1,0:T(8,128)(2,1)S(1)}, bf16[432,128]{1,0:T(8,128)(2,1)S(1)}, u32[]{:S(2)}, u32[]{:S(2)}) collective-permute-start(bf16[432,128]{1,0:T(8,128)(2,1)S(1)} %pad_maximum_fusion.5), channel_id=1, source_target_pairs={{0,4},{1,5},{2,6},{3,7},{4,0},{5,1},{6,2},{7,3},{8,12},{9,13},{10,... | collective-permute-start | bytes 331784 | tf_op jit(solution)/shard_map/ppermute | solution.py:44
  59.1 0.7 collective-permute-done.12
  59.9 0.6 fusion.69
  60.5 0.9 %collective-permute-start.13 = (f32[8,128]{1,0:T(8,128)S(1)}, f32[8,128]{1,0:T(8,128)S(1)}, u32[]{:S(2)}, u32[]{:S(2)}) collective-permute-start(f32[8,128]{1,0:T(8,128)S(1)} %fusion.69), channel_id=1, source_target_pairs={{0,4},{1,5},{2,6},{3,7},{4,0},{5,1},{6,2},{7,3},{8,12},{9,13},{10,... | collective-permute-start | bytes 12296 | tf_op jit(solution)/shard_map/ppermute | solution.py:44
  61.5 0.7 collective-permute-done.8
  62.3 1.7 %collective-permute-start.9 = (bf16[864,128]{1,0:T(8,128)(2,1)S(1)}, bf16[864,128]{1,0:T(8,128)(2,1)S(1)}, u32[]{:S(2)}, u32[]{:S(2)}) collective-permute-start(bf16[864,128]{1,0:T(8,128)(2,1)S(1)} %pad_maximum_fusion.2), channel_id=1, source_target_pairs={{0,2},{1,3},{2,0},{3,1},{4,6},{5,7},{6,4},{7,5},{8,10},{9,11},{10,... | collective-permute-start | bytes 663560 | tf_op jit(solution)/shard_map/ppermute | solution.py:44
  64.0 0.1 collective-permute-done.13
  64.2 1.6 %collective-permute-start.14 = (f32[8,128]{1,0:T(8,128)S(1)}, f32[8,128]{1,0:T(8,128)S(1)}, u32[]{:S(2)}, u32[]{:S(2)}) collective-permute-start(f32[8,128]{1,0:T(8,128)S(1)} %add.88), channel_id=1, source_target_pairs={{0,2},{1,3},{2,0},{3,1},{4,6},{5,7},{6,4},{7,5},{8,10},{9,11},{10,... | collective-permute-start | bytes 12296 | tf_op jit(solution)/shard_map/ppermute | solution.py:44
  65.8 2.4 %collective-permute-done.9 = bf16[864,128]{1,0:T(8,128)(2,1)S(1)} collective-permute-done((bf16[864,128]{1,0:T(8,128)(2,1)S(1)}, bf16[864,128]{1,0:T(8,128)(2,1)S(1)}, u32[]{:S(2)}, u32[]{:S(2)}) %collective-permute-start.9) | collective-permute-done | bytes 221216 | tf_op jit(solution)/shard_map/ppermute | solution.py:44
  68.3 0.1 broadcast_select_fusion.1
  68.6 0.6 collective-permute-start.15
  69.1 1.8 %fusion.22 = bf16[1,2,4,8,8,128]{5,4,3,2,1,0:T(8,128)(2,1)} fusion(bf16[27,128,128,1,1,1]{2,1,0,5,4,3:T(8,128)(2,1)S(1)} %bitcast.65, bf16[2,4,8,8,3456]{4,3,2,1,0:T(8,128)(2,1)S(1)} %constant_dynamic-update-slice_fusion.27, bf16[2,4,8,8,128]{4,3,2,1,0:T(8,128)(2,1)S(1)} %copy-done.1, bf16[2,4,8,8,128]{4,3,2,1,0:T(8,128)(2,1)S(1)} %collective-permute-done.2, ...), kind=kOutput, calls=%fused_computation.63 | convolution fusion | flops 453246976 | bytes 4816897 | tf_op jit(solution)/shard_map/dot_general | solution.py:77
  70.9 0.5 slice.351
  72.1 0.2 select_bitcast_fusion.1
  72.3 1.3 %convert_multiply_fusion = f32[1,3456,128]{2,1,0:T(8,128)} fusion(bf16[1,1728,128]{2,1,0:T(8,128)(2,1)S(1)} %get-tuple-element.3, bf16[1,1728,128]{2,1,0:T(8,128)(2,1)S(1)} %get-tuple-element.2, f32[]{:T(128)} %bitcast.15), kind=kLoop, calls=%fused_computation.52 | loop fusion | flops 2211840 | bytes 2654212 | tf_op jit(solution)/shard_map/mul | solution.py:134
  (119 shorter events, 5.2 us)
Async XLA Ops:
  0.6 10.9 %copy-start = (bf16[1,3456,128]{2,1,0:T(8,128)(2,1)S(1)}, bf16[1,3456,128]{2,1,0:T(8,128)(2,1)}, u32[]{:S(2)}) copy-start(bf16[1,3456,128]{2,1,0:T(8,128)(2,1)} %param.4) | copy-start | bytes 2654212
  0.6 9.2 %copy-start.3 = (bf16[1,2,4,8,8,128]{5,4,3,2,1,0:T(8,128)(2,1)S(1)}, bf16[1,2,4,8,8,128]{5,4,3,2,1,0:T(8,128)(2,1)}, u32[]{:S(2)}) copy-start(bf16[1,2,4,8,8,128]{5,4,3,2,1,0:T(8,128)(2,1)} %param.3) | copy-start | bytes 393220
  2.5 5.1 %collective-permute-start = (bf16[2,3,8,8,128]{4,3,2,1,0:T(8,128)(2,1)S(1)}, bf16[2,3,8,8,128]{4,3,2,1,0:T(8,128)(2,1)S(1)}, u32[]{:S(2)}, u32[]{:S(2)}) collective-permute-start(bf16[2,3,8,8,128]{4,3,2,1,0:T(8,128)(2,1)S(1)} %get-tuple-element.12), channel_id=1, source_target_pairs={{1,2},{2,1},{3,4},{4,3},{5,6},{6,5},{7,8},{8,7},{9,10},{10,9},{11,... | collective-permute-start | bytes 294920 | tf_op jit(solution)/shard_map/ppermute | solution.py:22
  3.2 5.3 %collective-permute-start.1 = (bf16[2,3,8,8,128]{4,3,2,1,0:T(8,128)(2,1)S(1)}, bf16[2,3,8,8,128]{4,3,2,1,0:T(8,128)(2,1)S(1)}, u32[]{:S(2)}, u32[]{:S(2)}) collective-permute-start(bf16[2,3,8,8,128]{4,3,2,1,0:T(8,128)(2,1)S(1)} %get-tuple-element.13), channel_id=1, source_target_pairs={{0,1},{1,0},{2,3},{3,2},{4,5},{5,4},{6,7},{7,6},{8,9},{9,8},{10,11... | collective-permute-start | bytes 294920 | tf_op jit(solution)/shard_map/ppermute | solution.py:21
  11.6 2.4 %copy-start.2 = (bf16[2,6,8,8,3456]{4,3,2,1,0:T(8,128)(2,1)}, bf16[2,6,8,8,3456]{4,3,2,1,0:T(8,128)(2,1)S(1)}, u32[]{:S(2)}) copy-start(bf16[2,6,8,8,3456]{4,3,2,1,0:T(8,128)(2,1)S(1)} %fusion.59) | copy-start | bytes 15925252
  11.6 2.3 %copy-start.1 = (bf16[2,4,8,8,128]{4,3,2,1,0:T(8,128)(2,1)S(1)}, bf16[2,4,8,8,128]{4,3,2,1,0:T(8,128)(2,1)}, u32[]{:S(2)}) copy-start(bf16[2,4,8,8,128]{4,3,2,1,0:T(8,128)(2,1)} %param.5) | copy-start | bytes 393220
  16.5 6.1 %collective-permute-start.2 = (bf16[2,4,8,8,128]{4,3,2,1,0:T(8,128)(2,1)S(1)}, bf16[2,4,8,8,128]{4,3,2,1,0:T(8,128)(2,1)S(1)}, u32[]{:S(2)}, u32[]{:S(2)}) collective-permute-start(bf16[2,4,8,8,128]{4,3,2,1,0:T(8,128)(2,1)S(1)} %fusion.16), channel_id=1, source_target_pairs={{0,16},{16,0},{1,17},{17,1},{2,18},{18,2},{3,19},{19,3},{4,20},{20... | collective-permute-start | bytes 393224 | tf_op jit(solution)/shard_map/ppermute | solution.py:88
  22.7 6.6 %collective-permute-start.16 = (bf16[2,1,8,8,128]{4,3,2,1,0:T(8,128)(2,1)S(1)}, bf16[2,1,8,8,128]{4,3,2,1,0:T(8,128)(2,1)S(1)}, u32[]{:S(2)}, u32[]{:S(2)}) collective-permute-start(bf16[2,1,8,8,128]{4,3,2,1,0:T(8,128)(2,1)S(1)} %get-tuple-element.14), channel_id=1, source_target_pairs={{1,2},{2,1},{3,4},{4,3},{5,6},{6,5},{7,8},{8,7},{9,10},{10,9},{11,... | collective-permute-start | bytes 98312 | tf_op jit(solution)/shard_map/ppermute | solution.py:22
  23.6 5.8 %collective-permute-start.17 = (bf16[2,1,8,8,128]{4,3,2,1,0:T(8,128)(2,1)S(1)}, bf16[2,1,8,8,128]{4,3,2,1,0:T(8,128)(2,1)S(1)}, u32[]{:S(2)}, u32[]{:S(2)}) collective-permute-start(bf16[2,1,8,8,128]{4,3,2,1,0:T(8,128)(2,1)S(1)} %get-tuple-element.15), channel_id=1, source_target_pairs={{0,1},{1,0},{2,3},{3,2},{4,5},{5,4},{6,7},{7,6},{8,9},{9,8},{10,11... | collective-permute-start | bytes 98312 | tf_op jit(solution)/shard_map/ppermute | solution.py:21
  29.3 1.9 %collective-permute-start.3 = (bf16[1728,128]{1,0:T(8,128)(2,1)S(1)}, bf16[1728,128]{1,0:T(8,128)(2,1)S(1)}, u32[]{:S(2)}, u32[]{:S(2)}) collective-permute-start(bf16[1728,128]{1,0:T(8,128)(2,1)S(1)} %dynamic-slice_convert_fusion), channel_id=1, source_target_pairs={{0,1},{1,0},{2,3},{3,2},{4,5},{5,4},{6,7},{7,6},{8,9},{9,8},{10,11... | collective-permute-start | bytes 1327112 | tf_op jit(solution)/shard_map/ppermute | solution.py:44
  31.3 7.6 %collective-permute-start.4 = (bf16[864,128]{1,0:T(8,128)(2,1)S(1)}, bf16[864,128]{1,0:T(8,128)(2,1)S(1)}, u32[]{:S(2)}, u32[]{:S(2)}) collective-permute-start(bf16[864,128]{1,0:T(8,128)(2,1)S(1)} %dynamic-slice_convert_fusion.1), channel_id=1, source_target_pairs={{0,2},{1,3},{2,0},{3,1},{4,6},{5,7},{6,4},{7,5},{8,10},{9,11},{10,... | collective-permute-start | bytes 663560 | tf_op jit(solution)/shard_map/ppermute | solution.py:44
  39.0 4.8 %collective-permute-start.5 = (bf16[432,128]{1,0:T(8,128)(2,1)S(1)}, bf16[432,128]{1,0:T(8,128)(2,1)S(1)}, u32[]{:S(2)}, u32[]{:S(2)}) collective-permute-start(bf16[432,128]{1,0:T(8,128)(2,1)S(1)} %dynamic-slice_convert_fusion.2), channel_id=1, source_target_pairs={{0,4},{1,5},{2,6},{3,7},{4,0},{5,1},{6,2},{7,3},{8,12},{9,13},{10,... | collective-permute-start | bytes 331784 | tf_op jit(solution)/shard_map/ppermute | solution.py:44
  43.8 5.1 %collective-permute-start.6 = (bf16[216,128]{1,0:T(8,128)(2,1)S(1)}, bf16[216,128]{1,0:T(8,128)(2,1)S(1)}, u32[]{:S(2)}, u32[]{:S(2)}) collective-permute-start(bf16[216,128]{1,0:T(8,128)(2,1)S(1)} %dynamic-slice_convert_fusion.3), channel_id=1, source_target_pairs={{0,8},{1,9},{2,10},{3,11},{4,12},{5,13},{6,14},{7,15},{8,0},{9,1},... | collective-permute-start | bytes 165896 | tf_op jit(solution)/shard_map/ppermute | solution.py:44
  50.3 4.4 %collective-permute-start.11 = (f32[8,128]{1,0:T(8,128)S(1)}, f32[8,128]{1,0:T(8,128)S(1)}, u32[]{:S(2)}, u32[]{:S(2)}) collective-permute-start(f32[8,128]{1,0:T(8,128)S(1)} %broadcast_in_dim.7), channel_id=1, source_target_pairs={{0,16},{16,0},{1,17},{17,1},{2,18},{18,2},{3,19},{19,3},{4,20},{20... | collective-permute-start | bytes 12296 | tf_op jit(solution)/shard_map/ppermute | solution.py:120
  51.9 5.5 %collective-permute-start.7 = (bf16[216,128]{1,0:T(8,128)(2,1)S(1)}, bf16[216,128]{1,0:T(8,128)(2,1)S(1)}, u32[]{:S(2)}, u32[]{:S(2)}) collective-permute-start(bf16[216,128]{1,0:T(8,128)(2,1)S(1)} %get-tuple-element.7), channel_id=1, source_target_pairs={{0,8},{1,9},{2,10},{3,11},{4,12},{5,13},{6,14},{7,15},{8,0},{9,1},... | collective-permute-start | bytes 165896 | tf_op jit(solution)/shard_map/ppermute | solution.py:44
  55.3 4.6 %collective-permute-start.12 = (f32[8,128]{1,0:T(8,128)S(1)}, f32[8,128]{1,0:T(8,128)S(1)}, u32[]{:S(2)}, u32[]{:S(2)}) collective-permute-start(f32[8,128]{1,0:T(8,128)S(1)} %broadcast_add_fusion), channel_id=1, source_target_pairs={{0,8},{1,9},{2,10},{3,11},{4,12},{5,13},{6,14},{7,15},{8,0},{9,1},... | collective-permute-start | bytes 12296 | tf_op jit(solution)/shard_map/ppermute | solution.py:44
  57.4 4.8 %collective-permute-start.8 = (bf16[432,128]{1,0:T(8,128)(2,1)S(1)}, bf16[432,128]{1,0:T(8,128)(2,1)S(1)}, u32[]{:S(2)}, u32[]{:S(2)}) collective-permute-start(bf16[432,128]{1,0:T(8,128)(2,1)S(1)} %pad_maximum_fusion.5), channel_id=1, source_target_pairs={{0,4},{1,5},{2,6},{3,7},{4,0},{5,1},{6,2},{7,3},{8,12},{9,13},{10,... | collective-permute-start | bytes 331784 | tf_op jit(solution)/shard_map/ppermute | solution.py:44
  60.5 3.7 %collective-permute-start.13 = (f32[8,128]{1,0:T(8,128)S(1)}, f32[8,128]{1,0:T(8,128)S(1)}, u32[]{:S(2)}, u32[]{:S(2)}) collective-permute-start(f32[8,128]{1,0:T(8,128)S(1)} %fusion.69), channel_id=1, source_target_pairs={{0,4},{1,5},{2,6},{3,7},{4,0},{5,1},{6,2},{7,3},{8,12},{9,13},{10,... | collective-permute-start | bytes 12296 | tf_op jit(solution)/shard_map/ppermute | solution.py:44
  62.3 6.0 %collective-permute-start.9 = (bf16[864,128]{1,0:T(8,128)(2,1)S(1)}, bf16[864,128]{1,0:T(8,128)(2,1)S(1)}, u32[]{:S(2)}, u32[]{:S(2)}) collective-permute-start(bf16[864,128]{1,0:T(8,128)(2,1)S(1)} %pad_maximum_fusion.2), channel_id=1, source_target_pairs={{0,2},{1,3},{2,0},{3,1},{4,6},{5,7},{6,4},{7,5},{8,10},{9,11},{10,... | collective-permute-start | bytes 663560 | tf_op jit(solution)/shard_map/ppermute | solution.py:44
  64.2 4.3 %collective-permute-start.14 = (f32[8,128]{1,0:T(8,128)S(1)}, f32[8,128]{1,0:T(8,128)S(1)}, u32[]{:S(2)}, u32[]{:S(2)}) collective-permute-start(f32[8,128]{1,0:T(8,128)S(1)} %add.88), channel_id=1, source_target_pairs={{0,2},{1,3},{2,0},{3,1},{4,6},{5,7},{6,4},{7,5},{8,10},{9,11},{10,... | collective-permute-start | bytes 12296 | tf_op jit(solution)/shard_map/ppermute | solution.py:44
  68.4 3.7 %collective-permute-start.10 = (bf16[1728,128]{1,0:T(8,128)(2,1)S(1)}, bf16[1728,128]{1,0:T(8,128)(2,1)S(1)}, u32[]{:S(2)}, u32[]{:S(2)}) collective-permute-start(bf16[1728,128]{1,0:T(8,128)(2,1)S(1)} %pad_maximum_fusion), channel_id=1, source_target_pairs={{0,1},{1,0},{2,3},{3,2},{4,5},{5,4},{6,7},{7,6},{8,9},{9,8},{10,11... | collective-permute-start | bytes 1327112 | tf_op jit(solution)/shard_map/ppermute | solution.py:44
  68.6 2.3 %collective-permute-start.15 = (f32[8,128]{1,0:T(8,128)S(1)}, f32[8,128]{1,0:T(8,128)S(1)}, u32[]{:S(2)}, u32[]{:S(2)}) collective-permute-start(f32[8,128]{1,0:T(8,128)S(1)} %add.89), channel_id=1, source_target_pairs={{0,1},{1,0},{2,3},{3,2},{4,5},{5,4},{6,7},{7,6},{8,9},{9,8},{10,11... | collective-permute-start | bytes 12296 | tf_op jit(solution)/shard_map/ppermute | solution.py:44

commit v2 on v1

--- a/solution.py
+++ b/solution.py
@@ -1,8 +1,11 @@
+import functools
 import math
 
 import jax
 import jax.numpy as jnp
 from jax import lax
+from jax.experimental import pallas as pl
+from jax.experimental.pallas import tpu as pltpu
 from jax.sharding import PartitionSpec as P
 
 BF16 = jnp.bfloat16
@@ -39,9 +42,41 @@
 BACKWARD = tuple(reversed(range(27)))
 
 
-def exchange(value, bit):
+def exchange(value, mask):
     count = lax.axis_size("slab")
-    return lax.ppermute(value, "slab", [(i, i ^ bit) for i in range(count)])
+    return lax.ppermute(value, "slab", [(i, i ^ mask) for i in range(count)])
+
+
+def cross(value, back, mask):
+    segments, count = lax.axis_size("segment"), lax.axis_size("slab")
+    if back == 0 and mask == 0:
+        return value
+    route = [
+        (s * count + i, (s - back) % segments * count + (i ^ mask))
+        for s in range(segments)
+        for i in range(count)
+    ]
+    return lax.ppermute(value, ("segment", "slab"), route)
+
+
+def block(value, place, rows, dtype):
+    return lax.dynamic_slice_in_dim(value, place * rows, rows, 0).astype(dtype)
+
+
+def place_kernel(bound, spot_ref, *refs):
+    pieces, out_ref = refs[:-1], refs[-1]
+    rows = out_ref.shape[1]
+    here = pl.program_id(0)
+    sums = [piece[rows:].astype(F32) for piece in pieces]
+    while len(sums) > 1:
+        sums = [a + b for a, b in zip(sums[::2], sums[1::2], strict=True)]
+    norm = jnp.sqrt(jnp.sum(sums[0], axis=0, keepdims=True))
+    factor = jnp.minimum(1.0, bound / (norm + 1e-06))
+    for number, piece in enumerate(pieces):
+
+        @pl.when(spot_ref[0] ^ number == here)
+        def _():
+            out_ref[0] = piece[:rows].astype(F32) * factor
 
 
 def shards(activations, weights, out_grad):
@@ -99,40 +134,82 @@
         (((0,), (0,)), ((), ())),
         preferred_element_type=F32,
     )
+
+    bits = [1 << n for n in range(1, count.bit_length() - 1)]
+    inner = [bits[n : n + 2] for n in range(2, len(bits), 2)]
+    crossing = inner[-1][0] if len(inner[-1]) == 1 else 0
+    side = lax.rem(index, 2) ^ jnp.where(index & crossing, 1, 0)
+    quarter = jnp.where(index & 2, 2, 0) + jnp.where(index & 4, 1, 0)
+    rows = partial.shape[0] // 8
+    masks = {1: 4, 2: 2, 3: 6}
+
+    pieces = {}
+    far = []
+    for turn in (3, 2, 1, 0):
+        there = quarter ^ turn
+        got = exchange(block(partial, (1 - side) * 4 + there, rows, BF16), 1)
+        if turn == 0:
+            got, deltas = lax.optimization_barrier((got, deltas))
+        piece = block(partial, side * 4 + there, rows, F32) + got.astype(F32)
+        if turn:
+            far.append(exchange(piece.astype(BF16), masks[turn]))
+    chunk = piece + sum(other.astype(F32) for other in far)
+
     below, above = rims(deltas[:, :1], deltas[:, -1:])
     around = jnp.concatenate([below, deltas, above], axis=1)
     gradients = (upstream.astype(F32) + conv_back(around)).astype(BF16)
 
-    bits = []
-    while 1 << len(bits) < count:
-        bits.append(1 << len(bits))
-    for bit in bits:
-        half = partial.shape[0] // 2
-        mine = jnp.where(index & bit, half, 0)
-        keep = lax.dynamic_slice_in_dim(partial, mine, half, 0)
-        send = lax.dynamic_slice_in_dim(partial, half - mine, half, 0).astype(BF16)
-        partial = keep + exchange(send, bit).astype(F32)
-
-    squares = jnp.broadcast_to(jnp.sum(partial * partial), (8, 128))
-    total = squares
-    turn = squares
-    for _ in range(segments - 1):
-        turn = lax.ppermute(turn, "segment", back)
-        total = total + turn
-    for bit in reversed(bits):
-        total = total + exchange(total, bit)
+    def places(group):
+        own = sum(jnp.where(index & bit, 1 << n, 0) for n, bit in enumerate(group))
+        others = []
+        for turn in range(1, 1 << len(group)):
+            mask = sum(bit for n, bit in enumerate(group) if turn >> n & 1)
+            others.append((mask | 1 if mask == crossing else mask, own ^ turn))
+        return own, others
+
+    for group in inner:
+        own, others = places(group)
+        part = chunk.shape[0] >> len(group)
+        got = [exchange(block(chunk, there, part, BF16), mask) for mask, there in others]
+        chunk = block(chunk, own, part, F32) + sum(g.astype(F32) for g in got)
+
+    gathered = chunk.astype(BF16)
+    for group in reversed(inner):
+        own, others = places(group)
+        got = [(there, exchange(gathered, mask)) for mask, there in others]
+        if group is inner[-1]:
+            squares = jnp.broadcast_to(jnp.sum(chunk * chunk), (8, 128))
+            sums = []
+            for mask in [0] + [mask for mask, _ in others]:
+                sums.append(sum(cross(squares, back, mask) for back in range(segments)))
+            while len(sums) > 1:
+                sums = [a + b for a, b in zip(sums[::2], sums[1::2], strict=True)]
+            squares = sums[0][0]
+        blocks = []
+        for n in range(1 << len(group)):
+            value = jnp.where(own == n, gathered, got[0][1])
+            for there, other in got[1:]:
+                value = jnp.where(there == n, other, value)
+            blocks.append(value)
+        gathered = jnp.concatenate(blocks, axis=0)
+
+    first = lax.reduce_precision(squares, 8, 7)
+    second = lax.reduce_precision(squares - first, 8, 7)
+    third = squares - first - second
+    terms = jnp.zeros((16, channels), F32).at[0].set(first).at[1].set(second).at[2].set(third)
+    payload = jnp.concatenate([gathered, terms.astype(BF16)], axis=0)
+    near = [payload] + [exchange(payload, masks[turn]) for turn in (1, 2, 3)]
+    both = near + [exchange(piece, 1) for piece in near]
     bound = math.sqrt(27.0 * channels * channels * segments)
-    factor = jnp.minimum(1.0, bound / (jnp.sqrt(total[0, 0]) + 1e-06))
-
-    gathered = partial.astype(BF16)
-    for bit in reversed(bits):
-        got = exchange(gathered, bit)
-        odd = (index & bit) != 0
-        gathered = jnp.concatenate(
-            [jnp.where(odd, got, gathered), jnp.where(odd, gathered, got)], axis=0
-        )
-    update = gathered.astype(F32) * factor
-    return (update[None], gradients[None])
+    whole = [pl.BlockSpec(memory_space=pltpu.VMEM)] * 8
+    update = pl.pallas_call(
+        functools.partial(place_kernel, bound),
+        out_shape=jax.ShapeDtypeStruct((8, rows, channels), F32),
+        grid=(8,),
+        in_specs=[pl.BlockSpec(memory_space=pltpu.SMEM)] + whole,
+        out_specs=pl.BlockSpec((1, rows, channels), lambda j: (j, 0, 0)),
+    )((side * 4 + quarter).reshape(1), *both)
+    return (update.reshape(1, 8 * rows, channels), gradients[None])
 
 
 def solution(mesh):

time: 74 us -> 88.8 us (1.20)
  local copies, waits for them, and re-layouts: 10.6 us -> 27.8 us
  starting transfers between devices: 31.2 us -> 26.2 us
  Pallas kernels: 0 us -> 4.48 us
  waiting for transfers between devices: 18.9 us -> 16.8 us
  matrix products: 5.54 us -> 7.59 us
  other arithmetic: 5.29 us -> 4.2 us
    unnamed x82 -> x102, local copies, waits for them, and re-layouts: 5.12 us -> 21.5 us
    ppermute x13 -> x19, starting transfers between devices: 19.2 us -> 14.3 us  [the longest x16 10.1 us: exchange(): return lax.ppermute(value, 'slab', [(i, i ^ mask) for i in range(count)])]
    pallas_call x0 -> x1, Pallas kernels: none -> 4.48 us  [shards(): pl.pallas_call(functools.partial(place_kernel, bound), out_shape=jax.Shap...]
    ppermute x13 -> x19, waiting for transfers between devices: 15.6 us -> 13.5 us  [the longest x16 11.2 us: exchange(): return lax.ppermute(value, 'slab', [(i, i ^ mask) for i in range(count)])]
    dot_general x2, matrix products: 2.84 us -> 4.87 us  [conv_back(): lax.dot_general(moved, kernel, (((1, 2), (0, 2)), ((), ())), preferred_el...]
    mul x1 -> x0, other arithmetic: 1.32 us -> none  [shards(): update = gathered.astype(F32) * factor]
    unnamed x4, other arithmetic: 0.16 us -> 1.45 us
  transfers between devices with their start and end apart: 18 -> 24, of which waited for: 10 -> 9; matrix products, arithmetic and copies ran while one was open for 12% -> 30% of each run, Pallas kernels for 0% -> 0%
where the time goes in v2:
time: 88.8 us; the launch traced here: 88.5 us
  local copies, waits for them, and re-layouts  27.8 us (31%)
  starting transfers between devices  26.2 us (30%)
  waiting for transfers between devices  16.8 us (19%)
  matrix products  7.59 us (9%)
  Pallas kernels  4.48 us (5%)
  other arithmetic  4.2 us (5%)
  between operations  1.36 us (2%)
    unnamed x102, local copies, waits for them, and re-layouts  21.5 us
    ppermute x16, waiting for transfers between devices, exchange(): return lax.ppermute(value, 'slab', [(i, i ^ mask) for i in range(count)])  11.2 us
    ppermute x16, starting transfers between devices, exchange(): return lax.ppermute(value, 'slab', [(i, i ^ mask) for i in range(count)])  10.1 us
    ppermute x2, starting transfers between devices, rims(): lax.ppermute(jnp.where(even, high_planes, low_planes), 'slab', near)  9.02 us
    dot_general x2, matrix products, conv_back(): lax.dot_general(moved, kernel, (((1, 2), (0, 2)), ((), ())), preferred_el...  4.87 us
    pallas_call x1, Pallas kernels, shards(): pl.pallas_call(functools.partial(place_kernel, bound), out_shape=jax.Shap...  4.48 us
    ppermute x3, starting transfers between devices, cross(): return lax.ppermute(value, ('segment', 'slab'), route)  4.2 us
    ppermute x3, waiting for transfers between devices, cross(): return lax.ppermute(value, ('segment', 'slab'), route)  2.36 us
  transfers between devices with their start and end apart: 24, of which 9 were waited for; matrix products, arithmetic and copies ran while one was open for 30% of the time, Pallas kernels for 0%

profile of v2, /device:TPU:0, one launch (start us, length us, event | category | flops | bytes accessed | tf_op | source)
XLA Modules:
  0.0 88.5 jit_solution(9112978633699153867)
XLA Ops:
  0.7 0.9 %fusion.63 = (bf16[2,1,8,8,128]{4,3,2,1,0:T(8,128)(2,1)S(1)}, bf16[2,1,8,8,128]{4,3,2,1,0:T(8,128)(2,1)S(1)}) fusion(bf16[2,4,8,8,128]{4,3,2,1,0:T(8,128)(2,1)} %param.11), kind=kLoop, calls=%fused_computation.193 | loop fusion | bytes 131072 | tf_op jit(solution)/shard_map/slice | solution.py:94
  1.6 0.9 fusion.62
  3.2 4.4 %collective-permute-start.1 = (bf16[2,3,8,8,128]{4,3,2,1,0:T(8,128)(2,1)S(1)}, bf16[2,3,8,8,128]{4,3,2,1,0:T(8,128)(2,1)S(1)}, u32[]{:S(2)}, u32[]{:S(2)}) collective-permute-start(bf16[2,3,8,8,128]{4,3,2,1,0:T(8,128)(2,1)S(1)} %get-tuple-element.54), channel_id=1, source_target_pairs={{0,1},{1,0},{2,3},{3,2},{4,5},{5,4},{6,7},{7,6},{8,9},{9,8},{10,11... | collective-permute-start | bytes 294920 | tf_op jit(solution)/shard_map/ppermute | solution.py:24
  7.5 0.9 %collective-permute-done.1 = bf16[2,3,8,8,128]{4,3,2,1,0:T(8,128)(2,1)S(1)} collective-permute-done((bf16[2,3,8,8,128]{4,3,2,1,0:T(8,128)(2,1)S(1)}, bf16[2,3,8,8,128]{4,3,2,1,0:T(8,128)(2,1)S(1)}, u32[]{:S(2)}, u32[]{:S(2)}) %collective-permute-start.1) | collective-permute-done | bytes 98336 | tf_op jit(solution)/shard_map/ppermute | solution.py:24
  8.6 0.9 %pad_maximum_fusion = bf16[2,8,8,8,128]{4,3,2,1,0:T(8,128)(2,1)S(1)} fusion(bf16[2,2,8,8,128]{4,3,2,1,0:T(8,128)(2,1)S(1)} %slice.427, bf16[2,4,8,8,128]{4,3,2,1,0:T(8,128)(2,1)} %bitcast.68, bf16[2,2,8,8,128]{4,3,2,1,0:T(8,128)(2,1)S(1)} %slice.426), kind=kLoop, calls=%fused_computation.77 | loop fusion | flops 262144 | bytes 524288 | tf_op jit(solution)/shard_map/concatenate | solution.py:97
  11.6 1.6 %add_multiply_fusion = f32[768,128]{1,0:T(8,128)S(1)} fusion(bf16[768,3456]{1,0:T(8,128)(2,1)S(1)} %bitcast.65, bf16[1,3456,128]{2,1,0:T(8,128)(2,1)S(1)} %copy-done), kind=kOutput, calls=%fused_computation.74 | convolution fusion | flops 680165376 | bytes 6586368 | tf_op jit(solution)/shard_map/dot_general | solution.py:101
  13.2 0.7 copy-done.2
  15.4 1.1 %fusion.16 = bf16[2,4,8,8,128]{4,3,2,1,0:T(8,128)(2,1)S(1)} fusion(bf16[27,128,128,1,1,1]{2,1,0,5,4,3:T(8,128)(2,1)S(1)} %bitcast.61, bf16[2,4,8,8,3456]{4,3,2,1,0:T(8,128)(2,1)S(1)} %constant_dynamic-update-slice_fusion, bf16[2,4,8,8,128]{4,3,2,1,0:T(8,128)(2,1)S(1)} %copy-done.1), kind=kOutput, calls=%fused_computation.60 | convolution fusion | flops 453181440 | bytes 4685824 | tf_op jit(solution)/shard_map/dot_general | solution.py:112
  16.5 1.6 %collective-permute-start.2 = (bf16[2,4,8,8,128]{4,3,2,1,0:T(8,128)(2,1)S(1)}, bf16[2,4,8,8,128]{4,3,2,1,0:T(8,128)(2,1)S(1)}, u32[]{:S(2)}, u32[]{:S(2)}) collective-permute-start(bf16[2,4,8,8,128]{4,3,2,1,0:T(8,128)(2,1)S(1)} %fusion.16), channel_id=1, source_target_pairs={{0,16},{16,0},{1,17},{17,1},{2,18},{18,2},{3,19},{19,3},{4,20},{20... | collective-permute-start | bytes 393224 | tf_op jit(solution)/shard_map/ppermute | solution.py:123
  18.1 2.2 %slice.429 = bf16[2,4,64,3456]{3,2,1,0:T(8,128)(2,1)S(1)} slice(bf16[2,6,64,3456]{3,2,1,0:T(8,128)(2,1)} %bitcast.66), slice={[0:2], [1:5], [0:64], [0:3456]} | slice | bytes 7077888 | tf_op jit(solution)/shard_map/slice | solution.py:104
  20.3 2.3 %collective-permute-done.2 = bf16[2,4,8,8,128]{4,3,2,1,0:T(8,128)(2,1)S(1)} collective-permute-done((bf16[2,4,8,8,128]{4,3,2,1,0:T(8,128)(2,1)S(1)}, bf16[2,4,8,8,128]{4,3,2,1,0:T(8,128)(2,1)S(1)}, u32[]{:S(2)}, u32[]{:S(2)}) %collective-permute-start.2) | collective-permute-done | bytes 131104 | tf_op jit(solution)/shard_map/ppermute | solution.py:123
  22.7 1.1 %fusion.64 = f32[3456,128]{1,0:T(8,128)S(1)} fusion(bf16[512,3456]{1,0:T(8,128)(2,1)S(1)} %bitcast.63, bf16[512,128]{1,0:T(8,128)(2,1)S(1)} %bitcast.64), kind=kOutput, calls=%fused_computation.194 | convolution fusion | flops 452984832 | bytes 5439488 | tf_op jit(solution)/shard_map/dot_general | solution.py:131
  23.8 0.7 dynamic-slice_convert_fusion.3
  26.8 4.6 %collective-permute-start.23 = (bf16[2,1,8,8,128]{4,3,2,1,0:T(8,128)(2,1)S(1)}, bf16[2,1,8,8,128]{4,3,2,1,0:T(8,128)(2,1)S(1)}, u32[]{:S(2)}, u32[]{:S(2)}) collective-permute-start(bf16[2,1,8,8,128]{4,3,2,1,0:T(8,128)(2,1)S(1)} %get-tuple-element.56), channel_id=1, source_target_pairs={{0,1},{1,0},{2,3},{3,2},{4,5},{5,4},{6,7},{7,6},{8,9},{9,8},{10,11... | collective-permute-start | bytes 98312 | tf_op jit(solution)/shard_map/ppermute | solution.py:24
  31.5 1.6 %collective-permute-start.9 = (bf16[432,128]{1,0:T(8,128)(2,1)S(1)}, bf16[432,128]{1,0:T(8,128)(2,1)S(1)}, u32[]{:S(2)}, u32[]{:S(2)}) collective-permute-start(bf16[432,128]{1,0:T(8,128)(2,1)S(1)} %get-tuple-element.47), channel_id=1, source_target_pairs={{0,4},{1,5},{2,6},{3,7},{4,0},{5,1},{6,2},{7,3},{8,12},{9,13},{10,... | collective-permute-start | bytes 331784 | tf_op jit(solution)/shard_map/ppermute | solution.py:47
  33.2 1.7 %collective-permute-start.7 = (bf16[432,128]{1,0:T(8,128)(2,1)S(1)}, bf16[432,128]{1,0:T(8,128)(2,1)S(1)}, u32[]{:S(2)}, u32[]{:S(2)}) collective-permute-start(bf16[432,128]{1,0:T(8,128)(2,1)S(1)} %get-tuple-element.48), channel_id=1, source_target_pairs={{0,2},{1,3},{2,0},{3,1},{4,6},{5,7},{6,4},{7,5},{8,10},{9,11},{10,... | collective-permute-start | bytes 331784 | tf_op jit(solution)/shard_map/ppermute | solution.py:47
  35.3 0.7 constant_dynamic-update-slice_fusion.53
  36.0 0.7 constant_dynamic-update-slice_fusion.52
  37.4 0.7 constant_dynamic-update-slice_fusion.50
  38.8 0.7 constant_dynamic-update-slice_fusion.48
  39.6 0.7 constant_dynamic-update-slice_fusion.47
  40.3 0.7 constant_dynamic-update-slice_fusion.46
  41.7 0.7 constant_dynamic-update-slice_fusion.44
  42.4 0.7 constant_dynamic-update-slice_fusion.43
  43.1 0.7 constant_dynamic-update-slice_fusion.42
  43.9 0.7 constant_dynamic-update-slice_fusion.41
  45.3 0.7 constant_dynamic-update-slice_fusion.39
  46.0 0.7 constant_dynamic-update-slice_fusion.38
  46.7 0.7 constant_dynamic-update-slice_fusion.37
  47.4 0.7 constant_dynamic-update-slice_fusion.36
  48.1 0.7 constant_dynamic-update-slice_fusion.35
  48.8 0.7 constant_dynamic-update-slice_fusion.34
  50.2 0.7 constant_dynamic-update-slice_fusion.32
  51.6 0.7 constant_dynamic-update-slice_fusion.30
  52.5 1.5 %collective-permute-start.10 = (bf16[216,128]{1,0:T(8,128)(2,1)S(1)}, bf16[216,128]{1,0:T(8,128)(2,1)S(1)}, u32[]{:S(2)}, u32[]{:S(2)}) collective-permute-start(bf16[216,128]{1,0:T(8,128)(2,1)S(1)} %dynamic-slice_convert_fusion.4), channel_id=1, source_target_pairs={{0,9},{1,8},{2,11},{3,10},{4,13},{5,12},{6,15},{7,14},{8,1},{9,0},... | collective-permute-start | bytes 165896 | tf_op jit(solution)/shard_map/ppermute | solution.py:47
  53.9 0.7 constant_dynamic-update-slice_fusion.29
  54.6 3.9 %collective-permute-done.10 = bf16[216,128]{1,0:T(8,128)(2,1)S(1)} collective-permute-done((bf16[216,128]{1,0:T(8,128)(2,1)S(1)}, bf16[216,128]{1,0:T(8,128)(2,1)S(1)}, u32[]{:S(2)}, u32[]{:S(2)}) %collective-permute-start.10) | collective-permute-done | bytes 55328 | tf_op jit(solution)/shard_map/ppermute | solution.py:47
  59.9 3.6 %collective-permute-start.14 = (f32[8,128]{1,0:T(8,128)S(1)}, f32[8,128]{1,0:T(8,128)S(1)}, u32[]{:S(2)}, u32[]{:S(2)}) collective-permute-start(f32[8,128]{1,0:T(8,128)S(1)} %broadcast_in_dim.7), channel_id=1, source_target_pairs={{0,25},{1,24},{2,27},{3,26},{4,29},{5,28},{6,31},{7,30},{8,17},{9,... | collective-permute-start | bytes 12296 | tf_op jit(solution)/shard_map/ppermute | solution.py:59
  64.0 0.7 constant_dynamic-update-slice_fusion.28
  64.8 2.3 %collective-permute-done.12 = f32[8,128]{1,0:T(8,128)S(1)} collective-permute-done((f32[8,128]{1,0:T(8,128)S(1)}, f32[8,128]{1,0:T(8,128)S(1)}, u32[]{:S(2)}, u32[]{:S(2)}) %collective-permute-start.12) | collective-permute-done | bytes 4128 | tf_op jit(solution)/shard_map/ppermute | solution.py:59
  67.9 3.1 %collective-permute-done.11 = bf16[216,128]{1,0:T(8,128)(2,1)S(1)} collective-permute-done((bf16[216,128]{1,0:T(8,128)(2,1)S(1)}, bf16[216,128]{1,0:T(8,128)(2,1)S(1)}, u32[]{:S(2)}, u32[]{:S(2)}) %collective-permute-start.11) | collective-permute-done | bytes 55328 | tf_op jit(solution)/shard_map/ppermute | solution.py:47
  71.1 1.3 %collective-permute-start.16 = (bf16[448,128]{1,0:T(8,128)(2,1)S(1)}, bf16[448,128]{1,0:T(8,128)(2,1)S(1)}, u32[]{:S(2)}, u32[]{:S(2)}) collective-permute-start(bf16[448,128]{1,0:T(8,128)(2,1)S(1)} %pad_maximum_fusion.3.refs_0_), channel_id=1, source_target_pairs={{0,2},{1,3},{2,0},{3,1},{4,6},{5,7},{6,4},{7,5},{8,10},{9,11},{10,... | collective-permute-start | bytes 344072 | tf_op jit(solution)/shard_map/ppermute | solution.py:47
  72.5 2.1 %collective-permute-start.17 = (bf16[448,128]{1,0:T(8,128)(2,1)S(1)}, bf16[448,128]{1,0:T(8,128)(2,1)S(1)}, u32[]{:S(2)}, u32[]{:S(2)}) collective-permute-start(bf16[448,128]{1,0:T(8,128)(2,1)S(1)} %pad_maximum_fusion.3.refs_0_), channel_id=1, source_target_pairs={{0,6},{1,7},{2,4},{3,5},{4,2},{5,3},{6,0},{7,1},{8,14},{9,15},{10,... | collective-permute-start | bytes 344072 | tf_op jit(solution)/shard_map/ppermute | solution.py:47
  74.6 0.7 constant_dynamic-update-slice_fusion.27
  75.3 1.8 %collective-permute-done.15.refs_1_ = bf16[448,128]{1,0:T(8,128)(2,1)S(1)} collective-permute-done((bf16[448,128]{1,0:T(8,128)(2,1)S(1)}, bf16[448,128]{1,0:T(8,128)(2,1)S(1)}, u32[]{:S(2)}, u32[]{:S(2)}) %collective-permute-start.15) | collective-permute-done | bytes 114720 | tf_op jit(solution)/shard_map/ppermute | solution.py:47
  77.6 1.8 %collective-permute-done.17.refs_3_ = bf16[448,128]{1,0:T(8,128)(2,1)S(1)} collective-permute-done((bf16[448,128]{1,0:T(8,128)(2,1)S(1)}, bf16[448,128]{1,0:T(8,128)(2,1)S(1)}, u32[]{:S(2)}, u32[]{:S(2)}) %collective-permute-start.17) | collective-permute-done | bytes 114720 | tf_op jit(solution)/shard_map/ppermute | solution.py:47
  79.5 3.8 %fusion.22 = bf16[1,2,4,8,8,128]{5,4,3,2,1,0:T(8,128)(2,1)} fusion(bf16[27,128,128,1,1,1]{2,1,0,5,4,3:T(8,128)(2,1)S(1)} %bitcast.62, bf16[2,4,8,8,3456]{4,3,2,1,0:T(8,128)(2,1)} %constant_dynamic-update-slice_fusion.27, bf16[2,4,8,8,128]{4,3,2,1,0:T(8,128)(2,1)S(1)} %copy-done.1, bf16[2,4,8,8,128]{4,3,2,1,0:T(8,128)(2,1)S(1)} %collective-permute-done.2, ...), kind=kOutput, calls=%fused_computation.62 | convolution fusion | flops 453246976 | bytes 4816897 | tf_op jit(solution)/shard_map/dot_general | solution.py:112
  84.0 4.5 %shard_map.50 = f32[8,432,128]{2,1,0:T(8,128)} custom-call(s32[1]{0:T(128)} %bitcast.spot_ref, bf16[448,128]{1,0:T(8,128)(2,1)} %copy-done.4, bf16[448,128]{1,0:T(8,128)(2,1)} %copy-done.5, bf16[448,128]{1,0:T(8,128)(2,1)} %copy-done.6, bf16[448,128]{1,0:T(8,128)(2,1)} %copy-done.7, bf16[448,128]{1,0:T(8,128)(2,1)} %copy-done.8, bf16[448,128]{1,0:T(8,128)(2,1)} %copy-done.9, ...), custom_call_target="tpu_custom_call" | custom-call | tf_op jit(solution)/shard_map/pallas_call | solution.py:205
  (142 shorter events, 14.9 us)
Async XLA Ops:
  0.6 10.9 %copy-start = (bf16[1,3456,128]{2,1,0:T(8,128)(2,1)S(1)}, bf16[1,3456,128]{2,1,0:T(8,128)(2,1)}, u32[]{:S(2)}) copy-start(bf16[1,3456,128]{2,1,0:T(8,128)(2,1)} %param.10) | copy-start | bytes 2654212
  0.6 9.2 %copy-start.3 = (bf16[1,2,4,8,8,128]{5,4,3,2,1,0:T(8,128)(2,1)S(1)}, bf16[1,2,4,8,8,128]{5,4,3,2,1,0:T(8,128)(2,1)}, u32[]{:S(2)}) copy-start(bf16[1,2,4,8,8,128]{5,4,3,2,1,0:T(8,128)(2,1)} %param.9) | copy-start | bytes 393220
  2.5 5.1 %collective-permute-start = (bf16[2,3,8,8,128]{4,3,2,1,0:T(8,128)(2,1)S(1)}, bf16[2,3,8,8,128]{4,3,2,1,0:T(8,128)(2,1)S(1)}, u32[]{:S(2)}, u32[]{:S(2)}) collective-permute-start(bf16[2,3,8,8,128]{4,3,2,1,0:T(8,128)(2,1)S(1)} %get-tuple-element.53), channel_id=1, source_target_pairs={{1,2},{2,1},{3,4},{4,3},{5,6},{6,5},{7,8},{8,7},{9,10},{10,9},{11,... | collective-permute-start | bytes 294920 | tf_op jit(solution)/shard_map/ppermute | solution.py:25
  3.2 5.3 %collective-permute-start.1 = (bf16[2,3,8,8,128]{4,3,2,1,0:T(8,128)(2,1)S(1)}, bf16[2,3,8,8,128]{4,3,2,1,0:T(8,128)(2,1)S(1)}, u32[]{:S(2)}, u32[]{:S(2)}) collective-permute-start(bf16[2,3,8,8,128]{4,3,2,1,0:T(8,128)(2,1)S(1)} %get-tuple-element.54), channel_id=1, source_target_pairs={{0,1},{1,0},{2,3},{3,2},{4,5},{5,4},{6,7},{7,6},{8,9},{9,8},{10,11... | collective-permute-start | bytes 294920 | tf_op jit(solution)/shard_map/ppermute | solution.py:24
  11.6 2.4 %copy-start.2 = (bf16[2,6,8,8,3456]{4,3,2,1,0:T(8,128)(2,1)}, bf16[2,6,8,8,3456]{4,3,2,1,0:T(8,128)(2,1)S(1)}, u32[]{:S(2)}) copy-start(bf16[2,6,8,8,3456]{4,3,2,1,0:T(8,128)(2,1)S(1)} %fusion.59) | copy-start | bytes 15925252
  11.6 2.3 %copy-start.1 = (bf16[2,4,8,8,128]{4,3,2,1,0:T(8,128)(2,1)S(1)}, bf16[2,4,8,8,128]{4,3,2,1,0:T(8,128)(2,1)}, u32[]{:S(2)}) copy-start(bf16[2,4,8,8,128]{4,3,2,1,0:T(8,128)(2,1)} %param.11) | copy-start | bytes 393220
  16.5 6.1 %collective-permute-start.2 = (bf16[2,4,8,8,128]{4,3,2,1,0:T(8,128)(2,1)S(1)}, bf16[2,4,8,8,128]{4,3,2,1,0:T(8,128)(2,1)S(1)}, u32[]{:S(2)}, u32[]{:S(2)}) collective-permute-start(bf16[2,4,8,8,128]{4,3,2,1,0:T(8,128)(2,1)S(1)} %fusion.16), channel_id=1, source_target_pairs={{0,16},{16,0},{1,17},{17,1},{2,18},{18,2},{3,19},{19,3},{4,20},{20... | collective-permute-start | bytes 393224 | tf_op jit(solution)/shard_map/ppermute | solution.py:123
  24.6 1.5 %collective-permute-start.3 = (bf16[432,128]{1,0:T(8,128)(2,1)}, bf16[432,128]{1,0:T(8,128)(2,1)S(1)}, u32[]{:S(2)}, u32[]{:S(2)}) collective-permute-start(bf16[432,128]{1,0:T(8,128)(2,1)} %get-tuple-element.42), channel_id=1, source_target_pairs={{0,1},{1,0},{2,3},{3,2},{4,5},{5,4},{6,7},{7,6},{8,9},{9,8},{10,11... | collective-permute-start | bytes 331784 | tf_op jit(solution)/shard_map/ppermute | solution.py:47
  24.7 6.7 %collective-permute-start.4 = (bf16[432,128]{1,0:T(8,128)(2,1)S(1)}, bf16[432,128]{1,0:T(8,128)(2,1)S(1)}, u32[]{:S(2)}, u32[]{:S(2)}) collective-permute-start(bf16[432,128]{1,0:T(8,128)(2,1)S(1)} %get-tuple-element.45), channel_id=1, source_target_pairs={{0,1},{1,0},{2,3},{3,2},{4,5},{5,4},{6,7},{7,6},{8,9},{9,8},{10,11... | collective-permute-start | bytes 331784 | tf_op jit(solution)/shard_map/ppermute | solution.py:47
  25.1 6.3 %collective-permute-start.8 = (bf16[432,128]{1,0:T(8,128)(2,1)S(1)}, bf16[432,128]{1,0:T(8,128)(2,1)S(1)}, u32[]{:S(2)}, u32[]{:S(2)}) collective-permute-start(bf16[432,128]{1,0:T(8,128)(2,1)S(1)} %get-tuple-element.43), channel_id=1, source_target_pairs={{0,1},{1,0},{2,3},{3,2},{4,5},{5,4},{6,7},{7,6},{8,9},{9,8},{10,11... | collective-permute-start | bytes 331784 | tf_op jit(solution)/shard_map/ppermute | solution.py:47
  25.2 6.2 %collective-permute-start.6 = (bf16[432,128]{1,0:T(8,128)(2,1)S(1)}, bf16[432,128]{1,0:T(8,128)(2,1)S(1)}, u32[]{:S(2)}, u32[]{:S(2)}) collective-permute-start(bf16[432,128]{1,0:T(8,128)(2,1)S(1)} %get-tuple-element.44), channel_id=1, source_target_pairs={{0,1},{1,0},{2,3},{3,2},{4,5},{5,4},{6,7},{7,6},{8,9},{9,8},{10,11... | collective-permute-start | bytes 331784 | tf_op jit(solution)/shard_map/ppermute | solution.py:47
  26.1 9.0 %copy-start.12 = (bf16[432,128]{1,0:T(8,128)(2,1)}, bf16[432,128]{1,0:T(8,128)(2,1)S(1)}, u32[]{:S(2)}) copy-start(bf16[432,128]{1,0:T(8,128)(2,1)S(1)} %collective-permute-done.3) | copy-start | bytes 331780
  26.1 9.0 %collective-permute-start.22 = (bf16[2,1,8,8,128]{4,3,2,1,0:T(8,128)(2,1)S(1)}, bf16[2,1,8,8,128]{4,3,2,1,0:T(8,128)(2,1)S(1)}, u32[]{:S(2)}, u32[]{:S(2)}) collective-permute-start(bf16[2,1,8,8,128]{4,3,2,1,0:T(8,128)(2,1)S(1)} %get-tuple-element.55), channel_id=1, source_target_pairs={{1,2},{2,1},{3,4},{4,3},{5,6},{6,5},{7,8},{8,7},{9,10},{10,9},{11,... | collective-permute-start | bytes 98312 | tf_op jit(solution)/shard_map/ppermute | solution.py:25
  26.8 8.3 %collective-permute-start.23 = (bf16[2,1,8,8,128]{4,3,2,1,0:T(8,128)(2,1)S(1)}, bf16[2,1,8,8,128]{4,3,2,1,0:T(8,128)(2,1)S(1)}, u32[]{:S(2)}, u32[]{:S(2)}) collective-permute-start(bf16[2,1,8,8,128]{4,3,2,1,0:T(8,128)(2,1)S(1)} %get-tuple-element.56), channel_id=1, source_target_pairs={{0,1},{1,0},{2,3},{3,2},{4,5},{5,4},{6,7},{7,6},{8,9},{9,8},{10,11... | collective-permute-start | bytes 98312 | tf_op jit(solution)/shard_map/ppermute | solution.py:24
  31.5 20.8 %collective-permute-start.9 = (bf16[432,128]{1,0:T(8,128)(2,1)S(1)}, bf16[432,128]{1,0:T(8,128)(2,1)S(1)}, u32[]{:S(2)}, u32[]{:S(2)}) collective-permute-start(bf16[432,128]{1,0:T(8,128)(2,1)S(1)} %get-tuple-element.47), channel_id=1, source_target_pairs={{0,4},{1,5},{2,6},{3,7},{4,0},{5,1},{6,2},{7,3},{8,12},{9,13},{10,... | collective-permute-start | bytes 331784 | tf_op jit(solution)/shard_map/ppermute | solution.py:47
  33.2 19.2 %collective-permute-start.7 = (bf16[432,128]{1,0:T(8,128)(2,1)S(1)}, bf16[432,128]{1,0:T(8,128)(2,1)S(1)}, u32[]{:S(2)}, u32[]{:S(2)}) collective-permute-start(bf16[432,128]{1,0:T(8,128)(2,1)S(1)} %get-tuple-element.48), channel_id=1, source_target_pairs={{0,2},{1,3},{2,0},{3,1},{4,6},{5,7},{6,4},{7,5},{8,10},{9,11},{10,... | collective-permute-start | bytes 331784 | tf_op jit(solution)/shard_map/ppermute | solution.py:47
  34.9 17.5 %collective-permute-start.5 = (bf16[432,128]{1,0:T(8,128)(2,1)S(1)}, bf16[432,128]{1,0:T(8,128)(2,1)S(1)}, u32[]{:S(2)}, u32[]{:S(2)}) collective-permute-start(bf16[432,128]{1,0:T(8,128)(2,1)S(1)} %get-tuple-element.46), channel_id=1, source_target_pairs={{0,6},{1,7},{2,4},{3,5},{4,2},{5,3},{6,0},{7,1},{8,14},{9,15},{10,... | collective-permute-start | bytes 331784 | tf_op jit(solution)/shard_map/ppermute | solution.py:47
  35.1 17.3 %copy-start.13 = (bf16[432,128]{1,0:T(8,128)(2,1)S(1)}, bf16[432,128]{1,0:T(8,128)(2,1)}, u32[]{:S(2)}) copy-start(bf16[432,128]{1,0:T(8,128)(2,1)} %copy-done.12) | copy-start | bytes 331780
  52.5 6.1 %collective-permute-start.10 = (bf16[216,128]{1,0:T(8,128)(2,1)S(1)}, bf16[216,128]{1,0:T(8,128)(2,1)S(1)}, u32[]{:S(2)}, u32[]{:S(2)}) collective-permute-start(bf16[216,128]{1,0:T(8,128)(2,1)S(1)} %dynamic-slice_convert_fusion.4), channel_id=1, source_target_pairs={{0,9},{1,8},{2,11},{3,10},{4,13},{5,12},{6,15},{7,14},{8,1},{9,0},... | collective-permute-start | bytes 165896 | tf_op jit(solution)/shard_map/ppermute | solution.py:47
  59.8 4.9 %collective-permute-start.13 = (f32[8,128]{1,0:T(8,128)S(1)}, f32[8,128]{1,0:T(8,128)S(1)}, u32[]{:S(2)}, u32[]{:S(2)}) collective-permute-start(f32[8,128]{1,0:T(8,128)S(1)} %broadcast_in_dim.7), channel_id=1, source_target_pairs={{0,9},{1,8},{2,11},{3,10},{4,13},{5,12},{6,15},{7,14},{8,1},{9,0},... | collective-permute-start | bytes 12296 | tf_op jit(solution)/shard_map/ppermute | solution.py:59
  59.9 4.9 %collective-permute-start.14 = (f32[8,128]{1,0:T(8,128)S(1)}, f32[8,128]{1,0:T(8,128)S(1)}, u32[]{:S(2)}, u32[]{:S(2)}) collective-permute-start(f32[8,128]{1,0:T(8,128)S(1)} %broadcast_in_dim.7), channel_id=1, source_target_pairs={{0,25},{1,24},{2,27},{3,26},{4,29},{5,28},{6,31},{7,30},{8,17},{9,... | collective-permute-start | bytes 12296 | tf_op jit(solution)/shard_map/ppermute | solution.py:59
  63.5 3.6 %collective-permute-start.12 = (f32[8,128]{1,0:T(8,128)S(1)}, f32[8,128]{1,0:T(8,128)S(1)}, u32[]{:S(2)}, u32[]{:S(2)}) collective-permute-start(f32[8,128]{1,0:T(8,128)S(1)} %broadcast_in_dim.7), channel_id=1, source_target_pairs={{0,16},{1,17},{2,18},{3,19},{4,20},{5,21},{6,22},{7,23},{8,24},{9,... | collective-permute-start | bytes 12296 | tf_op jit(solution)/shard_map/ppermute | solution.py:59
  64.8 6.2 %collective-permute-start.11 = (bf16[216,128]{1,0:T(8,128)(2,1)S(1)}, bf16[216,128]{1,0:T(8,128)(2,1)S(1)}, u32[]{:S(2)}, u32[]{:S(2)}) collective-permute-start(bf16[216,128]{1,0:T(8,128)(2,1)S(1)} %get-tuple-element.49), channel_id=1, source_target_pairs={{0,9},{1,8},{2,11},{3,10},{4,13},{5,12},{6,15},{7,14},{8,1},{9,0},... | collective-permute-start | bytes 165896 | tf_op jit(solution)/shard_map/ppermute | solution.py:47
  71.0 12.3 %copy-start.4 = (bf16[448,128]{1,0:T(8,128)(2,1)}, bf16[448,128]{1,0:T(8,128)(2,1)S(1)}, u32[]{:S(2)}) copy-start(bf16[448,128]{1,0:T(8,128)(2,1)S(1)} %pad_maximum_fusion.3.refs_0_) | copy-start | bytes 344068
  71.1 6.1 %collective-permute-start.15 = (bf16[448,128]{1,0:T(8,128)(2,1)S(1)}, bf16[448,128]{1,0:T(8,128)(2,1)S(1)}, u32[]{:S(2)}, u32[]{:S(2)}) collective-permute-start(bf16[448,128]{1,0:T(8,128)(2,1)S(1)} %pad_maximum_fusion.3.refs_0_), channel_id=1, source_target_pairs={{0,4},{1,5},{2,6},{3,7},{4,0},{5,1},{6,2},{7,3},{8,12},{9,13},{10,... | collective-permute-start | bytes 344072 | tf_op jit(solution)/shard_map/ppermute | solution.py:47
  71.1 6.0 %collective-permute-start.16 = (bf16[448,128]{1,0:T(8,128)(2,1)S(1)}, bf16[448,128]{1,0:T(8,128)(2,1)S(1)}, u32[]{:S(2)}, u32[]{:S(2)}) collective-permute-start(bf16[448,128]{1,0:T(8,128)(2,1)S(1)} %pad_maximum_fusion.3.refs_0_), channel_id=1, source_target_pairs={{0,2},{1,3},{2,0},{3,1},{4,6},{5,7},{6,4},{7,5},{8,10},{9,11},{10,... | collective-permute-start | bytes 344072 | tf_op jit(solution)/shard_map/ppermute | solution.py:47
  72.5 7.0 %collective-permute-start.17 = (bf16[448,128]{1,0:T(8,128)(2,1)S(1)}, bf16[448,128]{1,0:T(8,128)(2,1)S(1)}, u32[]{:S(2)}, u32[]{:S(2)}) collective-permute-start(bf16[448,128]{1,0:T(8,128)(2,1)S(1)} %pad_maximum_fusion.3.refs_0_), channel_id=1, source_target_pairs={{0,6},{1,7},{2,4},{3,5},{4,2},{5,3},{6,0},{7,1},{8,14},{9,15},{10,... | collective-permute-start | bytes 344072 | tf_op jit(solution)/shard_map/ppermute | solution.py:47
  75.3 7.9 %collective-permute-start.18 = (bf16[448,128]{1,0:T(8,128)(2,1)S(1)}, bf16[448,128]{1,0:T(8,128)(2,1)S(1)}, u32[]{:S(2)}, u32[]{:S(2)}) collective-permute-start(bf16[448,128]{1,0:T(8,128)(2,1)S(1)} %pad_maximum_fusion.3.refs_0_), channel_id=1, source_target_pairs={{0,1},{1,0},{2,3},{3,2},{4,5},{5,4},{6,7},{7,6},{8,9},{9,8},{10,11... | collective-permute-start | bytes 344072 | tf_op jit(solution)/shard_map/ppermute | solution.py:47
  77.1 6.2 %copy-start.5 = (bf16[448,128]{1,0:T(8,128)(2,1)}, bf16[448,128]{1,0:T(8,128)(2,1)S(1)}, u32[]{:S(2)}) copy-start(bf16[448,128]{1,0:T(8,128)(2,1)S(1)} %collective-permute-done.15.refs_1_) | copy-start | bytes 344068
  77.1 6.1 %collective-permute-start.19 = (bf16[448,128]{1,0:T(8,128)(2,1)S(1)}, bf16[448,128]{1,0:T(8,128)(2,1)S(1)}, u32[]{:S(2)}, u32[]{:S(2)}) collective-permute-start(bf16[448,128]{1,0:T(8,128)(2,1)S(1)} %collective-permute-done.15.refs_1_), channel_id=1, source_target_pairs={{0,1},{1,0},{2,3},{3,2},{4,5},{5,4},{6,7},{7,6},{8,9},{9,8},{10,11... | collective-permute-start | bytes 344072 | tf_op jit(solution)/shard_map/ppermute | solution.py:47
  77.1 6.2 %copy-start.6 = (bf16[448,128]{1,0:T(8,128)(2,1)}, bf16[448,128]{1,0:T(8,128)(2,1)S(1)}, u32[]{:S(2)}) copy-start(bf16[448,128]{1,0:T(8,128)(2,1)S(1)} %collective-permute-done.16.refs_2_) | copy-start | bytes 344068
  77.1 6.1 %collective-permute-start.20 = (bf16[448,128]{1,0:T(8,128)(2,1)S(1)}, bf16[448,128]{1,0:T(8,128)(2,1)S(1)}, u32[]{:S(2)}, u32[]{:S(2)}) collective-permute-start(bf16[448,128]{1,0:T(8,128)(2,1)S(1)} %collective-permute-done.16.refs_2_), channel_id=1, source_target_pairs={{0,1},{1,0},{2,3},{3,2},{4,5},{5,4},{6,7},{7,6},{8,9},{9,8},{10,11... | collective-permute-start | bytes 344072 | tf_op jit(solution)/shard_map/ppermute | solution.py:47
  79.5 3.9 %copy-start.7 = (bf16[448,128]{1,0:T(8,128)(2,1)}, bf16[448,128]{1,0:T(8,128)(2,1)S(1)}, u32[]{:S(2)}) copy-start(bf16[448,128]{1,0:T(8,128)(2,1)S(1)} %collective-permute-done.17.refs_3_) | copy-start | bytes 344068
  79.5 3.8 %collective-permute-start.21 = (bf16[448,128]{1,0:T(8,128)(2,1)S(1)}, bf16[448,128]{1,0:T(8,128)(2,1)S(1)}, u32[]{:S(2)}, u32[]{:S(2)}) collective-permute-start(bf16[448,128]{1,0:T(8,128)(2,1)S(1)} %collective-permute-done.17.refs_3_), channel_id=1, source_target_pairs={{0,1},{1,0},{2,3},{3,2},{4,5},{5,4},{6,7},{7,6},{8,9},{9,8},{10,11... | collective-permute-start | bytes 344072 | tf_op jit(solution)/shard_map/ppermute | solution.py:47
  83.2 0.6 copy-start.8
  83.3 0.7 copy-start.9
  83.3 0.7 copy-start.10
  83.3 0.7 copy-start.11

commit v3 on v2

v3 whole, which is shorter than its diff:
```python
import functools
import math

import jax
import jax.numpy as jnp
from jax import lax
from jax.experimental import pallas as pl
from jax.experimental.pallas import tpu as pltpu
from jax.sharding import PartitionSpec as P

BF16 = jnp.bfloat16
F32 = jnp.float32
VMEM = pl.BlockSpec(memory_space=pltpu.VMEM)
SMEM = pl.BlockSpec(memory_space=pltpu.SMEM)
ANY = pl.BlockSpec(memory_space=pl.ANY)


def swap(to_near, to_far):
    count = lax.axis_size("slab")
    near = [(i, i ^ 1) for i in range(count)]
    far = [(i, ((i + 1) ^ 1) - 1) for i in range(1, count - 1)]
    return lax.ppermute(to_near, "slab", near), lax.ppermute(to_far, "slab", far)


def exchange(value, mask):
    count = lax.axis_size("slab")
    return lax.ppermute(value, "slab", [(i, i ^ mask) for i in range(count)])


def cross(value, back, mask):
    segments, count = lax.axis_size("segment"), lax.axis_size("slab")
    if back == 0 and mask == 0:
        return value
    route = [
        (s * count + i, (s - back) % segments * count + (i ^ mask))
        for s in range(segments)
        for i in range(count)
    ]
    return lax.ppermute(value, ("segment", "slab"), route)


def block(value, place, rows, dtype):
    return lax.dynamic_slice_in_dim(value, place * rows, rows, 0).astype(dtype)


def write_shifts(plane, height, out_ref, first):
    cells, channels = plane.shape
    width = cells // height
    rows = plane.astype(F32).reshape(width, height, channels)
    at = lax.broadcasted_iota(jnp.int32, rows.shape, 1)
    zero = jnp.zeros((1, height, channels), F32)
    before = jnp.where(at == 0, 0.0, pltpu.roll(rows, 1, 1))
    after = jnp.where(at == height - 1, 0.0, pltpu.roll(rows, height - 1, 1))
    for dy, moved in enumerate((before, rows, after)):
        for dx in range(3):
            if dx == 0:
                value = jnp.concatenate([zero, moved[:-1]], axis=0)
            elif dx == 1:
                value = moved
            else:
                value = jnp.concatenate([moved[1:], zero], axis=0)
            j = dx * 3 + dy
            out_ref[first : first + cells, j * channels : (j + 1) * channels] = value.reshape(
                cells, channels
            ).astype(BF16)


def back_product(shifts, weight_ref, rows, cells):
    channels = weight_ref.shape[1]
    total = None
    for dz in range(3):
        mirrored = [26 - 9 * dz - j for j in range(9)]
        side = jnp.concatenate(
            [weight_ref[k * channels : (k + 1) * channels, :] for k in mirrored], axis=1
        )
        term = lax.dot_general(
            shifts[dz * cells : dz * cells + rows, :],
            side,
            (((1,), (1,)), ((), ())),
            preferred_element_type=F32,
        )
        total = term if total is None else total + term
    return total


def rim_kernel(flag, acts, grad, near, far, sems):
    micro, depth = acts.shape[:2]
    top = flag[0]
    copies = []
    for which, (out, high) in enumerate(((near, top), (far, 1 - top))):
        for m in range(micro):
            for part, (source, size, at) in enumerate(((acts, 2, 0), (grad, 1, 2))):
                copy = pltpu.make_async_copy(
                    source.at[m, pl.ds(high * (depth - size), size)],
                    out.at[m, at : at + size],
                    sems.at[which, m, part],
                )
                copy.start()
                copies.append(copy)
    for copy in copies:
        copy.wait()


def first_kernel(height, flag, acts, near, far, grad, weight, result, slopes, shifts, deltas):
    micro, depth, cells, channels = acts.shape
    even = flag[0] == 1
    span = 9 * channels
    rows = depth * cells
    for m in range(micro):

        def rim(a, b, n):
            return jnp.where(even, a[m, n].astype(F32), b[m, n].astype(F32))

        planes = [rim(far, near, n) for n in range(2)]
        planes += [acts[m, n] for n in range(depth)]
        planes += [rim(near, far, n) for n in range(2)]
        for n, plane in enumerate(planes):
            write_shifts(plane, height, shifts.at[m], n * cells)
        preact = None
        for dz in range(3):
            term = jnp.dot(
                shifts[m, dz * cells : dz * cells + rows + 2 * cells, :],
                weight[dz * span : (dz + 1) * span, :],
                preferred_element_type=F32,
            )
            preact = term if preact is None else preact + term
        sig = 1.0 / (1.0 + jnp.exp(-preact))
        slope = sig * (1.0 + preact * (1.0 - sig))
        slopes[m] = slope[cells : cells + rows]
        ups = [rim(far, near, 2)] + [grad[m, n].astype(F32) for n in range(depth)]
        ups.append(rim(near, far, 2))
        for n, up in enumerate(ups):
            delta = (up * slope[n * cells : (n + 1) * cells]).astype(BF16)
            write_shifts(delta, height, deltas.at[m], n * cells)
        back = back_product(deltas.at[m], weight, rows, cells)
        upstream = grad[m].reshape(rows, channels).astype(F32)
        result[m] = (upstream + back).astype(BF16)


def patch_kernel(cells, shifts, out):
    micro, total, span = shifts.shape
    rows = total - 4 * cells
    for m in range(micro):
        for dz in range(3):
            first = (1 + dz) * cells
            out[m * rows : (m + 1) * rows, dz * span : (dz + 1) * span] = shifts[
                m, first : first + rows, :
            ]


def back_kernel(height, flag, deltas, near, far, upstream, weight, out, shifts):
    micro, depth, cells, channels = deltas.shape
    even = flag[0] == 1
    rows = depth * cells
    for m in range(micro):
        low, high = near[m, 0].astype(F32), far[m, 0].astype(F32)
        planes = [jnp.where(even, high, low)] + [deltas[m, n] for n in range(depth)]
        planes.append(jnp.where(even, low, high))
        for n, plane in enumerate(planes):
            write_shifts(plane, height, shifts.at[m], n * cells)
        back = back_product(shifts.at[m], weight, rows, cells)
        total = upstream[m].reshape(rows, channels).astype(F32) + back
        out[m] = total.astype(BF16).reshape(depth, cells, channels)


def place_kernel(bound, spot, *refs):
    pieces, (out, scaled, sems) = refs[:-3], refs[-3:]
    rows = scaled.shape[1]
    sums = [piece[rows:].astype(F32) for piece in pieces]
    while len(sums) > 1:
        sums = [a + b for a, b in zip(sums[::2], sums[1::2], strict=True)]
    norm = jnp.sqrt(jnp.sum(sums[0], axis=0, keepdims=True))
    factor = jnp.minimum(1.0, bound / (norm + 1e-06))
    copies = []
    for n, piece in enumerate(pieces):
        scaled[n] = piece[:rows].astype(F32) * factor
        copies.append(pltpu.make_async_copy(scaled.at[n], out.at[spot[0] ^ n], sems.at[n]))
        copies[-1].start()
    for copy in copies:
        copy.wait()


def shards(activations, weights, out_grad):
    weight = weights[0]
    channels = weight.shape[1]
    micro, depth, width, height = activations.shape[1:5]
    cells = width * height
    acts = activations[0].reshape(micro, depth, cells, channels)
    grad = out_grad.reshape(micro, depth, cells, channels)
    rows = depth * cells
    segments = lax.axis_size("segment")
    count = lax.axis_size("slab")
    index = lax.axis_index("slab")
    last = lax.axis_index("segment") == segments - 1
    flag = (1 - lax.rem(index, 2)).astype(jnp.int32).reshape(1)
    params = pltpu.CompilerParams(vmem_limit_bytes=40 << 20)

    rim = jax.ShapeDtypeStruct((micro, 3, cells, channels), BF16)
    to_near, to_far = pl.pallas_call(
        rim_kernel,
        out_shape=(rim, rim),
        in_specs=[SMEM, ANY, ANY],
        out_specs=(VMEM, VMEM),
        scratch_shapes=[pltpu.SemaphoreType.DMA((2, micro, 2))],
    )(flag, acts, grad)
    near, far = swap(to_near, to_far)

    result, slopes, shifts = pl.pallas_call(
        functools.partial(first_kernel, height),
        out_shape=(
            jax.ShapeDtypeStruct((micro, rows, channels), BF16),
            jax.ShapeDtypeStruct((micro, rows, channels), F32),
            jax.ShapeDtypeStruct((micro, rows + 4 * cells, 9 * channels), BF16),
        ),
        in_specs=[SMEM] + [VMEM] * 5,
        out_specs=(VMEM, VMEM, VMEM),
        scratch_shapes=[pltpu.VMEM((micro, rows + 2 * cells, 9 * channels), BF16)],
        compiler_params=params,
    )(flag, acts, near, far, grad, weight)
    patches = pl.pallas_call(
        functools.partial(patch_kernel, cells),
        out_shape=jax.ShapeDtypeStruct((micro * rows, 27 * channels), BF16),
        in_specs=[VMEM],
        out_specs=VMEM,
        compiler_params=params,
    )(shifts)

    def rims(value):
        low, high = value[:, :1], value[:, -1:]
        even = flag[0] == 1
        return swap(jnp.where(even, high, low), jnp.where(even, low, high))

    def conv_back(value, near, far, upstream):
        return pl.pallas_call(
            functools.partial(back_kernel, height),
            out_shape=jax.ShapeDtypeStruct((micro, depth, cells, channels), BF16),
            in_specs=[SMEM] + [VMEM] * 5,
            out_specs=VMEM,
            scratch_shapes=[pltpu.VMEM((micro, rows + 2 * cells, 9 * channels), BF16)],
            compiler_params=params,
        )(flag, value, near, far, upstream, weight)

    result = result.reshape(micro, depth, cells, channels)
    upstream, deltas = grad, None
    for step in range(1, segments):
        incoming = cross(result, 1, 0)
        upstream = jnp.where(last, grad, incoming)
        slope = slopes.reshape(micro, depth, cells, channels)
        deltas = (upstream.astype(F32) * slope).astype(BF16)
        if step < segments - 1:
            result = conv_back(deltas, *rims(deltas), upstream)

    partial = lax.dot_general(
        patches,
        deltas.reshape(micro * rows, channels),
        (((0,), (0,)), ((), ())),
        preferred_element_type=F32,
    )

    bits = [1 << n for n in range(1, count.bit_length() - 1)]
    inner = [bits[n : n + 2] for n in range(2, len(bits), 2)]
    crossing = inner[-1][0] if len(inner[-1]) == 1 else 0
    side = lax.rem(index, 2) ^ jnp.where(index & crossing, 1, 0)
    quarter = jnp.where(index & 2, 2, 0) + jnp.where(index & 4, 1, 0)
    part = partial.shape[0] // 8
    masks = {1: 4, 2: 2, 3: 6}

    pieces = {}
    far = []
    for turn in (3, 2, 1, 0):
        there = quarter ^ turn
        got = exchange(block(partial, (1 - side) * 4 + there, part, BF16), 1)
        if turn == 0:
            got, deltas = lax.optimization_barrier((got, deltas))
        piece = block(partial, side * 4 + there, part, F32) + got.astype(F32)
        if turn:
            far.append(exchange(piece.astype(BF16), masks[turn]))
    chunk = piece + sum(other.astype(F32) for other in far)

    gradients = conv_back(deltas, *rims(deltas), upstream)

    def places(group):
        own = sum(jnp.where(index & bit, 1 << n, 0) for n, bit in enumerate(group))
        others = []
        for turn in range(1, 1 << len(group)):
            mask = sum(bit for n, bit in enumerate(group) if turn >> n & 1)
            others.append((mask | 1 if mask == crossing else mask, own ^ turn))
        return own, others

    for group in inner:
        own, others = places(group)
        size = chunk.shape[0] >> len(group)
        got = [exchange(block(chunk, there, size, BF16), mask) for mask, there in others]
        chunk = block(chunk, own, size, F32) + sum(g.astype(F32) for g in got)

    gathered = chunk.astype(BF16)
    for group in reversed(inner):
        own, others = places(group)
        got = [(there, exchange(gathered, mask)) for mask, there in others]
        if group is inner[-1]:
            squares = jnp.broadcast_to(jnp.sum(chunk * chunk), (8, 128))
            sums = []
            for mask in [0] + [mask for mask, _ in others]:
                sums.append(sum(cross(squares, back, mask) for back in range(segments)))
            while len(sums) > 1:
                sums = [a + b for a, b in zip(sums[::2], sums[1::2], strict=True)]
            squares = sums[0][0]
        blocks = []
        for n in range(1 << len(group)):
            value = jnp.where(own == n, gathered, got[0][1])
            for there, other in got[1:]:
                value = jnp.where(there == n, other, value)
            blocks.append(value)
        gathered = jnp.concatenate(blocks, axis=0)

    first = lax.reduce_precision(squares, 8, 7)
    second = lax.reduce_precision(squares - first, 8, 7)
    third = squares - first - second
    terms = jnp.zeros((16, channels), F32).at[0].set(first).at[1].set(second).at[2].set(third)
    payload = jnp.concatenate([gathered, terms.astype(BF16)], axis=0)
    near = [payload] + [exchange(payload, masks[turn]) for turn in (1, 2, 3)]
    both = near + [exchange(piece, 1) for piece in near]
    bound = math.sqrt(27.0 * channels * channels * segments)
    update = pl.pallas_call(
        functools.partial(place_kernel, bound),
        out_shape=jax.ShapeDtypeStruct((8, part, channels), F32),
        in_specs=[SMEM] + [VMEM] * 8,
        out_specs=ANY,
        scratch_shapes=[pltpu.VMEM((8, part, channels), F32), pltpu.SemaphoreType.DMA((8,))],
    )((side * 4 + quarter).astype(jnp.int32).reshape(1), *both)
    gradients = gradients.reshape(1, micro, depth, width, height, channels)
    return (update.reshape(1, 8 * part, channels), gradients)


def solution(mesh):
    return jax.shard_map(
        shards,
        mesh=mesh,
        in_specs=(
            P("segment", None, "slab", None, None, None),
            P("segment", None, None),
            P(None, "slab", None, None, None),
        ),
        out_specs=(P("segment", None, None), P("segment", None, "slab", None, None, None)),
        check_vma=False,
    )
```

time: 88.8 us -> 75.4 us (0.85)
  the two profiles are of different devices: /device:TPU:0 before, /device:TPU:5 now
where the time goes in v3:
time: 75.4 us; the launch traced here: 75 us
  waiting for transfers between devices  28.5 us (38%)
  starting transfers between devices  26.2 us (35%)
  Pallas kernels  9.65 us (13%)
  local copies, waits for them, and re-layouts  4.5 us (6%)
  other arithmetic  4.12 us (5%)
  matrix products  1.12 us (1%)
  between operations  0.87 us (1%)
    ppermute x16, waiting for transfers between devices, exchange(): return lax.ppermute(value, 'slab', [(i, i ^ mask) for i in range(count)])  14.7 us
    ppermute x16, starting transfers between devices, exchange(): return lax.ppermute(value, 'slab', [(i, i ^ mask) for i in range(count)])  13.7 us
    ppermute x2, waiting for transfers between devices, swap(): lax.ppermute(to_far, 'slab', far)  7.41 us
    ppermute x2, starting transfers between devices, swap(): lax.ppermute(to_far, 'slab', far)  5.72 us
    ppermute x4, starting transfers between devices, cross(): return lax.ppermute(value, ('segment', 'slab'), route)  5.6 us
    ppermute x4, waiting for transfers between devices, cross(): return lax.ppermute(value, ('segment', 'slab'), route)  5.56 us
    unnamed x26, local copies, waits for them, and re-layouts  3.7 us
    pallas_call x1, Pallas kernels, shards(): pl.pallas_call(functools.partial(first_kernel, height), out_shape=(jax.Sh...  3.46 us
  transfers between devices with their start and end apart: 24, of which 13 were waited for; matrix products, arithmetic and copies ran while one was open for 3% of the time, Pallas kernels for 3%

profile of v3, /device:TPU:5, one launch (start us, length us, event | category | flops | bytes accessed | tf_op | source)
XLA Modules:
  0.0 75.0 jit_solution(13786610526852739810)
XLA Ops:
  0.6 1.6 %shard_map.50 = (bf16[2,3,64,128]{3,2,1,0:T(8,128)(2,1)}, bf16[2,3,64,128]{3,2,1,0:T(8,128)(2,1)}) custom-call(s32[1]{0:T(128)} %bitcast.1.flag, bf16[2,4,64,128]{3,2,1,0:T(8,128)(2,1)} %bitcast.19, bf16[2,4,64,128]{3,2,1,0:T(8,128)(2,1)} %bitcast.17), custom_call_target="tpu_custom_call" | custom-call | tf_op jit(solution)/shard_map/pallas_call | solution.py:199
  2.2 0.7 collective-permute-start
  3.0 3.0 %collective-permute-start.1 = (bf16[2,3,64,128]{3,2,1,0:T(8,128)(2,1)}, bf16[2,3,64,128]{3,2,1,0:T(8,128)(2,1)S(1)}, u32[]{:S(2)}, u32[]{:S(2)}) collective-permute-start(bf16[2,3,64,128]{3,2,1,0:T(8,128)(2,1)} %get-tuple-element.46), channel_id=1, source_target_pairs={{1,2},{2,1},{3,4},{4,3},{5,6},{6,5},{7,8},{8,7},{9,10},{10,9},{11,... | collective-permute-start | bytes 294920 | tf_op jit(solution)/shard_map/ppermute | solution.py:22
  6.1 4.0 %collective-permute-done.1.far = bf16[2,3,64,128]{3,2,1,0:T(8,128)(2,1)S(1)} collective-permute-done((bf16[2,3,64,128]{3,2,1,0:T(8,128)(2,1)}, bf16[2,3,64,128]{3,2,1,0:T(8,128)(2,1)S(1)}, u32[]{:S(2)}, u32[]{:S(2)}) %collective-permute-start.1) | collective-permute-done | bytes 98336 | tf_op jit(solution)/shard_map/ppermute | solution.py:22
  10.0 1.2 %copy-done = bf16[1,3456,128]{2,1,0:T(8,128)(2,1)S(1)} copy-done((bf16[1,3456,128]{2,1,0:T(8,128)(2,1)S(1)}, bf16[1,3456,128]{2,1,0:T(8,128)(2,1)}, u32[]{:S(2)}) %copy-start) | copy-done | bytes 884760
  11.2 0.9 %copy-done.2 = bf16[2,4,8,8,128]{4,3,2,1,0:T(8,128)(2,1)S(1)} copy-done((bf16[2,4,8,8,128]{4,3,2,1,0:T(8,128)(2,1)S(1)}, bf16[2,4,8,8,128]{4,3,2,1,0:T(8,128)(2,1)}, u32[]{:S(2)}) %copy-start.2) | copy-done | bytes 131096
  12.1 0.9 %copy-done.4 = bf16[1,2,4,8,8,128]{5,4,3,2,1,0:T(8,128)(2,1)S(1)} copy-done((bf16[1,2,4,8,8,128]{5,4,3,2,1,0:T(8,128)(2,1)S(1)}, bf16[1,2,4,8,8,128]{5,4,3,2,1,0:T(8,128)(2,1)}, u32[]{:S(2)}) %copy-start.4) | copy-done | bytes 131096
  13.0 3.5 %shard_map.51 = (bf16[2,256,128]{2,1,0:T(8,128)(2,1)S(1)}, f32[2,256,128]{2,1,0:T(8,128)S(1)}, bf16[2,512,1152]{2,1,0:T(8,128)(2,1)S(1)}) custom-call(s32[1]{0:T(128)} %bitcast.1.flag, bf16[2,4,64,128]{3,2,1,0:T(8,128)(2,1)S(1)} %bitcast.20, bf16[2,3,64,128]{3,2,1,0:T(8,128)(2,1)S(1)} %collective-permute-done.near, ...), custom_call_target="tpu_custom_call" | custom-call | tf_op jit(solution)/shard_map/pallas_call | solution.py:208
  16.5 1.3 %collective-permute-start.2 = (bf16[2,4,64,128]{3,2,1,0:T(8,128)(2,1)S(1)}, bf16[2,4,64,128]{3,2,1,0:T(8,128)(2,1)S(1)}, u32[]{:S(2)}, u32[]{:S(2)}) collective-permute-start(bf16[2,4,64,128]{3,2,1,0:T(8,128)(2,1)S(1)} %bitcast.22), channel_id=1, source_target_pairs={{0,16},{1,17},{2,18},{3,19},{4,20},{5,21},{6,22},{7,23},{8,24},{9,... | collective-permute-start | bytes 393224 | tf_op jit(solution)/shard_map/ppermute | solution.py:39
  17.7 0.3 shard_map.52
  18.0 3.3 %collective-permute-done.2 = bf16[2,4,64,128]{3,2,1,0:T(8,128)(2,1)S(1)} collective-permute-done((bf16[2,4,64,128]{3,2,1,0:T(8,128)(2,1)S(1)}, bf16[2,4,64,128]{3,2,1,0:T(8,128)(2,1)S(1)}, u32[]{:S(2)}, u32[]{:S(2)}) %collective-permute-start.2) | collective-permute-done | bytes 131104 | tf_op jit(solution)/shard_map/ppermute | solution.py:39
  21.4 1.1 %fusion.2 = f32[3456,128]{1,0:T(8,128)S(1)} fusion(bf16[512,3456]{1,0:T(8,128)(2,1)S(1)} %shard_map.52, bf16[512,128]{1,0:T(8,128)(2,1)S(1)} %bitcast.16), kind=kOutput, calls=%fused_computation.24 | convolution fusion | flops 452984832 | bytes 5439488 | tf_op jit(solution)/shard_map/dot_general | solution.py:253
  22.6 0.4 collective-permute-start.4
  23.1 0.2 collective-permute-start.6
  23.2 0.4 collective-permute-start.8
  23.6 0.2 collective-permute-start.3
  23.7 0.4 collective-permute-done.4
  24.1 0.4 collective-permute-done.6
  24.5 0.2 collective-permute-done.8
  24.7 1.8 %add_convert_fusion.2 = (bf16[432,128]{1,0:T(8,128)(2,1)}, bf16[432,128]{1,0:T(8,128)(2,1)S(1)}, bf16[432,128]{1,0:T(8,128)(2,1)}) fusion(bf16[432,128]{1,0:T(8,128)(2,1)} %collective-permute-done.4, f32[3456,128]{1,0:T(8,128)S(1)} %fusion.2, s32[]{:T(128)S(6)} %select_n.84, bf16[432,128]{1,0:T(8,128)(2,1)} %collective-permute-done.8, s32[]{:T(128)S(6)} %select_n.88, ...), kind=kLoop, calls=%fused_computation.6 | loop fusion | flops 497664 | bytes 1327116 | tf_op jit(solution)/shard_map/convert_element_type | solution.py:277
  26.4 2.1 %collective-permute-start.5 = (bf16[432,128]{1,0:T(8,128)(2,1)}, bf16[432,128]{1,0:T(8,128)(2,1)S(1)}, u32[]{:S(2)}, u32[]{:S(2)}) collective-permute-start(bf16[432,128]{1,0:T(8,128)(2,1)} %get-tuple-element.58), channel_id=1, source_target_pairs={{0,6},{1,7},{2,4},{3,5},{4,2},{5,3},{6,0},{7,1},{8,14},{9,15},{10,... | collective-permute-start | bytes 331784 | tf_op jit(solution)/shard_map/ppermute | solution.py:27
  28.6 0.3 collective-permute-start.7
  28.9 0.2 collective-permute-start.9
  29.1 2.7 %collective-permute-done.5 = bf16[432,128]{1,0:T(8,128)(2,1)S(1)} collective-permute-done((bf16[432,128]{1,0:T(8,128)(2,1)}, bf16[432,128]{1,0:T(8,128)(2,1)S(1)}, u32[]{:S(2)}, u32[]{:S(2)}) %collective-permute-start.5) | collective-permute-done | bytes 110624 | tf_op jit(solution)/shard_map/ppermute | solution.py:27
  31.8 3.1 %collective-permute-done.7 = bf16[432,128]{1,0:T(8,128)(2,1)S(1)} collective-permute-done((bf16[432,128]{1,0:T(8,128)(2,1)}, bf16[432,128]{1,0:T(8,128)(2,1)S(1)}, u32[]{:S(2)}, u32[]{:S(2)}) %collective-permute-start.7) | collective-permute-done | bytes 110624 | tf_op jit(solution)/shard_map/ppermute | solution.py:27
  34.9 1.0 %add_add_fusion = f32[432,128]{1,0:T(8,128)S(1)} fusion(bf16[432,128]{1,0:T(8,128)(2,1)} %collective-permute-done.9, bf16[432,128]{1,0:T(8,128)(2,1)S(1)} %collective-permute-done.7, bf16[432,128]{1,0:T(8,128)(2,1)S(1)} %collective-permute-done.5, bf16[432,128]{1,0:T(8,128)(2,1)S(1)} %collective-permute-done.3, f32[3456,128]{1,0:T(8,128)S(1)} %fusion.2, ...), kind=kLoop, calls=%fused_computation.1 | loop fusion | flops 442368 | bytes 884740 | tf_op jit(solution)/shard_map/add | solution.py:278
  35.9 2.8 %collective-permute-start.10 = (bf16[216,128]{1,0:T(8,128)(2,1)S(1)}, bf16[216,128]{1,0:T(8,128)(2,1)S(1)}, u32[]{:S(2)}, u32[]{:S(2)}) collective-permute-start(bf16[216,128]{1,0:T(8,128)(2,1)S(1)} %dynamic-slice_convert_fusion.4), channel_id=1, source_target_pairs={{0,9},{1,8},{2,11},{3,10},{4,13},{5,12},{6,15},{7,14},{8,1},{9,0},... | collective-permute-start | bytes 165896 | tf_op jit(solution)/shard_map/ppermute | solution.py:27
  38.7 2.2 %collective-permute-done.10 = bf16[216,128]{1,0:T(8,128)(2,1)S(1)} collective-permute-done((bf16[216,128]{1,0:T(8,128)(2,1)S(1)}, bf16[216,128]{1,0:T(8,128)(2,1)S(1)}, u32[]{:S(2)}, u32[]{:S(2)}) %collective-permute-start.10) | collective-permute-done | bytes 55328 | tf_op jit(solution)/shard_map/ppermute | solution.py:27
  40.8 0.6 fusion
  41.5 0.6 broadcast_in_dim.4
  42.1 1.3 %collective-permute-start.12 = (f32[8,128]{1,0:T(8,128)S(1)}, f32[8,128]{1,0:T(8,128)S(1)}, u32[]{:S(2)}, u32[]{:S(2)}) collective-permute-start(f32[8,128]{1,0:T(8,128)S(1)} %broadcast_in_dim.4), channel_id=1, source_target_pairs={{0,16},{1,17},{2,18},{3,19},{4,20},{5,21},{6,22},{7,23},{8,24},{9,... | collective-permute-start | bytes 12296 | tf_op jit(solution)/shard_map/ppermute | solution.py:39
  43.4 3.0 %collective-permute-start.13 = (f32[8,128]{1,0:T(8,128)S(1)}, f32[8,128]{1,0:T(8,128)S(1)}, u32[]{:S(2)}, u32[]{:S(2)}) collective-permute-start(f32[8,128]{1,0:T(8,128)S(1)} %broadcast_in_dim.4), channel_id=1, source_target_pairs={{0,9},{1,8},{2,11},{3,10},{4,13},{5,12},{6,15},{7,14},{8,1},{9,0},... | collective-permute-start | bytes 12296 | tf_op jit(solution)/shard_map/ppermute | solution.py:39
  46.4 2.6 %collective-permute-start.11 = (bf16[216,128]{1,0:T(8,128)(2,1)S(1)}, bf16[216,128]{1,0:T(8,128)(2,1)S(1)}, u32[]{:S(2)}, u32[]{:S(2)}) collective-permute-start(bf16[216,128]{1,0:T(8,128)(2,1)S(1)} %get-tuple-element.61), channel_id=1, source_target_pairs={{0,9},{1,8},{2,11},{3,10},{4,13},{5,12},{6,15},{7,14},{8,1},{9,0},... | collective-permute-start | bytes 165896 | tf_op jit(solution)/shard_map/ppermute | solution.py:27
  49.1 2.2 %collective-permute-done.14 = f32[8,128]{1,0:T(8,128)S(1)} collective-permute-done((f32[8,128]{1,0:T(8,128)S(1)}, f32[8,128]{1,0:T(8,128)S(1)}, u32[]{:S(2)}, u32[]{:S(2)}) %collective-permute-start.14) | collective-permute-done | bytes 4128 | tf_op jit(solution)/shard_map/ppermute | solution.py:39
  51.3 0.6 add_add_fusion.1
  52.1 2.2 %collective-permute-start.15 = (bf16[448,128]{1,0:T(8,128)(2,1)S(1)}, bf16[448,128]{1,0:T(8,128)(2,1)S(1)}, u32[]{:S(2)}, u32[]{:S(2)}) collective-permute-start(bf16[448,128]{1,0:T(8,128)(2,1)S(1)} %pad_maximum_fusion.refs_0_), channel_id=1, source_target_pairs={{0,4},{1,5},{2,6},{3,7},{4,0},{5,1},{6,2},{7,3},{8,12},{9,13},{10,... | collective-permute-start | bytes 344072 | tf_op jit(solution)/shard_map/ppermute | solution.py:27
  54.3 0.5 collective-permute-start.16
  54.8 0.8 %collective-permute-start.17 = (bf16[448,128]{1,0:T(8,128)(2,1)S(1)}, bf16[448,128]{1,0:T(8,128)(2,1)S(1)}, u32[]{:S(2)}, u32[]{:S(2)}) collective-permute-start(bf16[448,128]{1,0:T(8,128)(2,1)S(1)} %pad_maximum_fusion.refs_0_), channel_id=1, source_target_pairs={{0,6},{1,7},{2,4},{3,5},{4,2},{5,3},{6,0},{7,1},{8,14},{9,15},{10,... | collective-permute-start | bytes 344072 | tf_op jit(solution)/shard_map/ppermute | solution.py:27
  55.7 2.1 %collective-permute-done.15.refs_1_ = bf16[448,128]{1,0:T(8,128)(2,1)S(1)} collective-permute-done((bf16[448,128]{1,0:T(8,128)(2,1)S(1)}, bf16[448,128]{1,0:T(8,128)(2,1)S(1)}, u32[]{:S(2)}, u32[]{:S(2)}) %collective-permute-start.15) | collective-permute-done | bytes 114720 | tf_op jit(solution)/shard_map/ppermute | solution.py:27
  57.9 3.7 %collective-permute-done.16.refs_2_ = bf16[448,128]{1,0:T(8,128)(2,1)S(1)} collective-permute-done((bf16[448,128]{1,0:T(8,128)(2,1)S(1)}, bf16[448,128]{1,0:T(8,128)(2,1)S(1)}, u32[]{:S(2)}, u32[]{:S(2)}) %collective-permute-start.16) | collective-permute-done | bytes 114720 | tf_op jit(solution)/shard_map/ppermute | solution.py:27
  61.6 0.7 collective-permute-start.20
  62.4 0.5 collective-permute-start.22
  62.9 0.9 %collective-permute-done.22.near = bf16[2,1,64,128]{3,2,1,0:T(8,128)(2,1)S(1)} collective-permute-done((bf16[2,1,64,128]{3,2,1,0:T(8,128)(2,1)S(1)}, bf16[2,1,64,128]{3,2,1,0:T(8,128)(2,1)S(1)}, u32[]{:S(2)}, u32[]{:S(2)}) %collective-permute-start.22) | collective-permute-done | bytes 32800 | tf_op jit(solution)/shard_map/ppermute | solution.py:22
  63.8 2.7 %collective-permute-start.23 = (bf16[2,1,64,128]{3,2,1,0:T(8,128)(2,1)S(1)}, bf16[2,1,64,128]{3,2,1,0:T(8,128)(2,1)S(1)}, u32[]{:S(2)}, u32[]{:S(2)}) collective-permute-start(bf16[2,1,64,128]{3,2,1,0:T(8,128)(2,1)S(1)} %get-tuple-element.63), channel_id=1, source_target_pairs={{1,2},{2,1},{3,4},{4,3},{5,6},{6,5},{7,8},{8,7},{9,10},{10,9},{11,... | collective-permute-start | bytes 98312 | tf_op jit(solution)/shard_map/ppermute | solution.py:22
  66.5 3.4 %collective-permute-done.23.far = bf16[2,1,64,128]{3,2,1,0:T(8,128)(2,1)S(1)} collective-permute-done((bf16[2,1,64,128]{3,2,1,0:T(8,128)(2,1)S(1)}, bf16[2,1,64,128]{3,2,1,0:T(8,128)(2,1)S(1)}, u32[]{:S(2)}, u32[]{:S(2)}) %collective-permute-start.23) | collective-permute-done | bytes 32800 | tf_op jit(solution)/shard_map/ppermute | solution.py:22
  69.9 1.8 %shard_map.54 = bf16[2,4,64,128]{3,2,1,0:T(8,128)(2,1)} custom-call(s32[1]{0:T(128)} %bitcast.1.flag, bf16[2,4,64,128]{3,2,1,0:T(8,128)(2,1)S(1)} %get-tuple-element.51.deltas, bf16[2,1,64,128]{3,2,1,0:T(8,128)(2,1)S(1)} %collective-permute-done.22.near, bf16[2,1,64,128]{3,2,1,0:T(8,128)(2,1)S(1)} %collective-permute-done.23.far, ...), custom_call_target="tpu_custom_call" | custom-call | tf_op jit(solution)/shard_map/pallas_call | solution.py:234
  71.8 0.5 copy-done.9
  72.5 2.6 %shard_map.53 = f32[8,432,128]{2,1,0:T(8,128)} custom-call(s32[1]{0:T(128)} %bitcast.spot, bf16[448,128]{1,0:T(8,128)(2,1)} %copy-done.5, bf16[448,128]{1,0:T(8,128)(2,1)} %copy-done.6, bf16[448,128]{1,0:T(8,128)(2,1)} %copy-done.7, bf16[448,128]{1,0:T(8,128)(2,1)} %copy-done.8, bf16[448,128]{1,0:T(8,128)(2,1)} %copy-done.9, bf16[448,128]{1,0:T(8,128)(2,1)} %copy-done.10, ...), custom_call_target="tpu_custom_call" | custom-call | tf_op jit(solution)/shard_map/pallas_call | solution.py:324
  (47 shorter events, 0.8 us)
Async XLA Ops:
  2.2 3.8 %collective-permute-start = (bf16[2,3,64,128]{3,2,1,0:T(8,128)(2,1)}, bf16[2,3,64,128]{3,2,1,0:T(8,128)(2,1)S(1)}, u32[]{:S(2)}, u32[]{:S(2)}) collective-permute-start(bf16[2,3,64,128]{3,2,1,0:T(8,128)(2,1)} %get-tuple-element.45), channel_id=1, source_target_pairs={{0,1},{1,0},{2,3},{3,2},{4,5},{5,4},{6,7},{7,6},{8,9},{9,8},{10,11... | collective-permute-start | bytes 294920 | tf_op jit(solution)/shard_map/ppermute | solution.py:22
  3.0 7.0 %collective-permute-start.1 = (bf16[2,3,64,128]{3,2,1,0:T(8,128)(2,1)}, bf16[2,3,64,128]{3,2,1,0:T(8,128)(2,1)S(1)}, u32[]{:S(2)}, u32[]{:S(2)}) collective-permute-start(bf16[2,3,64,128]{3,2,1,0:T(8,128)(2,1)} %get-tuple-element.46), channel_id=1, source_target_pairs={{1,2},{2,1},{3,4},{4,3},{5,6},{6,5},{7,8},{8,7},{9,10},{10,9},{11,... | collective-permute-start | bytes 294920 | tf_op jit(solution)/shard_map/ppermute | solution.py:22
  10.0 1.2 %copy-start = (bf16[1,3456,128]{2,1,0:T(8,128)(2,1)S(1)}, bf16[1,3456,128]{2,1,0:T(8,128)(2,1)}, u32[]{:S(2)}) copy-start(bf16[1,3456,128]{2,1,0:T(8,128)(2,1)} %param.10) | copy-start | bytes 2654212
  11.2 0.9 %copy-start.2 = (bf16[2,4,8,8,128]{4,3,2,1,0:T(8,128)(2,1)S(1)}, bf16[2,4,8,8,128]{4,3,2,1,0:T(8,128)(2,1)}, u32[]{:S(2)}) copy-start(bf16[2,4,8,8,128]{4,3,2,1,0:T(8,128)(2,1)} %param.11) | copy-start | bytes 393220
  12.1 0.9 %copy-start.4 = (bf16[1,2,4,8,8,128]{5,4,3,2,1,0:T(8,128)(2,1)S(1)}, bf16[1,2,4,8,8,128]{5,4,3,2,1,0:T(8,128)(2,1)}, u32[]{:S(2)}) copy-start(bf16[1,2,4,8,8,128]{5,4,3,2,1,0:T(8,128)(2,1)} %param.9) | copy-start | bytes 393220
  16.5 4.9 %collective-permute-start.2 = (bf16[2,4,64,128]{3,2,1,0:T(8,128)(2,1)S(1)}, bf16[2,4,64,128]{3,2,1,0:T(8,128)(2,1)S(1)}, u32[]{:S(2)}, u32[]{:S(2)}) collective-permute-start(bf16[2,4,64,128]{3,2,1,0:T(8,128)(2,1)S(1)} %bitcast.22), channel_id=1, source_target_pairs={{0,16},{1,17},{2,18},{3,19},{4,20},{5,21},{6,22},{7,23},{8,24},{9,... | collective-permute-start | bytes 393224 | tf_op jit(solution)/shard_map/ppermute | solution.py:39
  17.7 3.6 %copy-start.3 = (bf16[2,4,8,8,128]{4,3,2,1,0:T(8,128)(2,1)S(1)}, bf16[2,4,8,8,128]{4,3,2,1,0:T(8,128)(2,1)}, u32[]{:S(2)}) copy-start(bf16[2,4,8,8,128]{4,3,2,1,0:T(8,128)(2,1)} %param.11) | copy-start | bytes 393220
  22.6 47.3 %copy-start.1 = (bf16[1,3456,128]{2,1,0:T(8,128)(2,1)S(1)}, bf16[1,3456,128]{2,1,0:T(8,128)(2,1)}, u32[]{:S(2)}) copy-start(bf16[1,3456,128]{2,1,0:T(8,128)(2,1)} %param.10) | copy-start | bytes 2654212
  22.6 1.5 %collective-permute-start.4 = (bf16[432,128]{1,0:T(8,128)(2,1)S(1)}, bf16[432,128]{1,0:T(8,128)(2,1)}, u32[]{:S(2)}, u32[]{:S(2)}) collective-permute-start(bf16[432,128]{1,0:T(8,128)(2,1)S(1)} %get-tuple-element.57), channel_id=1, source_target_pairs={{0,1},{1,0},{2,3},{3,2},{4,5},{5,4},{6,7},{7,6},{8,9},{9,8},{10,11... | collective-permute-start | bytes 331784 | tf_op jit(solution)/shard_map/ppermute | solution.py:27
  23.1 1.5 %collective-permute-start.6 = (bf16[432,128]{1,0:T(8,128)(2,1)S(1)}, bf16[432,128]{1,0:T(8,128)(2,1)}, u32[]{:S(2)}, u32[]{:S(2)}) collective-permute-start(bf16[432,128]{1,0:T(8,128)(2,1)S(1)} %get-tuple-element.56), channel_id=1, source_target_pairs={{0,1},{1,0},{2,3},{3,2},{4,5},{5,4},{6,7},{7,6},{8,9},{9,8},{10,11... | collective-permute-start | bytes 331784 | tf_op jit(solution)/shard_map/ppermute | solution.py:27
  23.2 1.5 %collective-permute-start.8 = (bf16[432,128]{1,0:T(8,128)(2,1)S(1)}, bf16[432,128]{1,0:T(8,128)(2,1)}, u32[]{:S(2)}, u32[]{:S(2)}) collective-permute-start(bf16[432,128]{1,0:T(8,128)(2,1)S(1)} %get-tuple-element.55), channel_id=1, source_target_pairs={{0,1},{1,0},{2,3},{3,2},{4,5},{5,4},{6,7},{7,6},{8,9},{9,8},{10,11... | collective-permute-start | bytes 331784 | tf_op jit(solution)/shard_map/ppermute | solution.py:27
  23.6 5.5 %collective-permute-start.3 = (bf16[432,128]{1,0:T(8,128)(2,1)S(1)}, bf16[432,128]{1,0:T(8,128)(2,1)S(1)}, u32[]{:S(2)}, u32[]{:S(2)}) collective-permute-start(bf16[432,128]{1,0:T(8,128)(2,1)S(1)} %get-tuple-element.54), channel_id=1, source_target_pairs={{0,1},{1,0},{2,3},{3,2},{4,5},{5,4},{6,7},{7,6},{8,9},{9,8},{10,11... | collective-permute-start | bytes 331784 | tf_op jit(solution)/shard_map/ppermute | solution.py:27
  26.4 5.4 %collective-permute-start.5 = (bf16[432,128]{1,0:T(8,128)(2,1)}, bf16[432,128]{1,0:T(8,128)(2,1)S(1)}, u32[]{:S(2)}, u32[]{:S(2)}) collective-permute-start(bf16[432,128]{1,0:T(8,128)(2,1)} %get-tuple-element.58), channel_id=1, source_target_pairs={{0,6},{1,7},{2,4},{3,5},{4,2},{5,3},{6,0},{7,1},{8,14},{9,15},{10,... | collective-permute-start | bytes 331784 | tf_op jit(solution)/shard_map/ppermute | solution.py:27
  28.6 6.3 %collective-permute-start.7 = (bf16[432,128]{1,0:T(8,128)(2,1)}, bf16[432,128]{1,0:T(8,128)(2,1)S(1)}, u32[]{:S(2)}, u32[]{:S(2)}) collective-permute-start(bf16[432,128]{1,0:T(8,128)(2,1)} %get-tuple-element.60), channel_id=1, source_target_pairs={{0,2},{1,3},{2,0},{3,1},{4,6},{5,7},{6,4},{7,5},{8,10},{9,11},{10,... | collective-permute-start | bytes 331784 | tf_op jit(solution)/shard_map/ppermute | solution.py:27
  28.9 6.0 %collective-permute-start.9 = (bf16[432,128]{1,0:T(8,128)(2,1)S(1)}, bf16[432,128]{1,0:T(8,128)(2,1)}, u32[]{:S(2)}, u32[]{:S(2)}) collective-permute-start(bf16[432,128]{1,0:T(8,128)(2,1)S(1)} %get-tuple-element.59), channel_id=1, source_target_pairs={{0,4},{1,5},{2,6},{3,7},{4,0},{5,1},{6,2},{7,3},{8,12},{9,13},{10,... | collective-permute-start | bytes 331784 | tf_op jit(solution)/shard_map/ppermute | solution.py:27
  35.9 5.0 %collective-permute-start.10 = (bf16[216,128]{1,0:T(8,128)(2,1)S(1)}, bf16[216,128]{1,0:T(8,128)(2,1)S(1)}, u32[]{:S(2)}, u32[]{:S(2)}) collective-permute-start(bf16[216,128]{1,0:T(8,128)(2,1)S(1)} %dynamic-slice_convert_fusion.4), channel_id=1, source_target_pairs={{0,9},{1,8},{2,11},{3,10},{4,13},{5,12},{6,15},{7,14},{8,1},{9,0},... | collective-permute-start | bytes 165896 | tf_op jit(solution)/shard_map/ppermute | solution.py:27
  42.1 6.9 %collective-permute-start.12 = (f32[8,128]{1,0:T(8,128)S(1)}, f32[8,128]{1,0:T(8,128)S(1)}, u32[]{:S(2)}, u32[]{:S(2)}) collective-permute-start(f32[8,128]{1,0:T(8,128)S(1)} %broadcast_in_dim.4), channel_id=1, source_target_pairs={{0,16},{1,17},{2,18},{3,19},{4,20},{5,21},{6,22},{7,23},{8,24},{9,... | collective-permute-start | bytes 12296 | tf_op jit(solution)/shard_map/ppermute | solution.py:39
  43.4 5.7 %collective-permute-start.13 = (f32[8,128]{1,0:T(8,128)S(1)}, f32[8,128]{1,0:T(8,128)S(1)}, u32[]{:S(2)}, u32[]{:S(2)}) collective-permute-start(f32[8,128]{1,0:T(8,128)S(1)} %broadcast_in_dim.4), channel_id=1, source_target_pairs={{0,9},{1,8},{2,11},{3,10},{4,13},{5,12},{6,15},{7,14},{8,1},{9,0},... | collective-permute-start | bytes 12296 | tf_op jit(solution)/shard_map/ppermute | solution.py:39
  46.4 4.8 %collective-permute-start.14 = (f32[8,128]{1,0:T(8,128)S(1)}, f32[8,128]{1,0:T(8,128)S(1)}, u32[]{:S(2)}, u32[]{:S(2)}) collective-permute-start(f32[8,128]{1,0:T(8,128)S(1)} %broadcast_in_dim.4), channel_id=1, source_target_pairs={{0,25},{1,24},{2,27},{3,26},{4,29},{5,28},{6,31},{7,30},{8,17},{9,... | collective-permute-start | bytes 12296 | tf_op jit(solution)/shard_map/ppermute | solution.py:39
  46.4 5.6 %collective-permute-start.11 = (bf16[216,128]{1,0:T(8,128)(2,1)S(1)}, bf16[216,128]{1,0:T(8,128)(2,1)S(1)}, u32[]{:S(2)}, u32[]{:S(2)}) collective-permute-start(bf16[216,128]{1,0:T(8,128)(2,1)S(1)} %get-tuple-element.61), channel_id=1, source_target_pairs={{0,9},{1,8},{2,11},{3,10},{4,13},{5,12},{6,15},{7,14},{8,1},{9,0},... | collective-permute-start | bytes 165896 | tf_op jit(solution)/shard_map/ppermute | solution.py:27
  52.1 19.7 %copy-start.5 = (bf16[448,128]{1,0:T(8,128)(2,1)}, bf16[448,128]{1,0:T(8,128)(2,1)S(1)}, u32[]{:S(2)}) copy-start(bf16[448,128]{1,0:T(8,128)(2,1)S(1)} %pad_maximum_fusion.refs_0_) | copy-start | bytes 344068
  52.1 5.7 %collective-permute-start.15 = (bf16[448,128]{1,0:T(8,128)(2,1)S(1)}, bf16[448,128]{1,0:T(8,128)(2,1)S(1)}, u32[]{:S(2)}, u32[]{:S(2)}) collective-permute-start(bf16[448,128]{1,0:T(8,128)(2,1)S(1)} %pad_maximum_fusion.refs_0_), channel_id=1, source_target_pairs={{0,4},{1,5},{2,6},{3,7},{4,0},{5,1},{6,2},{7,3},{8,12},{9,13},{10,... | collective-permute-start | bytes 344072 | tf_op jit(solution)/shard_map/ppermute | solution.py:27
  54.3 7.3 %collective-permute-start.16 = (bf16[448,128]{1,0:T(8,128)(2,1)S(1)}, bf16[448,128]{1,0:T(8,128)(2,1)S(1)}, u32[]{:S(2)}, u32[]{:S(2)}) collective-permute-start(bf16[448,128]{1,0:T(8,128)(2,1)S(1)} %pad_maximum_fusion.refs_0_), channel_id=1, source_target_pairs={{0,2},{1,3},{2,0},{3,1},{4,6},{5,7},{6,4},{7,5},{8,10},{9,11},{10,... | collective-permute-start | bytes 344072 | tf_op jit(solution)/shard_map/ppermute | solution.py:27
  54.8 7.5 %collective-permute-start.17 = (bf16[448,128]{1,0:T(8,128)(2,1)S(1)}, bf16[448,128]{1,0:T(8,128)(2,1)S(1)}, u32[]{:S(2)}, u32[]{:S(2)}) collective-permute-start(bf16[448,128]{1,0:T(8,128)(2,1)S(1)} %pad_maximum_fusion.refs_0_), channel_id=1, source_target_pairs={{0,6},{1,7},{2,4},{3,5},{4,2},{5,3},{6,0},{7,1},{8,14},{9,15},{10,... | collective-permute-start | bytes 344072 | tf_op jit(solution)/shard_map/ppermute | solution.py:27
  55.6 16.1 %collective-permute-start.18 = (bf16[448,128]{1,0:T(8,128)(2,1)S(1)}, bf16[448,128]{1,0:T(8,128)(2,1)S(1)}, u32[]{:S(2)}, u32[]{:S(2)}) collective-permute-start(bf16[448,128]{1,0:T(8,128)(2,1)S(1)} %pad_maximum_fusion.refs_0_), channel_id=1, source_target_pairs={{0,1},{1,0},{2,3},{3,2},{4,5},{5,4},{6,7},{7,6},{8,9},{9,8},{10,11... | collective-permute-start | bytes 344072 | tf_op jit(solution)/shard_map/ppermute | solution.py:27
  57.8 14.0 %copy-start.6 = (bf16[448,128]{1,0:T(8,128)(2,1)}, bf16[448,128]{1,0:T(8,128)(2,1)S(1)}, u32[]{:S(2)}) copy-start(bf16[448,128]{1,0:T(8,128)(2,1)S(1)} %collective-permute-done.15.refs_1_) | copy-start | bytes 344068
  57.8 13.9 %collective-permute-start.19 = (bf16[448,128]{1,0:T(8,128)(2,1)S(1)}, bf16[448,128]{1,0:T(8,128)(2,1)S(1)}, u32[]{:S(2)}, u32[]{:S(2)}) collective-permute-start(bf16[448,128]{1,0:T(8,128)(2,1)S(1)} %collective-permute-done.15.refs_1_), channel_id=1, source_target_pairs={{0,1},{1,0},{2,3},{3,2},{4,5},{5,4},{6,7},{7,6},{8,9},{9,8},{10,11... | collective-permute-start | bytes 344072 | tf_op jit(solution)/shard_map/ppermute | solution.py:27
  61.6 10.1 %copy-start.7 = (bf16[448,128]{1,0:T(8,128)(2,1)}, bf16[448,128]{1,0:T(8,128)(2,1)S(1)}, u32[]{:S(2)}) copy-start(bf16[448,128]{1,0:T(8,128)(2,1)S(1)} %collective-permute-done.16.refs_2_) | copy-start | bytes 344068
  61.6 10.1 %collective-permute-start.20 = (bf16[448,128]{1,0:T(8,128)(2,1)S(1)}, bf16[448,128]{1,0:T(8,128)(2,1)S(1)}, u32[]{:S(2)}, u32[]{:S(2)}) collective-permute-start(bf16[448,128]{1,0:T(8,128)(2,1)S(1)} %collective-permute-done.16.refs_2_), channel_id=1, source_target_pairs={{0,1},{1,0},{2,3},{3,2},{4,5},{5,4},{6,7},{7,6},{8,9},{9,8},{10,11... | collective-permute-start | bytes 344072 | tf_op jit(solution)/shard_map/ppermute | solution.py:27
  62.4 9.4 %copy-start.8 = (bf16[448,128]{1,0:T(8,128)(2,1)}, bf16[448,128]{1,0:T(8,128)(2,1)S(1)}, u32[]{:S(2)}) copy-start(bf16[448,128]{1,0:T(8,128)(2,1)S(1)} %collective-permute-done.17.refs_3_) | copy-start | bytes 344068
  62.4 9.4 %collective-permute-start.21 = (bf16[448,128]{1,0:T(8,128)(2,1)S(1)}, bf16[448,128]{1,0:T(8,128)(2,1)S(1)}, u32[]{:S(2)}, u32[]{:S(2)}) collective-permute-start(bf16[448,128]{1,0:T(8,128)(2,1)S(1)} %collective-permute-done.17.refs_3_), channel_id=1, source_target_pairs={{0,1},{1,0},{2,3},{3,2},{4,5},{5,4},{6,7},{7,6},{8,9},{9,8},{10,11... | collective-permute-start | bytes 344072 | tf_op jit(solution)/shard_map/ppermute | solution.py:27
  62.4 1.4 %collective-permute-start.22 = (bf16[2,1,64,128]{3,2,1,0:T(8,128)(2,1)S(1)}, bf16[2,1,64,128]{3,2,1,0:T(8,128)(2,1)S(1)}, u32[]{:S(2)}, u32[]{:S(2)}) collective-permute-start(bf16[2,1,64,128]{3,2,1,0:T(8,128)(2,1)S(1)} %get-tuple-element.64), channel_id=1, source_target_pairs={{0,1},{1,0},{2,3},{3,2},{4,5},{5,4},{6,7},{7,6},{8,9},{9,8},{10,11... | collective-permute-start | bytes 98312 | tf_op jit(solution)/shard_map/ppermute | solution.py:22
  63.8 6.1 %collective-permute-start.23 = (bf16[2,1,64,128]{3,2,1,0:T(8,128)(2,1)S(1)}, bf16[2,1,64,128]{3,2,1,0:T(8,128)(2,1)S(1)}, u32[]{:S(2)}, u32[]{:S(2)}) collective-permute-start(bf16[2,1,64,128]{3,2,1,0:T(8,128)(2,1)S(1)} %get-tuple-element.63), channel_id=1, source_target_pairs={{1,2},{2,1},{3,4},{4,3},{5,6},{6,5},{7,8},{8,7},{9,10},{10,9},{11,... | collective-permute-start | bytes 98312 | tf_op jit(solution)/shard_map/ppermute | solution.py:22
  71.7 0.6 copy-start.9
  71.7 0.7 copy-start.10
  71.7 0.7 copy-start.11
  71.7 0.7 copy-start.12

commit v4 on v3

--- a/solution.py
+++ b/solution.py
@@ -83,27 +83,33 @@
     return total
 
 
-def rim_kernel(flag, acts, grad, near, far, sems):
+def rim_kernel(acts, grad, weight, near, far, acts_here, grad_here, weight_here, sems, loads):
     micro, depth = acts.shape[:2]
-    top = flag[0]
+    top = 1 - lax.rem(lax.axis_index("slab"), 2)
     copies = []
     for which, (out, high) in enumerate(((near, top), (far, 1 - top))):
         for m in range(micro):
             for part, (source, size, at) in enumerate(((acts, 2, 0), (grad, 1, 2))):
-                copy = pltpu.make_async_copy(
-                    source.at[m, pl.ds(high * (depth - size), size)],
-                    out.at[m, at : at + size],
-                    sems.at[which, m, part],
+                copies.append(
+                    pltpu.make_async_copy(
+                        source.at[m, pl.ds(high * (depth - size), size)],
+                        out.at[m, at : at + size],
+                        sems.at[which, m, part],
+                    )
                 )
-                copy.start()
-                copies.append(copy)
+    for n, (source, out) in enumerate(
+        ((acts, acts_here), (grad, grad_here), (weight, weight_here))
+    ):
+        copies.append(pltpu.make_async_copy(source, out, loads.at[n]))
+    for copy in copies:
+        copy.start()
     for copy in copies:
         copy.wait()
 
 
-def first_kernel(height, flag, acts, near, far, grad, weight, result, slopes, shifts, deltas):
+def first_kernel(height, acts, near, far, grad, weight, result, slopes, shifts, deltas):
     micro, depth, cells, channels = acts.shape
-    even = flag[0] == 1
+    even = lax.rem(lax.axis_index("slab"), 2) == 0
     span = 9 * channels
     rows = depth * cells
     for m in range(micro):
@@ -137,20 +143,86 @@
         result[m] = (upstream + back).astype(BF16)
 
 
-def patch_kernel(cells, shifts, out):
-    micro, total, span = shifts.shape
-    rows = total - 4 * cells
+def raw_kernel(spot, incoming, grad, slopes, shifts, upstream, deltas, near, far, *refs):
+    sends, (keep, raw) = refs[:4], refs[4:]
+    micro, depth, cells, channels = deltas.shape
+    rows = depth * cells
+    span = 9 * channels
+    last = lax.axis_index("segment") == lax.axis_size("segment") - 1
+    even = lax.rem(lax.axis_index("slab"), 2) == 0
+    deltas_of = []
     for m in range(micro):
-        for dz in range(3):
+        up = jnp.where(last, grad[m].astype(F32), incoming[m].astype(F32))
+        upstream[m] = up.astype(BF16)
+        delta = (up.reshape(rows, channels) * slopes[m]).astype(BF16)
+        deltas[m] = delta.reshape(depth, cells, channels)
+        low, high = delta[:cells].astype(F32), delta[-cells:].astype(F32)
+        near[m, 0] = jnp.where(even, high, low).astype(BF16)
+        far[m, 0] = jnp.where(even, low, high).astype(BF16)
+        deltas_of.append(delta)
+    for dz in range(3):
+        total = None
+        for m in range(micro):
             first = (1 + dz) * cells
-            out[m * rows : (m + 1) * rows, dz * span : (dz + 1) * span] = shifts[
-                m, first : first + rows, :
-            ]
-
-
-def back_kernel(height, flag, deltas, near, far, upstream, weight, out, shifts):
+            term = lax.dot_general(
+                shifts[m, first : first + rows, :],
+                deltas_of[m],
+                (((0,), (0,)), ((), ())),
+                preferred_element_type=F32,
+            )
+            total = term if total is None else total + term
+        raw[dz * span : (dz + 1) * span, :] = total
+    part = keep.shape[1]
+    for turn in range(4):
+        keep[turn] = raw[pl.ds((spot[0] ^ turn) * part, part), :]
+        sends[turn][...] = raw[pl.ds((spot[0] ^ turn ^ 4) * part, part), :].astype(BF16)
+
+
+def add_kernel(turn, keep, got, out):
+    out[...] = (keep[turn] + got[...].astype(F32)).astype(BF16)
+
+
+def sum_kernel(keep, *refs):
+    total = keep[0]
+    for got in refs[:-1]:
+        total = total + got[...].astype(F32)
+    refs[-1][...] = total
+
+
+def column_squares(value):
+    value = value.astype(F32)
+    return jnp.sum(value * value, axis=0, keepdims=True)
+
+
+def chunk_kernel(keep, *refs):
+    total = keep[...]
+    for got in refs[:-2]:
+        total = total + got[...].astype(F32)
+    chunk, squares = refs[-2:]
+    chunk[...] = total.astype(BF16)
+    squares[...] = jnp.broadcast_to(column_squares(chunk[...]), squares.shape)
+
+
+def payload_kernel(count, gathered, *refs):
+    own, values, out = refs[:count], refs[count:-1], refs[-1]
+    sums = [column_squares(piece[...]) for piece in own]
+    for n, value in enumerate(values):
+        sums[n % count] = sums[n % count] + value[:1, :]
+    while len(sums) > 1:
+        sums = [a + b for a, b in zip(sums[::2], sums[1::2], strict=True)]
+    rows = gathered.shape[0]
+    out[:rows] = gathered[...]
+    high = sums[0].astype(BF16).astype(F32)
+    middle = (sums[0] - high).astype(BF16).astype(F32)
+    low = sums[0] - high - middle
+    at = lax.broadcasted_iota(jnp.int32, (16, gathered.shape[1]), 0)
+    terms = jnp.where(at == 0, high, jnp.where(at == 1, middle, jnp.where(at == 2, low, 0.0)))
+    out[rows:] = terms.astype(BF16)
+
+
+def back_kernel(height, deltas, near, far, upstream, weight, out, shifts):
     micro, depth, cells, channels = deltas.shape
-    even = flag[0] == 1
+    even = lax.rem(lax.axis_index("slab"), 2) == 0
     rows = depth * cells
     for m in range(micro):
         low, high = near[m, 0].astype(F32), far[m, 0].astype(F32)
@@ -169,7 +241,7 @@
     sums = [piece[rows:].astype(F32) for piece in pieces]
     while len(sums) > 1:
         sums = [a + b for a, b in zip(sums[::2], sums[1::2], strict=True)]
-    norm = jnp.sqrt(jnp.sum(sums[0], axis=0, keepdims=True))
+    norm = jnp.sqrt(jnp.sum(jnp.sum(sums[0], axis=0, keepdims=True), axis=1, keepdims=True))
     factor = jnp.minimum(1.0, bound / (norm + 1e-06))
     copies = []
     for n, piece in enumerate(pieces):
@@ -192,92 +264,97 @@
     count = lax.axis_size("slab")
     index = lax.axis_index("slab")
     last = lax.axis_index("segment") == segments - 1
-    flag = (1 - lax.rem(index, 2)).astype(jnp.int32).reshape(1)
-    params = pltpu.CompilerParams(vmem_limit_bytes=40 << 20)
-
-    rim = jax.ShapeDtypeStruct((micro, 3, cells, channels), BF16)
-    to_near, to_far = pl.pallas_call(
+    large = pltpu.CompilerParams(vmem_limit_bytes=16 << 20)
+    small = pltpu.CompilerParams(vmem_limit_bytes=4 << 20)
+
+    shape = jax.ShapeDtypeStruct
+    rim = shape((micro, 3, cells, channels), BF16)
+    volume = shape((micro, depth, cells, channels), BF16)
+    to_near, to_far, acts, grad, weight = pl.pallas_call(
         rim_kernel,
-        out_shape=(rim, rim),
-        in_specs=[SMEM, ANY, ANY],
-        out_specs=(VMEM, VMEM),
-        scratch_shapes=[pltpu.SemaphoreType.DMA((2, micro, 2))],
-    )(flag, acts, grad)
+        out_shape=(rim, rim, volume, volume, shape(weight.shape, BF16)),
+        in_specs=[ANY, ANY, ANY],
+        out_specs=(VMEM,) * 5,
+        scratch_shapes=[pltpu.SemaphoreType.DMA((2, micro, 2)), pltpu.SemaphoreType.DMA((3,))],
+        compiler_params=small,
+    )(acts, grad, weight)
     near, far = swap(to_near, to_far)
 
     result, slopes, shifts = pl.pallas_call(
         functools.partial(first_kernel, height),
         out_shape=(
-            jax.ShapeDtypeStruct((micro, rows, channels), BF16),
-            jax.ShapeDtypeStruct((micro, rows, channels), F32),
-            jax.ShapeDtypeStruct((micro, rows + 4 * cells, 9 * channels), BF16),
+            shape((micro, rows, channels), BF16),
+            shape((micro, rows, channels), F32),
+            shape((micro, rows + 4 * cells, 9 * channels), BF16),
         ),
-        in_specs=[SMEM] + [VMEM] * 5,
+        in_specs=[VMEM] * 5,
         out_specs=(VMEM, VMEM, VMEM),
         scratch_shapes=[pltpu.VMEM((micro, rows + 2 * cells, 9 * channels), BF16)],
-        compiler_params=params,
-    )(flag, acts, near, far, grad, weight)
-    patches = pl.pallas_call(
-        functools.partial(patch_kernel, cells),
-        out_shape=jax.ShapeDtypeStruct((micro * rows, 27 * channels), BF16),
-        in_specs=[VMEM],
-        out_specs=VMEM,
-        compiler_params=params,
-    )(shifts)
+        compiler_params=large,
+    )(acts, near, far, grad, weight)
 
     def rims(value):
         low, high = value[:, :1], value[:, -1:]
-        even = flag[0] == 1
-        return swap(jnp.where(even, high, low), jnp.where(even, low, high))
+        even = lax.rem(index, 2) == 0
+        return jnp.where(even, high, low), jnp.where(even, low, high)
 
     def conv_back(value, near, far, upstream):
         return pl.pallas_call(
             functools.partial(back_kernel, height),
             out_shape=jax.ShapeDtypeStruct((micro, depth, cells, channels), BF16),
-            in_specs=[SMEM] + [VMEM] * 5,
+            in_specs=[VMEM] * 5,
             out_specs=VMEM,
             scratch_shapes=[pltpu.VMEM((micro, rows + 2 * cells, 9 * channels), BF16)],
-            compiler_params=params,
-        )(flag, value, near, far, upstream, weight)
+            compiler_params=large,
+        )(value, near, far, upstream, weight)
 
     result = result.reshape(micro, depth, cells, channels)
-    upstream, deltas = grad, None
-    for step in range(1, segments):
+    for step in range(1, segments - 1):
         incoming = cross(result, 1, 0)
         upstream = jnp.where(last, grad, incoming)
         slope = slopes.reshape(micro, depth, cells, channels)
         deltas = (upstream.astype(F32) * slope).astype(BF16)
-        if step < segments - 1:
-            result = conv_back(deltas, *rims(deltas), upstream)
-
-    partial = lax.dot_general(
-        patches,
-        deltas.reshape(micro * rows, channels),
-        (((0,), (0,)), ((), ())),
-        preferred_element_type=F32,
-    )
+        result = conv_back(deltas, *swap(*rims(deltas)), upstream)
+    incoming = cross(result, 1, 0)
 
     bits = [1 << n for n in range(1, count.bit_length() - 1)]
     inner = [bits[n : n + 2] for n in range(2, len(bits), 2)]
     crossing = inner[-1][0] if len(inner[-1]) == 1 else 0
     side = lax.rem(index, 2) ^ jnp.where(index & crossing, 1, 0)
     quarter = jnp.where(index & 2, 2, 0) + jnp.where(index & 4, 1, 0)
-    part = partial.shape[0] // 8
     masks = {1: 4, 2: 2, 3: 6}
-
-    pieces = {}
+    spot = (side * 4 + quarter).astype(jnp.int32).reshape(1)
+    part = weight.shape[0] // 8
+    piece = shape((part, channels), BF16)
+    edge = shape((micro, 1, cells, channels), BF16)
+
+    upstream, deltas, to_near, to_far, *rest = pl.pallas_call(
+        raw_kernel,
+        out_shape=(volume, volume, edge, edge) + (piece,) * 4 + (shape((4, part, channels), F32),),
+        in_specs=[SMEM] + [VMEM] * 4,
+        out_specs=(VMEM,) * 9,
+        scratch_shapes=[pltpu.VMEM((8 * part, channels), F32)],
+        compiler_params=large,
+    )(spot, incoming, grad, slopes, shifts)
+    sends, keep = rest[:4], rest[4]
+    got = {turn: exchange(sends[turn], 1) for turn in (3, 2, 1, 0)}
     far = []
-    for turn in (3, 2, 1, 0):
-        there = quarter ^ turn
-        got = exchange(block(partial, (1 - side) * 4 + there, part, BF16), 1)
-        if turn == 0:
-            got, deltas = lax.optimization_barrier((got, deltas))
-        piece = block(partial, side * 4 + there, part, F32) + got.astype(F32)
-        if turn:
-            far.append(exchange(piece.astype(BF16), masks[turn]))
-    chunk = piece + sum(other.astype(F32) for other in far)
-
-    gradients = conv_back(deltas, *rims(deltas), upstream)
+    for turn in (3, 2, 1):
+        added = pl.pallas_call(
+            functools.partial(add_kernel, turn),
+            out_shape=piece,
+            in_specs=[VMEM] * 2,
+            out_specs=VMEM,
+            compiler_params=small,
+        )(keep, got[turn])
+        far.append(exchange(added, masks[turn]))
+    chunk = pl.pallas_call(
+        sum_kernel,
+        out_shape=shape((part, channels), F32),
+        in_specs=[VMEM] * 5,
+        out_specs=VMEM,
+        compiler_params=small,
+    )(keep, got[0], *far)
 
     def places(group):
         own = sum(jnp.where(index & bit, 1 << n, 0) for n, bit in enumerate(group))
@@ -291,20 +368,27 @@
         own, others = places(group)
         size = chunk.shape[0] >> len(group)
         got = [exchange(block(chunk, there, size, BF16), mask) for mask, there in others]
-        chunk = block(chunk, own, size, F32) + sum(g.astype(F32) for g in got)
-
-    gathered = chunk.astype(BF16)
+        chunk = block(chunk, own, size, F32)
+        if group is not inner[-1]:
+            chunk = chunk + sum(g.astype(F32) for g in got)
+    gathered, squares = pl.pallas_call(
+        chunk_kernel,
+        out_shape=(shape(chunk.shape, BF16), shape((8, channels), F32)),
+        in_specs=[VMEM] * (1 + len(got)),
+        out_specs=(VMEM, VMEM),
+        compiler_params=small,
+    )(chunk, *got)
+
     for group in reversed(inner):
         own, others = places(group)
         got = [(there, exchange(gathered, mask)) for mask, there in others]
         if group is inner[-1]:
-            squares = jnp.broadcast_to(jnp.sum(chunk * chunk), (8, 128))
-            sums = []
-            for mask in [0] + [mask for mask, _ in others]:
-                sums.append(sum(cross(squares, back, mask) for back in range(segments)))
-            while len(sums) > 1:
-                sums = [a + b for a, b in zip(sums[::2], sums[1::2], strict=True)]
-            squares = sums[0][0]
+            members = [gathered] + [other for _, other in got]
+            met = [
+                cross(squares, back, mask)
+                for back in range(1, segments)
+                for mask in [0] + [mask for mask, _ in others]
+            ]
         blocks = []
         for n in range(1 << len(group)):
             value = jnp.where(own == n, gathered, got[0][1])
@@ -312,13 +396,17 @@
                 value = jnp.where(there == n, other, value)
             blocks.append(value)
         gathered = jnp.concatenate(blocks, axis=0)
-
-    first = lax.reduce_precision(squares, 8, 7)
-    second = lax.reduce_precision(squares - first, 8, 7)
-    third = squares - first - second
-    terms = jnp.zeros((16, channels), F32).at[0].set(first).at[1].set(second).at[2].set(third)
-    payload = jnp.concatenate([gathered, terms.astype(BF16)], axis=0)
-    near = [payload] + [exchange(payload, masks[turn]) for turn in (1, 2, 3)]
+    payload = pl.pallas_call(
+        functools.partial(payload_kernel, len(members)),
+        out_shape=shape((part + 16, channels), BF16),
+        in_specs=[VMEM] * (1 + len(members) + len(met)),
+        out_specs=VMEM,
+        compiler_params=small,
+    )(gathered, *members, *met)
+    pieces = {turn: exchange(payload, masks[turn]) for turn in (3, 2, 1)}
+    pieces[3], to_near, to_far = lax.optimization_barrier((pieces[3], to_near, to_far))
+    gradients = conv_back(deltas, *swap(to_near, to_far), upstream)
+    near = [payload] + [pieces[turn] for turn in (1, 2, 3)]
     both = near + [exchange(piece, 1) for piece in near]
     bound = math.sqrt(27.0 * channels * channels * segments)
     update = pl.pallas_call(
@@ -327,6 +415,7 @@
         in_specs=[SMEM] + [VMEM] * 8,
         out_specs=ANY,
         scratch_shapes=[pltpu.VMEM((8, part, channels), F32), pltpu.SemaphoreType.DMA((8,))],
+        compiler_params=large,
     )((side * 4 + quarter).astype(jnp.int32).reshape(1), *both)
     gradients = gradients.reshape(1, micro, depth, width, height, channels)
     return (update.reshape(1, 8 * part, channels), gradients)

time: 75.4 us -> 69 us (0.915)
  the two profiles are of different devices: /device:TPU:5 before, /device:TPU:1 now
where the time goes in v4:
time: 69 us; the launch traced here: 68.7 us
  starting transfers between devices  30.9 us (45%)
  waiting for transfers between devices  22 us (32%)
  Pallas kernels  8.96 us (13%)
  local copies, waits for them, and re-layouts  6.07 us (9%)
  between operations  0.78 us (1%)
    ppermute x16, starting transfers between devices, exchange(): return lax.ppermute(value, 'slab', [(i, i ^ mask) for i in range(count)])  18.6 us
    ppermute x16, waiting for transfers between devices, exchange(): return lax.ppermute(value, 'slab', [(i, i ^ mask) for i in range(count)])  12.1 us
    ppermute x2, starting transfers between devices, swap(): lax.ppermute(to_far, 'slab', far)  7.07 us
    unnamed x10, local copies, waits for them, and re-layouts  6.04 us
    ppermute x3, starting transfers between devices, cross(): return lax.ppermute(value, ('segment', 'slab'), route)  5.05 us
    ppermute x2, waiting for transfers between devices, swap(): lax.ppermute(to_far, 'slab', far)  4.91 us
    ppermute x3, waiting for transfers between devices, cross(): return lax.ppermute(value, ('segment', 'slab'), route)  3.84 us
    pallas_call x1, Pallas kernels, shards(): pl.pallas_call(functools.partial(first_kernel, height), out_shape=(shape(...  3.44 us
  transfers between devices with their start and end apart: 23, of which 14 were waited for; matrix products, arithmetic and copies ran while one was open for 0% of the time, Pallas kernels for 3%

profile of v4, /device:TPU:1, one launch (start us, length us, event | category | flops | bytes accessed | tf_op | source)
XLA Modules:
  0.0 68.7 jit_solution(5003631236186762267)
XLA Ops:
  0.6 1.2 %copy-done.2 = bf16[1,3456,128]{2,1,0:T(8,128)(2,1)S(1)} copy-done((bf16[1,3456,128]{2,1,0:T(8,128)(2,1)S(1)}, bf16[1,3456,128]{2,1,0:T(8,128)(2,1)}, u32[]{:S(2)}) %copy-start.2) | copy-done | bytes 884760
  1.8 0.9 %copy-done.3 = bf16[1,2,4,8,8,128]{5,4,3,2,1,0:T(8,128)(2,1)S(1)} copy-done((bf16[1,2,4,8,8,128]{5,4,3,2,1,0:T(8,128)(2,1)S(1)}, bf16[1,2,4,8,8,128]{5,4,3,2,1,0:T(8,128)(2,1)}, u32[]{:S(2)}) %copy-start.3) | copy-done | bytes 131096
  2.7 0.9 %copy-done.4 = bf16[2,4,8,8,128]{4,3,2,1,0:T(8,128)(2,1)S(1)} copy-done((bf16[2,4,8,8,128]{4,3,2,1,0:T(8,128)(2,1)S(1)}, bf16[2,4,8,8,128]{4,3,2,1,0:T(8,128)(2,1)}, u32[]{:S(2)}) %copy-start.4) | copy-done | bytes 131096
  3.6 0.9 %shard_map.50 = (bf16[2,3,64,128]{3,2,1,0:T(8,128)(2,1)S(1)}, bf16[2,3,64,128]{3,2,1,0:T(8,128)(2,1)S(1)}, bf16[2,4,64,128]{3,2,1,0:T(8,128)(2,1)S(1)}, bf16[2,4...) custom-call(bf16[2,4,64,128]{3,2,1,0:T(8,128)(2,1)S(1)} %bitcast.8, bf16[2,4,64,128]{3,2,1,0:T(8,128)(2,1)S(1)} %bitcast.9, ...), custom_call_target="tpu_custom_call" | custom-call | tf_op jit(solution)/shard_map/pallas_call | solution.py:273
  4.5 0.1 collective-permute-start
  4.6 4.5 %collective-permute-start.1 = (bf16[2,3,64,128]{3,2,1,0:T(8,128)(2,1)S(1)}, bf16[2,3,64,128]{3,2,1,0:T(8,128)(2,1)S(1)}, u32[]{:S(2)}, u32[]{:S(2)}) collective-permute-start(bf16[2,3,64,128]{3,2,1,0:T(8,128)(2,1)S(1)} %get-tuple-element.26), channel_id=1, source_target_pairs={{1,2},{2,1},{3,4},{4,3},{5,6},{6,5},{7,8},{8,7},{9,10},{10,9},{11,... | collective-permute-start | bytes 294920 | tf_op jit(solution)/shard_map/ppermute | solution.py:22
  9.1 2.3 %collective-permute-done.1.far = bf16[2,3,64,128]{3,2,1,0:T(8,128)(2,1)S(1)} collective-permute-done((bf16[2,3,64,128]{3,2,1,0:T(8,128)(2,1)S(1)}, bf16[2,3,64,128]{3,2,1,0:T(8,128)(2,1)S(1)}, u32[]{:S(2)}, u32[]{:S(2)}) %collective-permute-start.1) | collective-permute-done | bytes 98336 | tf_op jit(solution)/shard_map/ppermute | solution.py:22
  11.4 3.4 %shard_map.51 = (bf16[2,256,128]{2,1,0:T(8,128)(2,1)S(1)}, f32[2,256,128]{2,1,0:T(8,128)S(1)}, bf16[2,512,1152]{2,1,0:T(8,128)(2,1)S(1)}) custom-call(bf16[2,4,64,128]{3,2,1,0:T(8,128)(2,1)S(1)} %get-tuple-element.24.acts, bf16[2,3,64,128]{3,2,1,0:T(8,128)(2,1)S(1)} %collective-permute-done.near, bf16[2,3,64,128]{3,2,1,0:T(8,128)(2,1)S(1)} %collective-permute-done.1.far, ...), custom_call_target="tpu_custom_call" | custom-call | tf_op jit(solution)/shard_map/pallas_call | solution.py:283
  14.8 1.4 %copy-done = bf16[2,512,1152]{2,1,0:T(8,128)(2,1)} copy-done((bf16[2,512,1152]{2,1,0:T(8,128)(2,1)}, bf16[2,512,1152]{2,1,0:T(8,128)(2,1)S(1)}, u32[]{:S(2)}) %copy-start) | copy-done | bytes 2359320
  16.2 1.8 %collective-permute-start.2 = (bf16[2,4,64,128]{3,2,1,0:T(8,128)(2,1)S(1)}, bf16[2,4,64,128]{3,2,1,0:T(8,128)(2,1)S(1)}, u32[]{:S(2)}, u32[]{:S(2)}) collective-permute-start(bf16[2,4,64,128]{3,2,1,0:T(8,128)(2,1)S(1)} %bitcast.10), channel_id=1, source_target_pairs={{0,16},{1,17},{2,18},{3,19},{4,20},{5,21},{6,22},{7,23},{8,24},{9,... | collective-permute-start | bytes 393224 | tf_op jit(solution)/shard_map/ppermute | solution.py:39
  18.0 2.4 %collective-permute-done.2.incoming = bf16[2,4,64,128]{3,2,1,0:T(8,128)(2,1)S(1)} collective-permute-done((bf16[2,4,64,128]{3,2,1,0:T(8,128)(2,1)S(1)}, bf16[2,4,64,128]{3,2,1,0:T(8,128)(2,1)S(1)}, u32[]{:S(2)}, u32[]{:S(2)}) %collective-permute-start.2) | collective-permute-done | bytes 131104 | tf_op jit(solution)/shard_map/ppermute | solution.py:39
  20.4 1.7 %copy-done.1 = bf16[2,512,1152]{2,1,0:T(8,128)(2,1)S(1)} copy-done((bf16[2,512,1152]{2,1,0:T(8,128)(2,1)S(1)}, bf16[2,512,1152]{2,1,0:T(8,128)(2,1)}, u32[]{:S(2)}) %copy-start.1) | copy-done | bytes 2359320
  22.1 1.2 %shard_map.52 = (bf16[2,4,64,128]{3,2,1,0:T(8,128)(2,1)S(1)}, bf16[2,4,64,128]{3,2,1,0:T(8,128)(2,1)S(1)}, bf16[2,1,64,128]{3,2,1,0:T(8,128)(2,1)S(1)}, bf16[2,1...) custom-call(s32[1]{0:T(128)} %bitcast.spot, ...), custom_call_target="tpu_custom_call" | custom-call | tf_op jit(solution)/shard_map/pallas_call | solution.py:331
  23.3 0.1 collective-permute-start.8
  23.4 0.5 collective-permute-start.6
  23.9 0.1 collective-permute-start.4
  24.0 0.4 collective-permute-start.3
  24.4 0.3 collective-permute-done.8.got
  24.7 4.4 %collective-permute-start.9 = (bf16[432,128]{1,0:T(8,128)(2,1)S(1)}, bf16[432,128]{1,0:T(8,128)(2,1)S(1)}, u32[]{:S(2)}, u32[]{:S(2)}) collective-permute-start(bf16[432,128]{1,0:T(8,128)(2,1)S(1)} %shard_map.55), channel_id=1, source_target_pairs={{0,4},{1,5},{2,6},{3,7},{4,0},{5,1},{6,2},{7,3},{8,12},{9,13},{10,... | collective-permute-start | bytes 331784 | tf_op jit(solution)/shard_map/ppermute | solution.py:27
  29.1 0.4 collective-permute-start.7
  29.6 1.2 %collective-permute-start.5 = (bf16[432,128]{1,0:T(8,128)(2,1)S(1)}, bf16[432,128]{1,0:T(8,128)(2,1)S(1)}, u32[]{:S(2)}, u32[]{:S(2)}) collective-permute-start(bf16[432,128]{1,0:T(8,128)(2,1)S(1)} %shard_map.53), channel_id=1, source_target_pairs={{0,6},{1,7},{2,4},{3,5},{4,2},{5,3},{6,0},{7,1},{8,14},{9,15},{10,... | collective-permute-start | bytes 331784 | tf_op jit(solution)/shard_map/ppermute | solution.py:27
  30.8 1.5 %collective-permute-done.9.refs_3_ = bf16[432,128]{1,0:T(8,128)(2,1)S(1)} collective-permute-done((bf16[432,128]{1,0:T(8,128)(2,1)S(1)}, bf16[432,128]{1,0:T(8,128)(2,1)S(1)}, u32[]{:S(2)}, u32[]{:S(2)}) %collective-permute-start.9) | collective-permute-done | bytes 110624 | tf_op jit(solution)/shard_map/ppermute | solution.py:27
  32.3 0.9 %collective-permute-done.7.refs_2_ = bf16[432,128]{1,0:T(8,128)(2,1)S(1)} collective-permute-done((bf16[432,128]{1,0:T(8,128)(2,1)S(1)}, bf16[432,128]{1,0:T(8,128)(2,1)S(1)}, u32[]{:S(2)}, u32[]{:S(2)}) %collective-permute-start.7) | collective-permute-done | bytes 110624 | tf_op jit(solution)/shard_map/ppermute | solution.py:27
  33.2 1.1 %collective-permute-done.5.refs_1_ = bf16[432,128]{1,0:T(8,128)(2,1)S(1)} collective-permute-done((bf16[432,128]{1,0:T(8,128)(2,1)S(1)}, bf16[432,128]{1,0:T(8,128)(2,1)S(1)}, u32[]{:S(2)}, u32[]{:S(2)}) %collective-permute-start.5) | collective-permute-done | bytes 110624 | tf_op jit(solution)/shard_map/ppermute | solution.py:27
  34.3 0.1 shard_map.56
  34.4 5.1 %collective-permute-start.10 = (bf16[216,128]{1,0:T(8,128)(2,1)S(1)}, bf16[216,128]{1,0:T(8,128)(2,1)S(1)}, u32[]{:S(2)}, u32[]{:S(2)}) collective-permute-start(bf16[216,128]{1,0:T(8,128)(2,1)S(1)} %dynamic-slice_convert_fusion), channel_id=1, source_target_pairs={{0,9},{1,8},{2,11},{3,10},{4,13},{5,12},{6,15},{7,14},{8,1},{9,0},... | collective-permute-start | bytes 165896 | tf_op jit(solution)/shard_map/ppermute | solution.py:27
  39.4 3.6 %collective-permute-done.10.refs_0_ = bf16[216,128]{1,0:T(8,128)(2,1)S(1)} collective-permute-done((bf16[216,128]{1,0:T(8,128)(2,1)S(1)}, bf16[216,128]{1,0:T(8,128)(2,1)S(1)}, u32[]{:S(2)}, u32[]{:S(2)}) %collective-permute-start.10) | collective-permute-done | bytes 55328 | tf_op jit(solution)/shard_map/ppermute | solution.py:27
  43.1 0.9 %collective-permute-start.11 = (bf16[216,128]{1,0:T(8,128)(2,1)S(1)}, bf16[216,128]{1,0:T(8,128)(2,1)S(1)}, u32[]{:S(2)}, u32[]{:S(2)}) collective-permute-start(bf16[216,128]{1,0:T(8,128)(2,1)S(1)} %get-tuple-element.37.refs_0_), channel_id=1, source_target_pairs={{0,9},{1,8},{2,11},{3,10},{4,13},{5,12},{6,15},{7,14},{8,1},{9,0},... | collective-permute-start | bytes 165896 | tf_op jit(solution)/shard_map/ppermute | solution.py:27
  44.0 1.2 %collective-permute-start.12 = (f32[8,128]{1,0:T(8,128)S(1)}, f32[8,128]{1,0:T(8,128)S(1)}, u32[]{:S(2)}, u32[]{:S(2)}) collective-permute-start(f32[8,128]{1,0:T(8,128)S(1)} %get-tuple-element.38), channel_id=1, source_target_pairs={{0,16},{1,17},{2,18},{3,19},{4,20},{5,21},{6,22},{7,23},{8,24},{9,... | collective-permute-start | bytes 12296 | tf_op jit(solution)/shard_map/ppermute | solution.py:39
  45.2 2.0 %collective-permute-start.13 = (f32[8,128]{1,0:T(8,128)S(1)}, f32[8,128]{1,0:T(8,128)S(1)}, u32[]{:S(2)}, u32[]{:S(2)}) collective-permute-start(f32[8,128]{1,0:T(8,128)S(1)} %get-tuple-element.38), channel_id=1, source_target_pairs={{0,25},{1,24},{2,27},{3,26},{4,29},{5,28},{6,31},{7,30},{8,17},{9,... | collective-permute-start | bytes 12296 | tf_op jit(solution)/shard_map/ppermute | solution.py:39
  47.3 1.2 %collective-permute-done.11.refs_1_ = bf16[216,128]{1,0:T(8,128)(2,1)S(1)} collective-permute-done((bf16[216,128]{1,0:T(8,128)(2,1)S(1)}, bf16[216,128]{1,0:T(8,128)(2,1)S(1)}, u32[]{:S(2)}, u32[]{:S(2)}) %collective-permute-start.11) | collective-permute-done | bytes 55328 | tf_op jit(solution)/shard_map/ppermute | solution.py:27
  48.6 1.5 %collective-permute-done.13.refs_3_ = f32[8,128]{1,0:T(8,128)S(1)} collective-permute-done((f32[8,128]{1,0:T(8,128)S(1)}, f32[8,128]{1,0:T(8,128)S(1)}, u32[]{:S(2)}, u32[]{:S(2)}) %collective-permute-start.13) | collective-permute-done | bytes 4128 | tf_op jit(solution)/shard_map/ppermute | solution.py:39
  50.0 0.1 shard_map.58.refs_0_
  50.1 1.6 %collective-permute-start.16 = (bf16[448,128]{1,0:T(8,128)(2,1)S(1)}, bf16[448,128]{1,0:T(8,128)(2,1)S(1)}, u32[]{:S(2)}, u32[]{:S(2)}) collective-permute-start(bf16[448,128]{1,0:T(8,128)(2,1)S(1)} %shard_map.58.refs_0_), channel_id=1, source_target_pairs={{0,6},{1,7},{2,4},{3,5},{4,2},{5,3},{6,0},{7,1},{8,14},{9,15},{10,... | collective-permute-start | bytes 344072 | tf_op jit(solution)/shard_map/ppermute | solution.py:27
  51.8 0.0 collective-permute-start.14
  51.8 1.0 %collective-permute-start.15 = (bf16[448,128]{1,0:T(8,128)(2,1)S(1)}, bf16[448,128]{1,0:T(8,128)(2,1)S(1)}, u32[]{:S(2)}, u32[]{:S(2)}) collective-permute-start(bf16[448,128]{1,0:T(8,128)(2,1)S(1)} %shard_map.58.refs_0_), channel_id=1, source_target_pairs={{0,2},{1,3},{2,0},{3,1},{4,6},{5,7},{6,4},{7,5},{8,10},{9,11},{10,... | collective-permute-start | bytes 344072 | tf_op jit(solution)/shard_map/ppermute | solution.py:27
  52.8 0.8 %collective-permute-start.17 = (bf16[448,128]{1,0:T(8,128)(2,1)S(1)}, bf16[448,128]{1,0:T(8,128)(2,1)S(1)}, u32[]{:S(2)}, u32[]{:S(2)}) collective-permute-start(bf16[448,128]{1,0:T(8,128)(2,1)S(1)} %shard_map.58.refs_0_), channel_id=1, source_target_pairs={{0,1},{1,0},{2,3},{3,2},{4,5},{5,4},{6,7},{7,6},{8,9},{9,8},{10,11... | collective-permute-start | bytes 344072 | tf_op jit(solution)/shard_map/ppermute | solution.py:27
  53.6 2.4 %collective-permute-done.16.refs_3_ = bf16[448,128]{1,0:T(8,128)(2,1)S(1)} collective-permute-done((bf16[448,128]{1,0:T(8,128)(2,1)S(1)}, bf16[448,128]{1,0:T(8,128)(2,1)S(1)}, u32[]{:S(2)}, u32[]{:S(2)}) %collective-permute-start.16) | collective-permute-done | bytes 114720 | tf_op jit(solution)/shard_map/ppermute | solution.py:27
  56.0 1.0 %collective-permute-start.20 = (bf16[448,128]{1,0:T(8,128)(2,1)S(1)}, bf16[448,128]{1,0:T(8,128)(2,1)S(1)}, u32[]{:S(2)}, u32[]{:S(2)}) collective-permute-start(bf16[448,128]{1,0:T(8,128)(2,1)S(1)} %collective-permute-done.16.refs_3_), channel_id=1, source_target_pairs={{0,1},{1,0},{2,3},{3,2},{4,5},{5,4},{6,7},{7,6},{8,9},{9,8},{10,11... | collective-permute-start | bytes 344072 | tf_op jit(solution)/shard_map/ppermute | solution.py:27
  56.9 0.7 %collective-permute-done.14.refs_1_ = bf16[448,128]{1,0:T(8,128)(2,1)S(1)} collective-permute-done((bf16[448,128]{1,0:T(8,128)(2,1)S(1)}, bf16[448,128]{1,0:T(8,128)(2,1)S(1)}, u32[]{:S(2)}, u32[]{:S(2)}) %collective-permute-start.14) | collective-permute-done | bytes 114720 | tf_op jit(solution)/shard_map/ppermute | solution.py:27
  57.7 0.7 collective-permute-start.18
  58.3 0.3 collective-permute-done.15.refs_2_
  58.6 0.5 collective-permute-start.19
  59.1 1.2 %collective-permute-done.21.near = bf16[2,1,64,128]{3,2,1,0:T(8,128)(2,1)S(1)} collective-permute-done((bf16[2,1,64,128]{3,2,1,0:T(8,128)(2,1)S(1)}, bf16[2,1,64,128]{3,2,1,0:T(8,128)(2,1)S(1)}, u32[]{:S(2)}, u32[]{:S(2)}) %collective-permute-start.21) | collective-permute-done | bytes 32800 | tf_op jit(solution)/shard_map/ppermute | solution.py:22
  60.3 2.6 %collective-permute-start.22 = (bf16[2,1,64,128]{3,2,1,0:T(8,128)(2,1)S(1)}, bf16[2,1,64,128]{3,2,1,0:T(8,128)(2,1)S(1)}, u32[]{:S(2)}, u32[]{:S(2)}) collective-permute-start(bf16[2,1,64,128]{3,2,1,0:T(8,128)(2,1)S(1)} %get-tuple-element.44), channel_id=1, source_target_pairs={{1,2},{2,1},{3,4},{4,3},{5,6},{6,5},{7,8},{8,7},{9,10},{10,9},{11,... | collective-permute-start | bytes 98312 | tf_op jit(solution)/shard_map/ppermute | solution.py:22
  62.9 2.6 %collective-permute-done.22.far = bf16[2,1,64,128]{3,2,1,0:T(8,128)(2,1)S(1)} collective-permute-done((bf16[2,1,64,128]{3,2,1,0:T(8,128)(2,1)S(1)}, bf16[2,1,64,128]{3,2,1,0:T(8,128)(2,1)S(1)}, u32[]{:S(2)}, u32[]{:S(2)}) %collective-permute-start.22) | collective-permute-done | bytes 32800 | tf_op jit(solution)/shard_map/ppermute | solution.py:22
  65.5 1.8 %shard_map.60 = bf16[2,4,64,128]{3,2,1,0:T(8,128)(2,1)} custom-call(bf16[2,4,64,128]{3,2,1,0:T(8,128)(2,1)S(1)} %get-tuple-element.42.deltas, bf16[2,1,64,128]{3,2,1,0:T(8,128)(2,1)S(1)} %collective-permute-done.21.near, bf16[2,1,64,128]{3,2,1,0:T(8,128)(2,1)S(1)} %collective-permute-done.22.far, bf16[2,4,64,128]{3,2,1,0:T(8,128)(2,1)S(1)} %get-tuple-element.45.upstream, ...), custom_call_target="tpu_custom_call" | custom-call | tf_op jit(solution)/shard_map/pallas_call | solution.py:302
  67.3 1.4 %shard_map.59 = f32[8,432,128]{2,1,0:T(8,128)} custom-call(s32[1]{0:T(128)} %bitcast.spot, bf16[448,128]{1,0:T(8,128)(2,1)S(1)} %shard_map.58.refs_0_, bf16[448,128]{1,0:T(8,128)(2,1)S(1)} %collective-permute-done.14.refs_1_, bf16[448,128]{1,0:T(8,128)(2,1)S(1)} %collective-permute-done.15.refs_2_, bf16[448,128]{1,0:T(8,128)(2,1)S(1)} %collective-permute-done.16.refs_3_, ...), custom_call_target="tpu_custom_call" | custom-call | tf_op jit(solution)/shard_map/pallas_call | solution.py:412
  (23 shorter events, 0.3 us)
Async XLA Ops:
  0.6 1.2 %copy-start.2 = (bf16[1,3456,128]{2,1,0:T(8,128)(2,1)S(1)}, bf16[1,3456,128]{2,1,0:T(8,128)(2,1)}, u32[]{:S(2)}) copy-start(bf16[1,3456,128]{2,1,0:T(8,128)(2,1)} %param.4) | copy-start | bytes 2654212
  1.8 0.9 %copy-start.3 = (bf16[1,2,4,8,8,128]{5,4,3,2,1,0:T(8,128)(2,1)S(1)}, bf16[1,2,4,8,8,128]{5,4,3,2,1,0:T(8,128)(2,1)}, u32[]{:S(2)}) copy-start(bf16[1,2,4,8,8,128]{5,4,3,2,1,0:T(8,128)(2,1)} %param.3) | copy-start | bytes 393220
  2.7 0.9 %copy-start.4 = (bf16[2,4,8,8,128]{4,3,2,1,0:T(8,128)(2,1)S(1)}, bf16[2,4,8,8,128]{4,3,2,1,0:T(8,128)(2,1)}, u32[]{:S(2)}) copy-start(bf16[2,4,8,8,128]{4,3,2,1,0:T(8,128)(2,1)} %param.5) | copy-start | bytes 393220
  4.5 4.6 %collective-permute-start = (bf16[2,3,64,128]{3,2,1,0:T(8,128)(2,1)S(1)}, bf16[2,3,64,128]{3,2,1,0:T(8,128)(2,1)S(1)}, u32[]{:S(2)}, u32[]{:S(2)}) collective-permute-start(bf16[2,3,64,128]{3,2,1,0:T(8,128)(2,1)S(1)} %get-tuple-element.25), channel_id=1, source_target_pairs={{0,1},{1,0},{2,3},{3,2},{4,5},{5,4},{6,7},{7,6},{8,9},{9,8},{10,11... | collective-permute-start | bytes 294920 | tf_op jit(solution)/shard_map/ppermute | solution.py:22
  4.6 6.8 %collective-permute-start.1 = (bf16[2,3,64,128]{3,2,1,0:T(8,128)(2,1)S(1)}, bf16[2,3,64,128]{3,2,1,0:T(8,128)(2,1)S(1)}, u32[]{:S(2)}, u32[]{:S(2)}) collective-permute-start(bf16[2,3,64,128]{3,2,1,0:T(8,128)(2,1)S(1)} %get-tuple-element.26), channel_id=1, source_target_pairs={{1,2},{2,1},{3,4},{4,3},{5,6},{6,5},{7,8},{8,7},{9,10},{10,9},{11,... | collective-permute-start | bytes 294920 | tf_op jit(solution)/shard_map/ppermute | solution.py:22
  14.8 1.4 %copy-start = (bf16[2,512,1152]{2,1,0:T(8,128)(2,1)}, bf16[2,512,1152]{2,1,0:T(8,128)(2,1)S(1)}, u32[]{:S(2)}) copy-start(bf16[2,512,1152]{2,1,0:T(8,128)(2,1)S(1)} %get-tuple-element.31.shifts) | copy-start | bytes 7077892
  16.2 4.2 %collective-permute-start.2 = (bf16[2,4,64,128]{3,2,1,0:T(8,128)(2,1)S(1)}, bf16[2,4,64,128]{3,2,1,0:T(8,128)(2,1)S(1)}, u32[]{:S(2)}, u32[]{:S(2)}) collective-permute-start(bf16[2,4,64,128]{3,2,1,0:T(8,128)(2,1)S(1)} %bitcast.10), channel_id=1, source_target_pairs={{0,16},{1,17},{2,18},{3,19},{4,20},{5,21},{6,22},{7,23},{8,24},{9,... | collective-permute-start | bytes 393224 | tf_op jit(solution)/shard_map/ppermute | solution.py:39
  20.4 1.7 %copy-start.1 = (bf16[2,512,1152]{2,1,0:T(8,128)(2,1)S(1)}, bf16[2,512,1152]{2,1,0:T(8,128)(2,1)}, u32[]{:S(2)}) copy-start(bf16[2,512,1152]{2,1,0:T(8,128)(2,1)} %copy-done) | copy-start | bytes 7077892
  23.3 1.4 %collective-permute-start.8 = (bf16[432,128]{1,0:T(8,128)(2,1)S(1)}, bf16[432,128]{1,0:T(8,128)(2,1)S(1)}, u32[]{:S(2)}, u32[]{:S(2)}) collective-permute-start(bf16[432,128]{1,0:T(8,128)(2,1)S(1)} %get-tuple-element.36), channel_id=1, source_target_pairs={{0,1},{1,0},{2,3},{3,2},{4,5},{5,4},{6,7},{7,6},{8,9},{9,8},{10,11... | collective-permute-start | bytes 331784 | tf_op jit(solution)/shard_map/ppermute | solution.py:27
  23.4 5.7 %collective-permute-start.6 = (bf16[432,128]{1,0:T(8,128)(2,1)S(1)}, bf16[432,128]{1,0:T(8,128)(2,1)S(1)}, u32[]{:S(2)}, u32[]{:S(2)}) collective-permute-start(bf16[432,128]{1,0:T(8,128)(2,1)S(1)} %get-tuple-element.35), channel_id=1, source_target_pairs={{0,1},{1,0},{2,3},{3,2},{4,5},{5,4},{6,7},{7,6},{8,9},{9,8},{10,11... | collective-permute-start | bytes 331784 | tf_op jit(solution)/shard_map/ppermute | solution.py:27
  23.9 5.7 %collective-permute-start.4 = (bf16[432,128]{1,0:T(8,128)(2,1)S(1)}, bf16[432,128]{1,0:T(8,128)(2,1)S(1)}, u32[]{:S(2)}, u32[]{:S(2)}) collective-permute-start(bf16[432,128]{1,0:T(8,128)(2,1)S(1)} %get-tuple-element.34), channel_id=1, source_target_pairs={{0,1},{1,0},{2,3},{3,2},{4,5},{5,4},{6,7},{7,6},{8,9},{9,8},{10,11... | collective-permute-start | bytes 331784 | tf_op jit(solution)/shard_map/ppermute | solution.py:27
  24.0 6.8 %collective-permute-start.3 = (bf16[432,128]{1,0:T(8,128)(2,1)S(1)}, bf16[432,128]{1,0:T(8,128)(2,1)S(1)}, u32[]{:S(2)}, u32[]{:S(2)}) collective-permute-start(bf16[432,128]{1,0:T(8,128)(2,1)S(1)} %get-tuple-element.33), channel_id=1, source_target_pairs={{0,1},{1,0},{2,3},{3,2},{4,5},{5,4},{6,7},{7,6},{8,9},{9,8},{10,11... | collective-permute-start | bytes 331784 | tf_op jit(solution)/shard_map/ppermute | solution.py:27
  24.7 7.5 %collective-permute-start.9 = (bf16[432,128]{1,0:T(8,128)(2,1)S(1)}, bf16[432,128]{1,0:T(8,128)(2,1)S(1)}, u32[]{:S(2)}, u32[]{:S(2)}) collective-permute-start(bf16[432,128]{1,0:T(8,128)(2,1)S(1)} %shard_map.55), channel_id=1, source_target_pairs={{0,4},{1,5},{2,6},{3,7},{4,0},{5,1},{6,2},{7,3},{8,12},{9,13},{10,... | collective-permute-start | bytes 331784 | tf_op jit(solution)/shard_map/ppermute | solution.py:27
  29.1 4.0 %collective-permute-start.7 = (bf16[432,128]{1,0:T(8,128)(2,1)S(1)}, bf16[432,128]{1,0:T(8,128)(2,1)S(1)}, u32[]{:S(2)}, u32[]{:S(2)}) collective-permute-start(bf16[432,128]{1,0:T(8,128)(2,1)S(1)} %shard_map.54), channel_id=1, source_target_pairs={{0,2},{1,3},{2,0},{3,1},{4,6},{5,7},{6,4},{7,5},{8,10},{9,11},{10,... | collective-permute-start | bytes 331784 | tf_op jit(solution)/shard_map/ppermute | solution.py:27
  29.6 4.7 %collective-permute-start.5 = (bf16[432,128]{1,0:T(8,128)(2,1)S(1)}, bf16[432,128]{1,0:T(8,128)(2,1)S(1)}, u32[]{:S(2)}, u32[]{:S(2)}) collective-permute-start(bf16[432,128]{1,0:T(8,128)(2,1)S(1)} %shard_map.53), channel_id=1, source_target_pairs={{0,6},{1,7},{2,4},{3,5},{4,2},{5,3},{6,0},{7,1},{8,14},{9,15},{10,... | collective-permute-start | bytes 331784 | tf_op jit(solution)/shard_map/ppermute | solution.py:27
  34.4 8.7 %collective-permute-start.10 = (bf16[216,128]{1,0:T(8,128)(2,1)S(1)}, bf16[216,128]{1,0:T(8,128)(2,1)S(1)}, u32[]{:S(2)}, u32[]{:S(2)}) collective-permute-start(bf16[216,128]{1,0:T(8,128)(2,1)S(1)} %dynamic-slice_convert_fusion), channel_id=1, source_target_pairs={{0,9},{1,8},{2,11},{3,10},{4,13},{5,12},{6,15},{7,14},{8,1},{9,0},... | collective-permute-start | bytes 165896 | tf_op jit(solution)/shard_map/ppermute | solution.py:27
  43.1 5.4 %collective-permute-start.11 = (bf16[216,128]{1,0:T(8,128)(2,1)S(1)}, bf16[216,128]{1,0:T(8,128)(2,1)S(1)}, u32[]{:S(2)}, u32[]{:S(2)}) collective-permute-start(bf16[216,128]{1,0:T(8,128)(2,1)S(1)} %get-tuple-element.37.refs_0_), channel_id=1, source_target_pairs={{0,9},{1,8},{2,11},{3,10},{4,13},{5,12},{6,15},{7,14},{8,1},{9,0},... | collective-permute-start | bytes 165896 | tf_op jit(solution)/shard_map/ppermute | solution.py:27
  44.0 4.6 %collective-permute-start.12 = (f32[8,128]{1,0:T(8,128)S(1)}, f32[8,128]{1,0:T(8,128)S(1)}, u32[]{:S(2)}, u32[]{:S(2)}) collective-permute-start(f32[8,128]{1,0:T(8,128)S(1)} %get-tuple-element.38), channel_id=1, source_target_pairs={{0,16},{1,17},{2,18},{3,19},{4,20},{5,21},{6,22},{7,23},{8,24},{9,... | collective-permute-start | bytes 12296 | tf_op jit(solution)/shard_map/ppermute | solution.py:39
  45.2 4.8 %collective-permute-start.13 = (f32[8,128]{1,0:T(8,128)S(1)}, f32[8,128]{1,0:T(8,128)S(1)}, u32[]{:S(2)}, u32[]{:S(2)}) collective-permute-start(f32[8,128]{1,0:T(8,128)S(1)} %get-tuple-element.38), channel_id=1, source_target_pairs={{0,25},{1,24},{2,27},{3,26},{4,29},{5,28},{6,31},{7,30},{8,17},{9,... | collective-permute-start | bytes 12296 | tf_op jit(solution)/shard_map/ppermute | solution.py:39
  50.1 5.8 %collective-permute-start.16 = (bf16[448,128]{1,0:T(8,128)(2,1)S(1)}, bf16[448,128]{1,0:T(8,128)(2,1)S(1)}, u32[]{:S(2)}, u32[]{:S(2)}) collective-permute-start(bf16[448,128]{1,0:T(8,128)(2,1)S(1)} %shard_map.58.refs_0_), channel_id=1, source_target_pairs={{0,6},{1,7},{2,4},{3,5},{4,2},{5,3},{6,0},{7,1},{8,14},{9,15},{10,... | collective-permute-start | bytes 344072 | tf_op jit(solution)/shard_map/ppermute | solution.py:27
  51.8 5.9 %collective-permute-start.14 = (bf16[448,128]{1,0:T(8,128)(2,1)S(1)}, bf16[448,128]{1,0:T(8,128)(2,1)S(1)}, u32[]{:S(2)}, u32[]{:S(2)}) collective-permute-start(bf16[448,128]{1,0:T(8,128)(2,1)S(1)} %shard_map.58.refs_0_), channel_id=1, source_target_pairs={{0,4},{1,5},{2,6},{3,7},{4,0},{5,1},{6,2},{7,3},{8,12},{9,13},{10,... | collective-permute-start | bytes 344072 | tf_op jit(solution)/shard_map/ppermute | solution.py:27
  51.8 6.8 %collective-permute-start.15 = (bf16[448,128]{1,0:T(8,128)(2,1)S(1)}, bf16[448,128]{1,0:T(8,128)(2,1)S(1)}, u32[]{:S(2)}, u32[]{:S(2)}) collective-permute-start(bf16[448,128]{1,0:T(8,128)(2,1)S(1)} %shard_map.58.refs_0_), channel_id=1, source_target_pairs={{0,2},{1,3},{2,0},{3,1},{4,6},{5,7},{6,4},{7,5},{8,10},{9,11},{10,... | collective-permute-start | bytes 344072 | tf_op jit(solution)/shard_map/ppermute | solution.py:27
  52.8 14.5 %collective-permute-start.17 = (bf16[448,128]{1,0:T(8,128)(2,1)S(1)}, bf16[448,128]{1,0:T(8,128)(2,1)S(1)}, u32[]{:S(2)}, u32[]{:S(2)}) collective-permute-start(bf16[448,128]{1,0:T(8,128)(2,1)S(1)} %shard_map.58.refs_0_), channel_id=1, source_target_pairs={{0,1},{1,0},{2,3},{3,2},{4,5},{5,4},{6,7},{7,6},{8,9},{9,8},{10,11... | collective-permute-start | bytes 344072 | tf_op jit(solution)/shard_map/ppermute | solution.py:27
  56.0 11.4 %collective-permute-start.20 = (bf16[448,128]{1,0:T(8,128)(2,1)S(1)}, bf16[448,128]{1,0:T(8,128)(2,1)S(1)}, u32[]{:S(2)}, u32[]{:S(2)}) collective-permute-start(bf16[448,128]{1,0:T(8,128)(2,1)S(1)} %collective-permute-done.16.refs_3_), channel_id=1, source_target_pairs={{0,1},{1,0},{2,3},{3,2},{4,5},{5,4},{6,7},{7,6},{8,9},{9,8},{10,11... | collective-permute-start | bytes 344072 | tf_op jit(solution)/shard_map/ppermute | solution.py:27
  57.7 9.7 %collective-permute-start.18 = (bf16[448,128]{1,0:T(8,128)(2,1)S(1)}, bf16[448,128]{1,0:T(8,128)(2,1)S(1)}, u32[]{:S(2)}, u32[]{:S(2)}) collective-permute-start(bf16[448,128]{1,0:T(8,128)(2,1)S(1)} %collective-permute-done.14.refs_1_), channel_id=1, source_target_pairs={{0,1},{1,0},{2,3},{3,2},{4,5},{5,4},{6,7},{7,6},{8,9},{9,8},{10,11... | collective-permute-start | bytes 344072 | tf_op jit(solution)/shard_map/ppermute | solution.py:27
  58.6 8.7 %collective-permute-start.19 = (bf16[448,128]{1,0:T(8,128)(2,1)S(1)}, bf16[448,128]{1,0:T(8,128)(2,1)S(1)}, u32[]{:S(2)}, u32[]{:S(2)}) collective-permute-start(bf16[448,128]{1,0:T(8,128)(2,1)S(1)} %collective-permute-done.15.refs_2_), channel_id=1, source_target_pairs={{0,1},{1,0},{2,3},{3,2},{4,5},{5,4},{6,7},{7,6},{8,9},{9,8},{10,11... | collective-permute-start | bytes 344072 | tf_op jit(solution)/shard_map/ppermute | solution.py:27
  59.1 1.2 %collective-permute-start.21 = (bf16[2,1,64,128]{3,2,1,0:T(8,128)(2,1)S(1)}, bf16[2,1,64,128]{3,2,1,0:T(8,128)(2,1)S(1)}, u32[]{:S(2)}, u32[]{:S(2)}) collective-permute-start(bf16[2,1,64,128]{3,2,1,0:T(8,128)(2,1)S(1)} %get-tuple-element.43), channel_id=1, source_target_pairs={{0,1},{1,0},{2,3},{3,2},{4,5},{5,4},{6,7},{7,6},{8,9},{9,8},{10,11... | collective-permute-start | bytes 98312 | tf_op jit(solution)/shard_map/ppermute | solution.py:22
  60.3 5.2 %collective-permute-start.22 = (bf16[2,1,64,128]{3,2,1,0:T(8,128)(2,1)S(1)}, bf16[2,1,64,128]{3,2,1,0:T(8,128)(2,1)S(1)}, u32[]{:S(2)}, u32[]{:S(2)}) collective-permute-start(bf16[2,1,64,128]{3,2,1,0:T(8,128)(2,1)S(1)} %get-tuple-element.44), channel_id=1, source_target_pairs={{1,2},{2,1},{3,4},{4,3},{5,6},{6,5},{7,8},{8,7},{9,10},{10,9},{11,... | collective-permute-start | bytes 98312 | tf_op jit(solution)/shard_map/ppermute | solution.py:22

commit v5 on v4

--- a/solution.py
+++ b/solution.py
@@ -13,13 +13,27 @@
 VMEM = pl.BlockSpec(memory_space=pltpu.VMEM)
 SMEM = pl.BlockSpec(memory_space=pltpu.SMEM)
 ANY = pl.BlockSpec(memory_space=pl.ANY)
+HBM = pl.BlockSpec(memory_space=pltpu.HBM)
+
+
+def far_route(count):
+    return [(i, ((i + 1) ^ 1) - 1) for i in range(1, count - 1)]
 
 
 def swap(to_near, to_far):
     count = lax.axis_size("slab")
     near = [(i, i ^ 1) for i in range(count)]
-    far = [(i, ((i + 1) ^ 1) - 1) for i in range(1, count - 1)]
-    return lax.ppermute(to_near, "slab", near), lax.ppermute(to_far, "slab", far)
+    return lax.ppermute(to_near, "slab", near), lax.ppermute(to_far, "slab", far_route(count))
+
+
+def cross_far(value):
+    segments, count = lax.axis_size("segment"), lax.axis_size("slab")
+    route = [
+        (s * count + i, (s - 1) % segments * count + j)
+        for s in range(segments)
+        for i, j in far_route(count)
+    ]
+    return lax.ppermute(value, ("segment", "slab"), route)
 
 
 def exchange(value, mask):
@@ -107,7 +121,9 @@
         copy.wait()
 
 
-def first_kernel(height, acts, near, far, grad, weight, result, slopes, shifts, deltas):
+def first_kernel(
+    height, acts, near, far, grad, weight, result, to_near, to_far, slopes, shifts, deltas
+):
     micro, depth, cells, channels = acts.shape
     even = lax.rem(lax.axis_index("slab"), 2) == 0
     span = 9 * channels
@@ -132,20 +148,36 @@
             preact = term if preact is None else preact + term
         sig = 1.0 / (1.0 + jnp.exp(-preact))
         slope = sig * (1.0 + preact * (1.0 - sig))
-        slopes[m] = slope[cells : cells + rows]
+        slopes[m] = slope
         ups = [rim(far, near, 2)] + [grad[m, n].astype(F32) for n in range(depth)]
         ups.append(rim(near, far, 2))
         for n, up in enumerate(ups):
             delta = (up * slope[n * cells : (n + 1) * cells]).astype(BF16)
             write_shifts(delta, height, deltas.at[m], n * cells)
         back = back_product(deltas.at[m], weight, rows, cells)
-        upstream = grad[m].reshape(rows, channels).astype(F32)
-        result[m] = (upstream + back).astype(BF16)
-
-
-def raw_kernel(spot, incoming, grad, slopes, shifts, upstream, deltas, near, far, *refs):
+        total = grad[m].reshape(rows, channels).astype(F32) + back
+        result[m] = total.astype(BF16).reshape(depth, cells, channels)
+        low, high = total[:cells], total[-cells:]
+        to_near[m, 0] = jnp.where(even, high, low).astype(BF16)
+        to_far[m, 0] = jnp.where(even, low, high).astype(BF16)
+
+
+def shift_kernel(height, acts, near, far, after, shifts):
+    micro, depth, cells, _ = acts.shape
+    even = lax.rem(lax.axis_index("slab"), 2) == 0
+    for m in range(micro):
+        below = jnp.where(even, far[m, 1].astype(F32), near[m, 1].astype(F32))
+        above = jnp.where(even, near[m, 0].astype(F32), far[m, 0].astype(F32))
+        planes = [below] + [acts[m, n] for n in range(depth)] + [above]
+        for n, plane in enumerate(planes):
+            write_shifts(plane, height, shifts.at[m], n * cells)
+
+
+def raw_kernel(
+    spot, incoming, in_near, in_far, grad, near, far, slopes, shifts, upstream, deltas, *refs
+):
     sends, (keep, raw) = refs[:4], refs[4:]
-    micro, depth, cells, channels = deltas.shape
+    micro, depth, cells, channels = upstream.shape
     rows = depth * cells
     span = 9 * channels
     last = lax.axis_index("segment") == lax.axis_size("segment") - 1
@@ -154,18 +186,19 @@
     for m in range(micro):
         up = jnp.where(last, grad[m].astype(F32), incoming[m].astype(F32))
         upstream[m] = up.astype(BF16)
-        delta = (up.reshape(rows, channels) * slopes[m]).astype(BF16)
-        deltas[m] = delta.reshape(depth, cells, channels)
-        low, high = delta[:cells].astype(F32), delta[-cells:].astype(F32)
-        near[m, 0] = jnp.where(even, high, low).astype(BF16)
-        far[m, 0] = jnp.where(even, low, high).astype(BF16)
+        by_near = jnp.where(last, near[m, 2].astype(F32), in_near[m, 0].astype(F32))
+        by_far = jnp.where(last, far[m, 2].astype(F32), in_far[m, 0].astype(F32))
+        below, above = jnp.where(even, by_far, by_near), jnp.where(even, by_near, by_far)
+        delta = (up.reshape(rows, channels) * slopes[m, cells : cells + rows]).astype(BF16)
+        deltas[m, :cells] = (below * slopes[m, :cells]).astype(BF16)
+        deltas[m, cells : cells + rows] = delta
+        deltas[m, cells + rows :] = (above * slopes[m, cells + rows :]).astype(BF16)
         deltas_of.append(delta)
     for dz in range(3):
         total = None
         for m in range(micro):
-            first = (1 + dz) * cells
             term = lax.dot_general(
-                shifts[m, first : first + rows, :],
+                shifts[m, dz * cells : dz * cells + rows, :],
                 deltas_of[m],
                 (((0,), (0,)), ((), ())),
                 preferred_element_type=F32,
@@ -220,15 +253,12 @@
     out[rows:] = terms.astype(BF16)
 
 
-def back_kernel(height, deltas, near, far, upstream, weight, out, shifts):
-    micro, depth, cells, channels = deltas.shape
-    even = lax.rem(lax.axis_index("slab"), 2) == 0
+def back_kernel(height, deltas, upstream, weight, out, shifts):
+    micro, depth, cells, channels = upstream.shape
     rows = depth * cells
     for m in range(micro):
-        low, high = near[m, 0].astype(F32), far[m, 0].astype(F32)
-        planes = [jnp.where(even, high, low)] + [deltas[m, n] for n in range(depth)]
-        planes.append(jnp.where(even, low, high))
-        for n, plane in enumerate(planes):
+        for n in range(depth + 2):
+            plane = deltas[m, n * cells : (n + 1) * cells, :]
             write_shifts(plane, height, shifts.at[m], n * cells)
         back = back_product(shifts.at[m], weight, rows, cells)
         total = upstream[m].reshape(rows, channels).astype(F32) + back
@@ -273,49 +303,54 @@
     to_near, to_far, acts, grad, weight = pl.pallas_call(
         rim_kernel,
         out_shape=(rim, rim, volume, volume, shape(weight.shape, BF16)),
-        in_specs=[ANY, ANY, ANY],
+        in_specs=[HBM, HBM, HBM],
         out_specs=(VMEM,) * 5,
         scratch_shapes=[pltpu.SemaphoreType.DMA((2, micro, 2)), pltpu.SemaphoreType.DMA((3,))],
         compiler_params=small,
-    )(acts, grad, weight)
+    )(*(pltpu.with_memory_space_constraint(a, pltpu.HBM) for a in (acts, grad, weight)))
     near, far = swap(to_near, to_far)
 
-    result, slopes, shifts = pl.pallas_call(
+    edge = shape((micro, 1, cells, channels), BF16)
+    wide = pltpu.VMEM((micro, rows + 2 * cells, 9 * channels), BF16)
+    result, to_near, to_far, slopes = pl.pallas_call(
         functools.partial(first_kernel, height),
-        out_shape=(
-            shape((micro, rows, channels), BF16),
-            shape((micro, rows, channels), F32),
-            shape((micro, rows + 4 * cells, 9 * channels), BF16),
-        ),
+        out_shape=(volume, edge, edge, shape((micro, rows + 2 * cells, channels), F32)),
         in_specs=[VMEM] * 5,
-        out_specs=(VMEM, VMEM, VMEM),
-        scratch_shapes=[pltpu.VMEM((micro, rows + 2 * cells, 9 * channels), BF16)],
+        out_specs=(VMEM,) * 4,
+        scratch_shapes=[pltpu.VMEM((micro, rows + 4 * cells, 9 * channels), BF16), wide],
         compiler_params=large,
     )(acts, near, far, grad, weight)
 
-    def rims(value):
-        low, high = value[:, :1], value[:, -1:]
-        even = lax.rem(index, 2) == 0
-        return jnp.where(even, high, low), jnp.where(even, low, high)
-
-    def conv_back(value, near, far, upstream):
+    def conv_back(deltas, upstream):
         return pl.pallas_call(
             functools.partial(back_kernel, height),
-            out_shape=jax.ShapeDtypeStruct((micro, depth, cells, channels), BF16),
-            in_specs=[VMEM] * 5,
+            out_shape=volume,
+            in_specs=[VMEM] * 3,
             out_specs=VMEM,
-            scratch_shapes=[pltpu.VMEM((micro, rows + 2 * cells, 9 * channels), BF16)],
+            scratch_shapes=[wide],
             compiler_params=large,
-        )(value, near, far, upstream, weight)
-
-    result = result.reshape(micro, depth, cells, channels)
+        )(deltas, upstream, weight)
+
+    even = lax.rem(index, 2) == 0
     for step in range(1, segments - 1):
-        incoming = cross(result, 1, 0)
+        incoming, in_near, in_far = cross(result, 1, 0), cross(to_near, 1, 1), cross_far(to_far)
         upstream = jnp.where(last, grad, incoming)
-        slope = slopes.reshape(micro, depth, cells, channels)
-        deltas = (upstream.astype(F32) * slope).astype(BF16)
-        result = conv_back(deltas, *swap(*rims(deltas)), upstream)
-    incoming = cross(result, 1, 0)
+        by_near = jnp.where(last, near[:, 2:], in_near)
+        by_far = jnp.where(last, far[:, 2:], in_far)
+        below, above = jnp.where(even, by_far, by_near), jnp.where(even, by_near, by_far)
+        around = jnp.concatenate([below, upstream, above], axis=1)
+        around = around.reshape(slopes.shape).astype(F32)
+        result = conv_back((around * slopes).astype(BF16), upstream)
+        low, high = result[:, :1], result[:, -1:]
+        to_near, to_far = jnp.where(even, high, low), jnp.where(even, low, high)
+    incoming, in_near, in_far = cross(result, 1, 0), cross(to_near, 1, 1), cross_far(to_far)
+    shifts = pl.pallas_call(
+        functools.partial(shift_kernel, height),
+        out_shape=shape((micro, rows + 2 * cells, 9 * channels), BF16),
+        in_specs=[VMEM] * 4,
+        out_specs=VMEM,
+        compiler_params=large,
+    )(acts, near, far, result)
 
     bits = [1 << n for n in range(1, count.bit_length() - 1)]
     inner = [bits[n : n + 2] for n in range(2, len(bits), 2)]
@@ -326,19 +361,20 @@
     spot = (side * 4 + quarter).astype(jnp.int32).reshape(1)
     part = weight.shape[0] // 8
     piece = shape((part, channels), BF16)
-    edge = shape((micro, 1, cells, channels), BF16)
-
-    upstream, deltas, to_near, to_far, *rest = pl.pallas_call(
+
+    upstream, deltas, *rest = pl.pallas_call(
         raw_kernel,
-        out_shape=(volume, volume, edge, edge) + (piece,) * 4 + (shape((4, part, channels), F32),),
-        in_specs=[SMEM] + [VMEM] * 4,
-        out_specs=(VMEM,) * 9,
+        out_shape=(volume, shape(slopes.shape, BF16))
+        + (piece,) * 4
+        + (shape((4, part, channels), F32),),
+        in_specs=[SMEM] + [VMEM] * 8,
+        out_specs=(VMEM,) * 7,
         scratch_shapes=[pltpu.VMEM((8 * part, channels), F32)],
         compiler_params=large,
-    )(spot, incoming, grad, slopes, shifts)
+    )(spot, incoming, in_near, in_far, grad, near, far, slopes, shifts)
     sends, keep = rest[:4], rest[4]
     got = {turn: exchange(sends[turn], 1) for turn in (3, 2, 1, 0)}
-    far = []
+    across = []
     for turn in (3, 2, 1):
         added = pl.pallas_call(
             functools.partial(add_kernel, turn),
@@ -347,14 +383,16 @@
             out_specs=VMEM,
             compiler_params=small,
         )(keep, got[turn])
-        far.append(exchange(added, masks[turn]))
+        across.append(exchange(added, masks[turn]))
+    gradients = conv_back(deltas, upstream)
+    across[1], gradients = lax.optimization_barrier((across[1], gradients))
     chunk = pl.pallas_call(
         sum_kernel,
         out_shape=shape((part, channels), F32),
         in_specs=[VMEM] * 5,
         out_specs=VMEM,
         compiler_params=small,
-    )(keep, got[0], *far)
+    )(keep, got[0], *across)
 
     def places(group):
         own = sum(jnp.where(index & bit, 1 << n, 0) for n, bit in enumerate(group))
@@ -404,10 +442,8 @@
         compiler_params=small,
     )(gathered, *members, *met)
     pieces = {turn: exchange(payload, masks[turn]) for turn in (3, 2, 1)}
-    pieces[3], to_near, to_far = lax.optimization_barrier((pieces[3], to_near, to_far))
-    gradients = conv_back(deltas, *swap(to_near, to_far), upstream)
-    near = [payload] + [pieces[turn] for turn in (1, 2, 3)]
-    both = near + [exchange(piece, 1) for piece in near]
+    ours = [payload] + [pieces[turn] for turn in (1, 2, 3)]
+    both = ours + [exchange(piece, 1) for piece in ours]
     bound = math.sqrt(27.0 * channels * channels * segments)
     update = pl.pallas_call(
         functools.partial(place_kernel, bound),

time: 69 us -> 61 us (0.88)
  the two profiles are of different devices: /device:TPU:1 before, /device:TPU:0 now
where the time goes in v5:
time: 61 us; the launch traced here: 60.8 us
  starting transfers between devices  30 us (49%)
  waiting for transfers between devices  20.1 us (33%)
  Pallas kernels  9.85 us (16%)
  between operations  0.76 us (1%)
    ppermute x16, starting transfers between devices, exchange(): return lax.ppermute(value, 'slab', [(i, i ^ mask) for i in range(count)])  17.9 us
    ppermute x16, waiting for transfers between devices, exchange(): return lax.ppermute(value, 'slab', [(i, i ^ mask) for i in range(count)])  15 us
    ppermute x4, starting transfers between devices, cross(): return lax.ppermute(value, ('segment', 'slab'), route)  10.2 us
    ppermute x4, waiting for transfers between devices, cross(): return lax.ppermute(value, ('segment', 'slab'), route)  4.86 us
    pallas_call x1, Pallas kernels, shards(): pl.pallas_call(functools.partial(first_kernel, height), out_shape=(volume...  3.43 us
    pallas_call x1, Pallas kernels, conv_back(): pl.pallas_call(functools.partial(back_kernel, height), out_shape=volume,...  1.77 us
    pallas_call x1, Pallas kernels, shards(): pl.pallas_call(rim_kernel, out_shape=(rim, rim, volume, volume, shape(wei...  1.55 us
    pallas_call x1, Pallas kernels, shards(): pl.pallas_call(functools.partial(place_kernel, bound), out_shape=jax.Shap...  1.39 us
  transfers between devices with their start and end apart: 23, of which 13 were waited for; matrix products, arithmetic and copies ran while one was open for 0% of the time, Pallas kernels for 3%

profile of v5, /device:TPU:0, one launch (start us, length us, event | category | flops | bytes accessed | tf_op | source)
XLA Modules:
  0.0 60.8 jit_solution(8163207185220990012)
XLA Ops:
  0.6 1.5 %shard_map.50 = (bf16[2,3,64,128]{3,2,1,0:T(8,128)(2,1)S(1)}, bf16[2,3,64,128]{3,2,1,0:T(8,128)(2,1)S(1)}, bf16[2,4,64,128]{3,2,1,0:T(8,128)(2,1)S(1)}, bf16[2,4...) custom-call(bf16[2,4,64,128]{3,2,1,0:T(8,128)(2,1)} %bitcast.8, bf16[2,4,64,128]{3,2,1,0:T(8,128)(2,1)} %bitcast.9, ...), custom_call_target="tpu_custom_call" | custom-call | tf_op jit(solution)/shard_map/pallas_call | solution.py:303
  2.2 0.5 collective-permute-start
  2.7 0.7 %collective-permute-start.1 = (bf16[2,3,64,128]{3,2,1,0:T(8,128)(2,1)S(1)}, bf16[2,3,64,128]{3,2,1,0:T(8,128)(2,1)S(1)}, u32[]{:S(2)}, u32[]{:S(2)}) collective-permute-start(bf16[2,3,64,128]{3,2,1,0:T(8,128)(2,1)S(1)} %get-tuple-element.24), channel_id=1, source_target_pairs={{1,2},{2,1},{3,4},{4,3},{5,6},{6,5},{7,8},{8,7},{9,10},{10,9},{11,... | collective-permute-start | bytes 294920 | tf_op jit(solution)/shard_map/ppermute | solution.py:26
  3.4 0.3 collective-permute-done.near
  3.6 0.0 collective-permute-done.1.far
  3.7 3.4 %shard_map.51 = (bf16[2,4,64,128]{3,2,1,0:T(8,128)(2,1)S(1)}, bf16[2,1,64,128]{3,2,1,0:T(8,128)(2,1)S(1)}, bf16[2,1,64,128]{3,2,1,0:T(8,128)(2,1)S(1)}, f32[2,384,128]{2,1,0:T(8,128)S(1)}) custom-call(bf16[2,4,64,128]{3,2,1,0:T(8,128)(2,1)S(1)} %get-tuple-element.22.acts, bf16[2,3,64,128]{3,2,1,0:T(8,128)(2,1)S(1)} %collective-permute-done.near, ...), custom_call_target="tpu_custom_call" | custom-call | tf_op jit(solution)/shard_map/pallas_call | solution.py:315
  7.1 2.9 %collective-permute-start.2 = (bf16[2,4,64,128]{3,2,1,0:T(8,128)(2,1)S(1)}, bf16[2,4,64,128]{3,2,1,0:T(8,128)(2,1)S(1)}, u32[]{:S(2)}, u32[]{:S(2)}) collective-permute-start(bf16[2,4,64,128]{3,2,1,0:T(8,128)(2,1)S(1)} %get-tuple-element.27.after), channel_id=1, source_target_pairs={{0,16},{1,17},{2,18},{3,19},{4,20},{5,21},{6,22},{7,23},{8,24},{9,... | collective-permute-start | bytes 393224 | tf_op jit(solution)/shard_map/ppermute | solution.py:53
  10.0 4.8 %collective-permute-start.3 = (bf16[2,1,64,128]{3,2,1,0:T(8,128)(2,1)S(1)}, bf16[2,1,64,128]{3,2,1,0:T(8,128)(2,1)S(1)}, u32[]{:S(2)}, u32[]{:S(2)}) collective-permute-start(bf16[2,1,64,128]{3,2,1,0:T(8,128)(2,1)S(1)} %get-tuple-element.28), channel_id=1, source_target_pairs={{0,17},{1,16},{2,19},{3,18},{4,21},{5,20},{6,23},{7,22},{8,25},{9,... | collective-permute-start | bytes 98312 | tf_op jit(solution)/shard_map/ppermute | solution.py:53
  14.8 0.7 %collective-permute-start.4 = (bf16[2,1,64,128]{3,2,1,0:T(8,128)(2,1)S(1)}, bf16[2,1,64,128]{3,2,1,0:T(8,128)(2,1)S(1)}, u32[]{:S(2)}, u32[]{:S(2)}) collective-permute-start(bf16[2,1,64,128]{3,2,1,0:T(8,128)(2,1)S(1)} %get-tuple-element.29), channel_id=1, source_target_pairs={{1,18},{2,17},{3,20},{4,19},{5,22},{6,21},{7,24},{8,23},{9,26},{10... | collective-permute-start | bytes 98312 | tf_op jit(solution)/shard_map/ppermute | solution.py:36
  15.5 0.2 shard_map.52.shifts
  15.7 2.0 %collective-permute-done.3.in_near = bf16[2,1,64,128]{3,2,1,0:T(8,128)(2,1)S(1)} collective-permute-done((bf16[2,1,64,128]{3,2,1,0:T(8,128)(2,1)S(1)}, bf16[2,1,64,128]{3,2,1,0:T(8,128)(2,1)S(1)}, u32[]{:S(2)}, u32[]{:S(2)}) %collective-permute-start.3) | collective-permute-done | bytes 32800 | tf_op jit(solution)/shard_map/ppermute | solution.py:53
  17.7 0.0 collective-permute-done.4.in_far
  17.7 0.0 collective-permute-done.2.incoming
  17.7 1.2 %shard_map.53 = (bf16[2,4,64,128]{3,2,1,0:T(8,128)(2,1)S(1)}, bf16[2,384,128]{2,1,0:T(8,128)(2,1)S(1)}, bf16[432,128]{1,0:T(8,128)(2,1)S(1)}, bf16[432,128]{1,0:...) custom-call(s32[1]{0:T(128)} %bitcast.spot, ...), custom_call_target="tpu_custom_call" | custom-call | tf_op jit(solution)/shard_map/pallas_call | solution.py:365
  19.0 4.3 %collective-permute-start.8 = (bf16[432,128]{1,0:T(8,128)(2,1)S(1)}, bf16[432,128]{1,0:T(8,128)(2,1)S(1)}, u32[]{:S(2)}, u32[]{:S(2)}) collective-permute-start(bf16[432,128]{1,0:T(8,128)(2,1)S(1)} %get-tuple-element.34), channel_id=1, source_target_pairs={{0,1},{1,0},{2,3},{3,2},{4,5},{5,4},{6,7},{7,6},{8,9},{9,8},{10,11... | collective-permute-start | bytes 331784 | tf_op jit(solution)/shard_map/ppermute | solution.py:41
  23.3 0.1 collective-permute-start.10
  23.3 0.4 collective-permute-start.6
  23.8 0.1 collective-permute-start.5
  23.8 0.4 collective-permute-done.8.got
  24.2 2.4 %collective-permute-start.9 = (bf16[432,128]{1,0:T(8,128)(2,1)S(1)}, bf16[432,128]{1,0:T(8,128)(2,1)S(1)}, u32[]{:S(2)}, u32[]{:S(2)}) collective-permute-start(bf16[432,128]{1,0:T(8,128)(2,1)S(1)} %shard_map.55), channel_id=1, source_target_pairs={{0,2},{1,3},{2,0},{3,1},{4,6},{5,7},{6,4},{7,5},{8,10},{9,11},{10,... | collective-permute-start | bytes 331784 | tf_op jit(solution)/shard_map/ppermute | solution.py:41
  26.7 1.6 %collective-permute-start.11 = (bf16[432,128]{1,0:T(8,128)(2,1)S(1)}, bf16[432,128]{1,0:T(8,128)(2,1)S(1)}, u32[]{:S(2)}, u32[]{:S(2)}) collective-permute-start(bf16[432,128]{1,0:T(8,128)(2,1)S(1)} %shard_map.57), channel_id=1, source_target_pairs={{0,4},{1,5},{2,6},{3,7},{4,0},{5,1},{6,2},{7,3},{8,12},{9,13},{10,... | collective-permute-start | bytes 331784 | tf_op jit(solution)/shard_map/ppermute | solution.py:41
  28.4 0.7 %collective-permute-start.7 = (bf16[432,128]{1,0:T(8,128)(2,1)S(1)}, bf16[432,128]{1,0:T(8,128)(2,1)S(1)}, u32[]{:S(2)}, u32[]{:S(2)}) collective-permute-start(bf16[432,128]{1,0:T(8,128)(2,1)S(1)} %shard_map.54), channel_id=1, source_target_pairs={{0,6},{1,7},{2,4},{3,5},{4,2},{5,3},{6,0},{7,1},{8,14},{9,15},{10,... | collective-permute-start | bytes 331784 | tf_op jit(solution)/shard_map/ppermute | solution.py:41
  29.0 1.8 %shard_map.56 = bf16[2,4,64,128]{3,2,1,0:T(8,128)(2,1)} custom-call(bf16[2,384,128]{2,1,0:T(8,128)(2,1)S(1)} %get-tuple-element.35.deltas, bf16[2,4,64,128]{3,2,1,0:T(8,128)(2,1)S(1)} %get-tuple-element.36.upstream, bf16[3456,128]{1,0:T(8,128)(2,1)S(1)} %get-tuple-element.26.weight), custom_call_target="tpu_custom_call" | custom-call | tf_op jit(solution)/shard_map/pallas_call | solution.py:325
  30.8 0.0 collective-permute-done.9.refs_2_
  30.8 0.0 collective-permute-done.5.refs_0_
  30.8 1.6 %collective-permute-done.11.refs_3_ = bf16[432,128]{1,0:T(8,128)(2,1)S(1)} collective-permute-done((bf16[432,128]{1,0:T(8,128)(2,1)S(1)}, bf16[432,128]{1,0:T(8,128)(2,1)S(1)}, u32[]{:S(2)}, u32[]{:S(2)}) %collective-permute-start.11) | collective-permute-done | bytes 110624 | tf_op jit(solution)/shard_map/ppermute | solution.py:41
  32.4 2.0 %collective-permute-done.7.refs_1_ = bf16[432,128]{1,0:T(8,128)(2,1)S(1)} collective-permute-done((bf16[432,128]{1,0:T(8,128)(2,1)S(1)}, bf16[432,128]{1,0:T(8,128)(2,1)S(1)}, u32[]{:S(2)}, u32[]{:S(2)}) %collective-permute-start.7) | collective-permute-done | bytes 110624 | tf_op jit(solution)/shard_map/ppermute | solution.py:41
  34.4 0.1 shard_map.58
  34.5 1.5 %collective-permute-start.12 = (bf16[216,128]{1,0:T(8,128)(2,1)S(1)}, bf16[216,128]{1,0:T(8,128)(2,1)S(1)}, u32[]{:S(2)}, u32[]{:S(2)}) collective-permute-start(bf16[216,128]{1,0:T(8,128)(2,1)S(1)} %dynamic-slice_convert_fusion), channel_id=1, source_target_pairs={{0,9},{1,8},{2,11},{3,10},{4,13},{5,12},{6,15},{7,14},{8,1},{9,0},... | collective-permute-start | bytes 165896 | tf_op jit(solution)/shard_map/ppermute | solution.py:41
  36.0 3.3 %collective-permute-done.12.refs_0_ = bf16[216,128]{1,0:T(8,128)(2,1)S(1)} collective-permute-done((bf16[216,128]{1,0:T(8,128)(2,1)S(1)}, bf16[216,128]{1,0:T(8,128)(2,1)S(1)}, u32[]{:S(2)}, u32[]{:S(2)}) %collective-permute-start.12) | collective-permute-done | bytes 55328 | tf_op jit(solution)/shard_map/ppermute | solution.py:41
  39.3 1.4 %collective-permute-start.13 = (bf16[216,128]{1,0:T(8,128)(2,1)S(1)}, bf16[216,128]{1,0:T(8,128)(2,1)S(1)}, u32[]{:S(2)}, u32[]{:S(2)}) collective-permute-start(bf16[216,128]{1,0:T(8,128)(2,1)S(1)} %get-tuple-element.39.refs_0_), channel_id=1, source_target_pairs={{0,9},{1,8},{2,11},{3,10},{4,13},{5,12},{6,15},{7,14},{8,1},{9,0},... | collective-permute-start | bytes 165896 | tf_op jit(solution)/shard_map/ppermute | solution.py:41
  40.7 1.5 %collective-permute-start.14 = (f32[8,128]{1,0:T(8,128)S(1)}, f32[8,128]{1,0:T(8,128)S(1)}, u32[]{:S(2)}, u32[]{:S(2)}) collective-permute-start(f32[8,128]{1,0:T(8,128)S(1)} %get-tuple-element.40), channel_id=1, source_target_pairs={{0,16},{1,17},{2,18},{3,19},{4,20},{5,21},{6,22},{7,23},{8,24},{9,... | collective-permute-start | bytes 12296 | tf_op jit(solution)/shard_map/ppermute | solution.py:53
  42.2 1.0 %collective-permute-start.15 = (f32[8,128]{1,0:T(8,128)S(1)}, f32[8,128]{1,0:T(8,128)S(1)}, u32[]{:S(2)}, u32[]{:S(2)}) collective-permute-start(f32[8,128]{1,0:T(8,128)S(1)} %get-tuple-element.40), channel_id=1, source_target_pairs={{0,25},{1,24},{2,27},{3,26},{4,29},{5,28},{6,31},{7,30},{8,17},{9,... | collective-permute-start | bytes 12296 | tf_op jit(solution)/shard_map/ppermute | solution.py:53
  43.2 0.9 %collective-permute-done.13.refs_1_ = bf16[216,128]{1,0:T(8,128)(2,1)S(1)} collective-permute-done((bf16[216,128]{1,0:T(8,128)(2,1)S(1)}, bf16[216,128]{1,0:T(8,128)(2,1)S(1)}, u32[]{:S(2)}, u32[]{:S(2)}) %collective-permute-start.13) | collective-permute-done | bytes 55328 | tf_op jit(solution)/shard_map/ppermute | solution.py:41
  44.2 0.1 collective-permute-done.14.refs_2_
  44.3 2.7 %collective-permute-done.15.refs_3_ = f32[8,128]{1,0:T(8,128)S(1)} collective-permute-done((f32[8,128]{1,0:T(8,128)S(1)}, f32[8,128]{1,0:T(8,128)S(1)}, u32[]{:S(2)}, u32[]{:S(2)}) %collective-permute-start.15) | collective-permute-done | bytes 4128 | tf_op jit(solution)/shard_map/ppermute | solution.py:53
  47.0 0.1 shard_map.60.refs_0_
  47.1 3.4 %collective-permute-start.16 = (bf16[448,128]{1,0:T(8,128)(2,1)S(1)}, bf16[448,128]{1,0:T(8,128)(2,1)S(1)}, u32[]{:S(2)}, u32[]{:S(2)}) collective-permute-start(bf16[448,128]{1,0:T(8,128)(2,1)S(1)} %shard_map.60.refs_0_), channel_id=1, source_target_pairs={{0,4},{1,5},{2,6},{3,7},{4,0},{5,1},{6,2},{7,3},{8,12},{9,13},{10,... | collective-permute-start | bytes 344072 | tf_op jit(solution)/shard_map/ppermute | solution.py:41
  50.5 0.4 collective-permute-start.17
  50.9 1.2 %collective-permute-start.18 = (bf16[448,128]{1,0:T(8,128)(2,1)S(1)}, bf16[448,128]{1,0:T(8,128)(2,1)S(1)}, u32[]{:S(2)}, u32[]{:S(2)}) collective-permute-start(bf16[448,128]{1,0:T(8,128)(2,1)S(1)} %shard_map.60.refs_0_), channel_id=1, source_target_pairs={{0,6},{1,7},{2,4},{3,5},{4,2},{5,3},{6,0},{7,1},{8,14},{9,15},{10,... | collective-permute-start | bytes 344072 | tf_op jit(solution)/shard_map/ppermute | solution.py:41
  52.0 2.0 %collective-permute-done.16.refs_1_ = bf16[448,128]{1,0:T(8,128)(2,1)S(1)} collective-permute-done((bf16[448,128]{1,0:T(8,128)(2,1)S(1)}, bf16[448,128]{1,0:T(8,128)(2,1)S(1)}, u32[]{:S(2)}, u32[]{:S(2)}) %collective-permute-start.16) | collective-permute-done | bytes 114720 | tf_op jit(solution)/shard_map/ppermute | solution.py:41
  54.0 3.9 %collective-permute-done.17.refs_2_ = bf16[448,128]{1,0:T(8,128)(2,1)S(1)} collective-permute-done((bf16[448,128]{1,0:T(8,128)(2,1)S(1)}, bf16[448,128]{1,0:T(8,128)(2,1)S(1)}, u32[]{:S(2)}, u32[]{:S(2)}) %collective-permute-start.17) | collective-permute-done | bytes 114720 | tf_op jit(solution)/shard_map/ppermute | solution.py:41
  57.9 0.5 collective-permute-start.22
  58.4 0.0 collective-permute-done.19.refs_4_
  58.4 0.0 collective-permute-done.20.refs_5_
  58.5 0.8 %collective-permute-done.21.refs_6_ = bf16[448,128]{1,0:T(8,128)(2,1)S(1)} collective-permute-done((bf16[448,128]{1,0:T(8,128)(2,1)S(1)}, bf16[448,128]{1,0:T(8,128)(2,1)S(1)}, u32[]{:S(2)}, u32[]{:S(2)}) %collective-permute-start.21) | collective-permute-done | bytes 114720 | tf_op jit(solution)/shard_map/ppermute | solution.py:41
  59.3 0.2 collective-permute-done.22.refs_7_
  59.4 1.4 %shard_map.61 = f32[8,432,128]{2,1,0:T(8,128)} custom-call(s32[1]{0:T(128)} %bitcast.spot, bf16[448,128]{1,0:T(8,128)(2,1)S(1)} %shard_map.60.refs_0_, bf16[448,128]{1,0:T(8,128)(2,1)S(1)} %collective-permute-done.16.refs_1_, bf16[448,128]{1,0:T(8,128)(2,1)S(1)} %collective-permute-done.17.refs_2_, bf16[448,128]{1,0:T(8,128)(2,1)S(1)} %collective-permute-done.18.refs_3_, ...), custom_call_target="tpu_custom_call" | custom-call | tf_op jit(solution)/shard_map/pallas_call | solution.py:448
  (14 shorter events, 0.2 us)
Async XLA Ops:
  2.2 1.5 %collective-permute-start = (bf16[2,3,64,128]{3,2,1,0:T(8,128)(2,1)S(1)}, bf16[2,3,64,128]{3,2,1,0:T(8,128)(2,1)S(1)}, u32[]{:S(2)}, u32[]{:S(2)}) collective-permute-start(bf16[2,3,64,128]{3,2,1,0:T(8,128)(2,1)S(1)} %get-tuple-element.23), channel_id=1, source_target_pairs={{0,1},{1,0},{2,3},{3,2},{4,5},{5,4},{6,7},{7,6},{8,9},{9,8},{10,11... | collective-permute-start | bytes 294920 | tf_op jit(solution)/shard_map/ppermute | solution.py:26
  2.7 0.9 %collective-permute-start.1 = (bf16[2,3,64,128]{3,2,1,0:T(8,128)(2,1)S(1)}, bf16[2,3,64,128]{3,2,1,0:T(8,128)(2,1)S(1)}, u32[]{:S(2)}, u32[]{:S(2)}) collective-permute-start(bf16[2,3,64,128]{3,2,1,0:T(8,128)(2,1)S(1)} %get-tuple-element.24), channel_id=1, source_target_pairs={{1,2},{2,1},{3,4},{4,3},{5,6},{6,5},{7,8},{8,7},{9,10},{10,9},{11,... | collective-permute-start | bytes 294920 | tf_op jit(solution)/shard_map/ppermute | solution.py:26
  7.1 10.7 %collective-permute-start.2 = (bf16[2,4,64,128]{3,2,1,0:T(8,128)(2,1)S(1)}, bf16[2,4,64,128]{3,2,1,0:T(8,128)(2,1)S(1)}, u32[]{:S(2)}, u32[]{:S(2)}) collective-permute-start(bf16[2,4,64,128]{3,2,1,0:T(8,128)(2,1)S(1)} %get-tuple-element.27.after), channel_id=1, source_target_pairs={{0,16},{1,17},{2,18},{3,19},{4,20},{5,21},{6,22},{7,23},{8,24},{9,... | collective-permute-start | bytes 393224 | tf_op jit(solution)/shard_map/ppermute | solution.py:53
  10.0 7.7 %collective-permute-start.3 = (bf16[2,1,64,128]{3,2,1,0:T(8,128)(2,1)S(1)}, bf16[2,1,64,128]{3,2,1,0:T(8,128)(2,1)S(1)}, u32[]{:S(2)}, u32[]{:S(2)}) collective-permute-start(bf16[2,1,64,128]{3,2,1,0:T(8,128)(2,1)S(1)} %get-tuple-element.28), channel_id=1, source_target_pairs={{0,17},{1,16},{2,19},{3,18},{4,21},{5,20},{6,23},{7,22},{8,25},{9,... | collective-permute-start | bytes 98312 | tf_op jit(solution)/shard_map/ppermute | solution.py:53
  14.8 2.9 %collective-permute-start.4 = (bf16[2,1,64,128]{3,2,1,0:T(8,128)(2,1)S(1)}, bf16[2,1,64,128]{3,2,1,0:T(8,128)(2,1)S(1)}, u32[]{:S(2)}, u32[]{:S(2)}) collective-permute-start(bf16[2,1,64,128]{3,2,1,0:T(8,128)(2,1)S(1)} %get-tuple-element.29), channel_id=1, source_target_pairs={{1,18},{2,17},{3,20},{4,19},{5,22},{6,21},{7,24},{8,23},{9,26},{10... | collective-permute-start | bytes 98312 | tf_op jit(solution)/shard_map/ppermute | solution.py:36
  19.0 5.2 %collective-permute-start.8 = (bf16[432,128]{1,0:T(8,128)(2,1)S(1)}, bf16[432,128]{1,0:T(8,128)(2,1)S(1)}, u32[]{:S(2)}, u32[]{:S(2)}) collective-permute-start(bf16[432,128]{1,0:T(8,128)(2,1)S(1)} %get-tuple-element.34), channel_id=1, source_target_pairs={{0,1},{1,0},{2,3},{3,2},{4,5},{5,4},{6,7},{7,6},{8,9},{9,8},{10,11... | collective-permute-start | bytes 331784 | tf_op jit(solution)/shard_map/ppermute | solution.py:41
  23.3 3.4 %collective-permute-start.10 = (bf16[432,128]{1,0:T(8,128)(2,1)S(1)}, bf16[432,128]{1,0:T(8,128)(2,1)S(1)}, u32[]{:S(2)}, u32[]{:S(2)}) collective-permute-start(bf16[432,128]{1,0:T(8,128)(2,1)S(1)} %get-tuple-element.38), channel_id=1, source_target_pairs={{0,1},{1,0},{2,3},{3,2},{4,5},{5,4},{6,7},{7,6},{8,9},{9,8},{10,11... | collective-permute-start | bytes 331784 | tf_op jit(solution)/shard_map/ppermute | solution.py:41
  23.3 5.0 %collective-permute-start.6 = (bf16[432,128]{1,0:T(8,128)(2,1)S(1)}, bf16[432,128]{1,0:T(8,128)(2,1)S(1)}, u32[]{:S(2)}, u32[]{:S(2)}) collective-permute-start(bf16[432,128]{1,0:T(8,128)(2,1)S(1)} %get-tuple-element.33), channel_id=1, source_target_pairs={{0,1},{1,0},{2,3},{3,2},{4,5},{5,4},{6,7},{7,6},{8,9},{9,8},{10,11... | collective-permute-start | bytes 331784 | tf_op jit(solution)/shard_map/ppermute | solution.py:41
  23.8 7.1 %collective-permute-start.5 = (bf16[432,128]{1,0:T(8,128)(2,1)S(1)}, bf16[432,128]{1,0:T(8,128)(2,1)S(1)}, u32[]{:S(2)}, u32[]{:S(2)}) collective-permute-start(bf16[432,128]{1,0:T(8,128)(2,1)S(1)} %get-tuple-element.32), channel_id=1, source_target_pairs={{0,1},{1,0},{2,3},{3,2},{4,5},{5,4},{6,7},{7,6},{8,9},{9,8},{10,11... | collective-permute-start | bytes 331784 | tf_op jit(solution)/shard_map/ppermute | solution.py:41
  24.2 6.6 %collective-permute-start.9 = (bf16[432,128]{1,0:T(8,128)(2,1)S(1)}, bf16[432,128]{1,0:T(8,128)(2,1)S(1)}, u32[]{:S(2)}, u32[]{:S(2)}) collective-permute-start(bf16[432,128]{1,0:T(8,128)(2,1)S(1)} %shard_map.55), channel_id=1, source_target_pairs={{0,2},{1,3},{2,0},{3,1},{4,6},{5,7},{6,4},{7,5},{8,10},{9,11},{10,... | collective-permute-start | bytes 331784 | tf_op jit(solution)/shard_map/ppermute | solution.py:41
  26.7 5.7 %collective-permute-start.11 = (bf16[432,128]{1,0:T(8,128)(2,1)S(1)}, bf16[432,128]{1,0:T(8,128)(2,1)S(1)}, u32[]{:S(2)}, u32[]{:S(2)}) collective-permute-start(bf16[432,128]{1,0:T(8,128)(2,1)S(1)} %shard_map.57), channel_id=1, source_target_pairs={{0,4},{1,5},{2,6},{3,7},{4,0},{5,1},{6,2},{7,3},{8,12},{9,13},{10,... | collective-permute-start | bytes 331784 | tf_op jit(solution)/shard_map/ppermute | solution.py:41
  28.4 6.0 %collective-permute-start.7 = (bf16[432,128]{1,0:T(8,128)(2,1)S(1)}, bf16[432,128]{1,0:T(8,128)(2,1)S(1)}, u32[]{:S(2)}, u32[]{:S(2)}) collective-permute-start(bf16[432,128]{1,0:T(8,128)(2,1)S(1)} %shard_map.54), channel_id=1, source_target_pairs={{0,6},{1,7},{2,4},{3,5},{4,2},{5,3},{6,0},{7,1},{8,14},{9,15},{10,... | collective-permute-start | bytes 331784 | tf_op jit(solution)/shard_map/ppermute | solution.py:41
  34.5 4.8 %collective-permute-start.12 = (bf16[216,128]{1,0:T(8,128)(2,1)S(1)}, bf16[216,128]{1,0:T(8,128)(2,1)S(1)}, u32[]{:S(2)}, u32[]{:S(2)}) collective-permute-start(bf16[216,128]{1,0:T(8,128)(2,1)S(1)} %dynamic-slice_convert_fusion), channel_id=1, source_target_pairs={{0,9},{1,8},{2,11},{3,10},{4,13},{5,12},{6,15},{7,14},{8,1},{9,0},... | collective-permute-start | bytes 165896 | tf_op jit(solution)/shard_map/ppermute | solution.py:41
  39.3 4.8 %collective-permute-start.13 = (bf16[216,128]{1,0:T(8,128)(2,1)S(1)}, bf16[216,128]{1,0:T(8,128)(2,1)S(1)}, u32[]{:S(2)}, u32[]{:S(2)}) collective-permute-start(bf16[216,128]{1,0:T(8,128)(2,1)S(1)} %get-tuple-element.39.refs_0_), channel_id=1, source_target_pairs={{0,9},{1,8},{2,11},{3,10},{4,13},{5,12},{6,15},{7,14},{8,1},{9,0},... | collective-permute-start | bytes 165896 | tf_op jit(solution)/shard_map/ppermute | solution.py:41
  40.7 3.6 %collective-permute-start.14 = (f32[8,128]{1,0:T(8,128)S(1)}, f32[8,128]{1,0:T(8,128)S(1)}, u32[]{:S(2)}, u32[]{:S(2)}) collective-permute-start(f32[8,128]{1,0:T(8,128)S(1)} %get-tuple-element.40), channel_id=1, source_target_pairs={{0,16},{1,17},{2,18},{3,19},{4,20},{5,21},{6,22},{7,23},{8,24},{9,... | collective-permute-start | bytes 12296 | tf_op jit(solution)/shard_map/ppermute | solution.py:53
  42.2 4.8 %collective-permute-start.15 = (f32[8,128]{1,0:T(8,128)S(1)}, f32[8,128]{1,0:T(8,128)S(1)}, u32[]{:S(2)}, u32[]{:S(2)}) collective-permute-start(f32[8,128]{1,0:T(8,128)S(1)} %get-tuple-element.40), channel_id=1, source_target_pairs={{0,25},{1,24},{2,27},{3,26},{4,29},{5,28},{6,31},{7,30},{8,17},{9,... | collective-permute-start | bytes 12296 | tf_op jit(solution)/shard_map/ppermute | solution.py:53
  47.1 6.9 %collective-permute-start.16 = (bf16[448,128]{1,0:T(8,128)(2,1)S(1)}, bf16[448,128]{1,0:T(8,128)(2,1)S(1)}, u32[]{:S(2)}, u32[]{:S(2)}) collective-permute-start(bf16[448,128]{1,0:T(8,128)(2,1)S(1)} %shard_map.60.refs_0_), channel_id=1, source_target_pairs={{0,4},{1,5},{2,6},{3,7},{4,0},{5,1},{6,2},{7,3},{8,12},{9,13},{10,... | collective-permute-start | bytes 344072 | tf_op jit(solution)/shard_map/ppermute | solution.py:41
  50.5 7.5 %collective-permute-start.17 = (bf16[448,128]{1,0:T(8,128)(2,1)S(1)}, bf16[448,128]{1,0:T(8,128)(2,1)S(1)}, u32[]{:S(2)}, u32[]{:S(2)}) collective-permute-start(bf16[448,128]{1,0:T(8,128)(2,1)S(1)} %shard_map.60.refs_0_), channel_id=1, source_target_pairs={{0,2},{1,3},{2,0},{3,1},{4,6},{5,7},{6,4},{7,5},{8,10},{9,11},{10,... | collective-permute-start | bytes 344072 | tf_op jit(solution)/shard_map/ppermute | solution.py:41
  50.9 7.1 %collective-permute-start.18 = (bf16[448,128]{1,0:T(8,128)(2,1)S(1)}, bf16[448,128]{1,0:T(8,128)(2,1)S(1)}, u32[]{:S(2)}, u32[]{:S(2)}) collective-permute-start(bf16[448,128]{1,0:T(8,128)(2,1)S(1)} %shard_map.60.refs_0_), channel_id=1, source_target_pairs={{0,6},{1,7},{2,4},{3,5},{4,2},{5,3},{6,0},{7,1},{8,14},{9,15},{10,... | collective-permute-start | bytes 344072 | tf_op jit(solution)/shard_map/ppermute | solution.py:41
  52.0 6.4 %collective-permute-start.19 = (bf16[448,128]{1,0:T(8,128)(2,1)S(1)}, bf16[448,128]{1,0:T(8,128)(2,1)S(1)}, u32[]{:S(2)}, u32[]{:S(2)}) collective-permute-start(bf16[448,128]{1,0:T(8,128)(2,1)S(1)} %shard_map.60.refs_0_), channel_id=1, source_target_pairs={{0,1},{1,0},{2,3},{3,2},{4,5},{5,4},{6,7},{7,6},{8,9},{9,8},{10,11... | collective-permute-start | bytes 344072 | tf_op jit(solution)/shard_map/ppermute | solution.py:41
  54.0 4.4 %collective-permute-start.20 = (bf16[448,128]{1,0:T(8,128)(2,1)S(1)}, bf16[448,128]{1,0:T(8,128)(2,1)S(1)}, u32[]{:S(2)}, u32[]{:S(2)}) collective-permute-start(bf16[448,128]{1,0:T(8,128)(2,1)S(1)} %collective-permute-done.16.refs_1_), channel_id=1, source_target_pairs={{0,1},{1,0},{2,3},{3,2},{4,5},{5,4},{6,7},{7,6},{8,9},{9,8},{10,11... | collective-permute-start | bytes 344072 | tf_op jit(solution)/shard_map/ppermute | solution.py:41
  57.9 1.3 %collective-permute-start.21 = (bf16[448,128]{1,0:T(8,128)(2,1)S(1)}, bf16[448,128]{1,0:T(8,128)(2,1)S(1)}, u32[]{:S(2)}, u32[]{:S(2)}) collective-permute-start(bf16[448,128]{1,0:T(8,128)(2,1)S(1)} %collective-permute-done.17.refs_2_), channel_id=1, source_target_pairs={{0,1},{1,0},{2,3},{3,2},{4,5},{5,4},{6,7},{7,6},{8,9},{9,8},{10,11... | collective-permute-start | bytes 344072 | tf_op jit(solution)/shard_map/ppermute | solution.py:41
  57.9 1.5 %collective-permute-start.22 = (bf16[448,128]{1,0:T(8,128)(2,1)S(1)}, bf16[448,128]{1,0:T(8,128)(2,1)S(1)}, u32[]{:S(2)}, u32[]{:S(2)}) collective-permute-start(bf16[448,128]{1,0:T(8,128)(2,1)S(1)} %collective-permute-done.18.refs_3_), channel_id=1, source_target_pairs={{0,1},{1,0},{2,3},{3,2},{4,5},{5,4},{6,7},{7,6},{8,9},{9,8},{10,11... | collective-permute-start | bytes 344072 | tf_op jit(solution)/shard_map/ppermute | solution.py:41

commit v6 on v5

--- a/solution.py
+++ b/solution.py
@@ -219,7 +219,11 @@
     total = keep[0]
     for got in refs[:-1]:
         total = total + got[...].astype(F32)
-    refs[-1][...] = total
+    refs[-1][...] = total.astype(refs[-1].dtype)
+
+
+def both_kernel(mine, other, out):
+    out[...] = (mine[...].astype(F32) + other[...].astype(F32)).astype(BF16)
 
 
 def column_squares(value):
@@ -227,30 +231,11 @@
     return jnp.sum(value * value, axis=0, keepdims=True)
 
 
-def chunk_kernel(keep, *refs):
-    total = keep[...]
-    for got in refs[:-2]:
-        total = total + got[...].astype(F32)
-    chunk, squares = refs[-2:]
-    chunk[...] = total.astype(BF16)
-    squares[...] = jnp.broadcast_to(column_squares(chunk[...]), squares.shape)
-
-
-def payload_kernel(count, gathered, *refs):
-    own, values, out = refs[:count], refs[count:-1], refs[-1]
-    sums = [column_squares(piece[...]) for piece in own]
-    for n, value in enumerate(values):
-        sums[n % count] = sums[n % count] + value[:1, :]
+def norm_kernel(*refs):
+    sums = [column_squares(piece[...]) for piece in refs[:-1]]
     while len(sums) > 1:
         sums = [a + b for a, b in zip(sums[::2], sums[1::2], strict=True)]
-    rows = gathered.shape[0]
-    out[:rows] = gathered[...]
-    high = sums[0].astype(BF16).astype(F32)
-    middle = (sums[0] - high).astype(BF16).astype(F32)
-    low = sums[0] - high - middle
-    at = lax.broadcasted_iota(jnp.int32, (16, gathered.shape[1]), 0)
-    terms = jnp.where(at == 0, high, jnp.where(at == 1, middle, jnp.where(at == 2, low, 0.0)))
-    out[rows:] = terms.astype(BF16)
+    refs[-1][...] = jnp.broadcast_to(sums[0], refs[-1].shape)
 
 
 def back_kernel(height, deltas, upstream, weight, out, shifts):
@@ -265,17 +250,15 @@
         out[m] = total.astype(BF16).reshape(depth, cells, channels)
 
 
-def place_kernel(bound, spot, *refs):
-    pieces, (out, scaled, sems) = refs[:-3], refs[-3:]
-    rows = scaled.shape[1]
-    sums = [piece[rows:].astype(F32) for piece in pieces]
-    while len(sums) > 1:
-        sums = [a + b for a, b in zip(sums[::2], sums[1::2], strict=True)]
-    norm = jnp.sqrt(jnp.sum(jnp.sum(sums[0], axis=0, keepdims=True), axis=1, keepdims=True))
+def place_kernel(bound, count, spot, *refs):
+    sums, pieces, (out, scaled, sems) = refs[: 2 * count], refs[2 * count : -3], refs[-3:]
+    mine, other = (sum(value[:1, :] for value in sums[side::2]) for side in range(2))
+    squares = mine + other
+    norm = jnp.sqrt(jnp.sum(squares, axis=1, keepdims=True))
     factor = jnp.minimum(1.0, bound / (norm + 1e-06))
     copies = []
     for n, piece in enumerate(pieces):
-        scaled[n] = piece[:rows].astype(F32) * factor
+        scaled[n] = piece[...].astype(F32) * factor
         copies.append(pltpu.make_async_copy(scaled.at[n], out.at[spot[0] ^ n], sems.at[n]))
         copies[-1].start()
     for copy in copies:
@@ -386,9 +369,11 @@
         across.append(exchange(added, masks[turn]))
     gradients = conv_back(deltas, upstream)
     across[1], gradients = lax.optimization_barrier((across[1], gradients))
+    single = len(inner[-1]) == 1
+    direct = single and len(inner) == 1
     chunk = pl.pallas_call(
         sum_kernel,
-        out_shape=shape((part, channels), F32),
+        out_shape=shape((part, channels), BF16 if direct else F32),
         in_specs=[VMEM] * 5,
         out_specs=VMEM,
         compiler_params=small,
@@ -398,61 +383,58 @@
         own = sum(jnp.where(index & bit, 1 << n, 0) for n, bit in enumerate(group))
         others = []
         for turn in range(1, 1 << len(group)):
-            mask = sum(bit for n, bit in enumerate(group) if turn >> n & 1)
-            others.append((mask | 1 if mask == crossing else mask, own ^ turn))
+            others.append((sum(bit for n, bit in enumerate(group) if turn >> n & 1), own ^ turn))
         return own, others
 
-    for group in inner:
+    paired = inner[:-1] if single else inner
+    for group in paired:
         own, others = places(group)
         size = chunk.shape[0] >> len(group)
-        got = [exchange(block(chunk, there, size, BF16), mask) for mask, there in others]
-        chunk = block(chunk, own, size, F32)
-        if group is not inner[-1]:
-            chunk = chunk + sum(g.astype(F32) for g in got)
-    gathered, squares = pl.pallas_call(
-        chunk_kernel,
-        out_shape=(shape(chunk.shape, BF16), shape((8, channels), F32)),
-        in_specs=[VMEM] * (1 + len(got)),
-        out_specs=(VMEM, VMEM),
-        compiler_params=small,
-    )(chunk, *got)
-
-    for group in reversed(inner):
+        took = [exchange(block(chunk, there, size, BF16), mask) for mask, there in others]
+        chunk = block(chunk, own, size, F32) + sum(g.astype(F32) for g in took)
+    gathered = chunk.astype(BF16)
+    if single:
+        gathered = pl.pallas_call(
+            both_kernel,
+            out_shape=shape(gathered.shape, BF16),
+            in_specs=[VMEM] * 2,
+            out_specs=VMEM,
+            compiler_params=small,
+        )(gathered, exchange(gathered, crossing | 1))
+
+    for group in reversed(paired):
         own, others = places(group)
-        got = [(there, exchange(gathered, mask)) for mask, there in others]
-        if group is inner[-1]:
-            members = [gathered] + [other for _, other in got]
-            met = [
-                cross(squares, back, mask)
-                for back in range(1, segments)
-                for mask in [0] + [mask for mask, _ in others]
-            ]
+        took = [(there, exchange(gathered, mask)) for mask, there in others]
         blocks = []
         for n in range(1 << len(group)):
-            value = jnp.where(own == n, gathered, got[0][1])
-            for there, other in got[1:]:
+            value = jnp.where(own == n, gathered, took[0][1])
+            for there, other in took[1:]:
                 value = jnp.where(there == n, other, value)
             blocks.append(value)
         gathered = jnp.concatenate(blocks, axis=0)
-    payload = pl.pallas_call(
-        functools.partial(payload_kernel, len(members)),
-        out_shape=shape((part + 16, channels), BF16),
-        in_specs=[VMEM] * (1 + len(members) + len(met)),
-        out_specs=VMEM,
-        compiler_params=small,
-    )(gathered, *members, *met)
-    pieces = {turn: exchange(payload, masks[turn]) for turn in (3, 2, 1)}
-    ours = [payload] + [pieces[turn] for turn in (1, 2, 3)]
-    both = ours + [exchange(piece, 1) for piece in ours]
+    pieces = {turn: exchange(gathered, masks[turn]) for turn in (3, 2, 1)}
+    ours = [gathered] + [pieces[turn] for turn in (1, 2, 3)]
+    theirs = [exchange(piece, 1) for piece in ours]
+    sums = [
+        pl.pallas_call(
+            norm_kernel,
+            out_shape=shape((8, channels), F32),
+            in_specs=[VMEM] * 4,
+            out_specs=VMEM,
+            compiler_params=small,
+        )(*four)
+        for four in (ours, theirs)
+    ]
+    sums += [cross(sums[0], back, mask) for back in range(1, segments) for mask in (0, 1)]
     bound = math.sqrt(27.0 * channels * channels * segments)
     update = pl.pallas_call(
-        functools.partial(place_kernel, bound),
+        functools.partial(place_kernel, bound, segments),
         out_shape=jax.ShapeDtypeStruct((8, part, channels), F32),
-        in_specs=[SMEM] + [VMEM] * 8,
+        in_specs=[SMEM] + [VMEM] * (2 * segments + 8),
         out_specs=ANY,
         scratch_shapes=[pltpu.VMEM((8, part, channels), F32), pltpu.SemaphoreType.DMA((8,))],
         compiler_params=large,
-    )((side * 4 + quarter).astype(jnp.int32).reshape(1), *both)
+    )((side * 4 + quarter).astype(jnp.int32).reshape(1), *sums, *ours, *theirs)
     gradients = gradients.reshape(1, micro, depth, width, height, channels)
     return (update.reshape(1, 8 * part, channels), gradients)
 

time: 61 us -> 57.6 us (0.944)
  waiting for transfers between devices: 20.1 us -> 17.1 us
    ppermute x16 -> x15, waiting for transfers between devices: 15 us -> 12.3 us  [exchange(): return lax.ppermute(value, 'slab', [(i, i ^ mask) for i in range(count)])]
    pallas_call x4 -> x5, Pallas kernels: 1.56 us -> 1.73 us  [the longest x1 1.38 us: shards(): pl.pallas_call(functools.partial(place_kernel, bound, segments), out_shap...]
    ppermute x16 -> x15, starting transfers between devices: 17.9 us -> 17.9 us  [exchange(): return lax.ppermute(value, 'slab', [(i, i ^ mask) for i in range(count)])]
  transfers between devices with their start and end apart: 23 -> 22, of which waited for: 13 -> 12; matrix products, arithmetic and copies ran while one was open for 0% -> 0% of each run, Pallas kernels for 3% -> 4%
where the time goes in v6:
time: 57.6 us; the launch traced here: 57.5 us
  starting transfers between devices  29.6 us (51%)
  waiting for transfers between devices  17.1 us (30%)
  Pallas kernels  10 us (17%)
  between operations  0.74 us (1%)
    ppermute x15, starting transfers between devices, exchange(): return lax.ppermute(value, 'slab', [(i, i ^ mask) for i in range(count)])  17.9 us
    ppermute x15, waiting for transfers between devices, exchange(): return lax.ppermute(value, 'slab', [(i, i ^ mask) for i in range(count)])  12.3 us
    ppermute x4, starting transfers between devices, cross(): return lax.ppermute(value, ('segment', 'slab'), route)  9.92 us
    ppermute x4, waiting for transfers between devices, cross(): return lax.ppermute(value, ('segment', 'slab'), route)  4.5 us
    pallas_call x1, Pallas kernels, shards(): pl.pallas_call(functools.partial(first_kernel, height), out_shape=(volume...  3.43 us
    pallas_call x1, Pallas kernels, conv_back(): pl.pallas_call(functools.partial(back_kernel, height), out_shape=volume,...  1.77 us
    pallas_call x1, Pallas kernels, shards(): pl.pallas_call(rim_kernel, out_shape=(rim, rim, volume, volume, shape(wei...  1.55 us
    pallas_call x1, Pallas kernels, shards(): pl.pallas_call(functools.partial(place_kernel, bound, segments), out_shap...  1.38 us
  transfers between devices with their start and end apart: 22, of which 12 were waited for; matrix products, arithmetic and copies ran while one was open for 0% of the time, Pallas kernels for 4%

profile of v6, /device:TPU:0, one launch (start us, length us, event | category | flops | bytes accessed | tf_op | source)
XLA Modules:
  0.0 57.5 jit_solution(5567040703776745530)
XLA Ops:
  0.6 1.5 %shard_map.50 = (bf16[2,3,64,128]{3,2,1,0:T(8,128)(2,1)S(1)}, bf16[2,3,64,128]{3,2,1,0:T(8,128)(2,1)S(1)}, bf16[2,4,64,128]{3,2,1,0:T(8,128)(2,1)S(1)}, bf16[2,4...) custom-call(bf16[2,4,64,128]{3,2,1,0:T(8,128)(2,1)} %bitcast.8, bf16[2,4,64,128]{3,2,1,0:T(8,128)(2,1)} %bitcast.9, ...), custom_call_target="tpu_custom_call" | custom-call | tf_op jit(solution)/shard_map/pallas_call | solution.py:286
  2.2 0.5 collective-permute-start
  2.7 0.7 %collective-permute-start.1 = (bf16[2,3,64,128]{3,2,1,0:T(8,128)(2,1)S(1)}, bf16[2,3,64,128]{3,2,1,0:T(8,128)(2,1)S(1)}, u32[]{:S(2)}, u32[]{:S(2)}) collective-permute-start(bf16[2,3,64,128]{3,2,1,0:T(8,128)(2,1)S(1)} %get-tuple-element.22), channel_id=1, source_target_pairs={{1,2},{2,1},{3,4},{4,3},{5,6},{6,5},{7,8},{8,7},{9,10},{10,9},{11,... | collective-permute-start | bytes 294920 | tf_op jit(solution)/shard_map/ppermute | solution.py:26
  3.4 0.3 collective-permute-done.near
  3.6 0.0 collective-permute-done.1.far
  3.7 3.4 %shard_map.51 = (bf16[2,4,64,128]{3,2,1,0:T(8,128)(2,1)S(1)}, bf16[2,1,64,128]{3,2,1,0:T(8,128)(2,1)S(1)}, bf16[2,1,64,128]{3,2,1,0:T(8,128)(2,1)S(1)}, f32[2,384,128]{2,1,0:T(8,128)S(1)}) custom-call(bf16[2,4,64,128]{3,2,1,0:T(8,128)(2,1)S(1)} %get-tuple-element.20.acts, bf16[2,3,64,128]{3,2,1,0:T(8,128)(2,1)S(1)} %collective-permute-done.near, ...), custom_call_target="tpu_custom_call" | custom-call | tf_op jit(solution)/shard_map/pallas_call | solution.py:298
  7.1 2.9 %collective-permute-start.2 = (bf16[2,4,64,128]{3,2,1,0:T(8,128)(2,1)S(1)}, bf16[2,4,64,128]{3,2,1,0:T(8,128)(2,1)S(1)}, u32[]{:S(2)}, u32[]{:S(2)}) collective-permute-start(bf16[2,4,64,128]{3,2,1,0:T(8,128)(2,1)S(1)} %get-tuple-element.25.after), channel_id=1, source_target_pairs={{0,16},{1,17},{2,18},{3,19},{4,20},{5,21},{6,22},{7,23},{8,24},{9,... | collective-permute-start | bytes 393224 | tf_op jit(solution)/shard_map/ppermute | solution.py:53
  10.0 4.8 %collective-permute-start.3 = (bf16[2,1,64,128]{3,2,1,0:T(8,128)(2,1)S(1)}, bf16[2,1,64,128]{3,2,1,0:T(8,128)(2,1)S(1)}, u32[]{:S(2)}, u32[]{:S(2)}) collective-permute-start(bf16[2,1,64,128]{3,2,1,0:T(8,128)(2,1)S(1)} %get-tuple-element.26), channel_id=1, source_target_pairs={{0,17},{1,16},{2,19},{3,18},{4,21},{5,20},{6,23},{7,22},{8,25},{9,... | collective-permute-start | bytes 98312 | tf_op jit(solution)/shard_map/ppermute | solution.py:53
  14.8 0.7 %collective-permute-start.4 = (bf16[2,1,64,128]{3,2,1,0:T(8,128)(2,1)S(1)}, bf16[2,1,64,128]{3,2,1,0:T(8,128)(2,1)S(1)}, u32[]{:S(2)}, u32[]{:S(2)}) collective-permute-start(bf16[2,1,64,128]{3,2,1,0:T(8,128)(2,1)S(1)} %get-tuple-element.27), channel_id=1, source_target_pairs={{1,18},{2,17},{3,20},{4,19},{5,22},{6,21},{7,24},{8,23},{9,26},{10... | collective-permute-start | bytes 98312 | tf_op jit(solution)/shard_map/ppermute | solution.py:36
  15.5 0.2 shard_map.52.shifts
  15.7 2.0 %collective-permute-done.3.in_near = bf16[2,1,64,128]{3,2,1,0:T(8,128)(2,1)S(1)} collective-permute-done((bf16[2,1,64,128]{3,2,1,0:T(8,128)(2,1)S(1)}, bf16[2,1,64,128]{3,2,1,0:T(8,128)(2,1)S(1)}, u32[]{:S(2)}, u32[]{:S(2)}) %collective-permute-start.3) | collective-permute-done | bytes 32800 | tf_op jit(solution)/shard_map/ppermute | solution.py:53
  17.7 1.2 %shard_map.53 = (bf16[2,4,64,128]{3,2,1,0:T(8,128)(2,1)S(1)}, bf16[2,384,128]{2,1,0:T(8,128)(2,1)S(1)}, bf16[432,128]{1,0:T(8,128)(2,1)S(1)}, bf16[432,128]{1,0:...) custom-call(s32[1]{0:T(128)} %bitcast.spot, ...), custom_call_target="tpu_custom_call" | custom-call | tf_op jit(solution)/shard_map/pallas_call | solution.py:348
  19.0 4.3 %collective-permute-start.8 = (bf16[432,128]{1,0:T(8,128)(2,1)S(1)}, bf16[432,128]{1,0:T(8,128)(2,1)S(1)}, u32[]{:S(2)}, u32[]{:S(2)}) collective-permute-start(bf16[432,128]{1,0:T(8,128)(2,1)S(1)} %get-tuple-element.32), channel_id=1, source_target_pairs={{0,1},{1,0},{2,3},{3,2},{4,5},{5,4},{6,7},{7,6},{8,9},{9,8},{10,11... | collective-permute-start | bytes 331784 | tf_op jit(solution)/shard_map/ppermute | solution.py:41
  23.3 0.1 collective-permute-start.6
  23.3 0.4 collective-permute-start.10
  23.8 0.1 collective-permute-start.5
  23.8 0.4 collective-permute-done.8.got
  24.2 2.4 %collective-permute-start.9 = (bf16[432,128]{1,0:T(8,128)(2,1)S(1)}, bf16[432,128]{1,0:T(8,128)(2,1)S(1)}, u32[]{:S(2)}, u32[]{:S(2)}) collective-permute-start(bf16[432,128]{1,0:T(8,128)(2,1)S(1)} %shard_map.55), channel_id=1, source_target_pairs={{0,2},{1,3},{2,0},{3,1},{4,6},{5,7},{6,4},{7,5},{8,10},{9,11},{10,... | collective-permute-start | bytes 331784 | tf_op jit(solution)/shard_map/ppermute | solution.py:41
  26.7 2.2 %collective-permute-start.7 = (bf16[432,128]{1,0:T(8,128)(2,1)S(1)}, bf16[432,128]{1,0:T(8,128)(2,1)S(1)}, u32[]{:S(2)}, u32[]{:S(2)}) collective-permute-start(bf16[432,128]{1,0:T(8,128)(2,1)S(1)} %shard_map.54), channel_id=1, source_target_pairs={{0,6},{1,7},{2,4},{3,5},{4,2},{5,3},{6,0},{7,1},{8,14},{9,15},{10,... | collective-permute-start | bytes 331784 | tf_op jit(solution)/shard_map/ppermute | solution.py:41
  29.0 0.1 collective-permute-start.11
  29.0 1.8 %shard_map.56 = bf16[2,4,64,128]{3,2,1,0:T(8,128)(2,1)} custom-call(bf16[2,384,128]{2,1,0:T(8,128)(2,1)S(1)} %get-tuple-element.33.deltas, bf16[2,4,64,128]{3,2,1,0:T(8,128)(2,1)S(1)} %get-tuple-element.34.upstream, bf16[3456,128]{1,0:T(8,128)(2,1)S(1)} %get-tuple-element.24.weight), custom_call_target="tpu_custom_call" | custom-call | tf_op jit(solution)/shard_map/pallas_call | solution.py:308
  30.8 1.1 %collective-permute-done.9.refs_2_ = bf16[432,128]{1,0:T(8,128)(2,1)S(1)} collective-permute-done((bf16[432,128]{1,0:T(8,128)(2,1)S(1)}, bf16[432,128]{1,0:T(8,128)(2,1)S(1)}, u32[]{:S(2)}, u32[]{:S(2)}) %collective-permute-start.9) | collective-permute-done | bytes 110624 | tf_op jit(solution)/shard_map/ppermute | solution.py:41
  31.9 1.7 %collective-permute-done.7.refs_1_ = bf16[432,128]{1,0:T(8,128)(2,1)S(1)} collective-permute-done((bf16[432,128]{1,0:T(8,128)(2,1)S(1)}, bf16[432,128]{1,0:T(8,128)(2,1)S(1)}, u32[]{:S(2)}, u32[]{:S(2)}) %collective-permute-start.7) | collective-permute-done | bytes 110624 | tf_op jit(solution)/shard_map/ppermute | solution.py:41
  33.6 0.5 collective-permute-done.11.refs_3_
  34.0 0.1 shard_map.58.mine
  34.1 1.9 %collective-permute-start.12 = (bf16[432,128]{1,0:T(8,128)(2,1)S(1)}, bf16[432,128]{1,0:T(8,128)(2,1)S(1)}, u32[]{:S(2)}, u32[]{:S(2)}) collective-permute-start(bf16[432,128]{1,0:T(8,128)(2,1)S(1)} %shard_map.58.mine), channel_id=1, source_target_pairs={{0,9},{1,8},{2,11},{3,10},{4,13},{5,12},{6,15},{7,14},{8,1},{9,0},... | collective-permute-start | bytes 331784 | tf_op jit(solution)/shard_map/ppermute | solution.py:41
  36.0 3.7 %collective-permute-done.12.other = bf16[432,128]{1,0:T(8,128)(2,1)S(1)} collective-permute-done((bf16[432,128]{1,0:T(8,128)(2,1)S(1)}, bf16[432,128]{1,0:T(8,128)(2,1)S(1)}, u32[]{:S(2)}, u32[]{:S(2)}) %collective-permute-start.12) | collective-permute-done | bytes 110624 | tf_op jit(solution)/shard_map/ppermute | solution.py:41
  39.7 4.0 %collective-permute-start.15 = (bf16[432,128]{1,0:T(8,128)(2,1)S(1)}, bf16[432,128]{1,0:T(8,128)(2,1)S(1)}, u32[]{:S(2)}, u32[]{:S(2)}) collective-permute-start(bf16[432,128]{1,0:T(8,128)(2,1)S(1)} %shard_map.59.refs_0_.refs_4_), channel_id=1, source_target_pairs={{0,6},{1,7},{2,4},{3,5},{4,2},{5,3},{6,0},{7,1},{8,14},{9,15},{10,... | collective-permute-start | bytes 331784 | tf_op jit(solution)/shard_map/ppermute | solution.py:41
  43.8 0.9 %collective-permute-start.14 = (bf16[432,128]{1,0:T(8,128)(2,1)S(1)}, bf16[432,128]{1,0:T(8,128)(2,1)S(1)}, u32[]{:S(2)}, u32[]{:S(2)}) collective-permute-start(bf16[432,128]{1,0:T(8,128)(2,1)S(1)} %shard_map.59.refs_0_.refs_4_), channel_id=1, source_target_pairs={{0,2},{1,3},{2,0},{3,1},{4,6},{5,7},{6,4},{7,5},{8,10},{9,11},{10,... | collective-permute-start | bytes 331784 | tf_op jit(solution)/shard_map/ppermute | solution.py:41
  44.7 0.9 %collective-permute-start.13 = (bf16[432,128]{1,0:T(8,128)(2,1)S(1)}, bf16[432,128]{1,0:T(8,128)(2,1)S(1)}, u32[]{:S(2)}, u32[]{:S(2)}) collective-permute-start(bf16[432,128]{1,0:T(8,128)(2,1)S(1)} %shard_map.59.refs_0_.refs_4_), channel_id=1, source_target_pairs={{0,4},{1,5},{2,6},{3,7},{4,0},{5,1},{6,2},{7,3},{8,12},{9,13},{10,... | collective-permute-start | bytes 331784 | tf_op jit(solution)/shard_map/ppermute | solution.py:41
  45.7 0.0 collective-permute-start.16
  45.7 1.5 %collective-permute-done.15.refs_3_.refs_7_ = bf16[432,128]{1,0:T(8,128)(2,1)S(1)} collective-permute-done((bf16[432,128]{1,0:T(8,128)(2,1)S(1)}, bf16[432,128]{1,0:T(8,128)(2,1)S(1)}, u32[]{:S(2)}, u32[]{:S(2)}) %collective-permute-start.15) | collective-permute-done | bytes 110624 | tf_op jit(solution)/shard_map/ppermute | solution.py:41
  47.2 0.4 collective-permute-start.19
  47.6 2.4 %collective-permute-done.14.refs_2_.refs_6_ = bf16[432,128]{1,0:T(8,128)(2,1)S(1)} collective-permute-done((bf16[432,128]{1,0:T(8,128)(2,1)S(1)}, bf16[432,128]{1,0:T(8,128)(2,1)S(1)}, u32[]{:S(2)}, u32[]{:S(2)}) %collective-permute-start.14) | collective-permute-done | bytes 110624 | tf_op jit(solution)/shard_map/ppermute | solution.py:41
  50.1 0.0 collective-permute-start.18
  50.1 1.1 %collective-permute-done.13.refs_1_.refs_5_ = bf16[432,128]{1,0:T(8,128)(2,1)S(1)} collective-permute-done((bf16[432,128]{1,0:T(8,128)(2,1)S(1)}, bf16[432,128]{1,0:T(8,128)(2,1)S(1)}, u32[]{:S(2)}, u32[]{:S(2)}) %collective-permute-start.13) | collective-permute-done | bytes 110624 | tf_op jit(solution)/shard_map/ppermute | solution.py:41
  51.1 0.0 collective-permute-start.17
  51.1 0.1 shard_map.60.refs_0_
  51.3 1.2 %collective-permute-start.21 = (f32[8,128]{1,0:T(8,128)S(1)}, f32[8,128]{1,0:T(8,128)S(1)}, u32[]{:S(2)}, u32[]{:S(2)}) collective-permute-start(f32[8,128]{1,0:T(8,128)S(1)} %shard_map.60.refs_0_), channel_id=1, source_target_pairs={{0,17},{1,16},{2,19},{3,18},{4,21},{5,20},{6,23},{7,22},{8,25},{9,... | collective-permute-start | bytes 12296 | tf_op jit(solution)/shard_map/ppermute | solution.py:53
  52.5 0.0 collective-permute-done.16.refs_0_.refs_8_
  52.5 1.0 %collective-permute-start.20 = (f32[8,128]{1,0:T(8,128)S(1)}, f32[8,128]{1,0:T(8,128)S(1)}, u32[]{:S(2)}, u32[]{:S(2)}) collective-permute-start(f32[8,128]{1,0:T(8,128)S(1)} %shard_map.60.refs_0_), channel_id=1, source_target_pairs={{0,16},{1,17},{2,18},{3,19},{4,20},{5,21},{6,22},{7,23},{8,24},{9,... | collective-permute-start | bytes 12296 | tf_op jit(solution)/shard_map/ppermute | solution.py:53
  53.5 0.0 collective-permute-done.19.refs_3_.refs_11_
  53.5 0.0 collective-permute-done.18.refs_2_.refs_10_
  53.5 0.0 collective-permute-done.17.refs_1_.refs_9_
  53.5 0.1 shard_map.61.refs_1_
  53.6 0.8 %collective-permute-done.21.refs_3_ = f32[8,128]{1,0:T(8,128)S(1)} collective-permute-done((f32[8,128]{1,0:T(8,128)S(1)}, f32[8,128]{1,0:T(8,128)S(1)}, u32[]{:S(2)}, u32[]{:S(2)}) %collective-permute-start.21) | collective-permute-done | bytes 4128 | tf_op jit(solution)/shard_map/ppermute | solution.py:53
  54.4 1.7 %collective-permute-done.20.refs_2_ = f32[8,128]{1,0:T(8,128)S(1)} collective-permute-done((f32[8,128]{1,0:T(8,128)S(1)}, f32[8,128]{1,0:T(8,128)S(1)}, u32[]{:S(2)}, u32[]{:S(2)}) %collective-permute-start.20) | collective-permute-done | bytes 4128 | tf_op jit(solution)/shard_map/ppermute | solution.py:53
  56.1 1.4 %shard_map.62 = f32[8,432,128]{2,1,0:T(8,128)} custom-call(s32[1]{0:T(128)} %bitcast.spot, f32[8,128]{1,0:T(8,128)S(1)} %shard_map.60.refs_0_, f32[8,128]{1,0:T(8,128)S(1)} %shard_map.61.refs_1_, f32[8,128]{1,0:T(8,128)S(1)} %collective-permute-done.20.refs_2_, f32[8,128]{1,0:T(8,128)S(1)} %collective-permute-done.21.refs_3_, ...), custom_call_target="tpu_custom_call" | custom-call | tf_op jit(solution)/shard_map/pallas_call | solution.py:430
  (9 shorter events, 0.1 us)
Async XLA Ops:
  2.2 1.5 %collective-permute-start = (bf16[2,3,64,128]{3,2,1,0:T(8,128)(2,1)S(1)}, bf16[2,3,64,128]{3,2,1,0:T(8,128)(2,1)S(1)}, u32[]{:S(2)}, u32[]{:S(2)}) collective-permute-start(bf16[2,3,64,128]{3,2,1,0:T(8,128)(2,1)S(1)} %get-tuple-element.21), channel_id=1, source_target_pairs={{0,1},{1,0},{2,3},{3,2},{4,5},{5,4},{6,7},{7,6},{8,9},{9,8},{10,11... | collective-permute-start | bytes 294920 | tf_op jit(solution)/shard_map/ppermute | solution.py:26
  2.7 0.9 %collective-permute-start.1 = (bf16[2,3,64,128]{3,2,1,0:T(8,128)(2,1)S(1)}, bf16[2,3,64,128]{3,2,1,0:T(8,128)(2,1)S(1)}, u32[]{:S(2)}, u32[]{:S(2)}) collective-permute-start(bf16[2,3,64,128]{3,2,1,0:T(8,128)(2,1)S(1)} %get-tuple-element.22), channel_id=1, source_target_pairs={{1,2},{2,1},{3,4},{4,3},{5,6},{6,5},{7,8},{8,7},{9,10},{10,9},{11,... | collective-permute-start | bytes 294920 | tf_op jit(solution)/shard_map/ppermute | solution.py:26
  7.1 10.7 %collective-permute-start.2 = (bf16[2,4,64,128]{3,2,1,0:T(8,128)(2,1)S(1)}, bf16[2,4,64,128]{3,2,1,0:T(8,128)(2,1)S(1)}, u32[]{:S(2)}, u32[]{:S(2)}) collective-permute-start(bf16[2,4,64,128]{3,2,1,0:T(8,128)(2,1)S(1)} %get-tuple-element.25.after), channel_id=1, source_target_pairs={{0,16},{1,17},{2,18},{3,19},{4,20},{5,21},{6,22},{7,23},{8,24},{9,... | collective-permute-start | bytes 393224 | tf_op jit(solution)/shard_map/ppermute | solution.py:53
  10.0 7.7 %collective-permute-start.3 = (bf16[2,1,64,128]{3,2,1,0:T(8,128)(2,1)S(1)}, bf16[2,1,64,128]{3,2,1,0:T(8,128)(2,1)S(1)}, u32[]{:S(2)}, u32[]{:S(2)}) collective-permute-start(bf16[2,1,64,128]{3,2,1,0:T(8,128)(2,1)S(1)} %get-tuple-element.26), channel_id=1, source_target_pairs={{0,17},{1,16},{2,19},{3,18},{4,21},{5,20},{6,23},{7,22},{8,25},{9,... | collective-permute-start | bytes 98312 | tf_op jit(solution)/shard_map/ppermute | solution.py:53
  14.8 2.9 %collective-permute-start.4 = (bf16[2,1,64,128]{3,2,1,0:T(8,128)(2,1)S(1)}, bf16[2,1,64,128]{3,2,1,0:T(8,128)(2,1)S(1)}, u32[]{:S(2)}, u32[]{:S(2)}) collective-permute-start(bf16[2,1,64,128]{3,2,1,0:T(8,128)(2,1)S(1)} %get-tuple-element.27), channel_id=1, source_target_pairs={{1,18},{2,17},{3,20},{4,19},{5,22},{6,21},{7,24},{8,23},{9,26},{10... | collective-permute-start | bytes 98312 | tf_op jit(solution)/shard_map/ppermute | solution.py:36
  19.0 5.2 %collective-permute-start.8 = (bf16[432,128]{1,0:T(8,128)(2,1)S(1)}, bf16[432,128]{1,0:T(8,128)(2,1)S(1)}, u32[]{:S(2)}, u32[]{:S(2)}) collective-permute-start(bf16[432,128]{1,0:T(8,128)(2,1)S(1)} %get-tuple-element.32), channel_id=1, source_target_pairs={{0,1},{1,0},{2,3},{3,2},{4,5},{5,4},{6,7},{7,6},{8,9},{9,8},{10,11... | collective-permute-start | bytes 331784 | tf_op jit(solution)/shard_map/ppermute | solution.py:41
  23.3 3.4 %collective-permute-start.6 = (bf16[432,128]{1,0:T(8,128)(2,1)S(1)}, bf16[432,128]{1,0:T(8,128)(2,1)S(1)}, u32[]{:S(2)}, u32[]{:S(2)}) collective-permute-start(bf16[432,128]{1,0:T(8,128)(2,1)S(1)} %get-tuple-element.31), channel_id=1, source_target_pairs={{0,1},{1,0},{2,3},{3,2},{4,5},{5,4},{6,7},{7,6},{8,9},{9,8},{10,11... | collective-permute-start | bytes 331784 | tf_op jit(solution)/shard_map/ppermute | solution.py:41
  23.3 5.6 %collective-permute-start.10 = (bf16[432,128]{1,0:T(8,128)(2,1)S(1)}, bf16[432,128]{1,0:T(8,128)(2,1)S(1)}, u32[]{:S(2)}, u32[]{:S(2)}) collective-permute-start(bf16[432,128]{1,0:T(8,128)(2,1)S(1)} %get-tuple-element.36), channel_id=1, source_target_pairs={{0,1},{1,0},{2,3},{3,2},{4,5},{5,4},{6,7},{7,6},{8,9},{9,8},{10,11... | collective-permute-start | bytes 331784 | tf_op jit(solution)/shard_map/ppermute | solution.py:41
  23.8 8.1 %collective-permute-start.5 = (bf16[432,128]{1,0:T(8,128)(2,1)S(1)}, bf16[432,128]{1,0:T(8,128)(2,1)S(1)}, u32[]{:S(2)}, u32[]{:S(2)}) collective-permute-start(bf16[432,128]{1,0:T(8,128)(2,1)S(1)} %get-tuple-element.30), channel_id=1, source_target_pairs={{0,1},{1,0},{2,3},{3,2},{4,5},{5,4},{6,7},{7,6},{8,9},{9,8},{10,11... | collective-permute-start | bytes 331784 | tf_op jit(solution)/shard_map/ppermute | solution.py:41
  24.2 7.6 %collective-permute-start.9 = (bf16[432,128]{1,0:T(8,128)(2,1)S(1)}, bf16[432,128]{1,0:T(8,128)(2,1)S(1)}, u32[]{:S(2)}, u32[]{:S(2)}) collective-permute-start(bf16[432,128]{1,0:T(8,128)(2,1)S(1)} %shard_map.55), channel_id=1, source_target_pairs={{0,2},{1,3},{2,0},{3,1},{4,6},{5,7},{6,4},{7,5},{8,10},{9,11},{10,... | collective-permute-start | bytes 331784 | tf_op jit(solution)/shard_map/ppermute | solution.py:41
  26.7 6.9 %collective-permute-start.7 = (bf16[432,128]{1,0:T(8,128)(2,1)S(1)}, bf16[432,128]{1,0:T(8,128)(2,1)S(1)}, u32[]{:S(2)}, u32[]{:S(2)}) collective-permute-start(bf16[432,128]{1,0:T(8,128)(2,1)S(1)} %shard_map.54), channel_id=1, source_target_pairs={{0,6},{1,7},{2,4},{3,5},{4,2},{5,3},{6,0},{7,1},{8,14},{9,15},{10,... | collective-permute-start | bytes 331784 | tf_op jit(solution)/shard_map/ppermute | solution.py:41
  29.0 5.1 %collective-permute-start.11 = (bf16[432,128]{1,0:T(8,128)(2,1)S(1)}, bf16[432,128]{1,0:T(8,128)(2,1)S(1)}, u32[]{:S(2)}, u32[]{:S(2)}) collective-permute-start(bf16[432,128]{1,0:T(8,128)(2,1)S(1)} %shard_map.57), channel_id=1, source_target_pairs={{0,4},{1,5},{2,6},{3,7},{4,0},{5,1},{6,2},{7,3},{8,12},{9,13},{10,... | collective-permute-start | bytes 331784 | tf_op jit(solution)/shard_map/ppermute | solution.py:41
  34.1 5.6 %collective-permute-start.12 = (bf16[432,128]{1,0:T(8,128)(2,1)S(1)}, bf16[432,128]{1,0:T(8,128)(2,1)S(1)}, u32[]{:S(2)}, u32[]{:S(2)}) collective-permute-start(bf16[432,128]{1,0:T(8,128)(2,1)S(1)} %shard_map.58.mine), channel_id=1, source_target_pairs={{0,9},{1,8},{2,11},{3,10},{4,13},{5,12},{6,15},{7,14},{8,1},{9,0},... | collective-permute-start | bytes 331784 | tf_op jit(solution)/shard_map/ppermute | solution.py:41
  39.7 7.4 %collective-permute-start.15 = (bf16[432,128]{1,0:T(8,128)(2,1)S(1)}, bf16[432,128]{1,0:T(8,128)(2,1)S(1)}, u32[]{:S(2)}, u32[]{:S(2)}) collective-permute-start(bf16[432,128]{1,0:T(8,128)(2,1)S(1)} %shard_map.59.refs_0_.refs_4_), channel_id=1, source_target_pairs={{0,6},{1,7},{2,4},{3,5},{4,2},{5,3},{6,0},{7,1},{8,14},{9,15},{10,... | collective-permute-start | bytes 331784 | tf_op jit(solution)/shard_map/ppermute | solution.py:41
  43.8 6.3 %collective-permute-start.14 = (bf16[432,128]{1,0:T(8,128)(2,1)S(1)}, bf16[432,128]{1,0:T(8,128)(2,1)S(1)}, u32[]{:S(2)}, u32[]{:S(2)}) collective-permute-start(bf16[432,128]{1,0:T(8,128)(2,1)S(1)} %shard_map.59.refs_0_.refs_4_), channel_id=1, source_target_pairs={{0,2},{1,3},{2,0},{3,1},{4,6},{5,7},{6,4},{7,5},{8,10},{9,11},{10,... | collective-permute-start | bytes 331784 | tf_op jit(solution)/shard_map/ppermute | solution.py:41
  44.7 6.4 %collective-permute-start.13 = (bf16[432,128]{1,0:T(8,128)(2,1)S(1)}, bf16[432,128]{1,0:T(8,128)(2,1)S(1)}, u32[]{:S(2)}, u32[]{:S(2)}) collective-permute-start(bf16[432,128]{1,0:T(8,128)(2,1)S(1)} %shard_map.59.refs_0_.refs_4_), channel_id=1, source_target_pairs={{0,4},{1,5},{2,6},{3,7},{4,0},{5,1},{6,2},{7,3},{8,12},{9,13},{10,... | collective-permute-start | bytes 331784 | tf_op jit(solution)/shard_map/ppermute | solution.py:41
  45.7 6.8 %collective-permute-start.16 = (bf16[432,128]{1,0:T(8,128)(2,1)S(1)}, bf16[432,128]{1,0:T(8,128)(2,1)S(1)}, u32[]{:S(2)}, u32[]{:S(2)}) collective-permute-start(bf16[432,128]{1,0:T(8,128)(2,1)S(1)} %shard_map.59.refs_0_.refs_4_), channel_id=1, source_target_pairs={{0,1},{1,0},{2,3},{3,2},{4,5},{5,4},{6,7},{7,6},{8,9},{9,8},{10,11... | collective-permute-start | bytes 331784 | tf_op jit(solution)/shard_map/ppermute | solution.py:41
  47.2 6.3 %collective-permute-start.19 = (bf16[432,128]{1,0:T(8,128)(2,1)S(1)}, bf16[432,128]{1,0:T(8,128)(2,1)S(1)}, u32[]{:S(2)}, u32[]{:S(2)}) collective-permute-start(bf16[432,128]{1,0:T(8,128)(2,1)S(1)} %collective-permute-done.15.refs_3_.refs_7_), channel_id=1, source_target_pairs={{0,1},{1,0},{2,3},{3,2},{4,5},{5,4},{6,7},{7,6},{8,9},{9,8},{10,11... | collective-permute-start | bytes 331784 | tf_op jit(solution)/shard_map/ppermute | solution.py:41
  50.1 3.4 %collective-permute-start.18 = (bf16[432,128]{1,0:T(8,128)(2,1)S(1)}, bf16[432,128]{1,0:T(8,128)(2,1)S(1)}, u32[]{:S(2)}, u32[]{:S(2)}) collective-permute-start(bf16[432,128]{1,0:T(8,128)(2,1)S(1)} %collective-permute-done.14.refs_2_.refs_6_), channel_id=1, source_target_pairs={{0,1},{1,0},{2,3},{3,2},{4,5},{5,4},{6,7},{7,6},{8,9},{9,8},{10,11... | collective-permute-start | bytes 331784 | tf_op jit(solution)/shard_map/ppermute | solution.py:41
  51.1 2.3 %collective-permute-start.17 = (bf16[432,128]{1,0:T(8,128)(2,1)S(1)}, bf16[432,128]{1,0:T(8,128)(2,1)S(1)}, u32[]{:S(2)}, u32[]{:S(2)}) collective-permute-start(bf16[432,128]{1,0:T(8,128)(2,1)S(1)} %collective-permute-done.13.refs_1_.refs_5_), channel_id=1, source_target_pairs={{0,1},{1,0},{2,3},{3,2},{4,5},{5,4},{6,7},{7,6},{8,9},{9,8},{10,11... | collective-permute-start | bytes 331784 | tf_op jit(solution)/shard_map/ppermute | solution.py:41
  51.3 3.1 %collective-permute-start.21 = (f32[8,128]{1,0:T(8,128)S(1)}, f32[8,128]{1,0:T(8,128)S(1)}, u32[]{:S(2)}, u32[]{:S(2)}) collective-permute-start(f32[8,128]{1,0:T(8,128)S(1)} %shard_map.60.refs_0_), channel_id=1, source_target_pairs={{0,17},{1,16},{2,19},{3,18},{4,21},{5,20},{6,23},{7,22},{8,25},{9,... | collective-permute-start | bytes 12296 | tf_op jit(solution)/shard_map/ppermute | solution.py:53
  52.5 3.6 %collective-permute-start.20 = (f32[8,128]{1,0:T(8,128)S(1)}, f32[8,128]{1,0:T(8,128)S(1)}, u32[]{:S(2)}, u32[]{:S(2)}) collective-permute-start(f32[8,128]{1,0:T(8,128)S(1)} %shard_map.60.refs_0_), channel_id=1, source_target_pairs={{0,16},{1,17},{2,18},{3,19},{4,20},{5,21},{6,22},{7,23},{8,24},{9,... | collective-permute-start | bytes 12296 | tf_op jit(solution)/shard_map/ppermute | solution.py:53

commit v7 on v6

--- a/solution.py
+++ b/solution.py
@@ -79,25 +79,20 @@
             ).astype(BF16)
 
 
-def back_product(shifts, weight_ref, rows, cells):
-    channels = weight_ref.shape[1]
+def back_product(shifts, mirror, block, depth):
+    span = shifts.shape[1]
     total = None
     for dz in range(3):
-        mirrored = [26 - 9 * dz - j for j in range(9)]
-        side = jnp.concatenate(
-            [weight_ref[k * channels : (k + 1) * channels, :] for k in mirrored], axis=1
-        )
-        term = lax.dot_general(
-            shifts[dz * cells : dz * cells + rows, :],
-            side,
-            (((1,), (1,)), ((), ())),
+        term = jnp.dot(
+            shifts[dz * block : (dz + depth) * block, :],
+            mirror[dz * span : (dz + 1) * span, :],
             preferred_element_type=F32,
         )
         total = term if total is None else total + term
     return total
 
 
-def rim_kernel(acts, grad, weight, near, far, acts_here, grad_here, weight_here, sems, loads):
+def rim_kernel(acts, grad, near, far, acts_here, grad_here, sems, loads):
     micro, depth = acts.shape[:2]
     top = 1 - lax.rem(lax.axis_index("slab"), 2)
     copies = []
@@ -111,9 +106,7 @@
                         sems.at[which, m, part],
                     )
                 )
-    for n, (source, out) in enumerate(
-        ((acts, acts_here), (grad, grad_here), (weight, weight_here))
-    ):
+    for n, (source, out) in enumerate(((acts, acts_here), (grad, grad_here))):
         copies.append(pltpu.make_async_copy(source, out, loads.at[n]))
     for copy in copies:
         copy.start()
@@ -121,43 +114,78 @@
         copy.wait()
 
 
+def own_kernel(height, acts, stored, weight, mirror, part, own, sem):
+    micro, depth, cells, channels = acts.shape
+    block, span = micro * cells, 9 * channels
+    copy = pltpu.make_async_copy(stored, weight, sem)
+    copy.start()
+    for n in range(depth):
+        for m in range(micro):
+            write_shifts(acts[m, n], height, own, n * block + m * cells)
+    copy.wait()
+    part[...] = jnp.zeros(part.shape, F32)
+    for dz in range(3):
+        rows = slice((2 - dz) * block, (2 - dz + depth) * block)
+        part[rows, :] += jnp.dot(
+            own[...], weight[dz * span : (dz + 1) * span, :], preferred_element_type=F32
+        )
+    for k in range(27):
+        mirror[(26 - k) * channels : (27 - k) * channels, :] = weight[
+            k * channels : (k + 1) * channels, :
+        ].T
+
+
 def first_kernel(
-    height, acts, near, far, grad, weight, result, to_near, to_far, slopes, shifts, deltas
+    height, near, far, grad, weight, mirror, part, result, to_near, to_far, slopes, rim, shifts
 ):
-    micro, depth, cells, channels = acts.shape
+    micro, depth, cells, channels = grad.shape
     even = lax.rem(lax.axis_index("slab"), 2) == 0
-    span = 9 * channels
-    rows = depth * cells
-    for m in range(micro):
-
-        def rim(a, b, n):
-            return jnp.where(even, a[m, n].astype(F32), b[m, n].astype(F32))
-
-        planes = [rim(far, near, n) for n in range(2)]
-        planes += [acts[m, n] for n in range(depth)]
-        planes += [rim(near, far, n) for n in range(2)]
-        for n, plane in enumerate(planes):
-            write_shifts(plane, height, shifts.at[m], n * cells)
-        preact = None
-        for dz in range(3):
-            term = jnp.dot(
-                shifts[m, dz * cells : dz * cells + rows + 2 * cells, :],
-                weight[dz * span : (dz + 1) * span, :],
-                preferred_element_type=F32,
-            )
-            preact = term if preact is None else preact + term
+    block, span = micro * cells, 9 * channels
+
+    def pick(m, n, below):
+        a, b = near[m, n].astype(F32), far[m, n].astype(F32)
+        return jnp.where(even, b, a) if below else jnp.where(even, a, b)
+
+    for n in range(4):
+        for m in range(micro):
+            write_shifts(pick(m, n % 2, n < 2), height, rim, n * block + m * cells)
+    terms = [
+        jnp.dot(
+            rim[dz * block : (dz + 2) * block, :],
+            weight[dz * span : (dz + 1) * span, :],
+            preferred_element_type=F32,
+        )
+        for dz in range(3)
+    ]
+    head, tail = [term[:block] for term in terms], [term[block:] for term in terms]
+    extra = {0: [head[0], head[1]], 1: [tail[0]]}
+    extra.setdefault(depth, []).append(head[2])
+    extra.setdefault(depth + 1, []).extend([tail[1], tail[2]])
+    for n in range(depth + 2):
+        rows = slice(n * block, (n + 1) * block)
+        preact = part[rows, :]
+        for term in extra.get(n, []):
+            preact = preact + term
         sig = 1.0 / (1.0 + jnp.exp(-preact))
         slope = sig * (1.0 + preact * (1.0 - sig))
-        slopes[m] = slope
-        ups = [rim(far, near, 2)] + [grad[m, n].astype(F32) for n in range(depth)]
-        ups.append(rim(near, far, 2))
-        for n, up in enumerate(ups):
-            delta = (up * slope[n * cells : (n + 1) * cells]).astype(BF16)
-            write_shifts(delta, height, deltas.at[m], n * cells)
-        back = back_product(deltas.at[m], weight, rows, cells)
-        total = grad[m].reshape(rows, channels).astype(F32) + back
-        result[m] = total.astype(BF16).reshape(depth, cells, channels)
-        low, high = total[:cells], total[-cells:]
+        slopes[rows, :] = slope
+        for m in range(micro):
+            if n == 0 or n == depth + 1:
+                up = pick(m, 2, n == 0)
+            else:
+                up = grad[m, n - 1].astype(F32)
+            delta = (up * slope[m * cells : (m + 1) * cells]).astype(BF16)
+            write_shifts(delta, height, shifts, n * block + m * cells)
+    back = back_product(shifts, mirror, block, depth)
+    for m in range(micro):
+        ends = []
+        for n in range(depth):
+            first = n * block + m * cells
+            total = grad[m, n].astype(F32) + back[first : first + cells]
+            result[m, n] = total.astype(BF16)
+            if n in (0, depth - 1):
+                ends.append(total)
+        low, high = ends[0], ends[-1]
         to_near[m, 0] = jnp.where(even, high, low).astype(BF16)
         to_far[m, 0] = jnp.where(even, low, high).astype(BF16)
 
@@ -170,7 +198,7 @@
         above = jnp.where(even, near[m, 0].astype(F32), far[m, 0].astype(F32))
         planes = [below] + [acts[m, n] for n in range(depth)] + [above]
         for n, plane in enumerate(planes):
-            write_shifts(plane, height, shifts.at[m], n * cells)
+            write_shifts(plane, height, shifts, (n * micro + m) * cells)
 
 
 def raw_kernel(
@@ -178,28 +206,27 @@
 ):
     sends, (keep, raw) = refs[:4], refs[4:]
     micro, depth, cells, channels = upstream.shape
-    rows = depth * cells
-    span = 9 * channels
+    block, span = micro * cells, 9 * channels
     last = lax.axis_index("segment") == lax.axis_size("segment") - 1
     even = lax.rem(lax.axis_index("slab"), 2) == 0
-    deltas_of = []
     for m in range(micro):
-        up = jnp.where(last, grad[m].astype(F32), incoming[m].astype(F32))
-        upstream[m] = up.astype(BF16)
         by_near = jnp.where(last, near[m, 2].astype(F32), in_near[m, 0].astype(F32))
         by_far = jnp.where(last, far[m, 2].astype(F32), in_far[m, 0].astype(F32))
-        below, above = jnp.where(even, by_far, by_near), jnp.where(even, by_near, by_far)
-        delta = (up.reshape(rows, channels) * slopes[m, cells : cells + rows]).astype(BF16)
-        deltas[m, :cells] = (below * slopes[m, :cells]).astype(BF16)
-        deltas[m, cells : cells + rows] = delta
-        deltas[m, cells + rows :] = (above * slopes[m, cells + rows :]).astype(BF16)
-        deltas_of.append(delta)
+        planes = [jnp.where(even, by_far, by_near)]
+        for n in range(depth):
+            up = jnp.where(last, grad[m, n].astype(F32), incoming[m, n].astype(F32))
+            upstream[m, n] = up.astype(BF16)
+            planes.append(up)
+        planes.append(jnp.where(even, by_near, by_far))
+        for n, up in enumerate(planes):
+            rows = slice(n * block + m * cells, n * block + (m + 1) * cells)
+            deltas[rows, :] = (up * slopes[rows, :]).astype(BF16)
     for dz in range(3):
         total = None
-        for m in range(micro):
+        for n in range(depth):
             term = lax.dot_general(
-                shifts[m, dz * cells : dz * cells + rows, :],
-                deltas_of[m],
+                shifts[(dz + n) * block : (dz + n + 1) * block, :],
+                deltas[(n + 1) * block : (n + 2) * block, :],
                 (((0,), (0,)), ((), ())),
                 preferred_element_type=F32,
             )
@@ -238,16 +265,19 @@
     refs[-1][...] = jnp.broadcast_to(sums[0], refs[-1].shape)
 
 
-def back_kernel(height, deltas, upstream, weight, out, shifts):
+def back_kernel(height, deltas, upstream, mirror, out, shifts):
     micro, depth, cells, channels = upstream.shape
-    rows = depth * cells
+    block = micro * cells
+    for n in range(depth + 2):
+        for m in range(micro):
+            rows = slice(n * block + m * cells, n * block + (m + 1) * cells)
+            write_shifts(deltas[rows, :], height, shifts, rows.start)
+    back = back_product(shifts, mirror, block, depth)
     for m in range(micro):
-        for n in range(depth + 2):
-            plane = deltas[m, n * cells : (n + 1) * cells, :]
-            write_shifts(plane, height, shifts.at[m], n * cells)
-        back = back_product(shifts.at[m], weight, rows, cells)
-        total = upstream[m].reshape(rows, channels).astype(F32) + back
-        out[m] = total.astype(BF16).reshape(depth, cells, channels)
+        for n in range(depth):
+            first = n * block + m * cells
+            total = upstream[m, n].astype(F32) + back[first : first + cells]
+            out[m, n] = total.astype(BF16)
 
 
 def place_kernel(bound, count, spot, *refs):
@@ -283,26 +313,43 @@
     shape = jax.ShapeDtypeStruct
     rim = shape((micro, 3, cells, channels), BF16)
     volume = shape((micro, depth, cells, channels), BF16)
-    to_near, to_far, acts, grad, weight = pl.pallas_call(
+    to_near, to_far, acts, grad = pl.pallas_call(
         rim_kernel,
-        out_shape=(rim, rim, volume, volume, shape(weight.shape, BF16)),
-        in_specs=[HBM, HBM, HBM],
-        out_specs=(VMEM,) * 5,
-        scratch_shapes=[pltpu.SemaphoreType.DMA((2, micro, 2)), pltpu.SemaphoreType.DMA((3,))],
+        out_shape=(rim, rim, volume, volume),
+        in_specs=[HBM, HBM],
+        out_specs=(VMEM,) * 4,
+        scratch_shapes=[pltpu.SemaphoreType.DMA((2, micro, 2)), pltpu.SemaphoreType.DMA((2,))],
         compiler_params=small,
-    )(*(pltpu.with_memory_space_constraint(a, pltpu.HBM) for a in (acts, grad, weight)))
+    )(*(pltpu.with_memory_space_constraint(a, pltpu.HBM) for a in (acts, grad)))
     near, far = swap(to_near, to_far)
 
+    plane, span = micro * cells, 9 * channels
+    whole = shape(weight.shape, BF16)
+    outer = shape(((depth + 2) * plane, channels), F32)
+    weight, mirror, part = pl.pallas_call(
+        functools.partial(own_kernel, height),
+        out_shape=(whole, whole, outer),
+        in_specs=[VMEM, HBM],
+        out_specs=(VMEM,) * 3,
+        scratch_shapes=[pltpu.VMEM((depth * plane, span), BF16), pltpu.SemaphoreType.DMA],
+        compiler_params=large,
+    )(acts, pltpu.with_memory_space_constraint(weight, pltpu.HBM))
+
     edge = shape((micro, 1, cells, channels), BF16)
-    wide = pltpu.VMEM((micro, rows + 2 * cells, 9 * channels), BF16)
+    wide = pltpu.VMEM(((depth + 2) * plane, span), BF16)
     result, to_near, to_far, slopes = pl.pallas_call(
         functools.partial(first_kernel, height),
-        out_shape=(volume, edge, edge, shape((micro, rows + 2 * cells, channels), F32)),
-        in_specs=[VMEM] * 5,
+        out_shape=(
+            volume,
+            edge,
+            edge,
+            outer,
+        ),
+        in_specs=[VMEM] * 6,
         out_specs=(VMEM,) * 4,
-        scratch_shapes=[pltpu.VMEM((micro, rows + 4 * cells, 9 * channels), BF16), wide],
+        scratch_shapes=[pltpu.VMEM((4 * plane, span), BF16), wide],
         compiler_params=large,
-    )(acts, near, far, grad, weight)
+    )(near, far, grad, weight, mirror, part)
 
     def conv_back(deltas, upstream):
         return pl.pallas_call(
@@ -312,7 +359,7 @@
             out_specs=VMEM,
             scratch_shapes=[wide],
             compiler_params=large,
-        )(deltas, upstream, weight)
+        )(deltas, upstream, mirror)
 
     even = lax.rem(index, 2) == 0
     for step in range(1, segments - 1):
@@ -322,19 +369,18 @@
         by_far = jnp.where(last, far[:, 2:], in_far)
         below, above = jnp.where(even, by_far, by_near), jnp.where(even, by_near, by_far)
         around = jnp.concatenate([below, upstream, above], axis=1)
-        around = around.reshape(slopes.shape).astype(F32)
+        around = jnp.swapaxes(around, 0, 1).reshape(outer.shape).astype(F32)
         result = conv_back((around * slopes).astype(BF16), upstream)
         low, high = result[:, :1], result[:, -1:]
         to_near, to_far = jnp.where(even, high, low), jnp.where(even, low, high)
     incoming, in_near, in_far = cross(result, 1, 0), cross(to_near, 1, 1), cross_far(to_far)
     shifts = pl.pallas_call(
         functools.partial(shift_kernel, height),
-        out_shape=shape((micro, rows + 2 * cells, 9 * channels), BF16),
+        out_shape=shape(((depth + 2) * plane, span), BF16),
         in_specs=[VMEM] * 4,
         out_specs=VMEM,
         compiler_params=large,
     )(acts, near, far, result)
-
     bits = [1 << n for n in range(1, count.bit_length() - 1)]
     inner = [bits[n : n + 2] for n in range(2, len(bits), 2)]
     crossing = inner[-1][0] if len(inner[-1]) == 1 else 0
@@ -347,7 +393,7 @@
 
     upstream, deltas, *rest = pl.pallas_call(
         raw_kernel,
-        out_shape=(volume, shape(slopes.shape, BF16))
+        out_shape=(volume, shape(outer.shape, BF16))
         + (piece,) * 4
         + (shape((4, part, channels), F32),),
         in_specs=[SMEM] + [VMEM] * 8,

time: 57.6 us -> 55.7 us (0.967)
  starting transfers between devices: 29.6 us -> 27.6 us
    ppermute x4, starting transfers between devices: 9.92 us -> 7.92 us  [cross(): return lax.ppermute(value, ('segment', 'slab'), route)]
    pallas_call x2 -> x3, Pallas kernels: 2.79 us -> 4.68 us  [the longest x1 2.25 us: shards(): pl.pallas_call(functools.partial(own_kernel, height), out_shape=(whole, w...]
    pallas_call x1, Pallas kernels: 3.43 us -> 1.86 us  [shards(): pl.pallas_call(functools.partial(first_kernel, height), out_shape=(volume...]
  transfers between devices with their start and end apart: 22 -> 22, of which waited for: 12 -> 11; matrix products, arithmetic and copies ran while one was open for 0% -> 0% of each run, Pallas kernels for 4% -> 8%
where the time goes in v7:
time: 55.7 us; the launch traced here: 55.5 us
  starting transfers between devices  27.6 us (50%)
  waiting for transfers between devices  16.8 us (30%)
  Pallas kernels  10.4 us (19%)
  between operations  0.77 us (1%)
    ppermute x15, starting transfers between devices, exchange(): return lax.ppermute(value, 'slab', [(i, i ^ mask) for i in range(count)])  17.9 us
    ppermute x15, waiting for transfers between devices, exchange(): return lax.ppermute(value, 'slab', [(i, i ^ mask) for i in range(count)])  12.3 us
    ppermute x4, starting transfers between devices, cross(): return lax.ppermute(value, ('segment', 'slab'), route)  7.92 us
    ppermute x4, waiting for transfers between devices, cross(): return lax.ppermute(value, ('segment', 'slab'), route)  4.49 us
    pallas_call x1, Pallas kernels, shards(): pl.pallas_call(functools.partial(own_kernel, height), out_shape=(whole, w...  2.25 us
    pallas_call x1, Pallas kernels, shards(): pl.pallas_call(functools.partial(first_kernel, height), out_shape=(volume...  1.86 us
    pallas_call x1, Pallas kernels, conv_back(): pl.pallas_call(functools.partial(back_kernel, height), out_shape=volume,...  1.79 us
    pallas_call x1, Pallas kernels, shards(): pl.pallas_call(functools.partial(place_kernel, bound, segments), out_shap...  1.38 us
  transfers between devices with their start and end apart: 22, of which 11 were waited for; matrix products, arithmetic and copies ran while one was open for 0% of the time, Pallas kernels for 8%

profile of v7, /device:TPU:0, one launch (start us, length us, event | category | flops | bytes accessed | tf_op | source)
XLA Modules:
  0.0 55.5 jit_solution(6007734504171989445)
XLA Ops:
  0.6 1.2 %shard_map.50 = (bf16[2,3,64,128]{3,2,1,0:T(8,128)(2,1)S(1)}, bf16[2,3,64,128]{3,2,1,0:T(8,128)(2,1)S(1)}, bf16[2,4,64,128]{3,2,1,0:T(8,128)(2,1)S(1)}, bf16[2,4,64,128]{3,2,1,0:T(8,128)(2,1)S(1)}) custom-call(bf16[2,4,64,128]{3,2,1,0:T(8,128)(2,1)} %bitcast.8, bf16[2,4,64,128]{3,2,1,0:T(8,128)(2,1)} %bitcast.9), custom_call_target="tpu_custom_call" | custom-call | tf_op jit(solution)/shard_map/pallas_call | solution.py:316
  1.8 0.5 collective-permute-start
  2.4 0.7 %collective-permute-start.1 = (bf16[2,3,64,128]{3,2,1,0:T(8,128)(2,1)S(1)}, bf16[2,3,64,128]{3,2,1,0:T(8,128)(2,1)S(1)}, u32[]{:S(2)}, u32[]{:S(2)}) collective-permute-start(bf16[2,3,64,128]{3,2,1,0:T(8,128)(2,1)S(1)} %get-tuple-element.23), channel_id=1, source_target_pairs={{1,2},{2,1},{3,4},{4,3},{5,6},{6,5},{7,8},{8,7},{9,10},{10,9},{11,... | collective-permute-start | bytes 294920 | tf_op jit(solution)/shard_map/ppermute | solution.py:26
  3.0 2.3 %shard_map.51 = (bf16[3456,128]{1,0:T(8,128)(2,1)S(1)}, bf16[3456,128]{1,0:T(8,128)(2,1)S(1)}, f32[768,128]{1,0:T(8,128)S(1)}) custom-call(bf16[2,4,64,128]{3,2,1,0:T(8,128)(2,1)S(1)} %get-tuple-element.25.acts, bf16[3456,128]{1,0:T(8,128)(2,1)} %bitcast.7), custom_call_target="tpu_custom_call" | custom-call | tf_op jit(solution)/shard_map/pallas_call | solution.py:329
  5.3 0.0 collective-permute-done.near
  5.3 1.9 %shard_map.52 = (bf16[2,4,64,128]{3,2,1,0:T(8,128)(2,1)S(1)}, bf16[2,1,64,128]{3,2,1,0:T(8,128)(2,1)S(1)}, bf16[2,1,64,128]{3,2,1,0:T(8,128)(2,1)S(1)}, f32[768,128]{1,0:T(8,128)S(1)}) custom-call(bf16[2,3,64,128]{3,2,1,0:T(8,128)(2,1)S(1)} %collective-permute-done.near, bf16[2,3,64,128]{3,2,1,0:T(8,128)(2,1)S(1)} %collective-permute-done.1.far, ...), custom_call_target="tpu_custom_call" | custom-call | tf_op jit(solution)/shard_map/pallas_call | solution.py:340
  7.2 2.6 %collective-permute-start.2 = (bf16[2,4,64,128]{3,2,1,0:T(8,128)(2,1)S(1)}, bf16[2,4,64,128]{3,2,1,0:T(8,128)(2,1)S(1)}, u32[]{:S(2)}, u32[]{:S(2)}) collective-permute-start(bf16[2,4,64,128]{3,2,1,0:T(8,128)(2,1)S(1)} %get-tuple-element.29.after), channel_id=1, source_target_pairs={{0,16},{1,17},{2,18},{3,19},{4,20},{5,21},{6,22},{7,23},{8,24},{9,... | collective-permute-start | bytes 393224 | tf_op jit(solution)/shard_map/ppermute | solution.py:53
  9.7 3.1 %collective-permute-start.3 = (bf16[2,1,64,128]{3,2,1,0:T(8,128)(2,1)S(1)}, bf16[2,1,64,128]{3,2,1,0:T(8,128)(2,1)S(1)}, u32[]{:S(2)}, u32[]{:S(2)}) collective-permute-start(bf16[2,1,64,128]{3,2,1,0:T(8,128)(2,1)S(1)} %get-tuple-element.30), channel_id=1, source_target_pairs={{0,17},{1,16},{2,19},{3,18},{4,21},{5,20},{6,23},{7,22},{8,25},{9,... | collective-permute-start | bytes 98312 | tf_op jit(solution)/shard_map/ppermute | solution.py:53
  12.9 0.7 %collective-permute-start.4 = (bf16[2,1,64,128]{3,2,1,0:T(8,128)(2,1)S(1)}, bf16[2,1,64,128]{3,2,1,0:T(8,128)(2,1)S(1)}, u32[]{:S(2)}, u32[]{:S(2)}) collective-permute-start(bf16[2,1,64,128]{3,2,1,0:T(8,128)(2,1)S(1)} %get-tuple-element.31), channel_id=1, source_target_pairs={{1,18},{2,17},{3,20},{4,19},{5,22},{6,21},{7,24},{8,23},{9,26},{10... | collective-permute-start | bytes 98312 | tf_op jit(solution)/shard_map/ppermute | solution.py:36
  13.6 0.2 shard_map.53.shifts
  13.8 2.0 %collective-permute-done.3.in_near = bf16[2,1,64,128]{3,2,1,0:T(8,128)(2,1)S(1)} collective-permute-done((bf16[2,1,64,128]{3,2,1,0:T(8,128)(2,1)S(1)}, bf16[2,1,64,128]{3,2,1,0:T(8,128)(2,1)S(1)}, u32[]{:S(2)}, u32[]{:S(2)}) %collective-permute-start.3) | collective-permute-done | bytes 32800 | tf_op jit(solution)/shard_map/ppermute | solution.py:53
  15.8 0.0 collective-permute-done.4.in_far
  15.8 0.0 collective-permute-done.2.incoming
  15.8 1.2 %shard_map.54 = (bf16[2,4,64,128]{3,2,1,0:T(8,128)(2,1)S(1)}, bf16[768,128]{1,0:T(8,128)(2,1)S(1)}, bf16[432,128]{1,0:T(8,128)(2,1)S(1)}, bf16[432,128]{1,0:T(8,...) custom-call(s32[1]{0:T(128)} %bitcast.spot, ...), custom_call_target="tpu_custom_call" | custom-call | tf_op jit(solution)/shard_map/pallas_call | solution.py:394
  17.1 4.3 %collective-permute-start.8 = (bf16[432,128]{1,0:T(8,128)(2,1)S(1)}, bf16[432,128]{1,0:T(8,128)(2,1)S(1)}, u32[]{:S(2)}, u32[]{:S(2)}) collective-permute-start(bf16[432,128]{1,0:T(8,128)(2,1)S(1)} %get-tuple-element.36), channel_id=1, source_target_pairs={{0,1},{1,0},{2,3},{3,2},{4,5},{5,4},{6,7},{7,6},{8,9},{9,8},{10,11... | collective-permute-start | bytes 331784 | tf_op jit(solution)/shard_map/ppermute | solution.py:41
  21.3 0.1 collective-permute-start.6
  21.4 0.4 collective-permute-start.10
  21.8 0.1 collective-permute-start.5
  21.9 0.4 collective-permute-done.8.got
  22.3 2.4 %collective-permute-start.9 = (bf16[432,128]{1,0:T(8,128)(2,1)S(1)}, bf16[432,128]{1,0:T(8,128)(2,1)S(1)}, u32[]{:S(2)}, u32[]{:S(2)}) collective-permute-start(bf16[432,128]{1,0:T(8,128)(2,1)S(1)} %shard_map.56), channel_id=1, source_target_pairs={{0,2},{1,3},{2,0},{3,1},{4,6},{5,7},{6,4},{7,5},{8,10},{9,11},{10,... | collective-permute-start | bytes 331784 | tf_op jit(solution)/shard_map/ppermute | solution.py:41
  24.7 0.0 collective-permute-done.6.got
  24.8 2.2 %collective-permute-start.7 = (bf16[432,128]{1,0:T(8,128)(2,1)S(1)}, bf16[432,128]{1,0:T(8,128)(2,1)S(1)}, u32[]{:S(2)}, u32[]{:S(2)}) collective-permute-start(bf16[432,128]{1,0:T(8,128)(2,1)S(1)} %shard_map.55), channel_id=1, source_target_pairs={{0,6},{1,7},{2,4},{3,5},{4,2},{5,3},{6,0},{7,1},{8,14},{9,15},{10,... | collective-permute-start | bytes 331784 | tf_op jit(solution)/shard_map/ppermute | solution.py:41
  27.0 0.1 collective-permute-start.11
  27.1 1.8 %shard_map.57 = bf16[2,4,64,128]{3,2,1,0:T(8,128)(2,1)} custom-call(bf16[768,128]{1,0:T(8,128)(2,1)S(1)} %get-tuple-element.37.deltas, bf16[2,4,64,128]{3,2,1,0:T(8,128)(2,1)S(1)} %get-tuple-element.38.upstream, bf16[3456,128]{1,0:T(8,128)(2,1)S(1)} %get-tuple-element.27.mirror), custom_call_target="tpu_custom_call" | custom-call | tf_op jit(solution)/shard_map/pallas_call | solution.py:355
  28.9 1.0 %collective-permute-done.9.refs_2_ = bf16[432,128]{1,0:T(8,128)(2,1)S(1)} collective-permute-done((bf16[432,128]{1,0:T(8,128)(2,1)S(1)}, bf16[432,128]{1,0:T(8,128)(2,1)S(1)}, u32[]{:S(2)}, u32[]{:S(2)}) %collective-permute-start.9) | collective-permute-done | bytes 110624 | tf_op jit(solution)/shard_map/ppermute | solution.py:41
  29.9 0.0 collective-permute-done.5.refs_0_
  29.9 1.7 %collective-permute-done.7.refs_1_ = bf16[432,128]{1,0:T(8,128)(2,1)S(1)} collective-permute-done((bf16[432,128]{1,0:T(8,128)(2,1)S(1)}, bf16[432,128]{1,0:T(8,128)(2,1)S(1)}, u32[]{:S(2)}, u32[]{:S(2)}) %collective-permute-start.7) | collective-permute-done | bytes 110624 | tf_op jit(solution)/shard_map/ppermute | solution.py:41
  31.7 0.5 collective-permute-done.11.refs_3_
  32.1 0.1 shard_map.59.mine
  32.2 1.9 %collective-permute-start.12 = (bf16[432,128]{1,0:T(8,128)(2,1)S(1)}, bf16[432,128]{1,0:T(8,128)(2,1)S(1)}, u32[]{:S(2)}, u32[]{:S(2)}) collective-permute-start(bf16[432,128]{1,0:T(8,128)(2,1)S(1)} %shard_map.59.mine), channel_id=1, source_target_pairs={{0,9},{1,8},{2,11},{3,10},{4,13},{5,12},{6,15},{7,14},{8,1},{9,0},... | collective-permute-start | bytes 331784 | tf_op jit(solution)/shard_map/ppermute | solution.py:41
  34.1 3.7 %collective-permute-done.12.other = bf16[432,128]{1,0:T(8,128)(2,1)S(1)} collective-permute-done((bf16[432,128]{1,0:T(8,128)(2,1)S(1)}, bf16[432,128]{1,0:T(8,128)(2,1)S(1)}, u32[]{:S(2)}, u32[]{:S(2)}) %collective-permute-start.12) | collective-permute-done | bytes 110624 | tf_op jit(solution)/shard_map/ppermute | solution.py:41
  37.8 4.0 %collective-permute-start.15 = (bf16[432,128]{1,0:T(8,128)(2,1)S(1)}, bf16[432,128]{1,0:T(8,128)(2,1)S(1)}, u32[]{:S(2)}, u32[]{:S(2)}) collective-permute-start(bf16[432,128]{1,0:T(8,128)(2,1)S(1)} %shard_map.60.refs_0_.refs_4_), channel_id=1, source_target_pairs={{0,6},{1,7},{2,4},{3,5},{4,2},{5,3},{6,0},{7,1},{8,14},{9,15},{10,... | collective-permute-start | bytes 331784 | tf_op jit(solution)/shard_map/ppermute | solution.py:41
  41.8 0.9 %collective-permute-start.14 = (bf16[432,128]{1,0:T(8,128)(2,1)S(1)}, bf16[432,128]{1,0:T(8,128)(2,1)S(1)}, u32[]{:S(2)}, u32[]{:S(2)}) collective-permute-start(bf16[432,128]{1,0:T(8,128)(2,1)S(1)} %shard_map.60.refs_0_.refs_4_), channel_id=1, source_target_pairs={{0,2},{1,3},{2,0},{3,1},{4,6},{5,7},{6,4},{7,5},{8,10},{9,11},{10,... | collective-permute-start | bytes 331784 | tf_op jit(solution)/shard_map/ppermute | solution.py:41
  42.8 0.9 %collective-permute-start.13 = (bf16[432,128]{1,0:T(8,128)(2,1)S(1)}, bf16[432,128]{1,0:T(8,128)(2,1)S(1)}, u32[]{:S(2)}, u32[]{:S(2)}) collective-permute-start(bf16[432,128]{1,0:T(8,128)(2,1)S(1)} %shard_map.60.refs_0_.refs_4_), channel_id=1, source_target_pairs={{0,4},{1,5},{2,6},{3,7},{4,0},{5,1},{6,2},{7,3},{8,12},{9,13},{10,... | collective-permute-start | bytes 331784 | tf_op jit(solution)/shard_map/ppermute | solution.py:41
  43.7 1.5 %collective-permute-done.15.refs_3_.refs_7_ = bf16[432,128]{1,0:T(8,128)(2,1)S(1)} collective-permute-done((bf16[432,128]{1,0:T(8,128)(2,1)S(1)}, bf16[432,128]{1,0:T(8,128)(2,1)S(1)}, u32[]{:S(2)}, u32[]{:S(2)}) %collective-permute-start.15) | collective-permute-done | bytes 110624 | tf_op jit(solution)/shard_map/ppermute | solution.py:41
  45.2 0.4 collective-permute-start.19
  45.7 2.4 %collective-permute-done.14.refs_2_.refs_6_ = bf16[432,128]{1,0:T(8,128)(2,1)S(1)} collective-permute-done((bf16[432,128]{1,0:T(8,128)(2,1)S(1)}, bf16[432,128]{1,0:T(8,128)(2,1)S(1)}, u32[]{:S(2)}, u32[]{:S(2)}) %collective-permute-start.14) | collective-permute-done | bytes 110624 | tf_op jit(solution)/shard_map/ppermute | solution.py:41
  48.1 0.0 collective-permute-start.18
  48.1 1.1 %collective-permute-done.13.refs_1_.refs_5_ = bf16[432,128]{1,0:T(8,128)(2,1)S(1)} collective-permute-done((bf16[432,128]{1,0:T(8,128)(2,1)S(1)}, bf16[432,128]{1,0:T(8,128)(2,1)S(1)}, u32[]{:S(2)}, u32[]{:S(2)}) %collective-permute-start.13) | collective-permute-done | bytes 110624 | tf_op jit(solution)/shard_map/ppermute | solution.py:41
  49.2 0.1 shard_map.61.refs_0_
  49.3 1.2 %collective-permute-start.21 = (f32[8,128]{1,0:T(8,128)S(1)}, f32[8,128]{1,0:T(8,128)S(1)}, u32[]{:S(2)}, u32[]{:S(2)}) collective-permute-start(f32[8,128]{1,0:T(8,128)S(1)} %shard_map.61.refs_0_), channel_id=1, source_target_pairs={{0,17},{1,16},{2,19},{3,18},{4,21},{5,20},{6,23},{7,22},{8,25},{9,... | collective-permute-start | bytes 12296 | tf_op jit(solution)/shard_map/ppermute | solution.py:53
  50.5 0.0 collective-permute-done.16.refs_0_.refs_8_
  50.5 1.0 %collective-permute-start.20 = (f32[8,128]{1,0:T(8,128)S(1)}, f32[8,128]{1,0:T(8,128)S(1)}, u32[]{:S(2)}, u32[]{:S(2)}) collective-permute-start(f32[8,128]{1,0:T(8,128)S(1)} %shard_map.61.refs_0_), channel_id=1, source_target_pairs={{0,16},{1,17},{2,18},{3,19},{4,20},{5,21},{6,22},{7,23},{8,24},{9,... | collective-permute-start | bytes 12296 | tf_op jit(solution)/shard_map/ppermute | solution.py:53
  51.5 0.0 collective-permute-done.18.refs_2_.refs_10_
  51.5 0.1 shard_map.62.refs_1_
  51.7 0.8 %collective-permute-done.21.refs_3_ = f32[8,128]{1,0:T(8,128)S(1)} collective-permute-done((f32[8,128]{1,0:T(8,128)S(1)}, f32[8,128]{1,0:T(8,128)S(1)}, u32[]{:S(2)}, u32[]{:S(2)}) %collective-permute-start.21) | collective-permute-done | bytes 4128 | tf_op jit(solution)/shard_map/ppermute | solution.py:53
  52.4 1.7 %collective-permute-done.20.refs_2_ = f32[8,128]{1,0:T(8,128)S(1)} collective-permute-done((f32[8,128]{1,0:T(8,128)S(1)}, f32[8,128]{1,0:T(8,128)S(1)}, u32[]{:S(2)}, u32[]{:S(2)}) %collective-permute-start.20) | collective-permute-done | bytes 4128 | tf_op jit(solution)/shard_map/ppermute | solution.py:53
  54.1 1.4 %shard_map.63 = f32[8,432,128]{2,1,0:T(8,128)} custom-call(s32[1]{0:T(128)} %bitcast.spot, f32[8,128]{1,0:T(8,128)S(1)} %shard_map.61.refs_0_, f32[8,128]{1,0:T(8,128)S(1)} %shard_map.62.refs_1_, f32[8,128]{1,0:T(8,128)S(1)} %collective-permute-done.20.refs_2_, f32[8,128]{1,0:T(8,128)S(1)} %collective-permute-done.21.refs_3_, ...), custom_call_target="tpu_custom_call" | custom-call | tf_op jit(solution)/shard_map/pallas_call | solution.py:476
  (10 shorter events, 0.1 us)
Async XLA Ops:
  1.8 3.4 %collective-permute-start = (bf16[2,3,64,128]{3,2,1,0:T(8,128)(2,1)S(1)}, bf16[2,3,64,128]{3,2,1,0:T(8,128)(2,1)S(1)}, u32[]{:S(2)}, u32[]{:S(2)}) collective-permute-start(bf16[2,3,64,128]{3,2,1,0:T(8,128)(2,1)S(1)} %get-tuple-element.22), channel_id=1, source_target_pairs={{0,1},{1,0},{2,3},{3,2},{4,5},{5,4},{6,7},{7,6},{8,9},{9,8},{10,11... | collective-permute-start | bytes 294920 | tf_op jit(solution)/shard_map/ppermute | solution.py:26
  2.4 2.9 %collective-permute-start.1 = (bf16[2,3,64,128]{3,2,1,0:T(8,128)(2,1)S(1)}, bf16[2,3,64,128]{3,2,1,0:T(8,128)(2,1)S(1)}, u32[]{:S(2)}, u32[]{:S(2)}) collective-permute-start(bf16[2,3,64,128]{3,2,1,0:T(8,128)(2,1)S(1)} %get-tuple-element.23), channel_id=1, source_target_pairs={{1,2},{2,1},{3,4},{4,3},{5,6},{6,5},{7,8},{8,7},{9,10},{10,9},{11,... | collective-permute-start | bytes 294920 | tf_op jit(solution)/shard_map/ppermute | solution.py:26
  7.2 8.7 %collective-permute-start.2 = (bf16[2,4,64,128]{3,2,1,0:T(8,128)(2,1)S(1)}, bf16[2,4,64,128]{3,2,1,0:T(8,128)(2,1)S(1)}, u32[]{:S(2)}, u32[]{:S(2)}) collective-permute-start(bf16[2,4,64,128]{3,2,1,0:T(8,128)(2,1)S(1)} %get-tuple-element.29.after), channel_id=1, source_target_pairs={{0,16},{1,17},{2,18},{3,19},{4,20},{5,21},{6,22},{7,23},{8,24},{9,... | collective-permute-start | bytes 393224 | tf_op jit(solution)/shard_map/ppermute | solution.py:53
  9.7 6.1 %collective-permute-start.3 = (bf16[2,1,64,128]{3,2,1,0:T(8,128)(2,1)S(1)}, bf16[2,1,64,128]{3,2,1,0:T(8,128)(2,1)S(1)}, u32[]{:S(2)}, u32[]{:S(2)}) collective-permute-start(bf16[2,1,64,128]{3,2,1,0:T(8,128)(2,1)S(1)} %get-tuple-element.30), channel_id=1, source_target_pairs={{0,17},{1,16},{2,19},{3,18},{4,21},{5,20},{6,23},{7,22},{8,25},{9,... | collective-permute-start | bytes 98312 | tf_op jit(solution)/shard_map/ppermute | solution.py:53
  12.9 2.9 %collective-permute-start.4 = (bf16[2,1,64,128]{3,2,1,0:T(8,128)(2,1)S(1)}, bf16[2,1,64,128]{3,2,1,0:T(8,128)(2,1)S(1)}, u32[]{:S(2)}, u32[]{:S(2)}) collective-permute-start(bf16[2,1,64,128]{3,2,1,0:T(8,128)(2,1)S(1)} %get-tuple-element.31), channel_id=1, source_target_pairs={{1,18},{2,17},{3,20},{4,19},{5,22},{6,21},{7,24},{8,23},{9,26},{10... | collective-permute-start | bytes 98312 | tf_op jit(solution)/shard_map/ppermute | solution.py:36
  17.1 5.2 %collective-permute-start.8 = (bf16[432,128]{1,0:T(8,128)(2,1)S(1)}, bf16[432,128]{1,0:T(8,128)(2,1)S(1)}, u32[]{:S(2)}, u32[]{:S(2)}) collective-permute-start(bf16[432,128]{1,0:T(8,128)(2,1)S(1)} %get-tuple-element.36), channel_id=1, source_target_pairs={{0,1},{1,0},{2,3},{3,2},{4,5},{5,4},{6,7},{7,6},{8,9},{9,8},{10,11... | collective-permute-start | bytes 331784 | tf_op jit(solution)/shard_map/ppermute | solution.py:41
  21.3 3.4 %collective-permute-start.6 = (bf16[432,128]{1,0:T(8,128)(2,1)S(1)}, bf16[432,128]{1,0:T(8,128)(2,1)S(1)}, u32[]{:S(2)}, u32[]{:S(2)}) collective-permute-start(bf16[432,128]{1,0:T(8,128)(2,1)S(1)} %get-tuple-element.35), channel_id=1, source_target_pairs={{0,1},{1,0},{2,3},{3,2},{4,5},{5,4},{6,7},{7,6},{8,9},{9,8},{10,11... | collective-permute-start | bytes 331784 | tf_op jit(solution)/shard_map/ppermute | solution.py:41
  21.4 5.6 %collective-permute-start.10 = (bf16[432,128]{1,0:T(8,128)(2,1)S(1)}, bf16[432,128]{1,0:T(8,128)(2,1)S(1)}, u32[]{:S(2)}, u32[]{:S(2)}) collective-permute-start(bf16[432,128]{1,0:T(8,128)(2,1)S(1)} %get-tuple-element.40), channel_id=1, source_target_pairs={{0,1},{1,0},{2,3},{3,2},{4,5},{5,4},{6,7},{7,6},{8,9},{9,8},{10,11... | collective-permute-start | bytes 331784 | tf_op jit(solution)/shard_map/ppermute | solution.py:41
  21.8 8.1 %collective-permute-start.5 = (bf16[432,128]{1,0:T(8,128)(2,1)S(1)}, bf16[432,128]{1,0:T(8,128)(2,1)S(1)}, u32[]{:S(2)}, u32[]{:S(2)}) collective-permute-start(bf16[432,128]{1,0:T(8,128)(2,1)S(1)} %get-tuple-element.34), channel_id=1, source_target_pairs={{0,1},{1,0},{2,3},{3,2},{4,5},{5,4},{6,7},{7,6},{8,9},{9,8},{10,11... | collective-permute-start | bytes 331784 | tf_op jit(solution)/shard_map/ppermute | solution.py:41
  22.3 7.6 %collective-permute-start.9 = (bf16[432,128]{1,0:T(8,128)(2,1)S(1)}, bf16[432,128]{1,0:T(8,128)(2,1)S(1)}, u32[]{:S(2)}, u32[]{:S(2)}) collective-permute-start(bf16[432,128]{1,0:T(8,128)(2,1)S(1)} %shard_map.56), channel_id=1, source_target_pairs={{0,2},{1,3},{2,0},{3,1},{4,6},{5,7},{6,4},{7,5},{8,10},{9,11},{10,... | collective-permute-start | bytes 331784 | tf_op jit(solution)/shard_map/ppermute | solution.py:41
  24.8 6.9 %collective-permute-start.7 = (bf16[432,128]{1,0:T(8,128)(2,1)S(1)}, bf16[432,128]{1,0:T(8,128)(2,1)S(1)}, u32[]{:S(2)}, u32[]{:S(2)}) collective-permute-start(bf16[432,128]{1,0:T(8,128)(2,1)S(1)} %shard_map.55), channel_id=1, source_target_pairs={{0,6},{1,7},{2,4},{3,5},{4,2},{5,3},{6,0},{7,1},{8,14},{9,15},{10,... | collective-permute-start | bytes 331784 | tf_op jit(solution)/shard_map/ppermute | solution.py:41
  27.0 5.1 %collective-permute-start.11 = (bf16[432,128]{1,0:T(8,128)(2,1)S(1)}, bf16[432,128]{1,0:T(8,128)(2,1)S(1)}, u32[]{:S(2)}, u32[]{:S(2)}) collective-permute-start(bf16[432,128]{1,0:T(8,128)(2,1)S(1)} %shard_map.58), channel_id=1, source_target_pairs={{0,4},{1,5},{2,6},{3,7},{4,0},{5,1},{6,2},{7,3},{8,12},{9,13},{10,... | collective-permute-start | bytes 331784 | tf_op jit(solution)/shard_map/ppermute | solution.py:41
  32.2 5.6 %collective-permute-start.12 = (bf16[432,128]{1,0:T(8,128)(2,1)S(1)}, bf16[432,128]{1,0:T(8,128)(2,1)S(1)}, u32[]{:S(2)}, u32[]{:S(2)}) collective-permute-start(bf16[432,128]{1,0:T(8,128)(2,1)S(1)} %shard_map.59.mine), channel_id=1, source_target_pairs={{0,9},{1,8},{2,11},{3,10},{4,13},{5,12},{6,15},{7,14},{8,1},{9,0},... | collective-permute-start | bytes 331784 | tf_op jit(solution)/shard_map/ppermute | solution.py:41
  37.8 7.4 %collective-permute-start.15 = (bf16[432,128]{1,0:T(8,128)(2,1)S(1)}, bf16[432,128]{1,0:T(8,128)(2,1)S(1)}, u32[]{:S(2)}, u32[]{:S(2)}) collective-permute-start(bf16[432,128]{1,0:T(8,128)(2,1)S(1)} %shard_map.60.refs_0_.refs_4_), channel_id=1, source_target_pairs={{0,6},{1,7},{2,4},{3,5},{4,2},{5,3},{6,0},{7,1},{8,14},{9,15},{10,... | collective-permute-start | bytes 331784 | tf_op jit(solution)/shard_map/ppermute | solution.py:41
  41.8 6.3 %collective-permute-start.14 = (bf16[432,128]{1,0:T(8,128)(2,1)S(1)}, bf16[432,128]{1,0:T(8,128)(2,1)S(1)}, u32[]{:S(2)}, u32[]{:S(2)}) collective-permute-start(bf16[432,128]{1,0:T(8,128)(2,1)S(1)} %shard_map.60.refs_0_.refs_4_), channel_id=1, source_target_pairs={{0,2},{1,3},{2,0},{3,1},{4,6},{5,7},{6,4},{7,5},{8,10},{9,11},{10,... | collective-permute-start | bytes 331784 | tf_op jit(solution)/shard_map/ppermute | solution.py:41
  42.8 6.4 %collective-permute-start.13 = (bf16[432,128]{1,0:T(8,128)(2,1)S(1)}, bf16[432,128]{1,0:T(8,128)(2,1)S(1)}, u32[]{:S(2)}, u32[]{:S(2)}) collective-permute-start(bf16[432,128]{1,0:T(8,128)(2,1)S(1)} %shard_map.60.refs_0_.refs_4_), channel_id=1, source_target_pairs={{0,4},{1,5},{2,6},{3,7},{4,0},{5,1},{6,2},{7,3},{8,12},{9,13},{10,... | collective-permute-start | bytes 331784 | tf_op jit(solution)/shard_map/ppermute | solution.py:41
  43.7 6.8 %collective-permute-start.16 = (bf16[432,128]{1,0:T(8,128)(2,1)S(1)}, bf16[432,128]{1,0:T(8,128)(2,1)S(1)}, u32[]{:S(2)}, u32[]{:S(2)}) collective-permute-start(bf16[432,128]{1,0:T(8,128)(2,1)S(1)} %shard_map.60.refs_0_.refs_4_), channel_id=1, source_target_pairs={{0,1},{1,0},{2,3},{3,2},{4,5},{5,4},{6,7},{7,6},{8,9},{9,8},{10,11... | collective-permute-start | bytes 331784 | tf_op jit(solution)/shard_map/ppermute | solution.py:41
  45.2 6.3 %collective-permute-start.19 = (bf16[432,128]{1,0:T(8,128)(2,1)S(1)}, bf16[432,128]{1,0:T(8,128)(2,1)S(1)}, u32[]{:S(2)}, u32[]{:S(2)}) collective-permute-start(bf16[432,128]{1,0:T(8,128)(2,1)S(1)} %collective-permute-done.15.refs_3_.refs_7_), channel_id=1, source_target_pairs={{0,1},{1,0},{2,3},{3,2},{4,5},{5,4},{6,7},{7,6},{8,9},{9,8},{10,11... | collective-permute-start | bytes 331784 | tf_op jit(solution)/shard_map/ppermute | solution.py:41
  48.1 3.4 %collective-permute-start.18 = (bf16[432,128]{1,0:T(8,128)(2,1)S(1)}, bf16[432,128]{1,0:T(8,128)(2,1)S(1)}, u32[]{:S(2)}, u32[]{:S(2)}) collective-permute-start(bf16[432,128]{1,0:T(8,128)(2,1)S(1)} %collective-permute-done.14.refs_2_.refs_6_), channel_id=1, source_target_pairs={{0,1},{1,0},{2,3},{3,2},{4,5},{5,4},{6,7},{7,6},{8,9},{9,8},{10,11... | collective-permute-start | bytes 331784 | tf_op jit(solution)/shard_map/ppermute | solution.py:41
  49.2 2.3 %collective-permute-start.17 = (bf16[432,128]{1,0:T(8,128)(2,1)S(1)}, bf16[432,128]{1,0:T(8,128)(2,1)S(1)}, u32[]{:S(2)}, u32[]{:S(2)}) collective-permute-start(bf16[432,128]{1,0:T(8,128)(2,1)S(1)} %collective-permute-done.13.refs_1_.refs_5_), channel_id=1, source_target_pairs={{0,1},{1,0},{2,3},{3,2},{4,5},{5,4},{6,7},{7,6},{8,9},{9,8},{10,11... | collective-permute-start | bytes 331784 | tf_op jit(solution)/shard_map/ppermute | solution.py:41
  49.3 3.1 %collective-permute-start.21 = (f32[8,128]{1,0:T(8,128)S(1)}, f32[8,128]{1,0:T(8,128)S(1)}, u32[]{:S(2)}, u32[]{:S(2)}) collective-permute-start(f32[8,128]{1,0:T(8,128)S(1)} %shard_map.61.refs_0_), channel_id=1, source_target_pairs={{0,17},{1,16},{2,19},{3,18},{4,21},{5,20},{6,23},{7,22},{8,25},{9,... | collective-permute-start | bytes 12296 | tf_op jit(solution)/shard_map/ppermute | solution.py:53
  50.5 3.6 %collective-permute-start.20 = (f32[8,128]{1,0:T(8,128)S(1)}, f32[8,128]{1,0:T(8,128)S(1)}, u32[]{:S(2)}, u32[]{:S(2)}) collective-permute-start(f32[8,128]{1,0:T(8,128)S(1)} %shard_map.61.refs_0_), channel_id=1, source_target_pairs={{0,16},{1,17},{2,18},{3,19},{4,20},{5,21},{6,22},{7,23},{8,24},{9,... | collective-permute-start | bytes 12296 | tf_op jit(solution)/shard_map/ppermute | solution.py:53

commit v8 on v7

--- a/solution.py
+++ b/solution.py
@@ -136,8 +136,9 @@
 
 
 def first_kernel(
-    height, near, far, grad, weight, mirror, part, result, to_near, to_far, slopes, rim, shifts
+    height, near, far, grad, weight, mirror, part, result, slopes, to_far, *refs
 ):
+    rim, shifts = refs[-2:]
     micro, depth, cells, channels = grad.shape
     even = lax.rem(lax.axis_index("slab"), 2) == 0
     block, span = micro * cells, 9 * channels
@@ -186,7 +187,8 @@
             if n in (0, depth - 1):
                 ends.append(total)
         low, high = ends[0], ends[-1]
-        to_near[m, 0] = jnp.where(even, high, low).astype(BF16)
+        for to_near in refs[:-2]:
+            to_near[m, 0] = jnp.where(even, high, low).astype(BF16)
         to_far[m, 0] = jnp.where(even, low, high).astype(BF16)
 
 
@@ -202,25 +204,32 @@
 
 
 def raw_kernel(
-    spot, incoming, in_near, in_far, grad, near, far, slopes, shifts, upstream, deltas, *refs
+    spot, incoming, grad, far, slopes, shifts, upstream, deltas, far_slope, *refs
 ):
     sends, (keep, raw) = refs[:4], refs[4:]
+    part = keep.shape[1]
     micro, depth, cells, channels = upstream.shape
     block, span = micro * cells, 9 * channels
     last = lax.axis_index("segment") == lax.axis_size("segment") - 1
     even = lax.rem(lax.axis_index("slab"), 2) == 0
+    low, high = slice(0, block), slice((depth + 1) * block, (depth + 2) * block)
+    slope = jnp.where(even, slopes[low, :], slopes[high, :])
+    far_slope[...] = slope
     for m in range(micro):
-        by_near = jnp.where(last, near[m, 2].astype(F32), in_near[m, 0].astype(F32))
-        by_far = jnp.where(last, far[m, 2].astype(F32), in_far[m, 0].astype(F32))
-        planes = [jnp.where(even, by_far, by_near)]
+        inside = slice(m * cells, (m + 1) * cells)
+        rim = (far[m, 2].astype(F32) * slope[inside]).astype(BF16)
+        for first in (low.start, high.start):
+            deltas[first + m * cells : first + (m + 1) * cells, :] = rim
+        planes = []
         for n in range(depth):
             up = jnp.where(last, grad[m, n].astype(F32), incoming[m, n].astype(F32))
             upstream[m, n] = up.astype(BF16)
-            planes.append(up)
-        planes.append(jnp.where(even, by_near, by_far))
-        for n, up in enumerate(planes):
-            rows = slice(n * block + m * cells, n * block + (m + 1) * cells)
-            deltas[rows, :] = (up * slopes[rows, :]).astype(BF16)
+            first = (n + 1) * block + m * cells
+            delta = up * slopes[first : first + cells, :]
+            deltas[first : first + cells, :] = delta.astype(BF16)
+            planes.append(delta)
+        first = part + m * cells
+        sends[0][first : first + cells, :] = jnp.where(even, planes[-1], planes[0]).astype(BF16)
     for dz in range(3):
         total = None
         for n in range(depth):
@@ -232,10 +241,9 @@
             )
             total = term if total is None else total + term
         raw[dz * span : (dz + 1) * span, :] = total
-    part = keep.shape[1]
     for turn in range(4):
         keep[turn] = raw[pl.ds((spot[0] ^ turn) * part, part), :]
-        sends[turn][...] = raw[pl.ds((spot[0] ^ turn ^ 4) * part, part), :].astype(BF16)
+        sends[turn][:part, :] = raw[pl.ds((spot[0] ^ turn ^ 4) * part, part), :].astype(BF16)
 
 
 def add_kernel(turn, keep, got, out):
@@ -245,7 +253,7 @@
 def sum_kernel(keep, *refs):
     total = keep[0]
     for got in refs[:-1]:
-        total = total + got[...].astype(F32)
+        total = total + got[: total.shape[0], :].astype(F32)
     refs[-1][...] = total.astype(refs[-1].dtype)
 
 
@@ -265,13 +273,25 @@
     refs[-1][...] = jnp.broadcast_to(sums[0], refs[-1].shape)
 
 
-def back_kernel(height, deltas, upstream, mirror, out, shifts):
+def back_kernel(
+    height, deltas, by_near, in_far, far_slope, upstream, mirror, out, shifts
+):
     micro, depth, cells, channels = upstream.shape
     block = micro * cells
-    for n in range(depth + 2):
-        for m in range(micro):
-            rows = slice(n * block + m * cells, n * block + (m + 1) * cells)
-            write_shifts(deltas[rows, :], height, shifts, rows.start)
+    last = lax.axis_index("segment") == lax.axis_size("segment") - 1
+    even = lax.rem(lax.axis_index("slab"), 2) == 0
+    start = by_near.shape[0] - block
+    for m in range(micro):
+        inside = slice(m * cells, (m + 1) * cells)
+        near = by_near[start + m * cells : start + (m + 1) * cells, :].astype(F32)
+        far = (in_far[m, 0].astype(F32) * far_slope[inside, :]).astype(BF16).astype(F32)
+        far = jnp.where(last, deltas[inside, :].astype(F32), far)
+        write_shifts(jnp.where(even, far, near), height, shifts, m * cells)
+        first = (depth + 1) * block + m * cells
+        write_shifts(jnp.where(even, near, far), height, shifts, first)
+        for n in range(1, depth + 1):
+            first = n * block + m * cells
+            write_shifts(deltas[first : first + cells, :], height, shifts, first)
     back = back_product(shifts, mirror, block, depth)
     for m in range(micro):
         for n in range(depth):
@@ -337,43 +357,44 @@
 
     edge = shape((micro, 1, cells, channels), BF16)
     wide = pltpu.VMEM(((depth + 2) * plane, span), BF16)
-    result, to_near, to_far, slopes = pl.pallas_call(
+    edges = (edge,) * (1 if segments == 2 else 2)
+    result, slopes, to_far, *to_near = pl.pallas_call(
         functools.partial(first_kernel, height),
-        out_shape=(
-            volume,
-            edge,
-            edge,
-            outer,
-        ),
+        out_shape=(volume, outer) + edges,
         in_specs=[VMEM] * 6,
-        out_specs=(VMEM,) * 4,
+        out_specs=(VMEM,) * (2 + len(edges)),
         scratch_shapes=[pltpu.VMEM((4 * plane, span), BF16), wide],
         compiler_params=large,
     )(near, far, grad, weight, mirror, part)
 
-    def conv_back(deltas, upstream):
+    def conv_back(deltas, by_near, in_far, far_slope, upstream):
         return pl.pallas_call(
             functools.partial(back_kernel, height),
             out_shape=volume,
-            in_specs=[VMEM] * 3,
+            in_specs=[VMEM] * 6,
             out_specs=VMEM,
             scratch_shapes=[wide],
             compiler_params=large,
-        )(deltas, upstream, mirror)
-
+        )(deltas, by_near, in_far, far_slope, upstream, mirror)
+
+    part = weight.shape[0] // 8
     even = lax.rem(index, 2) == 0
     for step in range(1, segments - 1):
-        incoming, in_near, in_far = cross(result, 1, 0), cross(to_near, 1, 1), cross_far(to_far)
+        incoming, in_near, in_far = cross(result, 1, 0), cross(to_near[0], 1, 1), cross_far(to_far)
         upstream = jnp.where(last, grad, incoming)
-        by_near = jnp.where(last, near[:, 2:], in_near)
-        by_far = jnp.where(last, far[:, 2:], in_far)
-        below, above = jnp.where(even, by_far, by_near), jnp.where(even, by_near, by_far)
-        around = jnp.concatenate([below, upstream, above], axis=1)
-        around = jnp.swapaxes(around, 0, 1).reshape(outer.shape).astype(F32)
-        result = conv_back((around * slopes).astype(BF16), upstream)
+        stacked = jnp.swapaxes(upstream, 0, 1).reshape(depth * plane, channels).astype(F32)
+        deltas = (stacked * slopes[plane:-plane]).astype(BF16)
+        near_slope = jnp.where(even, slopes[-plane:], slopes[:plane])
+        far_slope = jnp.where(even, slopes[:plane], slopes[-plane:])
+        by_near = jnp.where(last, near[:, 2:], in_near).reshape(plane, channels).astype(F32)
+        rim = (far[:, 2:].reshape(plane, channels).astype(F32) * far_slope).astype(BF16)
+        deltas = jnp.concatenate([rim, deltas, rim], axis=0)
+        result = conv_back(
+            deltas, (by_near * near_slope).astype(BF16), in_far, far_slope, upstream
+        )
         low, high = result[:, :1], result[:, -1:]
-        to_near, to_far = jnp.where(even, high, low), jnp.where(even, low, high)
-    incoming, in_near, in_far = cross(result, 1, 0), cross(to_near, 1, 1), cross_far(to_far)
+        to_near, to_far = [jnp.where(even, high, low)], jnp.where(even, low, high)
+    incoming = cross(result, 1, 0)
     shifts = pl.pallas_call(
         functools.partial(shift_kernel, height),
         out_shape=shape(((depth + 2) * plane, span), BF16),
@@ -388,23 +409,30 @@
     quarter = jnp.where(index & 2, 2, 0) + jnp.where(index & 4, 1, 0)
     masks = {1: 4, 2: 2, 3: 6}
     spot = (side * 4 + quarter).astype(jnp.int32).reshape(1)
-    part = weight.shape[0] // 8
     piece = shape((part, channels), BF16)
 
-    upstream, deltas, *rest = pl.pallas_call(
+    upstream, deltas, far_slope, *rest = pl.pallas_call(
         raw_kernel,
-        out_shape=(volume, shape(outer.shape, BF16))
-        + (piece,) * 4
-        + (shape((4, part, channels), F32),),
-        in_specs=[SMEM] + [VMEM] * 8,
-        out_specs=(VMEM,) * 7,
+        out_shape=(
+            volume,
+            shape(outer.shape, BF16),
+            shape((plane, channels), F32),
+            shape((part + plane, channels), BF16),
+            piece,
+            piece,
+            piece,
+            shape((4, part, channels), F32),
+        ),
+        in_specs=[SMEM] + [VMEM] * 5,
+        out_specs=(VMEM,) * 8,
         scratch_shapes=[pltpu.VMEM((8 * part, channels), F32)],
         compiler_params=large,
-    )(spot, incoming, in_near, in_far, grad, near, far, slopes, shifts)
+    )(spot, incoming, grad, far, slopes, shifts)
     sends, keep = rest[:4], rest[4]
-    got = {turn: exchange(sends[turn], 1) for turn in (3, 2, 1, 0)}
+    order = (2, 1, 3)
+    got = {turn: exchange(sends[turn], 1) for turn in order + (0,)}
     across = []
-    for turn in (3, 2, 1):
+    for turn in order:
         added = pl.pallas_call(
             functools.partial(add_kernel, turn),
             out_shape=piece,
@@ -412,9 +440,12 @@
             out_specs=VMEM,
             compiler_params=small,
         )(keep, got[turn])
+        if turn == order[-1]:
+            added, to_far = lax.optimization_barrier((added, to_far))
         across.append(exchange(added, masks[turn]))
-    gradients = conv_back(deltas, upstream)
-    across[1], gradients = lax.optimization_barrier((across[1], gradients))
+    in_far = cross_far(to_far)
+    across[2], in_far = lax.optimization_barrier((across[2], in_far))
+    gradients = conv_back(deltas, got[0], in_far, far_slope, upstream)
     single = len(inner[-1]) == 1
     direct = single and len(inner) == 1
     chunk = pl.pallas_call(
@@ -440,13 +471,15 @@
         chunk = block(chunk, own, size, F32) + sum(g.astype(F32) for g in took)
     gathered = chunk.astype(BF16)
     if single:
+        other = exchange(gathered, crossing | 1)
+        other, gradients = lax.optimization_barrier((other, gradients))
         gathered = pl.pallas_call(
             both_kernel,
             out_shape=shape(gathered.shape, BF16),
             in_specs=[VMEM] * 2,
             out_specs=VMEM,
             compiler_params=small,
-        )(gathered, exchange(gathered, crossing | 1))
+        )(gathered, other)
 
     for group in reversed(paired):
         own, others = places(group)
@@ -458,7 +491,7 @@
                 value = jnp.where(there == n, other, value)
             blocks.append(value)
         gathered = jnp.concatenate(blocks, axis=0)
-    pieces = {turn: exchange(gathered, masks[turn]) for turn in (3, 2, 1)}
+    pieces = {turn: exchange(gathered, masks[turn]) for turn in (2, 1, 3)}
     ours = [gathered] + [pieces[turn] for turn in (1, 2, 3)]
     theirs = [exchange(piece, 1) for piece in ours]
     sums = [

time: 55.7 us -> 53.8 us (0.966)
  waiting for transfers between devices: 16.8 us -> 13.6 us
  starting transfers between devices: 27.6 us -> 28.9 us
    ppermute x15, starting transfers between devices: 17.9 us -> 22.3 us  [exchange(): return lax.ppermute(value, 'slab', [(i, i ^ mask) for i in range(count)])]
    ppermute x15, waiting for transfers between devices: 12.3 us -> 8.38 us  [exchange(): return lax.ppermute(value, 'slab', [(i, i ^ mask) for i in range(count)])]
    ppermute x4 -> x3, starting transfers between devices: 7.92 us -> 4.77 us  [cross(): return lax.ppermute(value, ('segment', 'slab'), route)]
    ppermute x4 -> x3, waiting for transfers between devices: 4.49 us -> 5.17 us  [cross(): return lax.ppermute(value, ('segment', 'slab'), route)]
  transfers between devices with their start and end apart: 22 -> 21, of which waited for: 11 -> 10; matrix products, arithmetic and copies ran while one was open for 0% -> 0% of each run, Pallas kernels for 8% -> 9%
where the time goes in v8:
time: 53.8 us; the launch traced here: 53.6 us
  starting transfers between devices  28.9 us (54%)
  waiting for transfers between devices  13.6 us (25%)
  Pallas kernels  10.4 us (19%)
  between operations  0.75 us (1%)
    ppermute x15, starting transfers between devices, exchange(): return lax.ppermute(value, 'slab', [(i, i ^ mask) for i in range(count)])  22.3 us
    ppermute x15, waiting for transfers between devices, exchange(): return lax.ppermute(value, 'slab', [(i, i ^ mask) for i in range(count)])  8.38 us
    ppermute x3, waiting for transfers between devices, cross(): return lax.ppermute(value, ('segment', 'slab'), route)  5.17 us
    ppermute x3, starting transfers between devices, cross(): return lax.ppermute(value, ('segment', 'slab'), route)  4.77 us
    pallas_call x1, Pallas kernels, shards(): pl.pallas_call(functools.partial(own_kernel, height), out_shape=(whole, w...  2.25 us
    pallas_call x1, Pallas kernels, shards(): pl.pallas_call(functools.partial(first_kernel, height), out_shape=(volume...  1.86 us
    pallas_call x1, Pallas kernels, conv_back(): pl.pallas_call(functools.partial(back_kernel, height), out_shape=volume,...  1.79 us
    pallas_call x1, Pallas kernels, shards(): pl.pallas_call(functools.partial(place_kernel, bound, segments), out_shap...  1.38 us
  transfers between devices with their start and end apart: 21, of which 10 were waited for; matrix products, arithmetic and copies ran while one was open for 0% of the time, Pallas kernels for 9%

profile of v8, /device:TPU:0, one launch (start us, length us, event | category | flops | bytes accessed | tf_op | source)
XLA Modules:
  0.0 53.6 jit_solution(12531850754191644645)
XLA Ops:
  0.6 1.2 %shard_map.50 = (bf16[2,3,64,128]{3,2,1,0:T(8,128)(2,1)S(1)}, bf16[2,3,64,128]{3,2,1,0:T(8,128)(2,1)S(1)}, bf16[2,4,64,128]{3,2,1,0:T(8,128)(2,1)S(1)}, bf16[2,4,64,128]{3,2,1,0:T(8,128)(2,1)S(1)}) custom-call(bf16[2,4,64,128]{3,2,1,0:T(8,128)(2,1)} %bitcast.9, bf16[2,4,64,128]{3,2,1,0:T(8,128)(2,1)} %bitcast.10), custom_call_target="tpu_custom_call" | custom-call | tf_op jit(solution)/shard_map/pallas_call | solution.py:336
  1.8 0.5 collective-permute-start
  2.4 0.7 %collective-permute-start.1 = (bf16[2,3,64,128]{3,2,1,0:T(8,128)(2,1)S(1)}, bf16[2,3,64,128]{3,2,1,0:T(8,128)(2,1)S(1)}, u32[]{:S(2)}, u32[]{:S(2)}) collective-permute-start(bf16[2,3,64,128]{3,2,1,0:T(8,128)(2,1)S(1)} %get-tuple-element.27), channel_id=1, source_target_pairs={{1,2},{2,1},{3,4},{4,3},{5,6},{6,5},{7,8},{8,7},{9,10},{10,9},{11,... | collective-permute-start | bytes 294920 | tf_op jit(solution)/shard_map/ppermute | solution.py:26
  3.0 2.3 %shard_map.51 = (bf16[3456,128]{1,0:T(8,128)(2,1)S(1)}, bf16[3456,128]{1,0:T(8,128)(2,1)S(1)}, f32[768,128]{1,0:T(8,128)S(1)}) custom-call(bf16[2,4,64,128]{3,2,1,0:T(8,128)(2,1)S(1)} %get-tuple-element.29.acts, bf16[3456,128]{1,0:T(8,128)(2,1)} %bitcast.7), custom_call_target="tpu_custom_call" | custom-call | tf_op jit(solution)/shard_map/pallas_call | solution.py:349
  5.3 0.0 collective-permute-done.near
  5.3 0.0 collective-permute-done.1.far
  5.3 1.9 %shard_map.52 = (bf16[2,4,64,128]{3,2,1,0:T(8,128)(2,1)S(1)}, f32[768,128]{1,0:T(8,128)S(1)}, bf16[2,1,64,128]{3,2,1,0:T(8,128)(2,1)S(1)}) custom-call(bf16[2,3,64,128]{3,2,1,0:T(8,128)(2,1)S(1)} %collective-permute-done.near, bf16[2,3,64,128]{3,2,1,0:T(8,128)(2,1)S(1)} %collective-permute-done.1.far, bf16[2,4,64,128]{3,2,1,0:T(8,128)(2,1)S(1)} %get-tuple-element.28.grad, ...), custom_call_target="tpu_custom_call" | custom-call | tf_op jit(solution)/shard_map/pallas_call | solution.py:361
  7.2 2.6 %collective-permute-start.2 = (bf16[2,4,64,128]{3,2,1,0:T(8,128)(2,1)S(1)}, bf16[2,4,64,128]{3,2,1,0:T(8,128)(2,1)S(1)}, u32[]{:S(2)}, u32[]{:S(2)}) collective-permute-start(bf16[2,4,64,128]{3,2,1,0:T(8,128)(2,1)S(1)} %get-tuple-element.33.after), channel_id=1, source_target_pairs={{0,16},{1,17},{2,18},{3,19},{4,20},{5,21},{6,22},{7,23},{8,24},{9,... | collective-permute-start | bytes 393224 | tf_op jit(solution)/shard_map/ppermute | solution.py:53
  9.7 0.2 shard_map.53.shifts
  10.0 2.7 %collective-permute-done.2.incoming = bf16[2,4,64,128]{3,2,1,0:T(8,128)(2,1)S(1)} collective-permute-done((bf16[2,4,64,128]{3,2,1,0:T(8,128)(2,1)S(1)}, bf16[2,4,64,128]{3,2,1,0:T(8,128)(2,1)S(1)}, u32[]{:S(2)}, u32[]{:S(2)}) %collective-permute-start.2) | collective-permute-done | bytes 131104 | tf_op jit(solution)/shard_map/ppermute | solution.py:53
  12.7 1.2 %shard_map.54 = (bf16[2,4,64,128]{3,2,1,0:T(8,128)(2,1)S(1)}, bf16[768,128]{1,0:T(8,128)(2,1)S(1)}, f32[128,128]{1,0:T(8,128)S(1)}, bf16[560,128]{1,0:T(8,128)(2...) custom-call(s32[1]{0:T(128)} %bitcast.spot, ...), custom_call_target="tpu_custom_call" | custom-call | tf_op jit(solution)/shard_map/pallas_call | solution.py:414
  13.9 2.7 %collective-permute-start.8 = (bf16[432,128]{1,0:T(8,128)(2,1)S(1)}, bf16[432,128]{1,0:T(8,128)(2,1)S(1)}, u32[]{:S(2)}, u32[]{:S(2)}) collective-permute-start(bf16[432,128]{1,0:T(8,128)(2,1)S(1)} %get-tuple-element.39), channel_id=1, source_target_pairs={{0,1},{1,0},{2,3},{3,2},{4,5},{5,4},{6,7},{7,6},{8,9},{9,8},{10,11... | collective-permute-start | bytes 331784 | tf_op jit(solution)/shard_map/ppermute | solution.py:41
  16.6 0.1 collective-permute-start.4
  16.7 0.4 collective-permute-start.6
  17.1 0.1 collective-permute-start.3
  17.2 0.4 collective-permute-done.8.got
  17.6 4.9 %collective-permute-start.9 = (bf16[432,128]{1,0:T(8,128)(2,1)S(1)}, bf16[432,128]{1,0:T(8,128)(2,1)S(1)}, u32[]{:S(2)}, u32[]{:S(2)}) collective-permute-start(bf16[432,128]{1,0:T(8,128)(2,1)S(1)} %shard_map.57), channel_id=1, source_target_pairs={{0,6},{1,7},{2,4},{3,5},{4,2},{5,3},{6,0},{7,1},{8,14},{9,15},{10,... | collective-permute-start | bytes 331784 | tf_op jit(solution)/shard_map/ppermute | solution.py:41
  22.5 0.0 collective-permute-done.4.got
  22.6 1.5 %collective-permute-start.5 = (bf16[432,128]{1,0:T(8,128)(2,1)S(1)}, bf16[432,128]{1,0:T(8,128)(2,1)S(1)}, u32[]{:S(2)}, u32[]{:S(2)}) collective-permute-start(bf16[432,128]{1,0:T(8,128)(2,1)S(1)} %shard_map.55), channel_id=1, source_target_pairs={{0,2},{1,3},{2,0},{3,1},{4,6},{5,7},{6,4},{7,5},{8,10},{9,11},{10,... | collective-permute-start | bytes 331784 | tf_op jit(solution)/shard_map/ppermute | solution.py:41
  24.1 0.1 collective-permute-start.7
  24.1 0.7 %collective-permute-start.10 = (bf16[2,1,64,128]{3,2,1,0:T(8,128)(2,1)S(1)}, bf16[2,1,64,128]{3,2,1,0:T(8,128)(2,1)S(1)}, u32[]{:S(2)}, u32[]{:S(2)}) collective-permute-start(bf16[2,1,64,128]{3,2,1,0:T(8,128)(2,1)S(1)} %get-tuple-element.42), channel_id=1, source_target_pairs={{1,18},{2,17},{3,20},{4,19},{5,22},{6,21},{7,24},{8,23},{9,26},{10... | collective-permute-start | bytes 98312 | tf_op jit(solution)/shard_map/ppermute | solution.py:36
  24.8 0.0 collective-permute-done.10.in_far
  24.8 1.2 %collective-permute-done.9.refs_3_ = bf16[432,128]{1,0:T(8,128)(2,1)S(1)} collective-permute-done((bf16[432,128]{1,0:T(8,128)(2,1)S(1)}, bf16[432,128]{1,0:T(8,128)(2,1)S(1)}, u32[]{:S(2)}, u32[]{:S(2)}) %collective-permute-start.9) | collective-permute-done | bytes 110624 | tf_op jit(solution)/shard_map/ppermute | solution.py:41
  26.0 2.3 %collective-permute-done.5.refs_1_ = bf16[432,128]{1,0:T(8,128)(2,1)S(1)} collective-permute-done((bf16[432,128]{1,0:T(8,128)(2,1)S(1)}, bf16[432,128]{1,0:T(8,128)(2,1)S(1)}, u32[]{:S(2)}, u32[]{:S(2)}) %collective-permute-start.5) | collective-permute-done | bytes 110624 | tf_op jit(solution)/shard_map/ppermute | solution.py:41
  28.3 0.6 %collective-permute-done.7.refs_2_ = bf16[432,128]{1,0:T(8,128)(2,1)S(1)} collective-permute-done((bf16[432,128]{1,0:T(8,128)(2,1)S(1)}, bf16[432,128]{1,0:T(8,128)(2,1)S(1)}, u32[]{:S(2)}, u32[]{:S(2)}) %collective-permute-start.7) | collective-permute-done | bytes 110624 | tf_op jit(solution)/shard_map/ppermute | solution.py:41
  28.9 0.1 shard_map.58.mine
  29.0 3.4 %collective-permute-start.11 = (bf16[432,128]{1,0:T(8,128)(2,1)S(1)}, bf16[432,128]{1,0:T(8,128)(2,1)S(1)}, u32[]{:S(2)}, u32[]{:S(2)}) collective-permute-start(bf16[432,128]{1,0:T(8,128)(2,1)S(1)} %shard_map.58.mine), channel_id=1, source_target_pairs={{0,9},{1,8},{2,11},{3,10},{4,13},{5,12},{6,15},{7,14},{8,1},{9,0},... | collective-permute-start | bytes 331784 | tf_op jit(solution)/shard_map/ppermute | solution.py:41
  32.4 1.8 %shard_map.59 = bf16[2,4,64,128]{3,2,1,0:T(8,128)(2,1)} custom-call(bf16[768,128]{1,0:T(8,128)(2,1)S(1)} %get-tuple-element.44.deltas, bf16[560,128]{1,0:T(8,128)(2,1)S(1)} %collective-permute-done.3.refs_0_.by_near, bf16[2,1,64,128]{3,2,1,0:T(8,128)(2,1)S(1)} %collective-permute-done.10.in_far, f32[128,128]{1,0:T(8,128)S(1)} %get-tuple-element.46.far_slope, ...), custom_call_target="tpu_custom_call" | custom-call | tf_op jit(solution)/shard_map/pallas_call | solution.py:371
  34.2 0.6 %collective-permute-done.11.other = bf16[432,128]{1,0:T(8,128)(2,1)S(1)} collective-permute-done((bf16[432,128]{1,0:T(8,128)(2,1)S(1)}, bf16[432,128]{1,0:T(8,128)(2,1)S(1)}, u32[]{:S(2)}, u32[]{:S(2)}) %collective-permute-start.11) | collective-permute-done | bytes 110624 | tf_op jit(solution)/shard_map/ppermute | solution.py:41
  34.8 3.1 %collective-permute-start.14 = (bf16[432,128]{1,0:T(8,128)(2,1)S(1)}, bf16[432,128]{1,0:T(8,128)(2,1)S(1)}, u32[]{:S(2)}, u32[]{:S(2)}) collective-permute-start(bf16[432,128]{1,0:T(8,128)(2,1)S(1)} %shard_map.60.refs_0_.refs_4_), channel_id=1, source_target_pairs={{0,6},{1,7},{2,4},{3,5},{4,2},{5,3},{6,0},{7,1},{8,14},{9,15},{10,... | collective-permute-start | bytes 331784 | tf_op jit(solution)/shard_map/ppermute | solution.py:41
  38.0 3.1 %collective-permute-start.13 = (bf16[432,128]{1,0:T(8,128)(2,1)S(1)}, bf16[432,128]{1,0:T(8,128)(2,1)S(1)}, u32[]{:S(2)}, u32[]{:S(2)}) collective-permute-start(bf16[432,128]{1,0:T(8,128)(2,1)S(1)} %shard_map.60.refs_0_.refs_4_), channel_id=1, source_target_pairs={{0,2},{1,3},{2,0},{3,1},{4,6},{5,7},{6,4},{7,5},{8,10},{9,11},{10,... | collective-permute-start | bytes 331784 | tf_op jit(solution)/shard_map/ppermute | solution.py:41
  41.0 0.5 collective-permute-start.12
  41.5 0.5 collective-permute-start.15
  42.0 0.0 collective-permute-done.14.refs_3_.refs_7_
  42.0 2.0 %collective-permute-start.18 = (bf16[432,128]{1,0:T(8,128)(2,1)S(1)}, bf16[432,128]{1,0:T(8,128)(2,1)S(1)}, u32[]{:S(2)}, u32[]{:S(2)}) collective-permute-start(bf16[432,128]{1,0:T(8,128)(2,1)S(1)} %collective-permute-done.14.refs_3_.refs_7_), channel_id=1, source_target_pairs={{0,1},{1,0},{2,3},{3,2},{4,5},{5,4},{6,7},{7,6},{8,9},{9,8},{10,11... | collective-permute-start | bytes 331784 | tf_op jit(solution)/shard_map/ppermute | solution.py:41
  44.0 2.0 %collective-permute-done.13.refs_2_.refs_6_ = bf16[432,128]{1,0:T(8,128)(2,1)S(1)} collective-permute-done((bf16[432,128]{1,0:T(8,128)(2,1)S(1)}, bf16[432,128]{1,0:T(8,128)(2,1)S(1)}, u32[]{:S(2)}, u32[]{:S(2)}) %collective-permute-start.13) | collective-permute-done | bytes 110624 | tf_op jit(solution)/shard_map/ppermute | solution.py:41
  46.0 0.0 collective-permute-start.17
  46.0 1.3 %collective-permute-done.12.refs_1_.refs_5_ = bf16[432,128]{1,0:T(8,128)(2,1)S(1)} collective-permute-done((bf16[432,128]{1,0:T(8,128)(2,1)S(1)}, bf16[432,128]{1,0:T(8,128)(2,1)S(1)}, u32[]{:S(2)}, u32[]{:S(2)}) %collective-permute-start.12) | collective-permute-done | bytes 110624 | tf_op jit(solution)/shard_map/ppermute | solution.py:41
  47.3 0.0 collective-permute-start.16
  47.3 0.1 shard_map.61.refs_0_
  47.4 1.2 %collective-permute-start.20 = (f32[8,128]{1,0:T(8,128)S(1)}, f32[8,128]{1,0:T(8,128)S(1)}, u32[]{:S(2)}, u32[]{:S(2)}) collective-permute-start(f32[8,128]{1,0:T(8,128)S(1)} %shard_map.61.refs_0_), channel_id=1, source_target_pairs={{0,17},{1,16},{2,19},{3,18},{4,21},{5,20},{6,23},{7,22},{8,25},{9,... | collective-permute-start | bytes 12296 | tf_op jit(solution)/shard_map/ppermute | solution.py:53
  48.6 0.0 collective-permute-done.15.refs_0_.refs_8_
  48.6 1.0 %collective-permute-start.19 = (f32[8,128]{1,0:T(8,128)S(1)}, f32[8,128]{1,0:T(8,128)S(1)}, u32[]{:S(2)}, u32[]{:S(2)}) collective-permute-start(f32[8,128]{1,0:T(8,128)S(1)} %shard_map.61.refs_0_), channel_id=1, source_target_pairs={{0,16},{1,17},{2,18},{3,19},{4,20},{5,21},{6,22},{7,23},{8,24},{9,... | collective-permute-start | bytes 12296 | tf_op jit(solution)/shard_map/ppermute | solution.py:53
  49.6 0.0 collective-permute-done.18.refs_3_.refs_11_
  49.6 0.1 shard_map.62.refs_1_
  49.8 0.8 %collective-permute-done.20.refs_3_ = f32[8,128]{1,0:T(8,128)S(1)} collective-permute-done((f32[8,128]{1,0:T(8,128)S(1)}, f32[8,128]{1,0:T(8,128)S(1)}, u32[]{:S(2)}, u32[]{:S(2)}) %collective-permute-start.20) | collective-permute-done | bytes 4128 | tf_op jit(solution)/shard_map/ppermute | solution.py:53
  50.5 1.7 %collective-permute-done.19.refs_2_ = f32[8,128]{1,0:T(8,128)S(1)} collective-permute-done((f32[8,128]{1,0:T(8,128)S(1)}, f32[8,128]{1,0:T(8,128)S(1)}, u32[]{:S(2)}, u32[]{:S(2)}) %collective-permute-start.19) | collective-permute-done | bytes 4128 | tf_op jit(solution)/shard_map/ppermute | solution.py:53
  52.2 1.4 %shard_map.63 = f32[8,432,128]{2,1,0:T(8,128)} custom-call(s32[1]{0:T(128)} %bitcast.spot, f32[8,128]{1,0:T(8,128)S(1)} %shard_map.61.refs_0_, f32[8,128]{1,0:T(8,128)S(1)} %shard_map.62.refs_1_, f32[8,128]{1,0:T(8,128)S(1)} %collective-permute-done.19.refs_2_, f32[8,128]{1,0:T(8,128)S(1)} %collective-permute-done.20.refs_3_, ...), custom_call_target="tpu_custom_call" | custom-call | tf_op jit(solution)/shard_map/pallas_call | solution.py:509
  (8 shorter events, 0.1 us)
Async XLA Ops:
  1.8 3.4 %collective-permute-start = (bf16[2,3,64,128]{3,2,1,0:T(8,128)(2,1)S(1)}, bf16[2,3,64,128]{3,2,1,0:T(8,128)(2,1)S(1)}, u32[]{:S(2)}, u32[]{:S(2)}) collective-permute-start(bf16[2,3,64,128]{3,2,1,0:T(8,128)(2,1)S(1)} %get-tuple-element.26), channel_id=1, source_target_pairs={{0,1},{1,0},{2,3},{3,2},{4,5},{5,4},{6,7},{7,6},{8,9},{9,8},{10,11... | collective-permute-start | bytes 294920 | tf_op jit(solution)/shard_map/ppermute | solution.py:26
  2.4 2.9 %collective-permute-start.1 = (bf16[2,3,64,128]{3,2,1,0:T(8,128)(2,1)S(1)}, bf16[2,3,64,128]{3,2,1,0:T(8,128)(2,1)S(1)}, u32[]{:S(2)}, u32[]{:S(2)}) collective-permute-start(bf16[2,3,64,128]{3,2,1,0:T(8,128)(2,1)S(1)} %get-tuple-element.27), channel_id=1, source_target_pairs={{1,2},{2,1},{3,4},{4,3},{5,6},{6,5},{7,8},{8,7},{9,10},{10,9},{11,... | collective-permute-start | bytes 294920 | tf_op jit(solution)/shard_map/ppermute | solution.py:26
  7.2 5.5 %collective-permute-start.2 = (bf16[2,4,64,128]{3,2,1,0:T(8,128)(2,1)S(1)}, bf16[2,4,64,128]{3,2,1,0:T(8,128)(2,1)S(1)}, u32[]{:S(2)}, u32[]{:S(2)}) collective-permute-start(bf16[2,4,64,128]{3,2,1,0:T(8,128)(2,1)S(1)} %get-tuple-element.33.after), channel_id=1, source_target_pairs={{0,16},{1,17},{2,18},{3,19},{4,20},{5,21},{6,22},{7,23},{8,24},{9,... | collective-permute-start | bytes 393224 | tf_op jit(solution)/shard_map/ppermute | solution.py:53
  13.9 3.6 %collective-permute-start.8 = (bf16[432,128]{1,0:T(8,128)(2,1)S(1)}, bf16[432,128]{1,0:T(8,128)(2,1)S(1)}, u32[]{:S(2)}, u32[]{:S(2)}) collective-permute-start(bf16[432,128]{1,0:T(8,128)(2,1)S(1)} %get-tuple-element.39), channel_id=1, source_target_pairs={{0,1},{1,0},{2,3},{3,2},{4,5},{5,4},{6,7},{7,6},{8,9},{9,8},{10,11... | collective-permute-start | bytes 331784 | tf_op jit(solution)/shard_map/ppermute | solution.py:41
  16.6 5.9 %collective-permute-start.4 = (bf16[432,128]{1,0:T(8,128)(2,1)S(1)}, bf16[432,128]{1,0:T(8,128)(2,1)S(1)}, u32[]{:S(2)}, u32[]{:S(2)}) collective-permute-start(bf16[432,128]{1,0:T(8,128)(2,1)S(1)} %get-tuple-element.37), channel_id=1, source_target_pairs={{0,1},{1,0},{2,3},{3,2},{4,5},{5,4},{6,7},{7,6},{8,9},{9,8},{10,11... | collective-permute-start | bytes 331784 | tf_op jit(solution)/shard_map/ppermute | solution.py:41
  16.7 7.4 %collective-permute-start.6 = (bf16[432,128]{1,0:T(8,128)(2,1)S(1)}, bf16[432,128]{1,0:T(8,128)(2,1)S(1)}, u32[]{:S(2)}, u32[]{:S(2)}) collective-permute-start(bf16[432,128]{1,0:T(8,128)(2,1)S(1)} %get-tuple-element.38), channel_id=1, source_target_pairs={{0,1},{1,0},{2,3},{3,2},{4,5},{5,4},{6,7},{7,6},{8,9},{9,8},{10,11... | collective-permute-start | bytes 331784 | tf_op jit(solution)/shard_map/ppermute | solution.py:41
  17.1 8.9 %collective-permute-start.3 = (bf16[560,128]{1,0:T(8,128)(2,1)S(1)}, bf16[560,128]{1,0:T(8,128)(2,1)S(1)}, u32[]{:S(2)}, u32[]{:S(2)}) collective-permute-start(bf16[560,128]{1,0:T(8,128)(2,1)S(1)} %get-tuple-element.36), channel_id=1, source_target_pairs={{0,1},{1,0},{2,3},{3,2},{4,5},{5,4},{6,7},{7,6},{8,9},{9,8},{10,11... | collective-permute-start | bytes 430088 | tf_op jit(solution)/shard_map/ppermute | solution.py:41
  17.6 8.4 %collective-permute-start.9 = (bf16[432,128]{1,0:T(8,128)(2,1)S(1)}, bf16[432,128]{1,0:T(8,128)(2,1)S(1)}, u32[]{:S(2)}, u32[]{:S(2)}) collective-permute-start(bf16[432,128]{1,0:T(8,128)(2,1)S(1)} %shard_map.57), channel_id=1, source_target_pairs={{0,6},{1,7},{2,4},{3,5},{4,2},{5,3},{6,0},{7,1},{8,14},{9,15},{10,... | collective-permute-start | bytes 331784 | tf_op jit(solution)/shard_map/ppermute | solution.py:41
  22.6 5.7 %collective-permute-start.5 = (bf16[432,128]{1,0:T(8,128)(2,1)S(1)}, bf16[432,128]{1,0:T(8,128)(2,1)S(1)}, u32[]{:S(2)}, u32[]{:S(2)}) collective-permute-start(bf16[432,128]{1,0:T(8,128)(2,1)S(1)} %shard_map.55), channel_id=1, source_target_pairs={{0,2},{1,3},{2,0},{3,1},{4,6},{5,7},{6,4},{7,5},{8,10},{9,11},{10,... | collective-permute-start | bytes 331784 | tf_op jit(solution)/shard_map/ppermute | solution.py:41
  24.1 4.8 %collective-permute-start.7 = (bf16[432,128]{1,0:T(8,128)(2,1)S(1)}, bf16[432,128]{1,0:T(8,128)(2,1)S(1)}, u32[]{:S(2)}, u32[]{:S(2)}) collective-permute-start(bf16[432,128]{1,0:T(8,128)(2,1)S(1)} %shard_map.56), channel_id=1, source_target_pairs={{0,4},{1,5},{2,6},{3,7},{4,0},{5,1},{6,2},{7,3},{8,12},{9,13},{10,... | collective-permute-start | bytes 331784 | tf_op jit(solution)/shard_map/ppermute | solution.py:41
  24.1 0.7 %collective-permute-start.10 = (bf16[2,1,64,128]{3,2,1,0:T(8,128)(2,1)S(1)}, bf16[2,1,64,128]{3,2,1,0:T(8,128)(2,1)S(1)}, u32[]{:S(2)}, u32[]{:S(2)}) collective-permute-start(bf16[2,1,64,128]{3,2,1,0:T(8,128)(2,1)S(1)} %get-tuple-element.42), channel_id=1, source_target_pairs={{1,18},{2,17},{3,20},{4,19},{5,22},{6,21},{7,24},{8,23},{9,26},{10... | collective-permute-start | bytes 98312 | tf_op jit(solution)/shard_map/ppermute | solution.py:36
  29.0 5.9 %collective-permute-start.11 = (bf16[432,128]{1,0:T(8,128)(2,1)S(1)}, bf16[432,128]{1,0:T(8,128)(2,1)S(1)}, u32[]{:S(2)}, u32[]{:S(2)}) collective-permute-start(bf16[432,128]{1,0:T(8,128)(2,1)S(1)} %shard_map.58.mine), channel_id=1, source_target_pairs={{0,9},{1,8},{2,11},{3,10},{4,13},{5,12},{6,15},{7,14},{8,1},{9,0},... | collective-permute-start | bytes 331784 | tf_op jit(solution)/shard_map/ppermute | solution.py:41
  34.8 7.2 %collective-permute-start.14 = (bf16[432,128]{1,0:T(8,128)(2,1)S(1)}, bf16[432,128]{1,0:T(8,128)(2,1)S(1)}, u32[]{:S(2)}, u32[]{:S(2)}) collective-permute-start(bf16[432,128]{1,0:T(8,128)(2,1)S(1)} %shard_map.60.refs_0_.refs_4_), channel_id=1, source_target_pairs={{0,6},{1,7},{2,4},{3,5},{4,2},{5,3},{6,0},{7,1},{8,14},{9,15},{10,... | collective-permute-start | bytes 331784 | tf_op jit(solution)/shard_map/ppermute | solution.py:41
  38.0 8.0 %collective-permute-start.13 = (bf16[432,128]{1,0:T(8,128)(2,1)S(1)}, bf16[432,128]{1,0:T(8,128)(2,1)S(1)}, u32[]{:S(2)}, u32[]{:S(2)}) collective-permute-start(bf16[432,128]{1,0:T(8,128)(2,1)S(1)} %shard_map.60.refs_0_.refs_4_), channel_id=1, source_target_pairs={{0,2},{1,3},{2,0},{3,1},{4,6},{5,7},{6,4},{7,5},{8,10},{9,11},{10,... | collective-permute-start | bytes 331784 | tf_op jit(solution)/shard_map/ppermute | solution.py:41
  41.0 6.2 %collective-permute-start.12 = (bf16[432,128]{1,0:T(8,128)(2,1)S(1)}, bf16[432,128]{1,0:T(8,128)(2,1)S(1)}, u32[]{:S(2)}, u32[]{:S(2)}) collective-permute-start(bf16[432,128]{1,0:T(8,128)(2,1)S(1)} %shard_map.60.refs_0_.refs_4_), channel_id=1, source_target_pairs={{0,4},{1,5},{2,6},{3,7},{4,0},{5,1},{6,2},{7,3},{8,12},{9,13},{10,... | collective-permute-start | bytes 331784 | tf_op jit(solution)/shard_map/ppermute | solution.py:41
  41.5 7.1 %collective-permute-start.15 = (bf16[432,128]{1,0:T(8,128)(2,1)S(1)}, bf16[432,128]{1,0:T(8,128)(2,1)S(1)}, u32[]{:S(2)}, u32[]{:S(2)}) collective-permute-start(bf16[432,128]{1,0:T(8,128)(2,1)S(1)} %shard_map.60.refs_0_.refs_4_), channel_id=1, source_target_pairs={{0,1},{1,0},{2,3},{3,2},{4,5},{5,4},{6,7},{7,6},{8,9},{9,8},{10,11... | collective-permute-start | bytes 331784 | tf_op jit(solution)/shard_map/ppermute | solution.py:41
  42.0 7.6 %collective-permute-start.18 = (bf16[432,128]{1,0:T(8,128)(2,1)S(1)}, bf16[432,128]{1,0:T(8,128)(2,1)S(1)}, u32[]{:S(2)}, u32[]{:S(2)}) collective-permute-start(bf16[432,128]{1,0:T(8,128)(2,1)S(1)} %collective-permute-done.14.refs_3_.refs_7_), channel_id=1, source_target_pairs={{0,1},{1,0},{2,3},{3,2},{4,5},{5,4},{6,7},{7,6},{8,9},{9,8},{10,11... | collective-permute-start | bytes 331784 | tf_op jit(solution)/shard_map/ppermute | solution.py:41
  46.0 3.7 %collective-permute-start.17 = (bf16[432,128]{1,0:T(8,128)(2,1)S(1)}, bf16[432,128]{1,0:T(8,128)(2,1)S(1)}, u32[]{:S(2)}, u32[]{:S(2)}) collective-permute-start(bf16[432,128]{1,0:T(8,128)(2,1)S(1)} %collective-permute-done.13.refs_2_.refs_6_), channel_id=1, source_target_pairs={{0,1},{1,0},{2,3},{3,2},{4,5},{5,4},{6,7},{7,6},{8,9},{9,8},{10,11... | collective-permute-start | bytes 331784 | tf_op jit(solution)/shard_map/ppermute | solution.py:41
  47.3 2.3 %collective-permute-start.16 = (bf16[432,128]{1,0:T(8,128)(2,1)S(1)}, bf16[432,128]{1,0:T(8,128)(2,1)S(1)}, u32[]{:S(2)}, u32[]{:S(2)}) collective-permute-start(bf16[432,128]{1,0:T(8,128)(2,1)S(1)} %collective-permute-done.12.refs_1_.refs_5_), channel_id=1, source_target_pairs={{0,1},{1,0},{2,3},{3,2},{4,5},{5,4},{6,7},{7,6},{8,9},{9,8},{10,11... | collective-permute-start | bytes 331784 | tf_op jit(solution)/shard_map/ppermute | solution.py:41
  47.4 3.1 %collective-permute-start.20 = (f32[8,128]{1,0:T(8,128)S(1)}, f32[8,128]{1,0:T(8,128)S(1)}, u32[]{:S(2)}, u32[]{:S(2)}) collective-permute-start(f32[8,128]{1,0:T(8,128)S(1)} %shard_map.61.refs_0_), channel_id=1, source_target_pairs={{0,17},{1,16},{2,19},{3,18},{4,21},{5,20},{6,23},{7,22},{8,25},{9,... | collective-permute-start | bytes 12296 | tf_op jit(solution)/shard_map/ppermute | solution.py:53
  48.6 3.6 %collective-permute-start.19 = (f32[8,128]{1,0:T(8,128)S(1)}, f32[8,128]{1,0:T(8,128)S(1)}, u32[]{:S(2)}, u32[]{:S(2)}) collective-permute-start(f32[8,128]{1,0:T(8,128)S(1)} %shard_map.61.refs_0_), channel_id=1, source_target_pairs={{0,16},{1,17},{2,18},{3,19},{4,20},{5,21},{6,22},{7,23},{8,24},{9,... | collective-permute-start | bytes 12296 | tf_op jit(solution)/shard_map/ppermute | solution.py:53

commit v9 on v8

--- a/solution.py
+++ b/solution.py
@@ -24,16 +24,6 @@
     count = lax.axis_size("slab")
     near = [(i, i ^ 1) for i in range(count)]
     return lax.ppermute(to_near, "slab", near), lax.ppermute(to_far, "slab", far_route(count))
-
-
-def cross_far(value):
-    segments, count = lax.axis_size("segment"), lax.axis_size("slab")
-    route = [
-        (s * count + i, (s - 1) % segments * count + j)
-        for s in range(segments)
-        for i, j in far_route(count)
-    ]
-    return lax.ppermute(value, ("segment", "slab"), route)
 
 
 def exchange(value, mask):
@@ -136,9 +126,8 @@
 
 
 def first_kernel(
-    height, near, far, grad, weight, mirror, part, result, slopes, to_far, *refs
+    height, near, far, grad, weight, mirror, part, result, slopes, rim, shifts
 ):
-    rim, shifts = refs[-2:]
     micro, depth, cells, channels = grad.shape
     even = lax.rem(lax.axis_index("slab"), 2) == 0
     block, span = micro * cells, 9 * channels
@@ -169,7 +158,8 @@
             preact = preact + term
         sig = 1.0 / (1.0 + jnp.exp(-preact))
         slope = sig * (1.0 + preact * (1.0 - sig))
-        slopes[rows, :] = slope
+        if 0 < n <= depth:
+            slopes[(n - 1) * block : n * block, :] = slope
         for m in range(micro):
             if n == 0 or n == depth + 1:
                 up = pick(m, 2, n == 0)
@@ -179,17 +169,10 @@
             write_shifts(delta, height, shifts, n * block + m * cells)
     back = back_product(shifts, mirror, block, depth)
     for m in range(micro):
-        ends = []
         for n in range(depth):
             first = n * block + m * cells
             total = grad[m, n].astype(F32) + back[first : first + cells]
             result[m, n] = total.astype(BF16)
-            if n in (0, depth - 1):
-                ends.append(total)
-        low, high = ends[0], ends[-1]
-        for to_near in refs[:-2]:
-            to_near[m, 0] = jnp.where(even, high, low).astype(BF16)
-        to_far[m, 0] = jnp.where(even, low, high).astype(BF16)
 
 
 def shift_kernel(height, acts, near, far, after, shifts):
@@ -203,39 +186,32 @@
             write_shifts(plane, height, shifts, (n * micro + m) * cells)
 
 
-def raw_kernel(
-    spot, incoming, grad, far, slopes, shifts, upstream, deltas, far_slope, *refs
-):
+def raw_kernel(spot, incoming, grad, slopes, shifts, upstream, deltas, far_rim, *refs):
     sends, (keep, raw) = refs[:4], refs[4:]
     part = keep.shape[1]
     micro, depth, cells, channels = upstream.shape
     block, span = micro * cells, 9 * channels
     last = lax.axis_index("segment") == lax.axis_size("segment") - 1
     even = lax.rem(lax.axis_index("slab"), 2) == 0
-    low, high = slice(0, block), slice((depth + 1) * block, (depth + 2) * block)
-    slope = jnp.where(even, slopes[low, :], slopes[high, :])
-    far_slope[...] = slope
     for m in range(micro):
-        inside = slice(m * cells, (m + 1) * cells)
-        rim = (far[m, 2].astype(F32) * slope[inside]).astype(BF16)
-        for first in (low.start, high.start):
-            deltas[first + m * cells : first + (m + 1) * cells, :] = rim
         planes = []
         for n in range(depth):
             up = jnp.where(last, grad[m, n].astype(F32), incoming[m, n].astype(F32))
             upstream[m, n] = up.astype(BF16)
-            first = (n + 1) * block + m * cells
+            first = n * block + m * cells
             delta = up * slopes[first : first + cells, :]
             deltas[first : first + cells, :] = delta.astype(BF16)
             planes.append(delta)
+        low, high = planes[0], planes[-1]
+        far_rim[m * cells : (m + 1) * cells, :] = jnp.where(even, low, high).astype(BF16)
         first = part + m * cells
-        sends[0][first : first + cells, :] = jnp.where(even, planes[-1], planes[0]).astype(BF16)
+        sends[0][first : first + cells, :] = jnp.where(even, high, low).astype(BF16)
     for dz in range(3):
         total = None
         for n in range(depth):
             term = lax.dot_general(
                 shifts[(dz + n) * block : (dz + n + 1) * block, :],
-                deltas[(n + 1) * block : (n + 2) * block, :],
+                deltas[n * block : (n + 1) * block, :],
                 (((0,), (0,)), ((), ())),
                 preferred_element_type=F32,
             )
@@ -246,19 +222,26 @@
         sends[turn][:part, :] = raw[pl.ds((spot[0] ^ turn ^ 4) * part, part), :].astype(BF16)
 
 
-def add_kernel(turn, keep, got, out):
-    out[...] = (keep[turn] + got[...].astype(F32)).astype(BF16)
-
-
-def sum_kernel(keep, *refs):
-    total = keep[0]
-    for got in refs[:-1]:
-        total = total + got[: total.shape[0], :].astype(F32)
-    refs[-1][...] = total.astype(refs[-1].dtype)
+def add_kernel(turn, keep, got, *refs):
+    rows, out = keep.shape[1], refs[-1]
+    out[:rows, :] = (keep[turn] + got[...].astype(F32)).astype(BF16)
+    if len(refs) > 1:
+        out[rows:, :] = refs[0][...]
+
+
+def sum_kernel(count, keep, *refs):
+    total, out = keep[0], refs[-1]
+    rows = total.shape[0]
+    for got in refs[:count]:
+        total = total + got[:rows, :].astype(F32)
+    out[:rows, :] = total.astype(out.dtype)
+    if out.shape[0] > rows:
+        out[rows:, :] = refs[count][...]
 
 
 def both_kernel(mine, other, out):
-    out[...] = (mine[...].astype(F32) + other[...].astype(F32)).astype(BF16)
+    rows = out.shape[0]
+    out[...] = (mine[:rows, :].astype(F32) + other[:rows, :].astype(F32)).astype(BF16)
 
 
 def column_squares(value):
@@ -273,25 +256,32 @@
     refs[-1][...] = jnp.broadcast_to(sums[0], refs[-1].shape)
 
 
-def back_kernel(
-    height, deltas, by_near, in_far, far_slope, upstream, mirror, out, shifts
-):
+def back_kernel(height, riders, deltas, by_near, upstream, mirror, *refs):
+    by_far, (out, shifts) = refs[:-2], refs[-2:]
     micro, depth, cells, channels = upstream.shape
     block = micro * cells
-    last = lax.axis_index("segment") == lax.axis_size("segment") - 1
-    even = lax.rem(lax.axis_index("slab"), 2) == 0
-    start = by_near.shape[0] - block
+    index = lax.axis_index("slab")
+    even = lax.rem(index, 2) == 0
+    link = index ^ jnp.where(even, index - 1, index + 1)
+
+    def tail(ref, m):
+        start = ref.shape[0] - block + m * cells
+        return ref[start : start + cells, :].astype(F32)
+
     for m in range(micro):
-        inside = slice(m * cells, (m + 1) * cells)
-        near = by_near[start + m * cells : start + (m + 1) * cells, :].astype(F32)
-        far = (in_far[m, 0].astype(F32) * far_slope[inside, :]).astype(BF16).astype(F32)
-        far = jnp.where(last, deltas[inside, :].astype(F32), far)
+        near = tail(by_near, m)
+        if riders:
+            far = jnp.zeros((cells, channels), F32)
+            for mask, ref in zip(riders, by_far, strict=True):
+                far = jnp.where(link == mask, tail(ref, m), far)
+        else:
+            far = tail(by_far[0], m)
         write_shifts(jnp.where(even, far, near), height, shifts, m * cells)
         first = (depth + 1) * block + m * cells
         write_shifts(jnp.where(even, near, far), height, shifts, first)
-        for n in range(1, depth + 1):
+        for n in range(depth):
             first = n * block + m * cells
-            write_shifts(deltas[first : first + cells, :], height, shifts, first)
+            write_shifts(deltas[first : first + cells, :], height, shifts, first + block)
     back = back_product(shifts, mirror, block, depth)
     for m in range(micro):
         for n in range(depth):
@@ -355,45 +345,37 @@
         compiler_params=large,
     )(acts, pltpu.with_memory_space_constraint(weight, pltpu.HBM))
 
-    edge = shape((micro, 1, cells, channels), BF16)
     wide = pltpu.VMEM(((depth + 2) * plane, span), BF16)
-    edges = (edge,) * (1 if segments == 2 else 2)
-    result, slopes, to_far, *to_near = pl.pallas_call(
+    inside = shape((depth * plane, channels), F32)
+    result, slopes = pl.pallas_call(
         functools.partial(first_kernel, height),
-        out_shape=(volume, outer) + edges,
+        out_shape=(volume, inside),
         in_specs=[VMEM] * 6,
-        out_specs=(VMEM,) * (2 + len(edges)),
+        out_specs=(VMEM,) * 2,
         scratch_shapes=[pltpu.VMEM((4 * plane, span), BF16), wide],
         compiler_params=large,
     )(near, far, grad, weight, mirror, part)
 
-    def conv_back(deltas, by_near, in_far, far_slope, upstream):
+    def conv_back(riders, deltas, by_near, by_far, upstream):
         return pl.pallas_call(
-            functools.partial(back_kernel, height),
+            functools.partial(back_kernel, height, riders),
             out_shape=volume,
-            in_specs=[VMEM] * 6,
+            in_specs=[VMEM] * (4 + len(by_far)),
             out_specs=VMEM,
             scratch_shapes=[wide],
             compiler_params=large,
-        )(deltas, by_near, in_far, far_slope, upstream, mirror)
-
-    part = weight.shape[0] // 8
+        )(deltas, by_near, upstream, mirror, *by_far)
+
+    part = whole.shape[0] // 8
     even = lax.rem(index, 2) == 0
     for step in range(1, segments - 1):
-        incoming, in_near, in_far = cross(result, 1, 0), cross(to_near[0], 1, 1), cross_far(to_far)
+        incoming = cross(result, 1, 0)
         upstream = jnp.where(last, grad, incoming)
-        stacked = jnp.swapaxes(upstream, 0, 1).reshape(depth * plane, channels).astype(F32)
-        deltas = (stacked * slopes[plane:-plane]).astype(BF16)
-        near_slope = jnp.where(even, slopes[-plane:], slopes[:plane])
-        far_slope = jnp.where(even, slopes[:plane], slopes[-plane:])
-        by_near = jnp.where(last, near[:, 2:], in_near).reshape(plane, channels).astype(F32)
-        rim = (far[:, 2:].reshape(plane, channels).astype(F32) * far_slope).astype(BF16)
-        deltas = jnp.concatenate([rim, deltas, rim], axis=0)
-        result = conv_back(
-            deltas, (by_near * near_slope).astype(BF16), in_far, far_slope, upstream
-        )
-        low, high = result[:, :1], result[:, -1:]
-        to_near, to_far = [jnp.where(even, high, low)], jnp.where(even, low, high)
+        stacked = jnp.swapaxes(upstream, 0, 1).reshape(inside.shape).astype(F32)
+        deltas = (stacked * slopes).astype(BF16)
+        low, high = deltas[:plane], deltas[-plane:]
+        by_near, by_far = swap(jnp.where(even, high, low), jnp.where(even, low, high))
+        result = conv_back((), deltas, by_near, [by_far], upstream)
     incoming = cross(result, 1, 0)
     shifts = pl.pallas_call(
         functools.partial(shift_kernel, height),
@@ -407,54 +389,57 @@
     crossing = inner[-1][0] if len(inner[-1]) == 1 else 0
     side = lax.rem(index, 2) ^ jnp.where(index & crossing, 1, 0)
     quarter = jnp.where(index & 2, 2, 0) + jnp.where(index & 4, 1, 0)
-    masks = {1: 4, 2: 2, 3: 6}
+    masks, across_mask, riders = {1: 4, 2: 2, 3: 6}, crossing | 1, ()
+    if count == 16:
+        side = lax.rem(index, 2) ^ jnp.where(index & 2, 1, 0)
+        quarter = quarter ^ jnp.where(index & 8, 3, 0)
+        masks, across_mask, riders = {1: 4, 2: 3, 3: 7}, 15, (3, 7, 15)
     spot = (side * 4 + quarter).astype(jnp.int32).reshape(1)
     piece = shape((part, channels), BF16)
-
-    upstream, deltas, far_slope, *rest = pl.pallas_call(
+    longer = shape((part + plane, channels), BF16)
+
+    upstream, deltas, far_rim, *rest = pl.pallas_call(
         raw_kernel,
         out_shape=(
             volume,
-            shape(outer.shape, BF16),
-            shape((plane, channels), F32),
-            shape((part + plane, channels), BF16),
+            shape(inside.shape, BF16),
+            shape((plane, channels), BF16),
+            longer,
             piece,
             piece,
             piece,
             shape((4, part, channels), F32),
         ),
-        in_specs=[SMEM] + [VMEM] * 5,
+        in_specs=[SMEM] + [VMEM] * 4,
         out_specs=(VMEM,) * 8,
         scratch_shapes=[pltpu.VMEM((8 * part, channels), F32)],
         compiler_params=large,
-    )(spot, incoming, grad, far, slopes, shifts)
+    )(spot, incoming, grad, slopes, shifts)
     sends, keep = rest[:4], rest[4]
     order = (2, 1, 3)
     got = {turn: exchange(sends[turn], 1) for turn in order + (0,)}
-    across = []
+    across = {}
     for turn in order:
+        rides = masks[turn] in riders
         added = pl.pallas_call(
             functools.partial(add_kernel, turn),
-            out_shape=piece,
-            in_specs=[VMEM] * 2,
+            out_shape=longer if rides else piece,
+            in_specs=[VMEM] * (3 if rides else 2),
             out_specs=VMEM,
             compiler_params=small,
-        )(keep, got[turn])
-        if turn == order[-1]:
-            added, to_far = lax.optimization_barrier((added, to_far))
-        across.append(exchange(added, masks[turn]))
-    in_far = cross_far(to_far)
-    across[2], in_far = lax.optimization_barrier((across[2], in_far))
-    gradients = conv_back(deltas, got[0], in_far, far_slope, upstream)
+        )(keep, got[turn], *([far_rim] if rides else []))
+        across[turn] = exchange(added, masks[turn])
     single = len(inner[-1]) == 1
     direct = single and len(inner) == 1
+    rides = across_mask in riders
+    rows = part + plane if rides else part
     chunk = pl.pallas_call(
-        sum_kernel,
-        out_shape=shape((part, channels), BF16 if direct else F32),
-        in_specs=[VMEM] * 5,
+        functools.partial(sum_kernel, 4),
+        out_shape=shape((rows, channels), BF16 if direct else F32),
+        in_specs=[VMEM] * (6 if rides else 5),
         out_specs=VMEM,
         compiler_params=small,
-    )(keep, got[0], *across)
+    )(keep, got[0], *across.values(), *([far_rim] if rides else []))
 
     def places(group):
         own = sum(jnp.where(index & bit, 1 << n, 0) for n, bit in enumerate(group))
@@ -471,11 +456,10 @@
         chunk = block(chunk, own, size, F32) + sum(g.astype(F32) for g in took)
     gathered = chunk.astype(BF16)
     if single:
-        other = exchange(gathered, crossing | 1)
-        other, gradients = lax.optimization_barrier((other, gradients))
+        other = exchange(gathered, across_mask)
         gathered = pl.pallas_call(
             both_kernel,
-            out_shape=shape(gathered.shape, BF16),
+            out_shape=piece if rides else shape(gathered.shape, BF16),
             in_specs=[VMEM] * 2,
             out_specs=VMEM,
             compiler_params=small,
@@ -492,6 +476,12 @@
             blocks.append(value)
         gathered = jnp.concatenate(blocks, axis=0)
     pieces = {turn: exchange(gathered, masks[turn]) for turn in (2, 1, 3)}
+    if riders:
+        by_far = [across[2], across[3], other]
+    else:
+        by_far = [lax.ppermute(far_rim, "slab", far_route(count))]
+    gradients = conv_back(riders, deltas, got[0], by_far, upstream)
+    pieces[3], gradients = lax.optimization_barrier((pieces[3], gradients))
     ours = [gathered] + [pieces[turn] for turn in (1, 2, 3)]
     theirs = [exchange(piece, 1) for piece in ours]
     sums = [

time: 53.8 us -> 54.8 us (1.019)
  waiting for transfers between devices: 13.6 us -> 19.7 us
  starting transfers between devices: 28.9 us -> 23.8 us
    ppermute x15, waiting for transfers between devices: 8.38 us -> 14 us  [exchange(): return lax.ppermute(value, 'slab', [(i, i ^ mask) for i in range(count)])]
    ppermute x15, starting transfers between devices: 22.3 us -> 18.2 us  [exchange(): return lax.ppermute(value, 'slab', [(i, i ^ mask) for i in range(count)])]
    ppermute x1 -> x0, starting transfers between devices: 0.66 us -> none  [cross_far(): return lax.ppermute(value, ('segment', 'slab'), route)]
  transfers between devices with their start and end apart: 21 -> 20, of which waited for: 10 -> 9; matrix products, arithmetic and copies ran while one was open for 0% -> 0% of each run, Pallas kernels for 9% -> 8%
where the time goes in v9:
time: 54.8 us; the launch traced here: 54.6 us
  starting transfers between devices  23.8 us (43%)
  waiting for transfers between devices  19.7 us (36%)
  Pallas kernels  10.4 us (19%)
  between operations  0.74 us (1%)
    ppermute x15, starting transfers between devices, exchange(): return lax.ppermute(value, 'slab', [(i, i ^ mask) for i in range(count)])  18.2 us
    ppermute x15, waiting for transfers between devices, exchange(): return lax.ppermute(value, 'slab', [(i, i ^ mask) for i in range(count)])  14 us
    ppermute x3, waiting for transfers between devices, cross(): return lax.ppermute(value, ('segment', 'slab'), route)  5.66 us
    ppermute x3, starting transfers between devices, cross(): return lax.ppermute(value, ('segment', 'slab'), route)  4.43 us
    pallas_call x1, Pallas kernels, shards(): pl.pallas_call(functools.partial(own_kernel, height), out_shape=(whole, w...  2.25 us
    pallas_call x1, Pallas kernels, shards(): pl.pallas_call(functools.partial(first_kernel, height), out_shape=(volume...  1.85 us
    pallas_call x1, Pallas kernels, conv_back(): pl.pallas_call(functools.partial(back_kernel, height, riders), out_shape=...  1.79 us
    pallas_call x1, Pallas kernels, shards(): pl.pallas_call(functools.partial(place_kernel, bound, segments), out_shap...  1.38 us
  transfers between devices with their start and end apart: 20, of which 9 were waited for; matrix products, arithmetic and copies ran while one was open for 0% of the time, Pallas kernels for 8%

profile of v9, /device:TPU:0, one launch (start us, length us, event | category | flops | bytes accessed | tf_op | source)
XLA Modules:
  0.0 54.6 jit_solution(5739504662162327063)
XLA Ops:
  0.6 1.2 %shard_map.50 = (bf16[2,3,64,128]{3,2,1,0:T(8,128)(2,1)S(1)}, bf16[2,3,64,128]{3,2,1,0:T(8,128)(2,1)S(1)}, bf16[2,4,64,128]{3,2,1,0:T(8,128)(2,1)S(1)}, bf16[2,4,64,128]{3,2,1,0:T(8,128)(2,1)S(1)}) custom-call(bf16[2,4,64,128]{3,2,1,0:T(8,128)(2,1)} %bitcast.9, bf16[2,4,64,128]{3,2,1,0:T(8,128)(2,1)} %bitcast.10), custom_call_target="tpu_custom_call" | custom-call | tf_op jit(solution)/shard_map/pallas_call | solution.py:326
  1.8 0.5 collective-permute-start
  2.4 0.7 %collective-permute-start.1 = (bf16[2,3,64,128]{3,2,1,0:T(8,128)(2,1)S(1)}, bf16[2,3,64,128]{3,2,1,0:T(8,128)(2,1)S(1)}, u32[]{:S(2)}, u32[]{:S(2)}) collective-permute-start(bf16[2,3,64,128]{3,2,1,0:T(8,128)(2,1)S(1)} %get-tuple-element.22), channel_id=1, source_target_pairs={{1,2},{2,1},{3,4},{4,3},{5,6},{6,5},{7,8},{8,7},{9,10},{10,9},{11,... | collective-permute-start | bytes 294920 | tf_op jit(solution)/shard_map/ppermute | solution.py:26
  3.0 2.3 %shard_map.51 = (bf16[3456,128]{1,0:T(8,128)(2,1)S(1)}, bf16[3456,128]{1,0:T(8,128)(2,1)S(1)}, f32[768,128]{1,0:T(8,128)S(1)}) custom-call(bf16[2,4,64,128]{3,2,1,0:T(8,128)(2,1)S(1)} %get-tuple-element.24.acts, bf16[3456,128]{1,0:T(8,128)(2,1)} %bitcast.7), custom_call_target="tpu_custom_call" | custom-call | tf_op jit(solution)/shard_map/pallas_call | solution.py:339
  5.3 0.0 collective-permute-done.near
  5.3 0.0 collective-permute-done.1.far
  5.3 1.9 %shard_map.52 = (bf16[2,4,64,128]{3,2,1,0:T(8,128)(2,1)S(1)}, f32[512,128]{1,0:T(8,128)S(1)}) custom-call(bf16[2,3,64,128]{3,2,1,0:T(8,128)(2,1)S(1)} %collective-permute-done.near, bf16[2,3,64,128]{3,2,1,0:T(8,128)(2,1)S(1)} %collective-permute-done.1.far, bf16[2,4,64,128]{3,2,1,0:T(8,128)(2,1)S(1)} %get-tuple-element.23.grad, ...), custom_call_target="tpu_custom_call" | custom-call | tf_op jit(solution)/shard_map/pallas_call | solution.py:350
  7.2 2.6 %collective-permute-start.2 = (bf16[2,4,64,128]{3,2,1,0:T(8,128)(2,1)S(1)}, bf16[2,4,64,128]{3,2,1,0:T(8,128)(2,1)S(1)}, u32[]{:S(2)}, u32[]{:S(2)}) collective-permute-start(bf16[2,4,64,128]{3,2,1,0:T(8,128)(2,1)S(1)} %get-tuple-element.28.after), channel_id=1, source_target_pairs={{0,16},{1,17},{2,18},{3,19},{4,20},{5,21},{6,22},{7,23},{8,24},{9,... | collective-permute-start | bytes 393224 | tf_op jit(solution)/shard_map/ppermute | solution.py:43
  9.7 0.2 shard_map.53.shifts
  10.0 2.7 %collective-permute-done.2.incoming = bf16[2,4,64,128]{3,2,1,0:T(8,128)(2,1)S(1)} collective-permute-done((bf16[2,4,64,128]{3,2,1,0:T(8,128)(2,1)S(1)}, bf16[2,4,64,128]{3,2,1,0:T(8,128)(2,1)S(1)}, u32[]{:S(2)}, u32[]{:S(2)}) %collective-permute-start.2) | collective-permute-done | bytes 131104 | tf_op jit(solution)/shard_map/ppermute | solution.py:43
  12.7 1.3 %shard_map.54 = (bf16[2,4,64,128]{3,2,1,0:T(8,128)(2,1)S(1)}, bf16[512,128]{1,0:T(8,128)(2,1)S(1)}, bf16[128,128]{1,0:T(8,128)(2,1)S(1)}, bf16[560,128]{1,0:T(8,...) custom-call(s32[1]{0:T(128)} %bitcast.spot, ...), custom_call_target="tpu_custom_call" | custom-call | tf_op jit(solution)/shard_map/pallas_call | solution.py:401
  13.9 2.6 %collective-permute-start.8 = (bf16[432,128]{1,0:T(8,128)(2,1)S(1)}, bf16[432,128]{1,0:T(8,128)(2,1)S(1)}, u32[]{:S(2)}, u32[]{:S(2)}) collective-permute-start(bf16[432,128]{1,0:T(8,128)(2,1)S(1)} %get-tuple-element.35), channel_id=1, source_target_pairs={{0,1},{1,0},{2,3},{3,2},{4,5},{5,4},{6,7},{7,6},{8,9},{9,8},{10,11... | collective-permute-start | bytes 331784 | tf_op jit(solution)/shard_map/ppermute | solution.py:31
  16.6 0.1 collective-permute-start.4
  16.7 0.4 collective-permute-start.6
  17.1 0.1 collective-permute-start.3
  17.2 0.4 collective-permute-done.8.got
  17.6 4.7 %collective-permute-start.9 = (bf16[560,128]{1,0:T(8,128)(2,1)S(1)}, bf16[560,128]{1,0:T(8,128)(2,1)S(1)}, u32[]{:S(2)}, u32[]{:S(2)}) collective-permute-start(bf16[560,128]{1,0:T(8,128)(2,1)S(1)} %shard_map.57), channel_id=1, source_target_pairs={{0,7},{1,6},{2,5},{3,4},{4,3},{5,2},{6,1},{7,0},{8,15},{9,14},{10,... | collective-permute-start | bytes 430088 | tf_op jit(solution)/shard_map/ppermute | solution.py:31
  22.3 0.0 collective-permute-done.4.got
  22.3 1.4 %collective-permute-start.5 = (bf16[560,128]{1,0:T(8,128)(2,1)S(1)}, bf16[560,128]{1,0:T(8,128)(2,1)S(1)}, u32[]{:S(2)}, u32[]{:S(2)}) collective-permute-start(bf16[560,128]{1,0:T(8,128)(2,1)S(1)} %shard_map.55), channel_id=1, source_target_pairs={{0,3},{1,2},{2,1},{3,0},{4,7},{5,6},{6,5},{7,4},{8,11},{9,10},{10,... | collective-permute-start | bytes 430088 | tf_op jit(solution)/shard_map/ppermute | solution.py:31
  23.8 0.0 collective-permute-done.6.got
  23.8 0.1 collective-permute-start.7
  23.9 0.0 collective-permute-done.3.refs_0_.by_near
  23.9 5.5 %collective-permute-done.7.refs_2_ = bf16[432,128]{1,0:T(8,128)(2,1)S(1)} collective-permute-done((bf16[432,128]{1,0:T(8,128)(2,1)S(1)}, bf16[432,128]{1,0:T(8,128)(2,1)S(1)}, u32[]{:S(2)}, u32[]{:S(2)}) %collective-permute-start.7) | collective-permute-done | bytes 110624 | tf_op jit(solution)/shard_map/ppermute | solution.py:31
  29.4 0.0 collective-permute-done.9.refs_3_.refs_1_
  29.4 0.2 collective-permute-done.5.refs_1_.refs_0_
  29.6 0.1 shard_map.58.mine
  29.7 3.7 %collective-permute-start.10 = (bf16[560,128]{1,0:T(8,128)(2,1)S(1)}, bf16[560,128]{1,0:T(8,128)(2,1)S(1)}, u32[]{:S(2)}, u32[]{:S(2)}) collective-permute-start(bf16[560,128]{1,0:T(8,128)(2,1)S(1)} %shard_map.58.mine), channel_id=1, source_target_pairs={{0,15},{1,14},{2,13},{3,12},{4,11},{5,10},{6,9},{7,8},{8,7},{9,6},... | collective-permute-start | bytes 430088 | tf_op jit(solution)/shard_map/ppermute | solution.py:31
  33.4 4.9 %collective-permute-done.10.other.refs_2_ = bf16[560,128]{1,0:T(8,128)(2,1)S(1)} collective-permute-done((bf16[560,128]{1,0:T(8,128)(2,1)S(1)}, bf16[560,128]{1,0:T(8,128)(2,1)S(1)}, u32[]{:S(2)}, u32[]{:S(2)}) %collective-permute-start.10) | collective-permute-done | bytes 143392 | tf_op jit(solution)/shard_map/ppermute | solution.py:31
  38.4 3.4 %collective-permute-start.13 = (bf16[432,128]{1,0:T(8,128)(2,1)S(1)}, bf16[432,128]{1,0:T(8,128)(2,1)S(1)}, u32[]{:S(2)}, u32[]{:S(2)}) collective-permute-start(bf16[432,128]{1,0:T(8,128)(2,1)S(1)} %shard_map.59.refs_0_.refs_4_), channel_id=1, source_target_pairs={{0,7},{1,6},{2,5},{3,4},{4,3},{5,2},{6,1},{7,0},{8,15},{9,14},{10,... | collective-permute-start | bytes 331784 | tf_op jit(solution)/shard_map/ppermute | solution.py:31
  41.7 0.9 %collective-permute-start.12 = (bf16[432,128]{1,0:T(8,128)(2,1)S(1)}, bf16[432,128]{1,0:T(8,128)(2,1)S(1)}, u32[]{:S(2)}, u32[]{:S(2)}) collective-permute-start(bf16[432,128]{1,0:T(8,128)(2,1)S(1)} %shard_map.59.refs_0_.refs_4_), channel_id=1, source_target_pairs={{0,3},{1,2},{2,1},{3,0},{4,7},{5,6},{6,5},{7,4},{8,11},{9,10},{10,... | collective-permute-start | bytes 331784 | tf_op jit(solution)/shard_map/ppermute | solution.py:31
  42.6 0.2 collective-permute-start.14
  42.8 1.8 %shard_map.60 = bf16[2,4,64,128]{3,2,1,0:T(8,128)(2,1)} custom-call(bf16[512,128]{1,0:T(8,128)(2,1)S(1)} %get-tuple-element.36.deltas, bf16[560,128]{1,0:T(8,128)(2,1)S(1)} %collective-permute-done.3.refs_0_.by_near, bf16[2,4,64,128]{3,2,1,0:T(8,128)(2,1)S(1)} %get-tuple-element.37.upstream, bf16[3456,128]{1,0:T(8,128)(2,1)S(1)} %get-tuple-element.26.mirror, ...), custom_call_target="tpu_custom_call" | custom-call | tf_op jit(solution)/shard_map/pallas_call | solution.py:360
  44.6 0.5 collective-permute-done.13.refs_3_.refs_7_
  45.2 0.1 collective-permute-start.17
  45.2 2.4 %collective-permute-done.12.refs_2_.refs_6_ = bf16[432,128]{1,0:T(8,128)(2,1)S(1)} collective-permute-done((bf16[432,128]{1,0:T(8,128)(2,1)S(1)}, bf16[432,128]{1,0:T(8,128)(2,1)S(1)}, u32[]{:S(2)}, u32[]{:S(2)}) %collective-permute-start.12) | collective-permute-done | bytes 110624 | tf_op jit(solution)/shard_map/ppermute | solution.py:31
  47.7 0.2 collective-permute-start.16
  47.8 0.4 collective-permute-start.15
  48.2 0.1 shard_map.61.refs_0_
  48.3 1.3 %collective-permute-start.19 = (f32[8,128]{1,0:T(8,128)S(1)}, f32[8,128]{1,0:T(8,128)S(1)}, u32[]{:S(2)}, u32[]{:S(2)}) collective-permute-start(f32[8,128]{1,0:T(8,128)S(1)} %shard_map.61.refs_0_), channel_id=1, source_target_pairs={{0,17},{1,16},{2,19},{3,18},{4,21},{5,20},{6,23},{7,22},{8,25},{9,... | collective-permute-start | bytes 12296 | tf_op jit(solution)/shard_map/ppermute | solution.py:43
  49.6 0.0 collective-permute-done.14.refs_0_.refs_8_
  49.6 0.5 collective-permute-start.18
  50.2 0.0 collective-permute-done.17.refs_3_.refs_11_
  50.2 0.0 collective-permute-done.16.refs_2_.refs_10_
  50.2 0.0 collective-permute-done.15.refs_1_.refs_9_
  50.2 0.1 shard_map.62.refs_1_
  50.3 1.1 %collective-permute-done.19.refs_3_ = f32[8,128]{1,0:T(8,128)S(1)} collective-permute-done((f32[8,128]{1,0:T(8,128)S(1)}, f32[8,128]{1,0:T(8,128)S(1)}, u32[]{:S(2)}, u32[]{:S(2)}) %collective-permute-start.19) | collective-permute-done | bytes 4128 | tf_op jit(solution)/shard_map/ppermute | solution.py:43
  51.4 1.9 %collective-permute-done.18.refs_2_ = f32[8,128]{1,0:T(8,128)S(1)} collective-permute-done((f32[8,128]{1,0:T(8,128)S(1)}, f32[8,128]{1,0:T(8,128)S(1)}, u32[]{:S(2)}, u32[]{:S(2)}) %collective-permute-start.18) | collective-permute-done | bytes 4128 | tf_op jit(solution)/shard_map/ppermute | solution.py:43
  53.3 1.4 %shard_map.63 = f32[8,432,128]{2,1,0:T(8,128)} custom-call(s32[1]{0:T(128)} %bitcast.spot, f32[8,128]{1,0:T(8,128)S(1)} %shard_map.61.refs_0_, f32[8,128]{1,0:T(8,128)S(1)} %shard_map.62.refs_1_, f32[8,128]{1,0:T(8,128)S(1)} %collective-permute-done.18.refs_2_, f32[8,128]{1,0:T(8,128)S(1)} %collective-permute-done.19.refs_3_, ...), custom_call_target="tpu_custom_call" | custom-call | tf_op jit(solution)/shard_map/pallas_call | solution.py:499
  (6 shorter events, 0.1 us)
Async XLA Ops:
  1.8 3.4 %collective-permute-start = (bf16[2,3,64,128]{3,2,1,0:T(8,128)(2,1)S(1)}, bf16[2,3,64,128]{3,2,1,0:T(8,128)(2,1)S(1)}, u32[]{:S(2)}, u32[]{:S(2)}) collective-permute-start(bf16[2,3,64,128]{3,2,1,0:T(8,128)(2,1)S(1)} %get-tuple-element.21), channel_id=1, source_target_pairs={{0,1},{1,0},{2,3},{3,2},{4,5},{5,4},{6,7},{7,6},{8,9},{9,8},{10,11... | collective-permute-start | bytes 294920 | tf_op jit(solution)/shard_map/ppermute | solution.py:26
  2.4 2.9 %collective-permute-start.1 = (bf16[2,3,64,128]{3,2,1,0:T(8,128)(2,1)S(1)}, bf16[2,3,64,128]{3,2,1,0:T(8,128)(2,1)S(1)}, u32[]{:S(2)}, u32[]{:S(2)}) collective-permute-start(bf16[2,3,64,128]{3,2,1,0:T(8,128)(2,1)S(1)} %get-tuple-element.22), channel_id=1, source_target_pairs={{1,2},{2,1},{3,4},{4,3},{5,6},{6,5},{7,8},{8,7},{9,10},{10,9},{11,... | collective-permute-start | bytes 294920 | tf_op jit(solution)/shard_map/ppermute | solution.py:26
  7.2 5.5 %collective-permute-start.2 = (bf16[2,4,64,128]{3,2,1,0:T(8,128)(2,1)S(1)}, bf16[2,4,64,128]{3,2,1,0:T(8,128)(2,1)S(1)}, u32[]{:S(2)}, u32[]{:S(2)}) collective-permute-start(bf16[2,4,64,128]{3,2,1,0:T(8,128)(2,1)S(1)} %get-tuple-element.28.after), channel_id=1, source_target_pairs={{0,16},{1,17},{2,18},{3,19},{4,20},{5,21},{6,22},{7,23},{8,24},{9,... | collective-permute-start | bytes 393224 | tf_op jit(solution)/shard_map/ppermute | solution.py:43
  13.9 3.6 %collective-permute-start.8 = (bf16[432,128]{1,0:T(8,128)(2,1)S(1)}, bf16[432,128]{1,0:T(8,128)(2,1)S(1)}, u32[]{:S(2)}, u32[]{:S(2)}) collective-permute-start(bf16[432,128]{1,0:T(8,128)(2,1)S(1)} %get-tuple-element.35), channel_id=1, source_target_pairs={{0,1},{1,0},{2,3},{3,2},{4,5},{5,4},{6,7},{7,6},{8,9},{9,8},{10,11... | collective-permute-start | bytes 331784 | tf_op jit(solution)/shard_map/ppermute | solution.py:31
  16.6 5.7 %collective-permute-start.4 = (bf16[432,128]{1,0:T(8,128)(2,1)S(1)}, bf16[432,128]{1,0:T(8,128)(2,1)S(1)}, u32[]{:S(2)}, u32[]{:S(2)}) collective-permute-start(bf16[432,128]{1,0:T(8,128)(2,1)S(1)} %get-tuple-element.32), channel_id=1, source_target_pairs={{0,1},{1,0},{2,3},{3,2},{4,5},{5,4},{6,7},{7,6},{8,9},{9,8},{10,11... | collective-permute-start | bytes 331784 | tf_op jit(solution)/shard_map/ppermute | solution.py:31
  16.7 7.1 %collective-permute-start.6 = (bf16[432,128]{1,0:T(8,128)(2,1)S(1)}, bf16[432,128]{1,0:T(8,128)(2,1)S(1)}, u32[]{:S(2)}, u32[]{:S(2)}) collective-permute-start(bf16[432,128]{1,0:T(8,128)(2,1)S(1)} %get-tuple-element.34), channel_id=1, source_target_pairs={{0,1},{1,0},{2,3},{3,2},{4,5},{5,4},{6,7},{7,6},{8,9},{9,8},{10,11... | collective-permute-start | bytes 331784 | tf_op jit(solution)/shard_map/ppermute | solution.py:31
  17.1 6.8 %collective-permute-start.3 = (bf16[560,128]{1,0:T(8,128)(2,1)S(1)}, bf16[560,128]{1,0:T(8,128)(2,1)S(1)}, u32[]{:S(2)}, u32[]{:S(2)}) collective-permute-start(bf16[560,128]{1,0:T(8,128)(2,1)S(1)} %get-tuple-element.31), channel_id=1, source_target_pairs={{0,1},{1,0},{2,3},{3,2},{4,5},{5,4},{6,7},{7,6},{8,9},{9,8},{10,11... | collective-permute-start | bytes 430088 | tf_op jit(solution)/shard_map/ppermute | solution.py:31
  17.6 11.8 %collective-permute-start.9 = (bf16[560,128]{1,0:T(8,128)(2,1)S(1)}, bf16[560,128]{1,0:T(8,128)(2,1)S(1)}, u32[]{:S(2)}, u32[]{:S(2)}) collective-permute-start(bf16[560,128]{1,0:T(8,128)(2,1)S(1)} %shard_map.57), channel_id=1, source_target_pairs={{0,7},{1,6},{2,5},{3,4},{4,3},{5,2},{6,1},{7,0},{8,15},{9,14},{10,... | collective-permute-start | bytes 430088 | tf_op jit(solution)/shard_map/ppermute | solution.py:31
  22.3 7.3 %collective-permute-start.5 = (bf16[560,128]{1,0:T(8,128)(2,1)S(1)}, bf16[560,128]{1,0:T(8,128)(2,1)S(1)}, u32[]{:S(2)}, u32[]{:S(2)}) collective-permute-start(bf16[560,128]{1,0:T(8,128)(2,1)S(1)} %shard_map.55), channel_id=1, source_target_pairs={{0,3},{1,2},{2,1},{3,0},{4,7},{5,6},{6,5},{7,4},{8,11},{9,10},{10,... | collective-permute-start | bytes 430088 | tf_op jit(solution)/shard_map/ppermute | solution.py:31
  23.8 5.6 %collective-permute-start.7 = (bf16[432,128]{1,0:T(8,128)(2,1)S(1)}, bf16[432,128]{1,0:T(8,128)(2,1)S(1)}, u32[]{:S(2)}, u32[]{:S(2)}) collective-permute-start(bf16[432,128]{1,0:T(8,128)(2,1)S(1)} %shard_map.56), channel_id=1, source_target_pairs={{0,4},{1,5},{2,6},{3,7},{4,0},{5,1},{6,2},{7,3},{8,12},{9,13},{10,... | collective-permute-start | bytes 331784 | tf_op jit(solution)/shard_map/ppermute | solution.py:31
  29.7 8.6 %collective-permute-start.10 = (bf16[560,128]{1,0:T(8,128)(2,1)S(1)}, bf16[560,128]{1,0:T(8,128)(2,1)S(1)}, u32[]{:S(2)}, u32[]{:S(2)}) collective-permute-start(bf16[560,128]{1,0:T(8,128)(2,1)S(1)} %shard_map.58.mine), channel_id=1, source_target_pairs={{0,15},{1,14},{2,13},{3,12},{4,11},{5,10},{6,9},{7,8},{8,7},{9,6},... | collective-permute-start | bytes 430088 | tf_op jit(solution)/shard_map/ppermute | solution.py:31
  38.4 6.8 %collective-permute-start.13 = (bf16[432,128]{1,0:T(8,128)(2,1)S(1)}, bf16[432,128]{1,0:T(8,128)(2,1)S(1)}, u32[]{:S(2)}, u32[]{:S(2)}) collective-permute-start(bf16[432,128]{1,0:T(8,128)(2,1)S(1)} %shard_map.59.refs_0_.refs_4_), channel_id=1, source_target_pairs={{0,7},{1,6},{2,5},{3,4},{4,3},{5,2},{6,1},{7,0},{8,15},{9,14},{10,... | collective-permute-start | bytes 331784 | tf_op jit(solution)/shard_map/ppermute | solution.py:31
  41.7 5.9 %collective-permute-start.12 = (bf16[432,128]{1,0:T(8,128)(2,1)S(1)}, bf16[432,128]{1,0:T(8,128)(2,1)S(1)}, u32[]{:S(2)}, u32[]{:S(2)}) collective-permute-start(bf16[432,128]{1,0:T(8,128)(2,1)S(1)} %shard_map.59.refs_0_.refs_4_), channel_id=1, source_target_pairs={{0,3},{1,2},{2,1},{3,0},{4,7},{5,6},{6,5},{7,4},{8,11},{9,10},{10,... | collective-permute-start | bytes 331784 | tf_op jit(solution)/shard_map/ppermute | solution.py:31
  42.6 5.2 %collective-permute-start.11 = (bf16[432,128]{1,0:T(8,128)(2,1)S(1)}, bf16[432,128]{1,0:T(8,128)(2,1)S(1)}, u32[]{:S(2)}, u32[]{:S(2)}) collective-permute-start(bf16[432,128]{1,0:T(8,128)(2,1)S(1)} %shard_map.59.refs_0_.refs_4_), channel_id=1, source_target_pairs={{0,4},{1,5},{2,6},{3,7},{4,0},{5,1},{6,2},{7,3},{8,12},{9,13},{10,... | collective-permute-start | bytes 331784 | tf_op jit(solution)/shard_map/ppermute | solution.py:31
  42.6 7.0 %collective-permute-start.14 = (bf16[432,128]{1,0:T(8,128)(2,1)S(1)}, bf16[432,128]{1,0:T(8,128)(2,1)S(1)}, u32[]{:S(2)}, u32[]{:S(2)}) collective-permute-start(bf16[432,128]{1,0:T(8,128)(2,1)S(1)} %shard_map.59.refs_0_.refs_4_), channel_id=1, source_target_pairs={{0,1},{1,0},{2,3},{3,2},{4,5},{5,4},{6,7},{7,6},{8,9},{9,8},{10,11... | collective-permute-start | bytes 331784 | tf_op jit(solution)/shard_map/ppermute | solution.py:31
  45.2 5.0 %collective-permute-start.17 = (bf16[432,128]{1,0:T(8,128)(2,1)S(1)}, bf16[432,128]{1,0:T(8,128)(2,1)S(1)}, u32[]{:S(2)}, u32[]{:S(2)}) collective-permute-start(bf16[432,128]{1,0:T(8,128)(2,1)S(1)} %collective-permute-done.13.refs_3_.refs_7_), channel_id=1, source_target_pairs={{0,1},{1,0},{2,3},{3,2},{4,5},{5,4},{6,7},{7,6},{8,9},{9,8},{10,11... | collective-permute-start | bytes 331784 | tf_op jit(solution)/shard_map/ppermute | solution.py:31
  47.7 2.5 %collective-permute-start.16 = (bf16[432,128]{1,0:T(8,128)(2,1)S(1)}, bf16[432,128]{1,0:T(8,128)(2,1)S(1)}, u32[]{:S(2)}, u32[]{:S(2)}) collective-permute-start(bf16[432,128]{1,0:T(8,128)(2,1)S(1)} %collective-permute-done.12.refs_2_.refs_6_), channel_id=1, source_target_pairs={{0,1},{1,0},{2,3},{3,2},{4,5},{5,4},{6,7},{7,6},{8,9},{9,8},{10,11... | collective-permute-start | bytes 331784 | tf_op jit(solution)/shard_map/ppermute | solution.py:31
  47.8 2.4 %collective-permute-start.15 = (bf16[432,128]{1,0:T(8,128)(2,1)S(1)}, bf16[432,128]{1,0:T(8,128)(2,1)S(1)}, u32[]{:S(2)}, u32[]{:S(2)}) collective-permute-start(bf16[432,128]{1,0:T(8,128)(2,1)S(1)} %collective-permute-done.11.refs_1_.refs_5_), channel_id=1, source_target_pairs={{0,1},{1,0},{2,3},{3,2},{4,5},{5,4},{6,7},{7,6},{8,9},{9,8},{10,11... | collective-permute-start | bytes 331784 | tf_op jit(solution)/shard_map/ppermute | solution.py:31
  48.3 3.1 %collective-permute-start.19 = (f32[8,128]{1,0:T(8,128)S(1)}, f32[8,128]{1,0:T(8,128)S(1)}, u32[]{:S(2)}, u32[]{:S(2)}) collective-permute-start(f32[8,128]{1,0:T(8,128)S(1)} %shard_map.61.refs_0_), channel_id=1, source_target_pairs={{0,17},{1,16},{2,19},{3,18},{4,21},{5,20},{6,23},{7,22},{8,25},{9,... | collective-permute-start | bytes 12296 | tf_op jit(solution)/shard_map/ppermute | solution.py:43
  49.6 3.6 %collective-permute-start.18 = (f32[8,128]{1,0:T(8,128)S(1)}, f32[8,128]{1,0:T(8,128)S(1)}, u32[]{:S(2)}, u32[]{:S(2)}) collective-permute-start(f32[8,128]{1,0:T(8,128)S(1)} %shard_map.61.refs_0_), channel_id=1, source_target_pairs={{0,16},{1,17},{2,18},{3,19},{4,20},{5,21},{6,22},{7,23},{8,24},{9,... | collective-permute-start | bytes 12296 | tf_op jit(solution)/shard_map/ppermute | solution.py:43

commit v10 on v8

--- a/solution.py
+++ b/solution.py
@@ -92,7 +92,7 @@
     return total
 
 
-def rim_kernel(acts, grad, near, far, acts_here, grad_here, sems, loads):
+def rim_kernel(acts, grad, near, far, sems):
     micro, depth = acts.shape[:2]
     top = 1 - lax.rem(lax.axis_index("slab"), 2)
     copies = []
@@ -106,23 +106,27 @@
                         sems.at[which, m, part],
                     )
                 )
-    for n, (source, out) in enumerate(((acts, acts_here), (grad, grad_here))):
-        copies.append(pltpu.make_async_copy(source, out, loads.at[n]))
     for copy in copies:
         copy.start()
     for copy in copies:
         copy.wait()
 
 
-def own_kernel(height, acts, stored, weight, mirror, part, own, sem):
+def own_kernel(
+    height, stored_acts, stored_grad, stored, acts, grad, weight, mirror, part, own, sems
+):
     micro, depth, cells, channels = acts.shape
     block, span = micro * cells, 9 * channels
-    copy = pltpu.make_async_copy(stored, weight, sem)
-    copy.start()
+    pairs = ((stored_acts, acts), (stored, weight), (stored_grad, grad))
+    copies = [pltpu.make_async_copy(a, b, sems.at[n]) for n, (a, b) in enumerate(pairs)]
+    for copy in copies:
+        copy.start()
+    copies[0].wait()
     for n in range(depth):
         for m in range(micro):
             write_shifts(acts[m, n], height, own, n * block + m * cells)
-    copy.wait()
+    copies[1].wait()
+    copies[2].wait()
     part[...] = jnp.zeros(part.shape, F32)
     for dz in range(3):
         rows = slice((2 - dz) * block, (2 - dz + depth) * block)
@@ -333,27 +337,32 @@
     shape = jax.ShapeDtypeStruct
     rim = shape((micro, 3, cells, channels), BF16)
     volume = shape((micro, depth, cells, channels), BF16)
-    to_near, to_far, acts, grad = pl.pallas_call(
+    acts, grad = (pltpu.with_memory_space_constraint(a, pltpu.HBM) for a in (acts, grad))
+    to_near, to_far = pl.pallas_call(
         rim_kernel,
-        out_shape=(rim, rim, volume, volume),
+        out_shape=(rim, rim),
         in_specs=[HBM, HBM],
-        out_specs=(VMEM,) * 4,
-        scratch_shapes=[pltpu.SemaphoreType.DMA((2, micro, 2)), pltpu.SemaphoreType.DMA((2,))],
+        out_specs=(VMEM,) * 2,
+        scratch_shapes=[pltpu.SemaphoreType.DMA((2, micro, 2))],
         compiler_params=small,
-    )(*(pltpu.with_memory_space_constraint(a, pltpu.HBM) for a in (acts, grad)))
+    )(acts, grad)
     near, far = swap(to_near, to_far)
 
     plane, span = micro * cells, 9 * channels
     whole = shape(weight.shape, BF16)
     outer = shape(((depth + 2) * plane, channels), F32)
-    weight, mirror, part = pl.pallas_call(
+    stored = acts, grad, pltpu.with_memory_space_constraint(weight, pltpu.HBM)
+    acts, grad, weight, mirror, part = pl.pallas_call(
         functools.partial(own_kernel, height),
-        out_shape=(whole, whole, outer),
-        in_specs=[VMEM, HBM],
-        out_specs=(VMEM,) * 3,
-        scratch_shapes=[pltpu.VMEM((depth * plane, span), BF16), pltpu.SemaphoreType.DMA],
+        out_shape=(volume, volume, whole, whole, outer),
+        in_specs=[HBM] * 3,
+        out_specs=(VMEM,) * 5,
+        scratch_shapes=[
+            pltpu.VMEM((depth * plane, span), BF16),
+            pltpu.SemaphoreType.DMA((3,)),
+        ],
         compiler_params=large,
-    )(acts, pltpu.with_memory_space_constraint(weight, pltpu.HBM))
+    )(*stored)
 
     edge = shape((micro, 1, cells, channels), BF16)
     wide = pltpu.VMEM(((depth + 2) * plane, span), BF16)
@@ -405,7 +414,7 @@
     bits = [1 << n for n in range(1, count.bit_length() - 1)]
     inner = [bits[n : n + 2] for n in range(2, len(bits), 2)]
     crossing = inner[-1][0] if len(inner[-1]) == 1 else 0
-    side = lax.rem(index, 2) ^ jnp.where(index & crossing, 1, 0)
+    side = lax.rem(index, 2)
     quarter = jnp.where(index & 2, 2, 0) + jnp.where(index & 4, 1, 0)
     masks = {1: 4, 2: 2, 3: 6}
     spot = (side * 4 + quarter).astype(jnp.int32).reshape(1)
@@ -471,7 +480,7 @@
         chunk = block(chunk, own, size, F32) + sum(g.astype(F32) for g in took)
     gathered = chunk.astype(BF16)
     if single:
-        other = exchange(gathered, crossing | 1)
+        other = exchange(gathered, crossing)
         other, gradients = lax.optimization_barrier((other, gradients))
         gathered = pl.pallas_call(
             both_kernel,

time: 53.8 us -> 53.1 us (0.987)
  starting transfers between devices: 28.9 us -> 26.6 us
  waiting for transfers between devices: 13.6 us -> 15.3 us
    ppermute x15, waiting for transfers between devices: 8.38 us -> 10.8 us  [exchange(): return lax.ppermute(value, 'slab', [(i, i ^ mask) for i in range(count)])]
    ppermute x15, starting transfers between devices: 22.3 us -> 19.9 us  [exchange(): return lax.ppermute(value, 'slab', [(i, i ^ mask) for i in range(count)])]
    ppermute x3, waiting for transfers between devices: 5.17 us -> 4.53 us  [cross(): return lax.ppermute(value, ('segment', 'slab'), route)]
  transfers between devices with their start and end apart: 21 -> 21, of which waited for: 10 -> 11; matrix products, arithmetic and copies ran while one was open for 0% -> 0% of each run, Pallas kernels for 9% -> 9%
where the time goes in v10:
time: 53.1 us; the launch traced here: 52.8 us
  starting transfers between devices  26.6 us (50%)
  waiting for transfers between devices  15.3 us (29%)
  Pallas kernels  10.2 us (19%)
  between operations  0.75 us (1%)
    ppermute x15, starting transfers between devices, exchange(): return lax.ppermute(value, 'slab', [(i, i ^ mask) for i in range(count)])  19.9 us
    ppermute x15, waiting for transfers between devices, exchange(): return lax.ppermute(value, 'slab', [(i, i ^ mask) for i in range(count)])  10.8 us
    ppermute x3, starting transfers between devices, cross(): return lax.ppermute(value, ('segment', 'slab'), route)  4.77 us
    ppermute x3, waiting for transfers between devices, cross(): return lax.ppermute(value, ('segment', 'slab'), route)  4.53 us
    pallas_call x1, Pallas kernels, shards(): pl.pallas_call(functools.partial(own_kernel, height), out_shape=(volume,...  2.35 us
    pallas_call x1, Pallas kernels, shards(): pl.pallas_call(functools.partial(first_kernel, height), out_shape=(volume...  1.86 us
    pallas_call x1, Pallas kernels, conv_back(): pl.pallas_call(functools.partial(back_kernel, height), out_shape=volume,...  1.79 us
    pallas_call x1, Pallas kernels, shards(): pl.pallas_call(functools.partial(place_kernel, bound, segments), out_shap...  1.38 us
  transfers between devices with their start and end apart: 21, of which 11 were waited for; matrix products, arithmetic and copies ran while one was open for 0% of the time, Pallas kernels for 9%

profile of v10, /device:TPU:0, one launch (start us, length us, event | category | flops | bytes accessed | tf_op | source)
XLA Modules:
  0.0 52.8 jit_solution(3279495415573001772)
XLA Ops:
  0.6 0.9 %shard_map.50 = (bf16[2,3,64,128]{3,2,1,0:T(8,128)(2,1)S(1)}, bf16[2,3,64,128]{3,2,1,0:T(8,128)(2,1)S(1)}) custom-call(bf16[2,4,64,128]{3,2,1,0:T(8,128)(2,1)} %bitcast.8, bf16[2,4,64,128]{3,2,1,0:T(8,128)(2,1)} %bitcast.10), custom_call_target="tpu_custom_call" | custom-call | tf_op jit(solution)/shard_map/pallas_call | solution.py:341
  1.6 0.5 collective-permute-start
  2.1 0.7 %collective-permute-start.1 = (bf16[2,3,64,128]{3,2,1,0:T(8,128)(2,1)S(1)}, bf16[2,3,64,128]{3,2,1,0:T(8,128)(2,1)S(1)}, u32[]{:S(2)}, u32[]{:S(2)}) collective-permute-start(bf16[2,3,64,128]{3,2,1,0:T(8,128)(2,1)S(1)} %get-tuple-element.27), channel_id=1, source_target_pairs={{1,2},{2,1},{3,4},{4,3},{5,6},{6,5},{7,8},{8,7},{9,10},{10,9},{11,... | collective-permute-start | bytes 294920 | tf_op jit(solution)/shard_map/ppermute | solution.py:26
  2.8 2.3 %shard_map.51 = (bf16[2,4,64,128]{3,2,1,0:T(8,128)(2,1)S(1)}, bf16[2,4,64,128]{3,2,1,0:T(8,128)(2,1)S(1)}, bf16[3456,128]{1,0:T(8,128)(2,1)S(1)}, bf16[3456,128]{1,0:T(8,128)(2,1)S(1)}, f32[768,128]{1,0:T(8,128)S(1)}) custom-call(bf16[2,4,64,128]{3,2,1,0:T(8,128)(2,1)} %bitcast.9, bf16[2,4,64,128]{3,2,1,0:T(8,128)(2,1)} %bitcast.11, bf16[3456,128]{1,0:T(8,128)(2,1)} %bitcast.7), custom_call_target="tpu_custom_call" | custom-call | tf_op jit(solution)/shard_map/pallas_call | solution.py:355
  5.1 0.0 collective-permute-done.near
  5.1 0.0 collective-permute-done.1.far
  5.1 1.9 %shard_map.52 = (bf16[2,4,64,128]{3,2,1,0:T(8,128)(2,1)S(1)}, f32[768,128]{1,0:T(8,128)S(1)}, bf16[2,1,64,128]{3,2,1,0:T(8,128)(2,1)S(1)}) custom-call(bf16[2,3,64,128]{3,2,1,0:T(8,128)(2,1)S(1)} %collective-permute-done.near, bf16[2,3,64,128]{3,2,1,0:T(8,128)(2,1)S(1)} %collective-permute-done.1.far, bf16[2,4,64,128]{3,2,1,0:T(8,128)(2,1)S(1)} %get-tuple-element.28.grad, ...), custom_call_target="tpu_custom_call" | custom-call | tf_op jit(solution)/shard_map/pallas_call | solution.py:370
  7.0 2.6 %collective-permute-start.2 = (bf16[2,4,64,128]{3,2,1,0:T(8,128)(2,1)S(1)}, bf16[2,4,64,128]{3,2,1,0:T(8,128)(2,1)S(1)}, u32[]{:S(2)}, u32[]{:S(2)}) collective-permute-start(bf16[2,4,64,128]{3,2,1,0:T(8,128)(2,1)S(1)} %get-tuple-element.32.after), channel_id=1, source_target_pairs={{0,16},{1,17},{2,18},{3,19},{4,20},{5,21},{6,22},{7,23},{8,24},{9,... | collective-permute-start | bytes 393224 | tf_op jit(solution)/shard_map/ppermute | solution.py:53
  9.6 0.2 shard_map.53.shifts
  9.8 2.7 %collective-permute-done.2.incoming = bf16[2,4,64,128]{3,2,1,0:T(8,128)(2,1)S(1)} collective-permute-done((bf16[2,4,64,128]{3,2,1,0:T(8,128)(2,1)S(1)}, bf16[2,4,64,128]{3,2,1,0:T(8,128)(2,1)S(1)}, u32[]{:S(2)}, u32[]{:S(2)}) %collective-permute-start.2) | collective-permute-done | bytes 131104 | tf_op jit(solution)/shard_map/ppermute | solution.py:53
  12.5 1.2 %shard_map.54 = (bf16[2,4,64,128]{3,2,1,0:T(8,128)(2,1)S(1)}, bf16[768,128]{1,0:T(8,128)(2,1)S(1)}, f32[128,128]{1,0:T(8,128)S(1)}, bf16[560,128]{1,0:T(8,128)(2...) custom-call(s32[1]{0:T(128)} %bitcast.spot, ...), custom_call_target="tpu_custom_call" | custom-call | tf_op jit(solution)/shard_map/pallas_call | solution.py:423
  13.8 2.6 %collective-permute-start.8 = (bf16[432,128]{1,0:T(8,128)(2,1)S(1)}, bf16[432,128]{1,0:T(8,128)(2,1)S(1)}, u32[]{:S(2)}, u32[]{:S(2)}) collective-permute-start(bf16[432,128]{1,0:T(8,128)(2,1)S(1)} %get-tuple-element.39), channel_id=1, source_target_pairs={{0,1},{1,0},{2,3},{3,2},{4,5},{5,4},{6,7},{7,6},{8,9},{9,8},{10,11... | collective-permute-start | bytes 331784 | tf_op jit(solution)/shard_map/ppermute | solution.py:41
  16.3 0.1 collective-permute-start.4
  16.4 0.4 collective-permute-start.6
  16.8 0.1 collective-permute-start.3
  16.9 0.4 collective-permute-done.8.got
  17.3 4.9 %collective-permute-start.9 = (bf16[432,128]{1,0:T(8,128)(2,1)S(1)}, bf16[432,128]{1,0:T(8,128)(2,1)S(1)}, u32[]{:S(2)}, u32[]{:S(2)}) collective-permute-start(bf16[432,128]{1,0:T(8,128)(2,1)S(1)} %shard_map.57), channel_id=1, source_target_pairs={{0,6},{1,7},{2,4},{3,5},{4,2},{5,3},{6,0},{7,1},{8,14},{9,15},{10,... | collective-permute-start | bytes 331784 | tf_op jit(solution)/shard_map/ppermute | solution.py:41
  22.3 0.0 collective-permute-done.4.got
  22.3 1.5 %collective-permute-start.5 = (bf16[432,128]{1,0:T(8,128)(2,1)S(1)}, bf16[432,128]{1,0:T(8,128)(2,1)S(1)}, u32[]{:S(2)}, u32[]{:S(2)}) collective-permute-start(bf16[432,128]{1,0:T(8,128)(2,1)S(1)} %shard_map.55), channel_id=1, source_target_pairs={{0,2},{1,3},{2,0},{3,1},{4,6},{5,7},{6,4},{7,5},{8,10},{9,11},{10,... | collective-permute-start | bytes 331784 | tf_op jit(solution)/shard_map/ppermute | solution.py:41
  23.8 0.1 collective-permute-start.7
  23.9 0.7 %collective-permute-start.10 = (bf16[2,1,64,128]{3,2,1,0:T(8,128)(2,1)S(1)}, bf16[2,1,64,128]{3,2,1,0:T(8,128)(2,1)S(1)}, u32[]{:S(2)}, u32[]{:S(2)}) collective-permute-start(bf16[2,1,64,128]{3,2,1,0:T(8,128)(2,1)S(1)} %get-tuple-element.42), channel_id=1, source_target_pairs={{1,18},{2,17},{3,20},{4,19},{5,22},{6,21},{7,24},{8,23},{9,26},{10... | collective-permute-start | bytes 98312 | tf_op jit(solution)/shard_map/ppermute | solution.py:36
  24.5 0.0 collective-permute-done.10.in_far
  24.6 1.2 %collective-permute-done.9.refs_3_ = bf16[432,128]{1,0:T(8,128)(2,1)S(1)} collective-permute-done((bf16[432,128]{1,0:T(8,128)(2,1)S(1)}, bf16[432,128]{1,0:T(8,128)(2,1)S(1)}, u32[]{:S(2)}, u32[]{:S(2)}) %collective-permute-start.9) | collective-permute-done | bytes 110624 | tf_op jit(solution)/shard_map/ppermute | solution.py:41
  25.7 2.3 %collective-permute-done.5.refs_1_ = bf16[432,128]{1,0:T(8,128)(2,1)S(1)} collective-permute-done((bf16[432,128]{1,0:T(8,128)(2,1)S(1)}, bf16[432,128]{1,0:T(8,128)(2,1)S(1)}, u32[]{:S(2)}, u32[]{:S(2)}) %collective-permute-start.5) | collective-permute-done | bytes 110624 | tf_op jit(solution)/shard_map/ppermute | solution.py:41
  28.0 0.6 %collective-permute-done.7.refs_2_ = bf16[432,128]{1,0:T(8,128)(2,1)S(1)} collective-permute-done((bf16[432,128]{1,0:T(8,128)(2,1)S(1)}, bf16[432,128]{1,0:T(8,128)(2,1)S(1)}, u32[]{:S(2)}, u32[]{:S(2)}) %collective-permute-start.7) | collective-permute-done | bytes 110624 | tf_op jit(solution)/shard_map/ppermute | solution.py:41
  28.6 0.1 shard_map.58.mine
  28.7 5.4 %collective-permute-start.11 = (bf16[432,128]{1,0:T(8,128)(2,1)S(1)}, bf16[432,128]{1,0:T(8,128)(2,1)S(1)}, u32[]{:S(2)}, u32[]{:S(2)}) collective-permute-start(bf16[432,128]{1,0:T(8,128)(2,1)S(1)} %shard_map.58.mine), channel_id=1, source_target_pairs={{0,8},{1,9},{2,10},{3,11},{4,12},{5,13},{6,14},{7,15},{8,0},{9,1},... | collective-permute-start | bytes 331784 | tf_op jit(solution)/shard_map/ppermute | solution.py:41
  34.1 1.8 %shard_map.59 = bf16[2,4,64,128]{3,2,1,0:T(8,128)(2,1)} custom-call(bf16[768,128]{1,0:T(8,128)(2,1)S(1)} %get-tuple-element.44.deltas, bf16[560,128]{1,0:T(8,128)(2,1)S(1)} %collective-permute-done.3.refs_0_.by_near, bf16[2,1,64,128]{3,2,1,0:T(8,128)(2,1)S(1)} %collective-permute-done.10.in_far, f32[128,128]{1,0:T(8,128)S(1)} %get-tuple-element.46.far_slope, ...), custom_call_target="tpu_custom_call" | custom-call | tf_op jit(solution)/shard_map/pallas_call | solution.py:380
  35.9 1.0 %collective-permute-done.11.other = bf16[432,128]{1,0:T(8,128)(2,1)S(1)} collective-permute-done((bf16[432,128]{1,0:T(8,128)(2,1)S(1)}, bf16[432,128]{1,0:T(8,128)(2,1)S(1)}, u32[]{:S(2)}, u32[]{:S(2)}) %collective-permute-start.11) | collective-permute-done | bytes 110624 | tf_op jit(solution)/shard_map/ppermute | solution.py:41
  37.0 2.2 %collective-permute-start.14 = (bf16[432,128]{1,0:T(8,128)(2,1)S(1)}, bf16[432,128]{1,0:T(8,128)(2,1)S(1)}, u32[]{:S(2)}, u32[]{:S(2)}) collective-permute-start(bf16[432,128]{1,0:T(8,128)(2,1)S(1)} %shard_map.60.refs_0_.refs_4_), channel_id=1, source_target_pairs={{0,6},{1,7},{2,4},{3,5},{4,2},{5,3},{6,0},{7,1},{8,14},{9,15},{10,... | collective-permute-start | bytes 331784 | tf_op jit(solution)/shard_map/ppermute | solution.py:41
  39.1 1.5 %collective-permute-start.13 = (bf16[432,128]{1,0:T(8,128)(2,1)S(1)}, bf16[432,128]{1,0:T(8,128)(2,1)S(1)}, u32[]{:S(2)}, u32[]{:S(2)}) collective-permute-start(bf16[432,128]{1,0:T(8,128)(2,1)S(1)} %shard_map.60.refs_0_.refs_4_), channel_id=1, source_target_pairs={{0,2},{1,3},{2,0},{3,1},{4,6},{5,7},{6,4},{7,5},{8,10},{9,11},{10,... | collective-permute-start | bytes 331784 | tf_op jit(solution)/shard_map/ppermute | solution.py:41
  40.6 1.2 %collective-permute-start.12 = (bf16[432,128]{1,0:T(8,128)(2,1)S(1)}, bf16[432,128]{1,0:T(8,128)(2,1)S(1)}, u32[]{:S(2)}, u32[]{:S(2)}) collective-permute-start(bf16[432,128]{1,0:T(8,128)(2,1)S(1)} %shard_map.60.refs_0_.refs_4_), channel_id=1, source_target_pairs={{0,4},{1,5},{2,6},{3,7},{4,0},{5,1},{6,2},{7,3},{8,12},{9,13},{10,... | collective-permute-start | bytes 331784 | tf_op jit(solution)/shard_map/ppermute | solution.py:41
  41.9 0.0 collective-permute-start.15
  41.9 0.9 %collective-permute-done.14.refs_3_.refs_7_ = bf16[432,128]{1,0:T(8,128)(2,1)S(1)} collective-permute-done((bf16[432,128]{1,0:T(8,128)(2,1)S(1)}, bf16[432,128]{1,0:T(8,128)(2,1)S(1)}, u32[]{:S(2)}, u32[]{:S(2)}) %collective-permute-start.14) | collective-permute-done | bytes 110624 | tf_op jit(solution)/shard_map/ppermute | solution.py:41
  42.8 2.5 %collective-permute-done.13.refs_2_.refs_6_ = bf16[432,128]{1,0:T(8,128)(2,1)S(1)} collective-permute-done((bf16[432,128]{1,0:T(8,128)(2,1)S(1)}, bf16[432,128]{1,0:T(8,128)(2,1)S(1)}, u32[]{:S(2)}, u32[]{:S(2)}) %collective-permute-start.13) | collective-permute-done | bytes 110624 | tf_op jit(solution)/shard_map/ppermute | solution.py:41
  45.3 0.0 collective-permute-start.17
  45.3 1.8 %collective-permute-done.12.refs_1_.refs_5_ = bf16[432,128]{1,0:T(8,128)(2,1)S(1)} collective-permute-done((bf16[432,128]{1,0:T(8,128)(2,1)S(1)}, bf16[432,128]{1,0:T(8,128)(2,1)S(1)}, u32[]{:S(2)}, u32[]{:S(2)}) %collective-permute-start.12) | collective-permute-done | bytes 110624 | tf_op jit(solution)/shard_map/ppermute | solution.py:41
  47.2 0.0 collective-permute-start.16
  47.2 0.1 shard_map.61.refs_0_
  47.3 0.5 %collective-permute-start.20 = (f32[8,128]{1,0:T(8,128)S(1)}, f32[8,128]{1,0:T(8,128)S(1)}, u32[]{:S(2)}, u32[]{:S(2)}) collective-permute-start(f32[8,128]{1,0:T(8,128)S(1)} %shard_map.61.refs_0_), channel_id=1, source_target_pairs={{0,17},{1,16},{2,19},{3,18},{4,21},{5,20},{6,23},{7,22},{8,25},{9,... | collective-permute-start | bytes 12296 | tf_op jit(solution)/shard_map/ppermute | solution.py:53
  47.8 1.7 %collective-permute-start.19 = (f32[8,128]{1,0:T(8,128)S(1)}, f32[8,128]{1,0:T(8,128)S(1)}, u32[]{:S(2)}, u32[]{:S(2)}) collective-permute-start(f32[8,128]{1,0:T(8,128)S(1)} %shard_map.61.refs_0_), channel_id=1, source_target_pairs={{0,16},{1,17},{2,18},{3,19},{4,20},{5,21},{6,22},{7,23},{8,24},{9,... | collective-permute-start | bytes 12296 | tf_op jit(solution)/shard_map/ppermute | solution.py:53
  49.5 0.0 collective-permute-done.18.refs_3_.refs_11_
  49.5 0.0 collective-permute-done.17.refs_2_.refs_10_
  49.5 0.0 collective-permute-done.16.refs_1_.refs_9_
  49.5 0.1 shard_map.62.refs_1_
  49.6 0.8 %collective-permute-done.20.refs_3_ = f32[8,128]{1,0:T(8,128)S(1)} collective-permute-done((f32[8,128]{1,0:T(8,128)S(1)}, f32[8,128]{1,0:T(8,128)S(1)}, u32[]{:S(2)}, u32[]{:S(2)}) %collective-permute-start.20) | collective-permute-done | bytes 4128 | tf_op jit(solution)/shard_map/ppermute | solution.py:53
  50.4 1.1 %collective-permute-done.19.refs_2_ = f32[8,128]{1,0:T(8,128)S(1)} collective-permute-done((f32[8,128]{1,0:T(8,128)S(1)}, f32[8,128]{1,0:T(8,128)S(1)}, u32[]{:S(2)}, u32[]{:S(2)}) %collective-permute-start.19) | collective-permute-done | bytes 4128 | tf_op jit(solution)/shard_map/ppermute | solution.py:53
  51.5 1.4 %shard_map.63 = f32[8,432,128]{2,1,0:T(8,128)} custom-call(s32[1]{0:T(128)} %bitcast.spot, f32[8,128]{1,0:T(8,128)S(1)} %shard_map.61.refs_0_, f32[8,128]{1,0:T(8,128)S(1)} %shard_map.62.refs_1_, f32[8,128]{1,0:T(8,128)S(1)} %collective-permute-done.19.refs_2_, f32[8,128]{1,0:T(8,128)S(1)} %collective-permute-done.20.refs_3_, ...), custom_call_target="tpu_custom_call" | custom-call | tf_op jit(solution)/shard_map/pallas_call | solution.py:518
  (8 shorter events, 0.1 us)
Async XLA Ops:
  1.6 3.5 %collective-permute-start = (bf16[2,3,64,128]{3,2,1,0:T(8,128)(2,1)S(1)}, bf16[2,3,64,128]{3,2,1,0:T(8,128)(2,1)S(1)}, u32[]{:S(2)}, u32[]{:S(2)}) collective-permute-start(bf16[2,3,64,128]{3,2,1,0:T(8,128)(2,1)S(1)} %get-tuple-element.26), channel_id=1, source_target_pairs={{0,1},{1,0},{2,3},{3,2},{4,5},{5,4},{6,7},{7,6},{8,9},{9,8},{10,11... | collective-permute-start | bytes 294920 | tf_op jit(solution)/shard_map/ppermute | solution.py:26
  2.1 3.0 %collective-permute-start.1 = (bf16[2,3,64,128]{3,2,1,0:T(8,128)(2,1)S(1)}, bf16[2,3,64,128]{3,2,1,0:T(8,128)(2,1)S(1)}, u32[]{:S(2)}, u32[]{:S(2)}) collective-permute-start(bf16[2,3,64,128]{3,2,1,0:T(8,128)(2,1)S(1)} %get-tuple-element.27), channel_id=1, source_target_pairs={{1,2},{2,1},{3,4},{4,3},{5,6},{6,5},{7,8},{8,7},{9,10},{10,9},{11,... | collective-permute-start | bytes 294920 | tf_op jit(solution)/shard_map/ppermute | solution.py:26
  7.0 5.5 %collective-permute-start.2 = (bf16[2,4,64,128]{3,2,1,0:T(8,128)(2,1)S(1)}, bf16[2,4,64,128]{3,2,1,0:T(8,128)(2,1)S(1)}, u32[]{:S(2)}, u32[]{:S(2)}) collective-permute-start(bf16[2,4,64,128]{3,2,1,0:T(8,128)(2,1)S(1)} %get-tuple-element.32.after), channel_id=1, source_target_pairs={{0,16},{1,17},{2,18},{3,19},{4,20},{5,21},{6,22},{7,23},{8,24},{9,... | collective-permute-start | bytes 393224 | tf_op jit(solution)/shard_map/ppermute | solution.py:53
  13.8 3.5 %collective-permute-start.8 = (bf16[432,128]{1,0:T(8,128)(2,1)S(1)}, bf16[432,128]{1,0:T(8,128)(2,1)S(1)}, u32[]{:S(2)}, u32[]{:S(2)}) collective-permute-start(bf16[432,128]{1,0:T(8,128)(2,1)S(1)} %get-tuple-element.39), channel_id=1, source_target_pairs={{0,1},{1,0},{2,3},{3,2},{4,5},{5,4},{6,7},{7,6},{8,9},{9,8},{10,11... | collective-permute-start | bytes 331784 | tf_op jit(solution)/shard_map/ppermute | solution.py:41
  16.3 5.9 %collective-permute-start.4 = (bf16[432,128]{1,0:T(8,128)(2,1)S(1)}, bf16[432,128]{1,0:T(8,128)(2,1)S(1)}, u32[]{:S(2)}, u32[]{:S(2)}) collective-permute-start(bf16[432,128]{1,0:T(8,128)(2,1)S(1)} %get-tuple-element.37), channel_id=1, source_target_pairs={{0,1},{1,0},{2,3},{3,2},{4,5},{5,4},{6,7},{7,6},{8,9},{9,8},{10,11... | collective-permute-start | bytes 331784 | tf_op jit(solution)/shard_map/ppermute | solution.py:41
  16.4 7.4 %collective-permute-start.6 = (bf16[432,128]{1,0:T(8,128)(2,1)S(1)}, bf16[432,128]{1,0:T(8,128)(2,1)S(1)}, u32[]{:S(2)}, u32[]{:S(2)}) collective-permute-start(bf16[432,128]{1,0:T(8,128)(2,1)S(1)} %get-tuple-element.38), channel_id=1, source_target_pairs={{0,1},{1,0},{2,3},{3,2},{4,5},{5,4},{6,7},{7,6},{8,9},{9,8},{10,11... | collective-permute-start | bytes 331784 | tf_op jit(solution)/shard_map/ppermute | solution.py:41
  16.8 8.9 %collective-permute-start.3 = (bf16[560,128]{1,0:T(8,128)(2,1)S(1)}, bf16[560,128]{1,0:T(8,128)(2,1)S(1)}, u32[]{:S(2)}, u32[]{:S(2)}) collective-permute-start(bf16[560,128]{1,0:T(8,128)(2,1)S(1)} %get-tuple-element.36), channel_id=1, source_target_pairs={{0,1},{1,0},{2,3},{3,2},{4,5},{5,4},{6,7},{7,6},{8,9},{9,8},{10,11... | collective-permute-start | bytes 430088 | tf_op jit(solution)/shard_map/ppermute | solution.py:41
  17.3 8.4 %collective-permute-start.9 = (bf16[432,128]{1,0:T(8,128)(2,1)S(1)}, bf16[432,128]{1,0:T(8,128)(2,1)S(1)}, u32[]{:S(2)}, u32[]{:S(2)}) collective-permute-start(bf16[432,128]{1,0:T(8,128)(2,1)S(1)} %shard_map.57), channel_id=1, source_target_pairs={{0,6},{1,7},{2,4},{3,5},{4,2},{5,3},{6,0},{7,1},{8,14},{9,15},{10,... | collective-permute-start | bytes 331784 | tf_op jit(solution)/shard_map/ppermute | solution.py:41
  22.3 5.7 %collective-permute-start.5 = (bf16[432,128]{1,0:T(8,128)(2,1)S(1)}, bf16[432,128]{1,0:T(8,128)(2,1)S(1)}, u32[]{:S(2)}, u32[]{:S(2)}) collective-permute-start(bf16[432,128]{1,0:T(8,128)(2,1)S(1)} %shard_map.55), channel_id=1, source_target_pairs={{0,2},{1,3},{2,0},{3,1},{4,6},{5,7},{6,4},{7,5},{8,10},{9,11},{10,... | collective-permute-start | bytes 331784 | tf_op jit(solution)/shard_map/ppermute | solution.py:41
  23.8 4.8 %collective-permute-start.7 = (bf16[432,128]{1,0:T(8,128)(2,1)S(1)}, bf16[432,128]{1,0:T(8,128)(2,1)S(1)}, u32[]{:S(2)}, u32[]{:S(2)}) collective-permute-start(bf16[432,128]{1,0:T(8,128)(2,1)S(1)} %shard_map.56), channel_id=1, source_target_pairs={{0,4},{1,5},{2,6},{3,7},{4,0},{5,1},{6,2},{7,3},{8,12},{9,13},{10,... | collective-permute-start | bytes 331784 | tf_op jit(solution)/shard_map/ppermute | solution.py:41
  23.9 0.7 %collective-permute-start.10 = (bf16[2,1,64,128]{3,2,1,0:T(8,128)(2,1)S(1)}, bf16[2,1,64,128]{3,2,1,0:T(8,128)(2,1)S(1)}, u32[]{:S(2)}, u32[]{:S(2)}) collective-permute-start(bf16[2,1,64,128]{3,2,1,0:T(8,128)(2,1)S(1)} %get-tuple-element.42), channel_id=1, source_target_pairs={{1,18},{2,17},{3,20},{4,19},{5,22},{6,21},{7,24},{8,23},{9,26},{10... | collective-permute-start | bytes 98312 | tf_op jit(solution)/shard_map/ppermute | solution.py:36
  28.7 8.2 %collective-permute-start.11 = (bf16[432,128]{1,0:T(8,128)(2,1)S(1)}, bf16[432,128]{1,0:T(8,128)(2,1)S(1)}, u32[]{:S(2)}, u32[]{:S(2)}) collective-permute-start(bf16[432,128]{1,0:T(8,128)(2,1)S(1)} %shard_map.58.mine), channel_id=1, source_target_pairs={{0,8},{1,9},{2,10},{3,11},{4,12},{5,13},{6,14},{7,15},{8,0},{9,1},... | collective-permute-start | bytes 331784 | tf_op jit(solution)/shard_map/ppermute | solution.py:41
  37.0 5.8 %collective-permute-start.14 = (bf16[432,128]{1,0:T(8,128)(2,1)S(1)}, bf16[432,128]{1,0:T(8,128)(2,1)S(1)}, u32[]{:S(2)}, u32[]{:S(2)}) collective-permute-start(bf16[432,128]{1,0:T(8,128)(2,1)S(1)} %shard_map.60.refs_0_.refs_4_), channel_id=1, source_target_pairs={{0,6},{1,7},{2,4},{3,5},{4,2},{5,3},{6,0},{7,1},{8,14},{9,15},{10,... | collective-permute-start | bytes 331784 | tf_op jit(solution)/shard_map/ppermute | solution.py:41
  39.1 6.2 %collective-permute-start.13 = (bf16[432,128]{1,0:T(8,128)(2,1)S(1)}, bf16[432,128]{1,0:T(8,128)(2,1)S(1)}, u32[]{:S(2)}, u32[]{:S(2)}) collective-permute-start(bf16[432,128]{1,0:T(8,128)(2,1)S(1)} %shard_map.60.refs_0_.refs_4_), channel_id=1, source_target_pairs={{0,2},{1,3},{2,0},{3,1},{4,6},{5,7},{6,4},{7,5},{8,10},{9,11},{10,... | collective-permute-start | bytes 331784 | tf_op jit(solution)/shard_map/ppermute | solution.py:41
  40.6 6.6 %collective-permute-start.12 = (bf16[432,128]{1,0:T(8,128)(2,1)S(1)}, bf16[432,128]{1,0:T(8,128)(2,1)S(1)}, u32[]{:S(2)}, u32[]{:S(2)}) collective-permute-start(bf16[432,128]{1,0:T(8,128)(2,1)S(1)} %shard_map.60.refs_0_.refs_4_), channel_id=1, source_target_pairs={{0,4},{1,5},{2,6},{3,7},{4,0},{5,1},{6,2},{7,3},{8,12},{9,13},{10,... | collective-permute-start | bytes 331784 | tf_op jit(solution)/shard_map/ppermute | solution.py:41
  41.9 6.0 %collective-permute-start.15 = (bf16[432,128]{1,0:T(8,128)(2,1)S(1)}, bf16[432,128]{1,0:T(8,128)(2,1)S(1)}, u32[]{:S(2)}, u32[]{:S(2)}) collective-permute-start(bf16[432,128]{1,0:T(8,128)(2,1)S(1)} %shard_map.60.refs_0_.refs_4_), channel_id=1, source_target_pairs={{0,1},{1,0},{2,3},{3,2},{4,5},{5,4},{6,7},{7,6},{8,9},{9,8},{10,11... | collective-permute-start | bytes 331784 | tf_op jit(solution)/shard_map/ppermute | solution.py:41
  42.8 6.7 %collective-permute-start.18 = (bf16[432,128]{1,0:T(8,128)(2,1)S(1)}, bf16[432,128]{1,0:T(8,128)(2,1)S(1)}, u32[]{:S(2)}, u32[]{:S(2)}) collective-permute-start(bf16[432,128]{1,0:T(8,128)(2,1)S(1)} %collective-permute-done.14.refs_3_.refs_7_), channel_id=1, source_target_pairs={{0,1},{1,0},{2,3},{3,2},{4,5},{5,4},{6,7},{7,6},{8,9},{9,8},{10,11... | collective-permute-start | bytes 331784 | tf_op jit(solution)/shard_map/ppermute | solution.py:41
  45.3 4.2 %collective-permute-start.17 = (bf16[432,128]{1,0:T(8,128)(2,1)S(1)}, bf16[432,128]{1,0:T(8,128)(2,1)S(1)}, u32[]{:S(2)}, u32[]{:S(2)}) collective-permute-start(bf16[432,128]{1,0:T(8,128)(2,1)S(1)} %collective-permute-done.13.refs_2_.refs_6_), channel_id=1, source_target_pairs={{0,1},{1,0},{2,3},{3,2},{4,5},{5,4},{6,7},{7,6},{8,9},{9,8},{10,11... | collective-permute-start | bytes 331784 | tf_op jit(solution)/shard_map/ppermute | solution.py:41
  47.2 2.3 %collective-permute-start.16 = (bf16[432,128]{1,0:T(8,128)(2,1)S(1)}, bf16[432,128]{1,0:T(8,128)(2,1)S(1)}, u32[]{:S(2)}, u32[]{:S(2)}) collective-permute-start(bf16[432,128]{1,0:T(8,128)(2,1)S(1)} %collective-permute-done.12.refs_1_.refs_5_), channel_id=1, source_target_pairs={{0,1},{1,0},{2,3},{3,2},{4,5},{5,4},{6,7},{7,6},{8,9},{9,8},{10,11... | collective-permute-start | bytes 331784 | tf_op jit(solution)/shard_map/ppermute | solution.py:41
  47.3 3.1 %collective-permute-start.20 = (f32[8,128]{1,0:T(8,128)S(1)}, f32[8,128]{1,0:T(8,128)S(1)}, u32[]{:S(2)}, u32[]{:S(2)}) collective-permute-start(f32[8,128]{1,0:T(8,128)S(1)} %shard_map.61.refs_0_), channel_id=1, source_target_pairs={{0,17},{1,16},{2,19},{3,18},{4,21},{5,20},{6,23},{7,22},{8,25},{9,... | collective-permute-start | bytes 12296 | tf_op jit(solution)/shard_map/ppermute | solution.py:53
  47.8 3.6 %collective-permute-start.19 = (f32[8,128]{1,0:T(8,128)S(1)}, f32[8,128]{1,0:T(8,128)S(1)}, u32[]{:S(2)}, u32[]{:S(2)}) collective-permute-start(f32[8,128]{1,0:T(8,128)S(1)} %shard_map.61.refs_0_), channel_id=1, source_target_pairs={{0,16},{1,17},{2,18},{3,19},{4,20},{5,21},{6,22},{7,23},{8,24},{9,... | collective-permute-start | bytes 12296 | tf_op jit(solution)/shard_map/ppermute | solution.py:53

commit v11 on v10

--- a/solution.py
+++ b/solution.py
@@ -438,7 +438,7 @@
         compiler_params=large,
     )(spot, incoming, grad, far, slopes, shifts)
     sends, keep = rest[:4], rest[4]
-    order = (2, 1, 3)
+    order = (1, 2, 3)
     got = {turn: exchange(sends[turn], 1) for turn in order + (0,)}
     across = []
     for turn in order:
@@ -449,8 +449,6 @@
             out_specs=VMEM,
             compiler_params=small,
         )(keep, got[turn])
-        if turn == order[-1]:
-            added, to_far = lax.optimization_barrier((added, to_far))
         across.append(exchange(added, masks[turn]))
     in_far = cross_far(to_far)
     across[2], in_far = lax.optimization_barrier((across[2], in_far))
@@ -500,7 +498,7 @@
                 value = jnp.where(there == n, other, value)
             blocks.append(value)
         gathered = jnp.concatenate(blocks, axis=0)
-    pieces = {turn: exchange(gathered, masks[turn]) for turn in (2, 1, 3)}
+    pieces = {turn: exchange(gathered, masks[turn]) for turn in (1, 2, 3)}
     ours = [gathered] + [pieces[turn] for turn in (1, 2, 3)]
     theirs = [exchange(piece, 1) for piece in ours]
     sums = [

time: 53.1 us -> 53.1 us (level)
  transfers between devices with their start and end apart: 21 -> 21, of which waited for: 11 -> 10; matrix products, arithmetic and copies ran while one was open for 0% -> 0% of each run, Pallas kernels for 9% -> 9%
where the time goes in v11:
time: 53.1 us; the launch traced here: 52.8 us
  starting transfers between devices  27 us (51%)
  waiting for transfers between devices  14.9 us (28%)
  Pallas kernels  10.2 us (19%)
  between operations  0.74 us (1%)
    ppermute x15, starting transfers between devices, exchange(): return lax.ppermute(value, 'slab', [(i, i ^ mask) for i in range(count)])  20.4 us
    ppermute x15, waiting for transfers between devices, exchange(): return lax.ppermute(value, 'slab', [(i, i ^ mask) for i in range(count)])  10.3 us
    ppermute x3, starting transfers between devices, cross(): return lax.ppermute(value, ('segment', 'slab'), route)  4.77 us
    ppermute x3, waiting for transfers between devices, cross(): return lax.ppermute(value, ('segment', 'slab'), route)  4.53 us
    pallas_call x1, Pallas kernels, shards(): pl.pallas_call(functools.partial(own_kernel, height), out_shape=(volume,...  2.35 us
    pallas_call x1, Pallas kernels, shards(): pl.pallas_call(functools.partial(first_kernel, height), out_shape=(volume...  1.86 us
    pallas_call x1, Pallas kernels, conv_back(): pl.pallas_call(functools.partial(back_kernel, height), out_shape=volume,...  1.79 us
    pallas_call x1, Pallas kernels, shards(): pl.pallas_call(functools.partial(place_kernel, bound, segments), out_shap...  1.38 us
  transfers between devices with their start and end apart: 21, of which 10 were waited for; matrix products, arithmetic and copies ran while one was open for 0% of the time, Pallas kernels for 9%

profile of v11, /device:TPU:0, one launch (start us, length us, event | category | flops | bytes accessed | tf_op | source)
XLA Modules:
  0.0 52.8 jit_solution(7101156154257369415)
XLA Ops:
  0.6 0.9 %shard_map.50 = (bf16[2,3,64,128]{3,2,1,0:T(8,128)(2,1)S(1)}, bf16[2,3,64,128]{3,2,1,0:T(8,128)(2,1)S(1)}) custom-call(bf16[2,4,64,128]{3,2,1,0:T(8,128)(2,1)} %bitcast.8, bf16[2,4,64,128]{3,2,1,0:T(8,128)(2,1)} %bitcast.10), custom_call_target="tpu_custom_call" | custom-call | tf_op jit(solution)/shard_map/pallas_call | solution.py:341
  1.6 0.5 collective-permute-start
  2.1 0.7 %collective-permute-start.1 = (bf16[2,3,64,128]{3,2,1,0:T(8,128)(2,1)S(1)}, bf16[2,3,64,128]{3,2,1,0:T(8,128)(2,1)S(1)}, u32[]{:S(2)}, u32[]{:S(2)}) collective-permute-start(bf16[2,3,64,128]{3,2,1,0:T(8,128)(2,1)S(1)} %get-tuple-element.25), channel_id=1, source_target_pairs={{1,2},{2,1},{3,4},{4,3},{5,6},{6,5},{7,8},{8,7},{9,10},{10,9},{11,... | collective-permute-start | bytes 294920 | tf_op jit(solution)/shard_map/ppermute | solution.py:26
  2.8 2.3 %shard_map.51 = (bf16[2,4,64,128]{3,2,1,0:T(8,128)(2,1)S(1)}, bf16[2,4,64,128]{3,2,1,0:T(8,128)(2,1)S(1)}, bf16[3456,128]{1,0:T(8,128)(2,1)S(1)}, bf16[3456,128]{1,0:T(8,128)(2,1)S(1)}, f32[768,128]{1,0:T(8,128)S(1)}) custom-call(bf16[2,4,64,128]{3,2,1,0:T(8,128)(2,1)} %bitcast.9, bf16[2,4,64,128]{3,2,1,0:T(8,128)(2,1)} %bitcast.11, bf16[3456,128]{1,0:T(8,128)(2,1)} %bitcast.7), custom_call_target="tpu_custom_call" | custom-call | tf_op jit(solution)/shard_map/pallas_call | solution.py:355
  5.1 0.0 collective-permute-done.near
  5.1 1.9 %shard_map.52 = (bf16[2,4,64,128]{3,2,1,0:T(8,128)(2,1)S(1)}, f32[768,128]{1,0:T(8,128)S(1)}, bf16[2,1,64,128]{3,2,1,0:T(8,128)(2,1)S(1)}) custom-call(bf16[2,3,64,128]{3,2,1,0:T(8,128)(2,1)S(1)} %collective-permute-done.near, bf16[2,3,64,128]{3,2,1,0:T(8,128)(2,1)S(1)} %collective-permute-done.1.far, bf16[2,4,64,128]{3,2,1,0:T(8,128)(2,1)S(1)} %get-tuple-element.26.grad, ...), custom_call_target="tpu_custom_call" | custom-call | tf_op jit(solution)/shard_map/pallas_call | solution.py:370
  7.0 2.6 %collective-permute-start.2 = (bf16[2,4,64,128]{3,2,1,0:T(8,128)(2,1)S(1)}, bf16[2,4,64,128]{3,2,1,0:T(8,128)(2,1)S(1)}, u32[]{:S(2)}, u32[]{:S(2)}) collective-permute-start(bf16[2,4,64,128]{3,2,1,0:T(8,128)(2,1)S(1)} %get-tuple-element.30.after), channel_id=1, source_target_pairs={{0,16},{1,17},{2,18},{3,19},{4,20},{5,21},{6,22},{7,23},{8,24},{9,... | collective-permute-start | bytes 393224 | tf_op jit(solution)/shard_map/ppermute | solution.py:53
  9.6 0.2 shard_map.53.shifts
  9.8 2.7 %collective-permute-done.2.incoming = bf16[2,4,64,128]{3,2,1,0:T(8,128)(2,1)S(1)} collective-permute-done((bf16[2,4,64,128]{3,2,1,0:T(8,128)(2,1)S(1)}, bf16[2,4,64,128]{3,2,1,0:T(8,128)(2,1)S(1)}, u32[]{:S(2)}, u32[]{:S(2)}) %collective-permute-start.2) | collective-permute-done | bytes 131104 | tf_op jit(solution)/shard_map/ppermute | solution.py:53
  12.5 1.2 %shard_map.54 = (bf16[2,4,64,128]{3,2,1,0:T(8,128)(2,1)S(1)}, bf16[768,128]{1,0:T(8,128)(2,1)S(1)}, f32[128,128]{1,0:T(8,128)S(1)}, bf16[560,128]{1,0:T(8,128)(2...) custom-call(s32[1]{0:T(128)} %bitcast.spot, ...), custom_call_target="tpu_custom_call" | custom-call | tf_op jit(solution)/shard_map/pallas_call | solution.py:423
  13.8 2.6 %collective-permute-start.8 = (bf16[432,128]{1,0:T(8,128)(2,1)S(1)}, bf16[432,128]{1,0:T(8,128)(2,1)S(1)}, u32[]{:S(2)}, u32[]{:S(2)}) collective-permute-start(bf16[432,128]{1,0:T(8,128)(2,1)S(1)} %get-tuple-element.37), channel_id=1, source_target_pairs={{0,1},{1,0},{2,3},{3,2},{4,5},{5,4},{6,7},{7,6},{8,9},{9,8},{10,11... | collective-permute-start | bytes 331784 | tf_op jit(solution)/shard_map/ppermute | solution.py:41
  16.3 0.1 collective-permute-start.4
  16.4 0.4 collective-permute-start.6
  16.8 0.1 collective-permute-start.3
  16.9 0.4 collective-permute-done.8.got
  17.3 4.9 %collective-permute-start.9 = (bf16[432,128]{1,0:T(8,128)(2,1)S(1)}, bf16[432,128]{1,0:T(8,128)(2,1)S(1)}, u32[]{:S(2)}, u32[]{:S(2)}) collective-permute-start(bf16[432,128]{1,0:T(8,128)(2,1)S(1)} %shard_map.57), channel_id=1, source_target_pairs={{0,6},{1,7},{2,4},{3,5},{4,2},{5,3},{6,0},{7,1},{8,14},{9,15},{10,... | collective-permute-start | bytes 331784 | tf_op jit(solution)/shard_map/ppermute | solution.py:41
  22.3 0.5 collective-permute-start.5
  22.8 0.0 collective-permute-done.6.got
  22.8 1.0 %collective-permute-start.7 = (bf16[432,128]{1,0:T(8,128)(2,1)S(1)}, bf16[432,128]{1,0:T(8,128)(2,1)S(1)}, u32[]{:S(2)}, u32[]{:S(2)}) collective-permute-start(bf16[432,128]{1,0:T(8,128)(2,1)S(1)} %shard_map.56), channel_id=1, source_target_pairs={{0,2},{1,3},{2,0},{3,1},{4,6},{5,7},{6,4},{7,5},{8,10},{9,11},{10,... | collective-permute-start | bytes 331784 | tf_op jit(solution)/shard_map/ppermute | solution.py:41
  23.9 0.7 %collective-permute-start.10 = (bf16[2,1,64,128]{3,2,1,0:T(8,128)(2,1)S(1)}, bf16[2,1,64,128]{3,2,1,0:T(8,128)(2,1)S(1)}, u32[]{:S(2)}, u32[]{:S(2)}) collective-permute-start(bf16[2,1,64,128]{3,2,1,0:T(8,128)(2,1)S(1)} %get-tuple-element.38), channel_id=1, source_target_pairs={{1,18},{2,17},{3,20},{4,19},{5,22},{6,21},{7,24},{8,23},{9,26},{10... | collective-permute-start | bytes 98312 | tf_op jit(solution)/shard_map/ppermute | solution.py:36
  24.5 0.0 collective-permute-done.10.in_far
  24.6 1.1 %collective-permute-done.9.refs_3_ = bf16[432,128]{1,0:T(8,128)(2,1)S(1)} collective-permute-done((bf16[432,128]{1,0:T(8,128)(2,1)S(1)}, bf16[432,128]{1,0:T(8,128)(2,1)S(1)}, u32[]{:S(2)}, u32[]{:S(2)}) %collective-permute-start.9) | collective-permute-done | bytes 110624 | tf_op jit(solution)/shard_map/ppermute | solution.py:41
  25.7 0.0 collective-permute-done.3.refs_0_.by_near
  25.7 2.5 %collective-permute-done.5.refs_1_ = bf16[432,128]{1,0:T(8,128)(2,1)S(1)} collective-permute-done((bf16[432,128]{1,0:T(8,128)(2,1)S(1)}, bf16[432,128]{1,0:T(8,128)(2,1)S(1)}, u32[]{:S(2)}, u32[]{:S(2)}) %collective-permute-start.5) | collective-permute-done | bytes 110624 | tf_op jit(solution)/shard_map/ppermute | solution.py:41
  28.2 0.0 collective-permute-done.7.refs_2_
  28.2 0.1 shard_map.58.mine
  28.3 5.8 %collective-permute-start.11 = (bf16[432,128]{1,0:T(8,128)(2,1)S(1)}, bf16[432,128]{1,0:T(8,128)(2,1)S(1)}, u32[]{:S(2)}, u32[]{:S(2)}) collective-permute-start(bf16[432,128]{1,0:T(8,128)(2,1)S(1)} %shard_map.58.mine), channel_id=1, source_target_pairs={{0,8},{1,9},{2,10},{3,11},{4,12},{5,13},{6,14},{7,15},{8,0},{9,1},... | collective-permute-start | bytes 331784 | tf_op jit(solution)/shard_map/ppermute | solution.py:41
  34.1 1.8 %shard_map.59 = bf16[2,4,64,128]{3,2,1,0:T(8,128)(2,1)} custom-call(bf16[768,128]{1,0:T(8,128)(2,1)S(1)} %get-tuple-element.40.deltas, bf16[560,128]{1,0:T(8,128)(2,1)S(1)} %collective-permute-done.3.refs_0_.by_near, bf16[2,1,64,128]{3,2,1,0:T(8,128)(2,1)S(1)} %collective-permute-done.10.in_far, f32[128,128]{1,0:T(8,128)S(1)} %get-tuple-element.42.far_slope, ...), custom_call_target="tpu_custom_call" | custom-call | tf_op jit(solution)/shard_map/pallas_call | solution.py:380
  35.9 1.0 %collective-permute-done.11.other = bf16[432,128]{1,0:T(8,128)(2,1)S(1)} collective-permute-done((bf16[432,128]{1,0:T(8,128)(2,1)S(1)}, bf16[432,128]{1,0:T(8,128)(2,1)S(1)}, u32[]{:S(2)}, u32[]{:S(2)}) %collective-permute-start.11) | collective-permute-done | bytes 110624 | tf_op jit(solution)/shard_map/ppermute | solution.py:41
  37.0 2.2 %collective-permute-start.14 = (bf16[432,128]{1,0:T(8,128)(2,1)S(1)}, bf16[432,128]{1,0:T(8,128)(2,1)S(1)}, u32[]{:S(2)}, u32[]{:S(2)}) collective-permute-start(bf16[432,128]{1,0:T(8,128)(2,1)S(1)} %shard_map.60.refs_0_.refs_4_), channel_id=1, source_target_pairs={{0,6},{1,7},{2,4},{3,5},{4,2},{5,3},{6,0},{7,1},{8,14},{9,15},{10,... | collective-permute-start | bytes 331784 | tf_op jit(solution)/shard_map/ppermute | solution.py:41
  39.1 1.5 %collective-permute-start.13 = (bf16[432,128]{1,0:T(8,128)(2,1)S(1)}, bf16[432,128]{1,0:T(8,128)(2,1)S(1)}, u32[]{:S(2)}, u32[]{:S(2)}) collective-permute-start(bf16[432,128]{1,0:T(8,128)(2,1)S(1)} %shard_map.60.refs_0_.refs_4_), channel_id=1, source_target_pairs={{0,2},{1,3},{2,0},{3,1},{4,6},{5,7},{6,4},{7,5},{8,10},{9,11},{10,... | collective-permute-start | bytes 331784 | tf_op jit(solution)/shard_map/ppermute | solution.py:41
  40.6 1.2 %collective-permute-start.12 = (bf16[432,128]{1,0:T(8,128)(2,1)S(1)}, bf16[432,128]{1,0:T(8,128)(2,1)S(1)}, u32[]{:S(2)}, u32[]{:S(2)}) collective-permute-start(bf16[432,128]{1,0:T(8,128)(2,1)S(1)} %shard_map.60.refs_0_.refs_4_), channel_id=1, source_target_pairs={{0,4},{1,5},{2,6},{3,7},{4,0},{5,1},{6,2},{7,3},{8,12},{9,13},{10,... | collective-permute-start | bytes 331784 | tf_op jit(solution)/shard_map/ppermute | solution.py:41
  41.9 0.0 collective-permute-start.15
  41.9 0.9 %collective-permute-done.14.refs_3_.refs_7_ = bf16[432,128]{1,0:T(8,128)(2,1)S(1)} collective-permute-done((bf16[432,128]{1,0:T(8,128)(2,1)S(1)}, bf16[432,128]{1,0:T(8,128)(2,1)S(1)}, u32[]{:S(2)}, u32[]{:S(2)}) %collective-permute-start.14) | collective-permute-done | bytes 110624 | tf_op jit(solution)/shard_map/ppermute | solution.py:41
  42.8 2.5 %collective-permute-done.13.refs_2_.refs_6_ = bf16[432,128]{1,0:T(8,128)(2,1)S(1)} collective-permute-done((bf16[432,128]{1,0:T(8,128)(2,1)S(1)}, bf16[432,128]{1,0:T(8,128)(2,1)S(1)}, u32[]{:S(2)}, u32[]{:S(2)}) %collective-permute-start.13) | collective-permute-done | bytes 110624 | tf_op jit(solution)/shard_map/ppermute | solution.py:41
  45.3 0.0 collective-permute-start.17
  45.3 1.8 %collective-permute-done.12.refs_1_.refs_5_ = bf16[432,128]{1,0:T(8,128)(2,1)S(1)} collective-permute-done((bf16[432,128]{1,0:T(8,128)(2,1)S(1)}, bf16[432,128]{1,0:T(8,128)(2,1)S(1)}, u32[]{:S(2)}, u32[]{:S(2)}) %collective-permute-start.12) | collective-permute-done | bytes 110624 | tf_op jit(solution)/shard_map/ppermute | solution.py:41
  47.2 0.0 collective-permute-start.16
  47.2 0.1 shard_map.61.refs_0_
  47.3 0.5 %collective-permute-start.20 = (f32[8,128]{1,0:T(8,128)S(1)}, f32[8,128]{1,0:T(8,128)S(1)}, u32[]{:S(2)}, u32[]{:S(2)}) collective-permute-start(f32[8,128]{1,0:T(8,128)S(1)} %shard_map.61.refs_0_), channel_id=1, source_target_pairs={{0,17},{1,16},{2,19},{3,18},{4,21},{5,20},{6,23},{7,22},{8,25},{9,... | collective-permute-start | bytes 12296 | tf_op jit(solution)/shard_map/ppermute | solution.py:53
  47.8 1.7 %collective-permute-start.19 = (f32[8,128]{1,0:T(8,128)S(1)}, f32[8,128]{1,0:T(8,128)S(1)}, u32[]{:S(2)}, u32[]{:S(2)}) collective-permute-start(f32[8,128]{1,0:T(8,128)S(1)} %shard_map.61.refs_0_), channel_id=1, source_target_pairs={{0,16},{1,17},{2,18},{3,19},{4,20},{5,21},{6,22},{7,23},{8,24},{9,... | collective-permute-start | bytes 12296 | tf_op jit(solution)/shard_map/ppermute | solution.py:53
  49.5 0.0 collective-permute-done.18.refs_3_.refs_11_
  49.5 0.0 collective-permute-done.17.refs_2_.refs_10_
  49.5 0.0 collective-permute-done.16.refs_1_.refs_9_
  49.5 0.1 shard_map.62.refs_1_
  49.6 0.8 %collective-permute-done.20.refs_3_ = f32[8,128]{1,0:T(8,128)S(1)} collective-permute-done((f32[8,128]{1,0:T(8,128)S(1)}, f32[8,128]{1,0:T(8,128)S(1)}, u32[]{:S(2)}, u32[]{:S(2)}) %collective-permute-start.20) | collective-permute-done | bytes 4128 | tf_op jit(solution)/shard_map/ppermute | solution.py:53
  50.4 1.1 %collective-permute-done.19.refs_2_ = f32[8,128]{1,0:T(8,128)S(1)} collective-permute-done((f32[8,128]{1,0:T(8,128)S(1)}, f32[8,128]{1,0:T(8,128)S(1)}, u32[]{:S(2)}, u32[]{:S(2)}) %collective-permute-start.19) | collective-permute-done | bytes 4128 | tf_op jit(solution)/shard_map/ppermute | solution.py:53
  51.5 1.4 %shard_map.63 = f32[8,432,128]{2,1,0:T(8,128)} custom-call(s32[1]{0:T(128)} %bitcast.spot, f32[8,128]{1,0:T(8,128)S(1)} %shard_map.61.refs_0_, f32[8,128]{1,0:T(8,128)S(1)} %shard_map.62.refs_1_, f32[8,128]{1,0:T(8,128)S(1)} %collective-permute-done.19.refs_2_, f32[8,128]{1,0:T(8,128)S(1)} %collective-permute-done.20.refs_3_, ...), custom_call_target="tpu_custom_call" | custom-call | tf_op jit(solution)/shard_map/pallas_call | solution.py:516
  (8 shorter events, 0.1 us)
Async XLA Ops:
  1.6 3.5 %collective-permute-start = (bf16[2,3,64,128]{3,2,1,0:T(8,128)(2,1)S(1)}, bf16[2,3,64,128]{3,2,1,0:T(8,128)(2,1)S(1)}, u32[]{:S(2)}, u32[]{:S(2)}) collective-permute-start(bf16[2,3,64,128]{3,2,1,0:T(8,128)(2,1)S(1)} %get-tuple-element.24), channel_id=1, source_target_pairs={{0,1},{1,0},{2,3},{3,2},{4,5},{5,4},{6,7},{7,6},{8,9},{9,8},{10,11... | collective-permute-start | bytes 294920 | tf_op jit(solution)/shard_map/ppermute | solution.py:26
  2.1 3.0 %collective-permute-start.1 = (bf16[2,3,64,128]{3,2,1,0:T(8,128)(2,1)S(1)}, bf16[2,3,64,128]{3,2,1,0:T(8,128)(2,1)S(1)}, u32[]{:S(2)}, u32[]{:S(2)}) collective-permute-start(bf16[2,3,64,128]{3,2,1,0:T(8,128)(2,1)S(1)} %get-tuple-element.25), channel_id=1, source_target_pairs={{1,2},{2,1},{3,4},{4,3},{5,6},{6,5},{7,8},{8,7},{9,10},{10,9},{11,... | collective-permute-start | bytes 294920 | tf_op jit(solution)/shard_map/ppermute | solution.py:26
  7.0 5.5 %collective-permute-start.2 = (bf16[2,4,64,128]{3,2,1,0:T(8,128)(2,1)S(1)}, bf16[2,4,64,128]{3,2,1,0:T(8,128)(2,1)S(1)}, u32[]{:S(2)}, u32[]{:S(2)}) collective-permute-start(bf16[2,4,64,128]{3,2,1,0:T(8,128)(2,1)S(1)} %get-tuple-element.30.after), channel_id=1, source_target_pairs={{0,16},{1,17},{2,18},{3,19},{4,20},{5,21},{6,22},{7,23},{8,24},{9,... | collective-permute-start | bytes 393224 | tf_op jit(solution)/shard_map/ppermute | solution.py:53
  13.8 3.5 %collective-permute-start.8 = (bf16[432,128]{1,0:T(8,128)(2,1)S(1)}, bf16[432,128]{1,0:T(8,128)(2,1)S(1)}, u32[]{:S(2)}, u32[]{:S(2)}) collective-permute-start(bf16[432,128]{1,0:T(8,128)(2,1)S(1)} %get-tuple-element.37), channel_id=1, source_target_pairs={{0,1},{1,0},{2,3},{3,2},{4,5},{5,4},{6,7},{7,6},{8,9},{9,8},{10,11... | collective-permute-start | bytes 331784 | tf_op jit(solution)/shard_map/ppermute | solution.py:41
  16.3 5.9 %collective-permute-start.4 = (bf16[432,128]{1,0:T(8,128)(2,1)S(1)}, bf16[432,128]{1,0:T(8,128)(2,1)S(1)}, u32[]{:S(2)}, u32[]{:S(2)}) collective-permute-start(bf16[432,128]{1,0:T(8,128)(2,1)S(1)} %get-tuple-element.35), channel_id=1, source_target_pairs={{0,1},{1,0},{2,3},{3,2},{4,5},{5,4},{6,7},{7,6},{8,9},{9,8},{10,11... | collective-permute-start | bytes 331784 | tf_op jit(solution)/shard_map/ppermute | solution.py:41
  16.4 6.4 %collective-permute-start.6 = (bf16[432,128]{1,0:T(8,128)(2,1)S(1)}, bf16[432,128]{1,0:T(8,128)(2,1)S(1)}, u32[]{:S(2)}, u32[]{:S(2)}) collective-permute-start(bf16[432,128]{1,0:T(8,128)(2,1)S(1)} %get-tuple-element.36), channel_id=1, source_target_pairs={{0,1},{1,0},{2,3},{3,2},{4,5},{5,4},{6,7},{7,6},{8,9},{9,8},{10,11... | collective-permute-start | bytes 331784 | tf_op jit(solution)/shard_map/ppermute | solution.py:41
  16.8 8.9 %collective-permute-start.3 = (bf16[560,128]{1,0:T(8,128)(2,1)S(1)}, bf16[560,128]{1,0:T(8,128)(2,1)S(1)}, u32[]{:S(2)}, u32[]{:S(2)}) collective-permute-start(bf16[560,128]{1,0:T(8,128)(2,1)S(1)} %get-tuple-element.34), channel_id=1, source_target_pairs={{0,1},{1,0},{2,3},{3,2},{4,5},{5,4},{6,7},{7,6},{8,9},{9,8},{10,11... | collective-permute-start | bytes 430088 | tf_op jit(solution)/shard_map/ppermute | solution.py:41
  17.3 8.4 %collective-permute-start.9 = (bf16[432,128]{1,0:T(8,128)(2,1)S(1)}, bf16[432,128]{1,0:T(8,128)(2,1)S(1)}, u32[]{:S(2)}, u32[]{:S(2)}) collective-permute-start(bf16[432,128]{1,0:T(8,128)(2,1)S(1)} %shard_map.57), channel_id=1, source_target_pairs={{0,6},{1,7},{2,4},{3,5},{4,2},{5,3},{6,0},{7,1},{8,14},{9,15},{10,... | collective-permute-start | bytes 331784 | tf_op jit(solution)/shard_map/ppermute | solution.py:41
  22.3 5.9 %collective-permute-start.5 = (bf16[432,128]{1,0:T(8,128)(2,1)S(1)}, bf16[432,128]{1,0:T(8,128)(2,1)S(1)}, u32[]{:S(2)}, u32[]{:S(2)}) collective-permute-start(bf16[432,128]{1,0:T(8,128)(2,1)S(1)} %shard_map.55), channel_id=1, source_target_pairs={{0,4},{1,5},{2,6},{3,7},{4,0},{5,1},{6,2},{7,3},{8,12},{9,13},{10,... | collective-permute-start | bytes 331784 | tf_op jit(solution)/shard_map/ppermute | solution.py:41
  22.8 5.3 %collective-permute-start.7 = (bf16[432,128]{1,0:T(8,128)(2,1)S(1)}, bf16[432,128]{1,0:T(8,128)(2,1)S(1)}, u32[]{:S(2)}, u32[]{:S(2)}) collective-permute-start(bf16[432,128]{1,0:T(8,128)(2,1)S(1)} %shard_map.56), channel_id=1, source_target_pairs={{0,2},{1,3},{2,0},{3,1},{4,6},{5,7},{6,4},{7,5},{8,10},{9,11},{10,... | collective-permute-start | bytes 331784 | tf_op jit(solution)/shard_map/ppermute | solution.py:41
  23.9 0.7 %collective-permute-start.10 = (bf16[2,1,64,128]{3,2,1,0:T(8,128)(2,1)S(1)}, bf16[2,1,64,128]{3,2,1,0:T(8,128)(2,1)S(1)}, u32[]{:S(2)}, u32[]{:S(2)}) collective-permute-start(bf16[2,1,64,128]{3,2,1,0:T(8,128)(2,1)S(1)} %get-tuple-element.38), channel_id=1, source_target_pairs={{1,18},{2,17},{3,20},{4,19},{5,22},{6,21},{7,24},{8,23},{9,26},{10... | collective-permute-start | bytes 98312 | tf_op jit(solution)/shard_map/ppermute | solution.py:36
  28.3 8.7 %collective-permute-start.11 = (bf16[432,128]{1,0:T(8,128)(2,1)S(1)}, bf16[432,128]{1,0:T(8,128)(2,1)S(1)}, u32[]{:S(2)}, u32[]{:S(2)}) collective-permute-start(bf16[432,128]{1,0:T(8,128)(2,1)S(1)} %shard_map.58.mine), channel_id=1, source_target_pairs={{0,8},{1,9},{2,10},{3,11},{4,12},{5,13},{6,14},{7,15},{8,0},{9,1},... | collective-permute-start | bytes 331784 | tf_op jit(solution)/shard_map/ppermute | solution.py:41
  37.0 5.8 %collective-permute-start.14 = (bf16[432,128]{1,0:T(8,128)(2,1)S(1)}, bf16[432,128]{1,0:T(8,128)(2,1)S(1)}, u32[]{:S(2)}, u32[]{:S(2)}) collective-permute-start(bf16[432,128]{1,0:T(8,128)(2,1)S(1)} %shard_map.60.refs_0_.refs_4_), channel_id=1, source_target_pairs={{0,6},{1,7},{2,4},{3,5},{4,2},{5,3},{6,0},{7,1},{8,14},{9,15},{10,... | collective-permute-start | bytes 331784 | tf_op jit(solution)/shard_map/ppermute | solution.py:41
  39.1 6.2 %collective-permute-start.13 = (bf16[432,128]{1,0:T(8,128)(2,1)S(1)}, bf16[432,128]{1,0:T(8,128)(2,1)S(1)}, u32[]{:S(2)}, u32[]{:S(2)}) collective-permute-start(bf16[432,128]{1,0:T(8,128)(2,1)S(1)} %shard_map.60.refs_0_.refs_4_), channel_id=1, source_target_pairs={{0,2},{1,3},{2,0},{3,1},{4,6},{5,7},{6,4},{7,5},{8,10},{9,11},{10,... | collective-permute-start | bytes 331784 | tf_op jit(solution)/shard_map/ppermute | solution.py:41
  40.6 6.6 %collective-permute-start.12 = (bf16[432,128]{1,0:T(8,128)(2,1)S(1)}, bf16[432,128]{1,0:T(8,128)(2,1)S(1)}, u32[]{:S(2)}, u32[]{:S(2)}) collective-permute-start(bf16[432,128]{1,0:T(8,128)(2,1)S(1)} %shard_map.60.refs_0_.refs_4_), channel_id=1, source_target_pairs={{0,4},{1,5},{2,6},{3,7},{4,0},{5,1},{6,2},{7,3},{8,12},{9,13},{10,... | collective-permute-start | bytes 331784 | tf_op jit(solution)/shard_map/ppermute | solution.py:41
  41.9 6.0 %collective-permute-start.15 = (bf16[432,128]{1,0:T(8,128)(2,1)S(1)}, bf16[432,128]{1,0:T(8,128)(2,1)S(1)}, u32[]{:S(2)}, u32[]{:S(2)}) collective-permute-start(bf16[432,128]{1,0:T(8,128)(2,1)S(1)} %shard_map.60.refs_0_.refs_4_), channel_id=1, source_target_pairs={{0,1},{1,0},{2,3},{3,2},{4,5},{5,4},{6,7},{7,6},{8,9},{9,8},{10,11... | collective-permute-start | bytes 331784 | tf_op jit(solution)/shard_map/ppermute | solution.py:41
  42.8 6.7 %collective-permute-start.18 = (bf16[432,128]{1,0:T(8,128)(2,1)S(1)}, bf16[432,128]{1,0:T(8,128)(2,1)S(1)}, u32[]{:S(2)}, u32[]{:S(2)}) collective-permute-start(bf16[432,128]{1,0:T(8,128)(2,1)S(1)} %collective-permute-done.14.refs_3_.refs_7_), channel_id=1, source_target_pairs={{0,1},{1,0},{2,3},{3,2},{4,5},{5,4},{6,7},{7,6},{8,9},{9,8},{10,11... | collective-permute-start | bytes 331784 | tf_op jit(solution)/shard_map/ppermute | solution.py:41
  45.3 4.2 %collective-permute-start.17 = (bf16[432,128]{1,0:T(8,128)(2,1)S(1)}, bf16[432,128]{1,0:T(8,128)(2,1)S(1)}, u32[]{:S(2)}, u32[]{:S(2)}) collective-permute-start(bf16[432,128]{1,0:T(8,128)(2,1)S(1)} %collective-permute-done.13.refs_2_.refs_6_), channel_id=1, source_target_pairs={{0,1},{1,0},{2,3},{3,2},{4,5},{5,4},{6,7},{7,6},{8,9},{9,8},{10,11... | collective-permute-start | bytes 331784 | tf_op jit(solution)/shard_map/ppermute | solution.py:41
  47.2 2.3 %collective-permute-start.16 = (bf16[432,128]{1,0:T(8,128)(2,1)S(1)}, bf16[432,128]{1,0:T(8,128)(2,1)S(1)}, u32[]{:S(2)}, u32[]{:S(2)}) collective-permute-start(bf16[432,128]{1,0:T(8,128)(2,1)S(1)} %collective-permute-done.12.refs_1_.refs_5_), channel_id=1, source_target_pairs={{0,1},{1,0},{2,3},{3,2},{4,5},{5,4},{6,7},{7,6},{8,9},{9,8},{10,11... | collective-permute-start | bytes 331784 | tf_op jit(solution)/shard_map/ppermute | solution.py:41
  47.3 3.1 %collective-permute-start.20 = (f32[8,128]{1,0:T(8,128)S(1)}, f32[8,128]{1,0:T(8,128)S(1)}, u32[]{:S(2)}, u32[]{:S(2)}) collective-permute-start(f32[8,128]{1,0:T(8,128)S(1)} %shard_map.61.refs_0_), channel_id=1, source_target_pairs={{0,17},{1,16},{2,19},{3,18},{4,21},{5,20},{6,23},{7,22},{8,25},{9,... | collective-permute-start | bytes 12296 | tf_op jit(solution)/shard_map/ppermute | solution.py:53
  47.8 3.6 %collective-permute-start.19 = (f32[8,128]{1,0:T(8,128)S(1)}, f32[8,128]{1,0:T(8,128)S(1)}, u32[]{:S(2)}, u32[]{:S(2)}) collective-permute-start(f32[8,128]{1,0:T(8,128)S(1)} %shard_map.61.refs_0_), channel_id=1, source_target_pairs={{0,16},{1,17},{2,18},{3,19},{4,20},{5,21},{6,22},{7,23},{8,24},{9,... | collective-permute-start | bytes 12296 | tf_op jit(solution)/shard_map/ppermute | solution.py:53

commit v12 on v11

--- a/solution.py
+++ b/solution.py
@@ -117,15 +117,15 @@
 ):
     micro, depth, cells, channels = acts.shape
     block, span = micro * cells, 9 * channels
-    pairs = ((stored_acts, acts), (stored, weight), (stored_grad, grad))
+    pairs = ((stored, weight), (stored_acts, acts), (stored_grad, grad))
     copies = [pltpu.make_async_copy(a, b, sems.at[n]) for n, (a, b) in enumerate(pairs)]
     for copy in copies:
         copy.start()
-    copies[0].wait()
+    copies[1].wait()
     for n in range(depth):
         for m in range(micro):
             write_shifts(acts[m, n], height, own, n * block + m * cells)
-    copies[1].wait()
+    copies[0].wait()
     copies[2].wait()
     part[...] = jnp.zeros(part.shape, F32)
     for dz in range(3):

time: 53.1 us -> 53.1 us (level)
  no operation moved by 1% of the time
where the time goes in v12:
time: 53.1 us; the launch traced here: 52.8 us
  starting transfers between devices  26.9 us (51%)
  waiting for transfers between devices  14.9 us (28%)
  Pallas kernels  10.3 us (19%)
  between operations  0.74 us (1%)
    ppermute x15, starting transfers between devices, exchange(): return lax.ppermute(value, 'slab', [(i, i ^ mask) for i in range(count)])  20.3 us
    ppermute x15, waiting for transfers between devices, exchange(): return lax.ppermute(value, 'slab', [(i, i ^ mask) for i in range(count)])  10.3 us
    ppermute x3, starting transfers between devices, cross(): return lax.ppermute(value, ('segment', 'slab'), route)  4.77 us
    ppermute x3, waiting for transfers between devices, cross(): return lax.ppermute(value, ('segment', 'slab'), route)  4.53 us
    pallas_call x1, Pallas kernels, shards(): pl.pallas_call(functools.partial(own_kernel, height), out_shape=(volume,...  2.43 us
    pallas_call x1, Pallas kernels, shards(): pl.pallas_call(functools.partial(first_kernel, height), out_shape=(volume...  1.86 us
    pallas_call x1, Pallas kernels, conv_back(): pl.pallas_call(functools.partial(back_kernel, height), out_shape=volume,...  1.79 us
    pallas_call x1, Pallas kernels, shards(): pl.pallas_call(functools.partial(place_kernel, bound, segments), out_shap...  1.38 us
  transfers between devices with their start and end apart: 21, of which 10 were waited for; matrix products, arithmetic and copies ran while one was open for 0% of the time, Pallas kernels for 9%

profile of v12, /device:TPU:0, one launch (start us, length us, event | category | flops | bytes accessed | tf_op | source)
XLA Modules:
  0.0 52.8 jit_solution(3775426382942735271)
XLA Ops:
  0.6 0.9 %shard_map.50 = (bf16[2,3,64,128]{3,2,1,0:T(8,128)(2,1)S(1)}, bf16[2,3,64,128]{3,2,1,0:T(8,128)(2,1)S(1)}) custom-call(bf16[2,4,64,128]{3,2,1,0:T(8,128)(2,1)} %bitcast.8, bf16[2,4,64,128]{3,2,1,0:T(8,128)(2,1)} %bitcast.10), custom_call_target="tpu_custom_call" | custom-call | tf_op jit(solution)/shard_map/pallas_call | solution.py:341
  1.6 0.5 collective-permute-start
  2.1 0.7 %collective-permute-start.1 = (bf16[2,3,64,128]{3,2,1,0:T(8,128)(2,1)S(1)}, bf16[2,3,64,128]{3,2,1,0:T(8,128)(2,1)S(1)}, u32[]{:S(2)}, u32[]{:S(2)}) collective-permute-start(bf16[2,3,64,128]{3,2,1,0:T(8,128)(2,1)S(1)} %get-tuple-element.25), channel_id=1, source_target_pairs={{1,2},{2,1},{3,4},{4,3},{5,6},{6,5},{7,8},{8,7},{9,10},{10,9},{11,... | collective-permute-start | bytes 294920 | tf_op jit(solution)/shard_map/ppermute | solution.py:26
  2.8 2.4 %shard_map.51 = (bf16[2,4,64,128]{3,2,1,0:T(8,128)(2,1)S(1)}, bf16[2,4,64,128]{3,2,1,0:T(8,128)(2,1)S(1)}, bf16[3456,128]{1,0:T(8,128)(2,1)S(1)}, bf16[3456,128]{1,0:T(8,128)(2,1)S(1)}, f32[768,128]{1,0:T(8,128)S(1)}) custom-call(bf16[2,4,64,128]{3,2,1,0:T(8,128)(2,1)} %bitcast.9, bf16[2,4,64,128]{3,2,1,0:T(8,128)(2,1)} %bitcast.11, bf16[3456,128]{1,0:T(8,128)(2,1)} %bitcast.7), custom_call_target="tpu_custom_call" | custom-call | tf_op jit(solution)/shard_map/pallas_call | solution.py:355
  5.2 0.0 collective-permute-done.1.far
  5.2 1.9 %shard_map.52 = (bf16[2,4,64,128]{3,2,1,0:T(8,128)(2,1)S(1)}, f32[768,128]{1,0:T(8,128)S(1)}, bf16[2,1,64,128]{3,2,1,0:T(8,128)(2,1)S(1)}) custom-call(bf16[2,3,64,128]{3,2,1,0:T(8,128)(2,1)S(1)} %collective-permute-done.near, bf16[2,3,64,128]{3,2,1,0:T(8,128)(2,1)S(1)} %collective-permute-done.1.far, bf16[2,4,64,128]{3,2,1,0:T(8,128)(2,1)S(1)} %get-tuple-element.26.grad, ...), custom_call_target="tpu_custom_call" | custom-call | tf_op jit(solution)/shard_map/pallas_call | solution.py:370
  7.1 2.6 %collective-permute-start.2 = (bf16[2,4,64,128]{3,2,1,0:T(8,128)(2,1)S(1)}, bf16[2,4,64,128]{3,2,1,0:T(8,128)(2,1)S(1)}, u32[]{:S(2)}, u32[]{:S(2)}) collective-permute-start(bf16[2,4,64,128]{3,2,1,0:T(8,128)(2,1)S(1)} %get-tuple-element.30.after), channel_id=1, source_target_pairs={{0,16},{1,17},{2,18},{3,19},{4,20},{5,21},{6,22},{7,23},{8,24},{9,... | collective-permute-start | bytes 393224 | tf_op jit(solution)/shard_map/ppermute | solution.py:53
  9.7 0.2 shard_map.53.shifts
  9.9 2.7 %collective-permute-done.2.incoming = bf16[2,4,64,128]{3,2,1,0:T(8,128)(2,1)S(1)} collective-permute-done((bf16[2,4,64,128]{3,2,1,0:T(8,128)(2,1)S(1)}, bf16[2,4,64,128]{3,2,1,0:T(8,128)(2,1)S(1)}, u32[]{:S(2)}, u32[]{:S(2)}) %collective-permute-start.2) | collective-permute-done | bytes 131104 | tf_op jit(solution)/shard_map/ppermute | solution.py:53
  12.6 1.2 %shard_map.54 = (bf16[2,4,64,128]{3,2,1,0:T(8,128)(2,1)S(1)}, bf16[768,128]{1,0:T(8,128)(2,1)S(1)}, f32[128,128]{1,0:T(8,128)S(1)}, bf16[560,128]{1,0:T(8,128)(2...) custom-call(s32[1]{0:T(128)} %bitcast.spot, ...), custom_call_target="tpu_custom_call" | custom-call | tf_op jit(solution)/shard_map/pallas_call | solution.py:423
  13.8 2.5 %collective-permute-start.8 = (bf16[432,128]{1,0:T(8,128)(2,1)S(1)}, bf16[432,128]{1,0:T(8,128)(2,1)S(1)}, u32[]{:S(2)}, u32[]{:S(2)}) collective-permute-start(bf16[432,128]{1,0:T(8,128)(2,1)S(1)} %get-tuple-element.37), channel_id=1, source_target_pairs={{0,1},{1,0},{2,3},{3,2},{4,5},{5,4},{6,7},{7,6},{8,9},{9,8},{10,11... | collective-permute-start | bytes 331784 | tf_op jit(solution)/shard_map/ppermute | solution.py:41
  16.3 0.1 collective-permute-start.4
  16.4 0.4 collective-permute-start.6
  16.8 0.1 collective-permute-start.3
  16.9 0.4 collective-permute-done.8.got
  17.3 4.9 %collective-permute-start.9 = (bf16[432,128]{1,0:T(8,128)(2,1)S(1)}, bf16[432,128]{1,0:T(8,128)(2,1)S(1)}, u32[]{:S(2)}, u32[]{:S(2)}) collective-permute-start(bf16[432,128]{1,0:T(8,128)(2,1)S(1)} %shard_map.57), channel_id=1, source_target_pairs={{0,6},{1,7},{2,4},{3,5},{4,2},{5,3},{6,0},{7,1},{8,14},{9,15},{10,... | collective-permute-start | bytes 331784 | tf_op jit(solution)/shard_map/ppermute | solution.py:41
  22.3 0.5 collective-permute-start.5
  22.8 0.0 collective-permute-done.6.got
  22.8 1.0 %collective-permute-start.7 = (bf16[432,128]{1,0:T(8,128)(2,1)S(1)}, bf16[432,128]{1,0:T(8,128)(2,1)S(1)}, u32[]{:S(2)}, u32[]{:S(2)}) collective-permute-start(bf16[432,128]{1,0:T(8,128)(2,1)S(1)} %shard_map.56), channel_id=1, source_target_pairs={{0,2},{1,3},{2,0},{3,1},{4,6},{5,7},{6,4},{7,5},{8,10},{9,11},{10,... | collective-permute-start | bytes 331784 | tf_op jit(solution)/shard_map/ppermute | solution.py:41
  23.9 0.7 %collective-permute-start.10 = (bf16[2,1,64,128]{3,2,1,0:T(8,128)(2,1)S(1)}, bf16[2,1,64,128]{3,2,1,0:T(8,128)(2,1)S(1)}, u32[]{:S(2)}, u32[]{:S(2)}) collective-permute-start(bf16[2,1,64,128]{3,2,1,0:T(8,128)(2,1)S(1)} %get-tuple-element.38), channel_id=1, source_target_pairs={{1,18},{2,17},{3,20},{4,19},{5,22},{6,21},{7,24},{8,23},{9,26},{10... | collective-permute-start | bytes 98312 | tf_op jit(solution)/shard_map/ppermute | solution.py:36
  24.5 0.0 collective-permute-done.10.in_far
  24.6 1.1 %collective-permute-done.9.refs_3_ = bf16[432,128]{1,0:T(8,128)(2,1)S(1)} collective-permute-done((bf16[432,128]{1,0:T(8,128)(2,1)S(1)}, bf16[432,128]{1,0:T(8,128)(2,1)S(1)}, u32[]{:S(2)}, u32[]{:S(2)}) %collective-permute-start.9) | collective-permute-done | bytes 110624 | tf_op jit(solution)/shard_map/ppermute | solution.py:41
  25.7 0.0 collective-permute-done.3.refs_0_.by_near
  25.7 2.5 %collective-permute-done.5.refs_1_ = bf16[432,128]{1,0:T(8,128)(2,1)S(1)} collective-permute-done((bf16[432,128]{1,0:T(8,128)(2,1)S(1)}, bf16[432,128]{1,0:T(8,128)(2,1)S(1)}, u32[]{:S(2)}, u32[]{:S(2)}) %collective-permute-start.5) | collective-permute-done | bytes 110624 | tf_op jit(solution)/shard_map/ppermute | solution.py:41
  28.2 0.0 collective-permute-done.7.refs_2_
  28.2 0.1 shard_map.58.mine
  28.3 5.8 %collective-permute-start.11 = (bf16[432,128]{1,0:T(8,128)(2,1)S(1)}, bf16[432,128]{1,0:T(8,128)(2,1)S(1)}, u32[]{:S(2)}, u32[]{:S(2)}) collective-permute-start(bf16[432,128]{1,0:T(8,128)(2,1)S(1)} %shard_map.58.mine), channel_id=1, source_target_pairs={{0,8},{1,9},{2,10},{3,11},{4,12},{5,13},{6,14},{7,15},{8,0},{9,1},... | collective-permute-start | bytes 331784 | tf_op jit(solution)/shard_map/ppermute | solution.py:41
  34.1 1.8 %shard_map.59 = bf16[2,4,64,128]{3,2,1,0:T(8,128)(2,1)} custom-call(bf16[768,128]{1,0:T(8,128)(2,1)S(1)} %get-tuple-element.40.deltas, bf16[560,128]{1,0:T(8,128)(2,1)S(1)} %collective-permute-done.3.refs_0_.by_near, bf16[2,1,64,128]{3,2,1,0:T(8,128)(2,1)S(1)} %collective-permute-done.10.in_far, f32[128,128]{1,0:T(8,128)S(1)} %get-tuple-element.42.far_slope, ...), custom_call_target="tpu_custom_call" | custom-call | tf_op jit(solution)/shard_map/pallas_call | solution.py:380
  35.9 1.0 %collective-permute-done.11.other = bf16[432,128]{1,0:T(8,128)(2,1)S(1)} collective-permute-done((bf16[432,128]{1,0:T(8,128)(2,1)S(1)}, bf16[432,128]{1,0:T(8,128)(2,1)S(1)}, u32[]{:S(2)}, u32[]{:S(2)}) %collective-permute-start.11) | collective-permute-done | bytes 110624 | tf_op jit(solution)/shard_map/ppermute | solution.py:41
  37.0 2.2 %collective-permute-start.14 = (bf16[432,128]{1,0:T(8,128)(2,1)S(1)}, bf16[432,128]{1,0:T(8,128)(2,1)S(1)}, u32[]{:S(2)}, u32[]{:S(2)}) collective-permute-start(bf16[432,128]{1,0:T(8,128)(2,1)S(1)} %shard_map.60.refs_0_.refs_4_), channel_id=1, source_target_pairs={{0,6},{1,7},{2,4},{3,5},{4,2},{5,3},{6,0},{7,1},{8,14},{9,15},{10,... | collective-permute-start | bytes 331784 | tf_op jit(solution)/shard_map/ppermute | solution.py:41
  39.1 1.5 %collective-permute-start.13 = (bf16[432,128]{1,0:T(8,128)(2,1)S(1)}, bf16[432,128]{1,0:T(8,128)(2,1)S(1)}, u32[]{:S(2)}, u32[]{:S(2)}) collective-permute-start(bf16[432,128]{1,0:T(8,128)(2,1)S(1)} %shard_map.60.refs_0_.refs_4_), channel_id=1, source_target_pairs={{0,2},{1,3},{2,0},{3,1},{4,6},{5,7},{6,4},{7,5},{8,10},{9,11},{10,... | collective-permute-start | bytes 331784 | tf_op jit(solution)/shard_map/ppermute | solution.py:41
  40.6 1.2 %collective-permute-start.12 = (bf16[432,128]{1,0:T(8,128)(2,1)S(1)}, bf16[432,128]{1,0:T(8,128)(2,1)S(1)}, u32[]{:S(2)}, u32[]{:S(2)}) collective-permute-start(bf16[432,128]{1,0:T(8,128)(2,1)S(1)} %shard_map.60.refs_0_.refs_4_), channel_id=1, source_target_pairs={{0,4},{1,5},{2,6},{3,7},{4,0},{5,1},{6,2},{7,3},{8,12},{9,13},{10,... | collective-permute-start | bytes 331784 | tf_op jit(solution)/shard_map/ppermute | solution.py:41
  41.9 0.0 collective-permute-start.15
  41.9 0.9 %collective-permute-done.14.refs_3_.refs_7_ = bf16[432,128]{1,0:T(8,128)(2,1)S(1)} collective-permute-done((bf16[432,128]{1,0:T(8,128)(2,1)S(1)}, bf16[432,128]{1,0:T(8,128)(2,1)S(1)}, u32[]{:S(2)}, u32[]{:S(2)}) %collective-permute-start.14) | collective-permute-done | bytes 110624 | tf_op jit(solution)/shard_map/ppermute | solution.py:41
  42.8 2.5 %collective-permute-done.13.refs_2_.refs_6_ = bf16[432,128]{1,0:T(8,128)(2,1)S(1)} collective-permute-done((bf16[432,128]{1,0:T(8,128)(2,1)S(1)}, bf16[432,128]{1,0:T(8,128)(2,1)S(1)}, u32[]{:S(2)}, u32[]{:S(2)}) %collective-permute-start.13) | collective-permute-done | bytes 110624 | tf_op jit(solution)/shard_map/ppermute | solution.py:41
  45.3 0.0 collective-permute-start.17
  45.3 1.8 %collective-permute-done.12.refs_1_.refs_5_ = bf16[432,128]{1,0:T(8,128)(2,1)S(1)} collective-permute-done((bf16[432,128]{1,0:T(8,128)(2,1)S(1)}, bf16[432,128]{1,0:T(8,128)(2,1)S(1)}, u32[]{:S(2)}, u32[]{:S(2)}) %collective-permute-start.12) | collective-permute-done | bytes 110624 | tf_op jit(solution)/shard_map/ppermute | solution.py:41
  47.2 0.0 collective-permute-start.16
  47.2 0.1 shard_map.61.refs_0_
  47.3 0.5 %collective-permute-start.20 = (f32[8,128]{1,0:T(8,128)S(1)}, f32[8,128]{1,0:T(8,128)S(1)}, u32[]{:S(2)}, u32[]{:S(2)}) collective-permute-start(f32[8,128]{1,0:T(8,128)S(1)} %shard_map.61.refs_0_), channel_id=1, source_target_pairs={{0,17},{1,16},{2,19},{3,18},{4,21},{5,20},{6,23},{7,22},{8,25},{9,... | collective-permute-start | bytes 12296 | tf_op jit(solution)/shard_map/ppermute | solution.py:53
  47.8 1.7 %collective-permute-start.19 = (f32[8,128]{1,0:T(8,128)S(1)}, f32[8,128]{1,0:T(8,128)S(1)}, u32[]{:S(2)}, u32[]{:S(2)}) collective-permute-start(f32[8,128]{1,0:T(8,128)S(1)} %shard_map.61.refs_0_), channel_id=1, source_target_pairs={{0,16},{1,17},{2,18},{3,19},{4,20},{5,21},{6,22},{7,23},{8,24},{9,... | collective-permute-start | bytes 12296 | tf_op jit(solution)/shard_map/ppermute | solution.py:53
  49.5 0.0 collective-permute-done.18.refs_3_.refs_11_
  49.5 0.0 collective-permute-done.17.refs_2_.refs_10_
  49.5 0.0 collective-permute-done.16.refs_1_.refs_9_
  49.5 0.1 shard_map.62.refs_1_
  49.6 0.8 %collective-permute-done.20.refs_3_ = f32[8,128]{1,0:T(8,128)S(1)} collective-permute-done((f32[8,128]{1,0:T(8,128)S(1)}, f32[8,128]{1,0:T(8,128)S(1)}, u32[]{:S(2)}, u32[]{:S(2)}) %collective-permute-start.20) | collective-permute-done | bytes 4128 | tf_op jit(solution)/shard_map/ppermute | solution.py:53
  50.4 1.1 %collective-permute-done.19.refs_2_ = f32[8,128]{1,0:T(8,128)S(1)} collective-permute-done((f32[8,128]{1,0:T(8,128)S(1)}, f32[8,128]{1,0:T(8,128)S(1)}, u32[]{:S(2)}, u32[]{:S(2)}) %collective-permute-start.19) | collective-permute-done | bytes 4128 | tf_op jit(solution)/shard_map/ppermute | solution.py:53
  51.5 1.4 %shard_map.63 = f32[8,432,128]{2,1,0:T(8,128)} custom-call(s32[1]{0:T(128)} %bitcast.spot, f32[8,128]{1,0:T(8,128)S(1)} %shard_map.61.refs_0_, f32[8,128]{1,0:T(8,128)S(1)} %shard_map.62.refs_1_, f32[8,128]{1,0:T(8,128)S(1)} %collective-permute-done.19.refs_2_, f32[8,128]{1,0:T(8,128)S(1)} %collective-permute-done.20.refs_3_, ...), custom_call_target="tpu_custom_call" | custom-call | tf_op jit(solution)/shard_map/pallas_call | solution.py:516
  (8 shorter events, 0.1 us)
Async XLA Ops:
  1.6 3.6 %collective-permute-start = (bf16[2,3,64,128]{3,2,1,0:T(8,128)(2,1)S(1)}, bf16[2,3,64,128]{3,2,1,0:T(8,128)(2,1)S(1)}, u32[]{:S(2)}, u32[]{:S(2)}) collective-permute-start(bf16[2,3,64,128]{3,2,1,0:T(8,128)(2,1)S(1)} %get-tuple-element.24), channel_id=1, source_target_pairs={{0,1},{1,0},{2,3},{3,2},{4,5},{5,4},{6,7},{7,6},{8,9},{9,8},{10,11... | collective-permute-start | bytes 294920 | tf_op jit(solution)/shard_map/ppermute | solution.py:26
  2.1 3.1 %collective-permute-start.1 = (bf16[2,3,64,128]{3,2,1,0:T(8,128)(2,1)S(1)}, bf16[2,3,64,128]{3,2,1,0:T(8,128)(2,1)S(1)}, u32[]{:S(2)}, u32[]{:S(2)}) collective-permute-start(bf16[2,3,64,128]{3,2,1,0:T(8,128)(2,1)S(1)} %get-tuple-element.25), channel_id=1, source_target_pairs={{1,2},{2,1},{3,4},{4,3},{5,6},{6,5},{7,8},{8,7},{9,10},{10,9},{11,... | collective-permute-start | bytes 294920 | tf_op jit(solution)/shard_map/ppermute | solution.py:26
  7.1 5.5 %collective-permute-start.2 = (bf16[2,4,64,128]{3,2,1,0:T(8,128)(2,1)S(1)}, bf16[2,4,64,128]{3,2,1,0:T(8,128)(2,1)S(1)}, u32[]{:S(2)}, u32[]{:S(2)}) collective-permute-start(bf16[2,4,64,128]{3,2,1,0:T(8,128)(2,1)S(1)} %get-tuple-element.30.after), channel_id=1, source_target_pairs={{0,16},{1,17},{2,18},{3,19},{4,20},{5,21},{6,22},{7,23},{8,24},{9,... | collective-permute-start | bytes 393224 | tf_op jit(solution)/shard_map/ppermute | solution.py:53
  13.8 3.4 %collective-permute-start.8 = (bf16[432,128]{1,0:T(8,128)(2,1)S(1)}, bf16[432,128]{1,0:T(8,128)(2,1)S(1)}, u32[]{:S(2)}, u32[]{:S(2)}) collective-permute-start(bf16[432,128]{1,0:T(8,128)(2,1)S(1)} %get-tuple-element.37), channel_id=1, source_target_pairs={{0,1},{1,0},{2,3},{3,2},{4,5},{5,4},{6,7},{7,6},{8,9},{9,8},{10,11... | collective-permute-start | bytes 331784 | tf_op jit(solution)/shard_map/ppermute | solution.py:41
  16.3 5.9 %collective-permute-start.4 = (bf16[432,128]{1,0:T(8,128)(2,1)S(1)}, bf16[432,128]{1,0:T(8,128)(2,1)S(1)}, u32[]{:S(2)}, u32[]{:S(2)}) collective-permute-start(bf16[432,128]{1,0:T(8,128)(2,1)S(1)} %get-tuple-element.35), channel_id=1, source_target_pairs={{0,1},{1,0},{2,3},{3,2},{4,5},{5,4},{6,7},{7,6},{8,9},{9,8},{10,11... | collective-permute-start | bytes 331784 | tf_op jit(solution)/shard_map/ppermute | solution.py:41
  16.4 6.4 %collective-permute-start.6 = (bf16[432,128]{1,0:T(8,128)(2,1)S(1)}, bf16[432,128]{1,0:T(8,128)(2,1)S(1)}, u32[]{:S(2)}, u32[]{:S(2)}) collective-permute-start(bf16[432,128]{1,0:T(8,128)(2,1)S(1)} %get-tuple-element.36), channel_id=1, source_target_pairs={{0,1},{1,0},{2,3},{3,2},{4,5},{5,4},{6,7},{7,6},{8,9},{9,8},{10,11... | collective-permute-start | bytes 331784 | tf_op jit(solution)/shard_map/ppermute | solution.py:41
  16.8 8.9 %collective-permute-start.3 = (bf16[560,128]{1,0:T(8,128)(2,1)S(1)}, bf16[560,128]{1,0:T(8,128)(2,1)S(1)}, u32[]{:S(2)}, u32[]{:S(2)}) collective-permute-start(bf16[560,128]{1,0:T(8,128)(2,1)S(1)} %get-tuple-element.34), channel_id=1, source_target_pairs={{0,1},{1,0},{2,3},{3,2},{4,5},{5,4},{6,7},{7,6},{8,9},{9,8},{10,11... | collective-permute-start | bytes 430088 | tf_op jit(solution)/shard_map/ppermute | solution.py:41
  17.3 8.4 %collective-permute-start.9 = (bf16[432,128]{1,0:T(8,128)(2,1)S(1)}, bf16[432,128]{1,0:T(8,128)(2,1)S(1)}, u32[]{:S(2)}, u32[]{:S(2)}) collective-permute-start(bf16[432,128]{1,0:T(8,128)(2,1)S(1)} %shard_map.57), channel_id=1, source_target_pairs={{0,6},{1,7},{2,4},{3,5},{4,2},{5,3},{6,0},{7,1},{8,14},{9,15},{10,... | collective-permute-start | bytes 331784 | tf_op jit(solution)/shard_map/ppermute | solution.py:41
  22.3 5.9 %collective-permute-start.5 = (bf16[432,128]{1,0:T(8,128)(2,1)S(1)}, bf16[432,128]{1,0:T(8,128)(2,1)S(1)}, u32[]{:S(2)}, u32[]{:S(2)}) collective-permute-start(bf16[432,128]{1,0:T(8,128)(2,1)S(1)} %shard_map.55), channel_id=1, source_target_pairs={{0,4},{1,5},{2,6},{3,7},{4,0},{5,1},{6,2},{7,3},{8,12},{9,13},{10,... | collective-permute-start | bytes 331784 | tf_op jit(solution)/shard_map/ppermute | solution.py:41
  22.8 5.3 %collective-permute-start.7 = (bf16[432,128]{1,0:T(8,128)(2,1)S(1)}, bf16[432,128]{1,0:T(8,128)(2,1)S(1)}, u32[]{:S(2)}, u32[]{:S(2)}) collective-permute-start(bf16[432,128]{1,0:T(8,128)(2,1)S(1)} %shard_map.56), channel_id=1, source_target_pairs={{0,2},{1,3},{2,0},{3,1},{4,6},{5,7},{6,4},{7,5},{8,10},{9,11},{10,... | collective-permute-start | bytes 331784 | tf_op jit(solution)/shard_map/ppermute | solution.py:41
  23.9 0.7 %collective-permute-start.10 = (bf16[2,1,64,128]{3,2,1,0:T(8,128)(2,1)S(1)}, bf16[2,1,64,128]{3,2,1,0:T(8,128)(2,1)S(1)}, u32[]{:S(2)}, u32[]{:S(2)}) collective-permute-start(bf16[2,1,64,128]{3,2,1,0:T(8,128)(2,1)S(1)} %get-tuple-element.38), channel_id=1, source_target_pairs={{1,18},{2,17},{3,20},{4,19},{5,22},{6,21},{7,24},{8,23},{9,26},{10... | collective-permute-start | bytes 98312 | tf_op jit(solution)/shard_map/ppermute | solution.py:36
  28.3 8.7 %collective-permute-start.11 = (bf16[432,128]{1,0:T(8,128)(2,1)S(1)}, bf16[432,128]{1,0:T(8,128)(2,1)S(1)}, u32[]{:S(2)}, u32[]{:S(2)}) collective-permute-start(bf16[432,128]{1,0:T(8,128)(2,1)S(1)} %shard_map.58.mine), channel_id=1, source_target_pairs={{0,8},{1,9},{2,10},{3,11},{4,12},{5,13},{6,14},{7,15},{8,0},{9,1},... | collective-permute-start | bytes 331784 | tf_op jit(solution)/shard_map/ppermute | solution.py:41
  37.0 5.8 %collective-permute-start.14 = (bf16[432,128]{1,0:T(8,128)(2,1)S(1)}, bf16[432,128]{1,0:T(8,128)(2,1)S(1)}, u32[]{:S(2)}, u32[]{:S(2)}) collective-permute-start(bf16[432,128]{1,0:T(8,128)(2,1)S(1)} %shard_map.60.refs_0_.refs_4_), channel_id=1, source_target_pairs={{0,6},{1,7},{2,4},{3,5},{4,2},{5,3},{6,0},{7,1},{8,14},{9,15},{10,... | collective-permute-start | bytes 331784 | tf_op jit(solution)/shard_map/ppermute | solution.py:41
  39.1 6.2 %collective-permute-start.13 = (bf16[432,128]{1,0:T(8,128)(2,1)S(1)}, bf16[432,128]{1,0:T(8,128)(2,1)S(1)}, u32[]{:S(2)}, u32[]{:S(2)}) collective-permute-start(bf16[432,128]{1,0:T(8,128)(2,1)S(1)} %shard_map.60.refs_0_.refs_4_), channel_id=1, source_target_pairs={{0,2},{1,3},{2,0},{3,1},{4,6},{5,7},{6,4},{7,5},{8,10},{9,11},{10,... | collective-permute-start | bytes 331784 | tf_op jit(solution)/shard_map/ppermute | solution.py:41
  40.6 6.6 %collective-permute-start.12 = (bf16[432,128]{1,0:T(8,128)(2,1)S(1)}, bf16[432,128]{1,0:T(8,128)(2,1)S(1)}, u32[]{:S(2)}, u32[]{:S(2)}) collective-permute-start(bf16[432,128]{1,0:T(8,128)(2,1)S(1)} %shard_map.60.refs_0_.refs_4_), channel_id=1, source_target_pairs={{0,4},{1,5},{2,6},{3,7},{4,0},{5,1},{6,2},{7,3},{8,12},{9,13},{10,... | collective-permute-start | bytes 331784 | tf_op jit(solution)/shard_map/ppermute | solution.py:41
  41.9 6.0 %collective-permute-start.15 = (bf16[432,128]{1,0:T(8,128)(2,1)S(1)}, bf16[432,128]{1,0:T(8,128)(2,1)S(1)}, u32[]{:S(2)}, u32[]{:S(2)}) collective-permute-start(bf16[432,128]{1,0:T(8,128)(2,1)S(1)} %shard_map.60.refs_0_.refs_4_), channel_id=1, source_target_pairs={{0,1},{1,0},{2,3},{3,2},{4,5},{5,4},{6,7},{7,6},{8,9},{9,8},{10,11... | collective-permute-start | bytes 331784 | tf_op jit(solution)/shard_map/ppermute | solution.py:41
  42.8 6.7 %collective-permute-start.18 = (bf16[432,128]{1,0:T(8,128)(2,1)S(1)}, bf16[432,128]{1,0:T(8,128)(2,1)S(1)}, u32[]{:S(2)}, u32[]{:S(2)}) collective-permute-start(bf16[432,128]{1,0:T(8,128)(2,1)S(1)} %collective-permute-done.14.refs_3_.refs_7_), channel_id=1, source_target_pairs={{0,1},{1,0},{2,3},{3,2},{4,5},{5,4},{6,7},{7,6},{8,9},{9,8},{10,11... | collective-permute-start | bytes 331784 | tf_op jit(solution)/shard_map/ppermute | solution.py:41
  45.3 4.2 %collective-permute-start.17 = (bf16[432,128]{1,0:T(8,128)(2,1)S(1)}, bf16[432,128]{1,0:T(8,128)(2,1)S(1)}, u32[]{:S(2)}, u32[]{:S(2)}) collective-permute-start(bf16[432,128]{1,0:T(8,128)(2,1)S(1)} %collective-permute-done.13.refs_2_.refs_6_), channel_id=1, source_target_pairs={{0,1},{1,0},{2,3},{3,2},{4,5},{5,4},{6,7},{7,6},{8,9},{9,8},{10,11... | collective-permute-start | bytes 331784 | tf_op jit(solution)/shard_map/ppermute | solution.py:41
  47.2 2.3 %collective-permute-start.16 = (bf16[432,128]{1,0:T(8,128)(2,1)S(1)}, bf16[432,128]{1,0:T(8,128)(2,1)S(1)}, u32[]{:S(2)}, u32[]{:S(2)}) collective-permute-start(bf16[432,128]{1,0:T(8,128)(2,1)S(1)} %collective-permute-done.12.refs_1_.refs_5_), channel_id=1, source_target_pairs={{0,1},{1,0},{2,3},{3,2},{4,5},{5,4},{6,7},{7,6},{8,9},{9,8},{10,11... | collective-permute-start | bytes 331784 | tf_op jit(solution)/shard_map/ppermute | solution.py:41
  47.3 3.1 %collective-permute-start.20 = (f32[8,128]{1,0:T(8,128)S(1)}, f32[8,128]{1,0:T(8,128)S(1)}, u32[]{:S(2)}, u32[]{:S(2)}) collective-permute-start(f32[8,128]{1,0:T(8,128)S(1)} %shard_map.61.refs_0_), channel_id=1, source_target_pairs={{0,17},{1,16},{2,19},{3,18},{4,21},{5,20},{6,23},{7,22},{8,25},{9,... | collective-permute-start | bytes 12296 | tf_op jit(solution)/shard_map/ppermute | solution.py:53
  47.8 3.6 %collective-permute-start.19 = (f32[8,128]{1,0:T(8,128)S(1)}, f32[8,128]{1,0:T(8,128)S(1)}, u32[]{:S(2)}, u32[]{:S(2)}) collective-permute-start(f32[8,128]{1,0:T(8,128)S(1)} %shard_map.61.refs_0_), channel_id=1, source_target_pairs={{0,16},{1,17},{2,18},{3,19},{4,20},{5,21},{6,22},{7,23},{8,24},{9,... | collective-permute-start | bytes 12296 | tf_op jit(solution)/shard_map/ppermute | solution.py:53
